TPU v7x, 32 devices: a whole 2x2x4 slice. The times are simulated.
32 devices in a mesh: dp: 8 (over z, y), tensor: 4 (over x, core).
Axes of the slice: x: 2, y: 2, z: 4, core: 2. Of those that a mesh axis runs over, the one named last changes fastest.
Arguments:
- tokens: bfloat16 [16384, 768], P('dp'), may hold values from -6 to 6
- first_gain: float32 [768], replicated, may hold values from 0.5 to 1.5
- first_bias: float32 [768], replicated, may hold values from -1.5 to 1.5
- query_weight: bfloat16 [768, 768], P(None, 'tensor'), may hold values from -0.21875 to 0.21875
- key_weight: bfloat16 [768, 768], P(None, 'tensor'), may hold values from -0.21875 to 0.21875
- value_weight: bfloat16 [768, 768], P(None, 'tensor'), may hold values from -0.21875 to 0.21875
- output_weight: bfloat16 [768, 768], P('tensor'), may hold values from -3.5 to 3.5
- second_gain: float32 [768], replicated, may hold values from 0.5 to 1.5
- second_bias: float32 [768], replicated, may hold values from -1.5 to 1.5
- expert_up: bfloat16 [8, 768, 3072], P('dp'), may hold values from -0.21875 to 0.21875
- expert_down: bfloat16 [8, 3072, 768], P('dp'), may hold values from -0.109375 to 0.109375
- item_lengths: int32 [8, 5], P('dp'), may hold values from 64 to 1024, as said below
- routes: int32 [16384, 1], P(('dp', 'tensor')), may hold values from 0 to 7
- slot_order: int32 [32, 512], P(('dp', 'tensor')), may hold values from 0 to 511, each once within a row
- cotangent: bfloat16 [16384, 768], P(('dp', 'tensor')), may hold values from -6 to 6
Outputs:
- block_out: float32 [16384, 768], P(('dp', 'tensor'))
- token_grad: float32 [16384, 768], P(('dp', 'tensor'))
- first_gain_grad: float32 [768], replicated
- first_bias_grad: float32 [768], replicated
- query_grad: float32 [768, 768], P(None, 'tensor')
- key_grad: float32 [768, 768], P(None, 'tensor')
- value_grad: float32 [768, 768], P(None, 'tensor')
- output_grad: float32 [768, 768], P('tensor')
- second_gain_grad: float32 [768], replicated
- second_bias_grad: float32 [768], replicated
- expert_up_grad: float32 [8, 768, 3072], P('dp', None, 'tensor')
- expert_down_grad: float32 [8, 3072, 768], P('dp', 'tensor')
Inputs may be any that keep to these rules, and one draw needn't show every extreme that they name: `item_lengths`: each dp index holds 5 items laid end to end from its first slot, their lengths summing to at most 2048; its remaining slots are padding. In every draw some item has exactly 1024 slots and some exactly 64. Padding slots have routes too. `slot_order`: each row is a permutation of the numbers 0 to 511.
All inputs are finite; a program needn't handle non-finite values.
Results may differ from a plain program's by a relative error of at most 0.019.
Values may be sent and summed in bfloat16 or wider, within the bound.
No kernel may reach another device: no remote copies, remote signals or barrier semaphores. Data moves between devices by JAX's collectives and lax.ppermute only.
A program may use at most 128 MiB of HBM per device.

v0:
```python
import functools

import jax
import jax.numpy as jnp
from jax import lax
from jax.experimental import pallas as pl
from jax.experimental.pallas import tpu as pltpu
from jax.sharding import PartitionSpec as P

HEAD_DIM = 64
EPSILON = 1e-05
NEGATIVE = -1e30
f32 = jnp.float32
bf16 = jnp.bfloat16
VMEM = pl.BlockSpec(memory_space=pltpu.VMEM)
SMEM = pl.BlockSpec(memory_space=pltpu.SMEM)


def layer_norm(values, gain, shift):
    average = jnp.mean(values, axis=-1, keepdims=True)
    centred = values - average
    variance = jnp.mean(centred * centred, axis=-1, keepdims=True)
    return centred * lax.rsqrt(variance + EPSILON) * gain + shift


def contract_rows(left, right):
    return lax.dot_general(
        left, right, (((0,), (0,)), ((), ())), preferred_element_type=f32
    )


def swap(values, axis, step):
    count = lax.axis_size(axis)
    return lax.ppermute(values, axis, [(i, i ^ step) for i in range(count)])


def steps_of(count):
    steps = []
    step = 1
    while step < count:
        steps.append(step)
        step *= 2
    return steps


def normalized(values):
    average = jnp.mean(values, axis=-1, keepdims=True)
    centred = values - average
    variance = jnp.mean(centred * centred, axis=-1, keepdims=True)
    return centred * lax.rsqrt(variance + EPSILON)


def project_kernel(
    rank_ref, tokens_ref, gain_ref, bias_ref, qw_ref, kw_ref, vw_ref,
    normed_ref, qt_ref, kt_ref, vt_ref,
):
    values = tokens_ref[...].astype(f32)
    normed = (normalized(values) * gain_ref[...] + bias_ref[...]).astype(bf16)
    normed_ref[...] = normed
    for weight_ref, out_ref, factor in (
        (qw_ref, qt_ref, HEAD_DIM ** (-0.5)), (kw_ref, kt_ref, None), (vw_ref, vt_ref, None)
    ):
        made = lax.dot_general(
            weight_ref[...], normed, (((1,), (1,)), ((), ())), preferred_element_type=f32
        ).astype(bf16)
        if factor is not None:
            made = made * jnp.asarray(factor, bf16)
        out_ref[...] = made


def project(rank, tokens, gain, bias, qw, kw, vw, blocks):
    slots, width = tokens.shape
    cols = qw.shape[0]
    size = slots // blocks
    fixed = lambda i, r: (0, 0)
    return pl.pallas_call(
        project_kernel,
        grid_spec=pltpu.PrefetchScalarGridSpec(
            num_scalar_prefetch=1,
            grid=(blocks,),
            in_specs=[
                pl.BlockSpec((size, width), lambda i, r: (i ^ r[0], 0)),
                pl.BlockSpec((1, width), fixed),
                pl.BlockSpec((1, width), fixed),
                pl.BlockSpec((cols, width), fixed),
                pl.BlockSpec((cols, width), fixed),
                pl.BlockSpec((cols, width), fixed),
            ],
            out_specs=(
                pl.BlockSpec((size, width), lambda i, r: (i, 0)),
                pl.BlockSpec((cols, size), lambda i, r: (0, i)),
                pl.BlockSpec((cols, size), lambda i, r: (0, i)),
                pl.BlockSpec((cols, size), lambda i, r: (0, i)),
            ),
        ),
        out_shape=(jax.ShapeDtypeStruct((slots, width), bf16),)
        + (jax.ShapeDtypeStruct((cols, slots), bf16),) * 3,
        name="project",
        cost_estimate=pl.CostEstimate(
            flops=6 * slots * width * cols, bytes_accessed=6 * slots * width,
            transcendentals=slots,
        ),
    )(rank, tokens, gain[None], bias[None], qw, kw, vw)


def item_ends(lens_ref):
    ends = []
    total = jnp.int32(0)
    for i in range(lens_ref.shape[1]):
        total = total + lens_ref[0, i]
        ends.append(total)
    return ends


def segments_at(place, ends):
    segment = jnp.zeros_like(place)
    for end in ends:
        segment = segment + (place >= end).astype(jnp.int32)
    return segment


def block_span(first, size, unit, ends):
    last = jnp.minimum(first + size, ends[-1]) - 1
    low = jnp.int32(0)
    high = ends[-1]
    for end in ends:
        low = jnp.where(first >= end, end, low)
    for end in reversed(ends):
        high = jnp.where(last < end, end, high)
    empty = first >= ends[-1]
    low_block = jnp.where(empty, 0, low // unit)
    high_block = jnp.where(empty, 0, (high + unit - 1) // unit)
    return low_block, high_block


def rows_at(block, size):
    return pl.ds(pl.multiple_of(block * size, size), size)


def memory_segments(block, size, shard, rank, ends, axis):
    shape = (1, size) if axis else (size, 1)
    at = block * size + lax.broadcasted_iota(jnp.int32, shape, axis)
    place = ((at // shard) ^ rank) * shard + at % shard
    return segments_at(place, ends)


def lane_masked(values, head):
    lane = lax.broadcasted_iota(jnp.int32, values.shape, 1)
    inside = (lane >= head * HEAD_DIM) & (lane < (head + 1) * HEAD_DIM)
    return jnp.where(inside, values, jnp.zeros_like(values))


def forward_kernel(
    lens_ref, rank_ref, qt_ref, kt_ref, vt_ref, out_ref, log_ref, masked_ref
):
    blocks, width, shard = out_ref.shape
    heads = width // HEAD_DIM
    pair = 1
    size = shard * pair
    rank = rank_ref[0, 0]
    ends = item_ends(lens_ref)
    keys = jnp.transpose(kt_ref[...], (1, 0))
    for h in range(heads):
        masked_ref[h] = lane_masked(keys, h)

    def query_block(i, unused):
        at = i ^ (rank // pair)
        cols = rows_at(at, size)
        seg_q = memory_segments(at, size, shard, rank, ends, 1)
        queries = qt_ref[:, cols]

        def key_block(j, carry):
            rows = rows_at(j ^ rank, shard)
            seg_k = memory_segments(j ^ rank, shard, shard, rank, ends, 0)
            same = seg_k == seg_q
            result = []
            for h in range(heads):
                highest, summed, total = carry[h]
                scores = jnp.dot(
                    masked_ref[h, rows, :], queries, preferred_element_type=f32
                )
                scores = jnp.where(same, scores, NEGATIVE)
                raised = jnp.maximum(highest, jnp.max(scores, axis=0, keepdims=True))
                shrink = jnp.exp(highest - raised)
                soft = jnp.exp(scores - raised)
                summed = summed * shrink + jnp.sum(soft, axis=0, keepdims=True)
                total = total * shrink + jnp.dot(
                    vt_ref[pl.ds(h * HEAD_DIM, HEAD_DIM), rows],
                    soft.astype(bf16),
                    preferred_element_type=f32,
                )
                result.append((raised, summed, total))
            return tuple(result)

        start = tuple(
            (
                jnp.full((1, size), NEGATIVE, f32),
                jnp.zeros((1, size), f32),
                jnp.zeros((HEAD_DIM, size), f32),
            )
            for h in range(heads)
        )
        low, high = block_span(i * size, size, shard, ends)
        done = lax.fori_loop(low, high, key_block, start)
        live = seg_q < len(ends)
        for h in range(heads):
            highest, summed, total = done[h]
            summed = jnp.where(live, summed, 1.0)
            result = jnp.where(live, total / summed, 0.0).astype(bf16)
            logs = jnp.where(live, highest + jnp.log(summed), -NEGATIVE)
            for p in range(pair):
                part = slice(p * shard, (p + 1) * shard)
                out_ref[at * pair + p, pl.ds(h * HEAD_DIM, HEAD_DIM), :] = result[:, part]
            log_ref[h, :, cols] = logs
        return unused

    lax.fori_loop(0, blocks // pair, query_block, 0)


def attend(lens, rank, qt, kt, vt, blocks):
    width, slots = qt.shape
    size = slots // blocks
    heads = width // HEAD_DIM
    return pl.pallas_call(
        forward_kernel,
        out_shape=(
            jax.ShapeDtypeStruct((blocks, width, size), bf16),
            jax.ShapeDtypeStruct((heads, 1, slots), f32),
        ),
        in_specs=[SMEM, SMEM, VMEM, VMEM, VMEM],
        out_specs=(VMEM, VMEM),
        scratch_shapes=[pltpu.VMEM((heads, slots, width), bf16)],
        name="attend",
        compiler_params=pltpu.CompilerParams(vmem_limit_bytes=60 * 2**20),
        cost_estimate=pl.CostEstimate(
            flops=slots * slots * width * 3, bytes_accessed=6 * slots * width,
            transcendentals=slots * slots * heads // 2,
        ),
    )(lens, rank, qt, kt, vt)


def backward_kernel(
    first_head, heads, lens_ref, rank_ref, qt_ref, kt_ref, vt_ref, out_ref, log_ref, *rest
):
    blocks, width, shard = out_ref.shape
    dim = HEAD_DIM
    grad_refs = rest[:blocks]
    joint_ref, kv_ref, q0_ref, og_ref, right_ref, inner_ref, dq_ref = rest[blocks:]
    slots = blocks * shard
    unit = shard // 2
    rank = rank_ref[0, 0]
    ends = item_ends(lens_ref)
    zero = jnp.zeros((dim, slots), bf16)
    for n in range(heads):
        part = slice((first_head + n) * dim, (first_head + n + 1) * dim)
        both = jnp.concatenate([kt_ref[part, :], vt_ref[part, :]], axis=0)
        kv_ref[n] = jnp.transpose(both, (1, 0))
        padded = jnp.concatenate([qt_ref[part, :], zero], axis=0)
        q0_ref[n] = jnp.transpose(padded, (1, 0))
        right_ref[n, 0] = padded
        for b in range(blocks):
            grad = grad_refs[b][part, :]
            cols = slice(b * shard, (b + 1) * shard)
            padded = jnp.concatenate([zero[:, :shard], grad], axis=0)
            og_ref[n, cols, :] = jnp.transpose(padded, (1, 0))
            right_ref[n, 1, :, cols] = padded
            inner_ref[n, :, cols] = jnp.sum(
                out_ref[b, part, :].astype(f32) * grad.astype(f32), axis=0, keepdims=True
            )
    dq_ref[...] = jnp.zeros_like(dq_ref)

    def key_block(j, unused):
        at_key = ((j // 2) ^ rank) * 2 + j % 2
        rows = rows_at(at_key, unit)
        seg_k = memory_segments(at_key, unit, shard, rank, ends, 0)

        def query_block(i, totals):
            at = i ^ rank
            cols = rows_at(at, shard)
            same = seg_k == memory_segments(at, shard, shard, rank, ends, 1)
            result = []
            for n in range(heads):
                head = first_head + n
                kv = kv_ref[n, rows, :]
                scores = jnp.dot(kv, right_ref[n, 0, :, cols], preferred_element_type=f32)
                grad_soft = jnp.dot(kv, right_ref[n, 1, :, cols], preferred_element_type=f32)
                soft = jnp.where(same, jnp.exp(scores - log_ref[head, :, cols]), 0.0)
                grad_scores = (soft * (grad_soft - inner_ref[n, :, cols])).astype(bf16)
                total = totals[n] + jnp.dot(
                    soft.astype(bf16), og_ref[n, cols, :], preferred_element_type=f32
                )
                total = total + jnp.dot(
                    grad_scores, q0_ref[n, cols, :], preferred_element_type=f32
                )
                dq_ref[n, :, cols] += jnp.dot(
                    kt_ref[pl.ds(head * dim, dim), rows], grad_scores,
                    preferred_element_type=f32,
                )
                result.append(total)
            return tuple(result)

        low, high = block_span(j * unit, unit, shard, ends)
        start = (jnp.zeros((unit, 2 * dim), f32),) * heads
        totals = lax.fori_loop(low, high, query_block, start)
        for n in range(heads):
            joint_ref[rows, 2 * dim * n : 2 * dim * (n + 1)] = totals[n].astype(bf16)
        return unused

    lax.fori_loop(0, 2 * blocks, key_block, 0)
    dq = (dq_ref[...] * dim ** (-0.5)).astype(bf16).reshape(heads * dim, slots)
    joint_ref[:, 2 * dim * heads :] = jnp.transpose(dq, (1, 0))


def attend_back(first_head, heads, lens, rank, qt, kt, vt, out, logs, grads):
    blocks, width, size = out.shape
    slots = blocks * size
    dim = HEAD_DIM
    return pl.pallas_call(
        functools.partial(backward_kernel, first_head, heads),
        out_shape=jax.ShapeDtypeStruct((slots, 3 * dim * heads), bf16),
        in_specs=[SMEM, SMEM] + [VMEM] * (5 + blocks),
        out_specs=VMEM,
        scratch_shapes=[pltpu.VMEM((heads, slots, 2 * dim), bf16)] * 3
        + [
            pltpu.VMEM((heads, 2, 2 * dim, slots), bf16),
            pltpu.VMEM((heads, 1, slots), f32),
            pltpu.VMEM((heads, dim, slots), f32),
        ],
        name="attend_back",
        compiler_params=pltpu.CompilerParams(vmem_limit_bytes=60 * 2**20),
        cost_estimate=pl.CostEstimate(
            flops=slots * slots * dim * heads * 8, bytes_accessed=14 * slots * dim * heads,
            transcendentals=slots * slots * heads // 2,
        ),
    )(lens, rank, qt, kt, vt, out, logs, *grads)


def plan_kernel(capacity, lens_ref, rank_ref, routes_ref, order_ref, grad_ref,
                dispatch_ref, slots_ref):
    shard = routes_ref.shape[1]
    first = rank_ref[0, 0] * shard
    ends = item_ends(lens_ref)
    chosen_row = routes_ref[...]
    chosen_col = jnp.transpose(jnp.broadcast_to(chosen_row, (128, shard)), (1, 0))[:, 0:1]
    order_row = order_ref[...]
    order_col = jnp.transpose(jnp.broadcast_to(order_row, (128, shard)), (1, 0))[:, 0:1]
    alive_row = segments_at(
        first + lax.broadcasted_iota(jnp.int32, (1, shard), 1), ends
    ) < len(ends)
    alive_col = segments_at(
        first + lax.broadcasted_iota(jnp.int32, (shard, 1), 0), ends
    ) < len(ends)
    ahead = (chosen_col == chosen_row) & (order_col < order_row) & alive_col
    ranked = jnp.sum(ahead.astype(jnp.int32), axis=0, keepdims=True)
    kept = alive_row & (ranked < capacity)
    slot = jnp.where(kept, chosen_row * capacity + ranked, -1)
    dispatch = (
        lax.broadcasted_iota(jnp.int32, dispatch_ref.shape, 0) == slot
    ).astype(f32).astype(bf16)
    dispatch_ref[...] = dispatch
    slots_ref[...] = jnp.dot(
        dispatch, grad_ref[...], preferred_element_type=f32
    ).astype(bf16)


def plan(lens, rank, routes, order, grads, capacity, experts_all):
    shard, width = grads.shape
    count = experts_all * capacity
    return pl.pallas_call(
        functools.partial(plan_kernel, capacity),
        out_shape=(
            jax.ShapeDtypeStruct((count, shard), bf16),
            jax.ShapeDtypeStruct((count, width), bf16),
        ),
        in_specs=[SMEM, SMEM, VMEM, VMEM, VMEM],
        out_specs=(VMEM, VMEM),
        name="plan",
        cost_estimate=pl.CostEstimate(
            flops=2 * count * shard * width, bytes_accessed=4 * shard * width,
            transcendentals=0,
        ),
    )(lens, rank, routes.reshape(1, -1), order, grads)


def gelu_parts(values):
    below = 0.5 + 0.5 * lax.erf(values * (0.5**0.5))
    density = jnp.exp(-0.5 * values * values) * (0.5 / jnp.pi) ** 0.5
    return values * below, below + values * density


def expert_kernel(in_ref, grad_act_ref, up_ref, act_ref, mid_ref, sum_ref):
    step = pl.program_id(0)
    pre = jnp.dot(in_ref[...], up_ref[...], preferred_element_type=f32)
    act, slope = gelu_parts(pre)
    act_ref[...] = act.astype(bf16)
    grad_pre = (grad_act_ref[...] * slope).astype(bf16)
    mid = lax.dot_general(
        grad_pre, up_ref[...], (((1,), (1,)), ((), ())), preferred_element_type=f32
    )

    @pl.when(step == 0)
    def first():
        sum_ref[...] = mid

    @pl.when(step > 0)
    def later():
        sum_ref[...] += mid

    @pl.when(step == pl.num_programs(0) - 1)
    def last():
        mid_ref[...] = sum_ref[...].astype(bf16)


def expert(rows, grad_act, up):
    count, width = rows.shape
    hidden = up.shape[1]
    size = min(512, hidden)
    return pl.pallas_call(
        expert_kernel,
        grid=(hidden // size,),
        out_shape=(
            jax.ShapeDtypeStruct((count, hidden), bf16),
            jax.ShapeDtypeStruct((count, width), bf16),
        ),
        in_specs=[
            pl.BlockSpec((count, width), lambda i: (0, 0)),
            pl.BlockSpec((count, size), lambda i: (0, i)),
            pl.BlockSpec((width, size), lambda i: (0, i)),
        ],
        out_specs=(
            pl.BlockSpec((count, size), lambda i: (0, i)),
            pl.BlockSpec((count, width), lambda i: (0, 0)),
        ),
        scratch_shapes=[pltpu.VMEM((count, width), f32)],
        name="expert",
        cost_estimate=pl.CostEstimate(
            flops=4 * count * width * hidden, bytes_accessed=4 * width * hidden,
            transcendentals=2 * count * hidden,
        ),
    )(rows, grad_act, up)


def product_kernel(a_ref, b_ref, out_ref, sum_ref):
    step = pl.program_id(0)
    made = jnp.dot(a_ref[...], b_ref[...], preferred_element_type=f32)

    @pl.when(step == 0)
    def first():
        sum_ref[...] = made

    @pl.when(step > 0)
    def later():
        sum_ref[...] += made

    @pl.when(step == pl.num_programs(0) - 1)
    def last():
        out_ref[...] = sum_ref[...].astype(bf16)


def product(a, b):
    count, depth = a.shape
    width = b.shape[1]
    size = min(1024, depth)
    return pl.pallas_call(
        product_kernel,
        grid=(depth // size,),
        out_shape=jax.ShapeDtypeStruct((count, width), bf16),
        in_specs=[
            pl.BlockSpec((count, size), lambda i: (0, i)),
            pl.BlockSpec((size, width), lambda i: (i, 0)),
        ],
        out_specs=pl.BlockSpec((count, width), lambda i: (0, 0)),
        scratch_shapes=[pltpu.VMEM((count, width), f32)],
        name="product",
        cost_estimate=pl.CostEstimate(
            flops=2 * count * width * depth, bytes_accessed=2 * width * depth,
            transcendentals=0,
        ),
    )(a, b)


def weight_kernel(groups, rank_ref, up_ref, down_ref, *refs):
    dup_ref, ddown_ref = refs[-2:]
    dup = ddown = 0.0
    for g in range(groups):
        in_ref, grad_ref = refs[2 * g : 2 * g + 2]
        pre = jnp.dot(in_ref[...], up_ref[...], preferred_element_type=f32)
        grad_act = lax.dot_general(
            grad_ref[...], down_ref[...], (((1,), (1,)), ((), ())),
            preferred_element_type=f32,
        )
        act, slope = gelu_parts(pre)
        dup = dup + contract_rows(in_ref[...], (grad_act * slope).astype(bf16))
        ddown = ddown + contract_rows(act.astype(bf16), grad_ref[...])
    if len(refs) > 2 * groups + 2:
        dup = dup + refs[2 * groups][...]
        ddown = ddown + refs[2 * groups + 1][...]
    dup_ref[...] = dup
    ddown_ref[...] = ddown


def expert_weights(rank, group, up, down, parts, earlier=()):
    count, width = group[0][0].shape
    hidden = up.shape[1] // parts
    size = min(256, hidden)
    blocks = hidden // size
    up_block = pl.BlockSpec((width, size), lambda i, r: (0, i))
    down_block = pl.BlockSpec((size, width), lambda i, r: (i, 0))
    rows = [values for both in group for values in both]
    return pl.pallas_call(
        functools.partial(weight_kernel, len(group)),
        grid_spec=pltpu.PrefetchScalarGridSpec(
            num_scalar_prefetch=1,
            grid=(blocks,),
            in_specs=[
                pl.BlockSpec((width, size), lambda i, r: (0, r[0] * blocks + i)),
                pl.BlockSpec((size, width), lambda i, r: (r[0] * blocks + i, 0)),
            ]
            + [pl.BlockSpec((count, width), lambda i, r: (0, 0))] * len(rows)
            + ([up_block, down_block] if earlier else []),
            out_specs=(up_block, down_block),
        ),
        out_shape=(
            jax.ShapeDtypeStruct((width, hidden), f32),
            jax.ShapeDtypeStruct((hidden, width), f32),
        ),
        name="expert_weights",
        cost_estimate=pl.CostEstimate(
            flops=8 * count * width * hidden * len(group),
            bytes_accessed=16 * width * hidden,
            transcendentals=2 * count * hidden * len(group),
        ),
    )(rank, up, down, *rows, *earlier)


def input_grad_kernel(groups, normed_ref, qw_ref, kw_ref, vw_ref, *refs):
    joint_refs = refs[: len(groups)]
    part_ref, sums_ref, turned_ref = refs[len(groups) :]
    step = pl.program_id(0)
    dim = HEAD_DIM

    @pl.when(step == 0)
    def stack():
        at = 0
        for first_head, heads in groups:
            for n in range(first_head, first_head + heads):
                part = slice(n * dim, (n + 1) * dim)
                turned_ref[at : at + dim, :] = kw_ref[part, :]
                turned_ref[at + dim : at + 2 * dim, :] = vw_ref[part, :]
                at += 2 * dim
            part = slice(first_head * dim, (first_head + heads) * dim)
            turned_ref[at : at + heads * dim, :] = qw_ref[part, :]
            at += heads * dim

    total = 0.0
    at = 0
    for joint_ref in joint_refs:
        rows = slice(at, at + joint_ref.shape[1])
        total = total + jnp.dot(
            joint_ref[...], turned_ref[rows, :], preferred_element_type=f32
        )
        at += joint_ref.shape[1]
    part_ref[0] = total.astype(bf16)
    gains = jnp.sum(total * normed_ref[...].astype(f32), axis=0, keepdims=True)
    shifts = jnp.sum(total, axis=0, keepdims=True)

    @pl.when(step == 0)
    def first():
        sums_ref[0:1] = gains
        sums_ref[1:2] = shifts

    @pl.when(step > 0)
    def later():
        sums_ref[0:1] += gains
        sums_ref[1:2] += shifts


def input_grad(groups, normed, qw, kw, vw, joints, blocks):
    slots, width = normed.shape
    size = slots // blocks
    cols = qw.shape[0]
    fixed = pl.BlockSpec((cols, width), lambda i: (0, 0))
    far = blocks // 2
    return pl.pallas_call(
        functools.partial(input_grad_kernel, groups),
        grid=(blocks,),
        out_shape=(
            jax.ShapeDtypeStruct((blocks, size, width), bf16),
            jax.ShapeDtypeStruct((2, width), f32),
        ),
        in_specs=[pl.BlockSpec((size, width), lambda i: (i, 0)), fixed, fixed, fixed]
        + [pl.BlockSpec((size, joint.shape[1]), lambda i: (i, 0)) for joint in joints],
        out_specs=(
            pl.BlockSpec((1, size, width), lambda i: ((i % 2) * far + i // 2, 0, 0)),
            pl.BlockSpec((2, width), lambda i: (0, 0)),
        ),
        scratch_shapes=[pltpu.VMEM((3 * cols, width), bf16)],
        name="input_grad",
        cost_estimate=pl.CostEstimate(
            flops=6 * slots * width * cols,
            bytes_accessed=6 * slots * width, transcendentals=0,
        ),
    )(normed, qw, kw, vw, *joints)


def sum_halves(values, axis):
    low_bit = lax.axis_index(axis) & 1
    half = values.shape[0] // 2
    own = lax.dynamic_slice_in_dim(values, low_bit * half, half)
    away = lax.dynamic_slice_in_dim(values, (1 - low_bit) * half, half)
    for step in steps_of(lax.axis_size(axis)):
        arrived = swap(away if step == 1 else own, axis, step)
        own = (own.astype(f32) + arrived.astype(f32)).astype(bf16)
    return own, swap(own, axis, 1)


def finish_kernel(groups, bit_ref, *refs):
    pieces = refs[: 2 * len(groups)]
    outs = refs[2 * len(groups) : 2 * len(groups) + 3]
    whole_refs = refs[2 * len(groups) + 3 :]
    query_ref, key_ref, value_ref = outs
    dim = HEAD_DIM
    bit = bit_ref[0, 0]
    for g, (first_head, heads) in enumerate(groups):
        whole_ref = whole_refs[g]
        half = whole_ref.shape[0] // 2
        whole_ref[rows_at(bit, half), :] = pieces[2 * g][...].astype(f32)
        whole_ref[rows_at(1 - bit, half), :] = pieces[2 * g + 1][...].astype(f32)
        at = 0
        for n in range(first_head, first_head + heads):
            part = slice(n * dim, (n + 1) * dim)
            key_ref[part, :] = whole_ref[at : at + dim, :]
            value_ref[part, :] = whole_ref[at + dim : at + 2 * dim, :]
            at += 2 * dim
        part = slice(first_head * dim, (first_head + heads) * dim)
        query_ref[part, :] = whole_ref[at : at + heads * dim, :]


def finish(groups, bit, pieces):
    width = pieces[0][0].shape[1]
    cols = sum(heads for first_head, heads in groups) * HEAD_DIM
    flat = [half_piece for piece in pieces for half_piece in piece]
    return pl.pallas_call(
        functools.partial(finish_kernel, groups),
        out_shape=(jax.ShapeDtypeStruct((cols, width), f32),) * 3,
        in_specs=[SMEM] + [VMEM] * len(flat),
        out_specs=(VMEM,) * 3,
        scratch_shapes=[
            pltpu.VMEM((3 * heads * HEAD_DIM, width), f32) for first_head, heads in groups
        ],
        name="finish",
    )(bit, *flat)


def sum_rows_over(values, axis):
    count = lax.axis_size(axis)
    rows, cols = values.shape
    parts = values.reshape(count, rows // count, cols)
    arrived = lax.all_to_all(parts, axis, split_axis=0, concat_axis=0, tiled=True)
    mine = jnp.sum(arrived.astype(f32), axis=0).astype(bf16)
    spread = jnp.broadcast_to(mine[None], parts.shape)
    full = lax.all_to_all(spread, axis, split_axis=0, concat_axis=0, tiled=True)
    return full.reshape(rows, cols).astype(f32)


def pair_sums(parts, axis, last=f32):
    count = len(parts)
    for step in steps_of(count):
        kind = bf16 if 2 * step < count else last
        parts = [
            (a.astype(f32) + swap(b, axis, step).astype(f32)).astype(kind)
            for a, b in zip(parts[0::2], parts[1::2])
        ]
    return parts[0]


def sum_small(values, axes):
    for axis in axes:
        for step in steps_of(lax.axis_size(axis)):
            values = values + swap(values, axis, step)
    return values


def on_device(
    tokens,
    first_gain,
    first_bias,
    query_weight,
    key_weight,
    value_weight,
    output_weight,
    second_gain,
    second_bias,
    expert_up,
    expert_down,
    item_lengths,
    routes,
    slot_order,
    cotangent,
):
    slots_all, width = tokens.shape
    members = lax.axis_size("tensor")
    shard_rows = slots_all // members
    rank = lax.axis_index("tensor")
    sources = lax.axis_size("dp")
    experts_all = sources * expert_up.shape[0]
    capacity = shard_rows // experts_all
    head_cols = query_weight.shape[1]
    heads = head_cols // HEAD_DIM
    up_matrix = expert_up[0]
    down_matrix = expert_down[0]
    rank_cell = rank.astype(jnp.int32).reshape(1, 1)

    def exchange(rows):
        return lax.all_to_all(
            rows.reshape(sources, -1, width), "dp", split_axis=0, concat_axis=0, tiled=True
        ).reshape(-1, width)

    qw, kw, vw = query_weight.T, key_weight.T, value_weight.T

    dispatch, grad_slots = plan(
        item_lengths, rank_cell, routes, slot_order, cotangent, capacity, experts_all
    )
    flat_grad = exchange(grad_slots)
    tokens, grad_slots = lax.optimization_barrier((tokens, grad_slots))
    normed_in, qt, kt, vt = project(
        rank_cell[0], tokens, first_gain, first_bias, qw, kw, vw, members
    )
    output_x = jnp.concatenate(
        [output_weight]
        + [swap(output_weight, "tensor", k) for k in range(1, members)]
    )
    heads_t, logs = attend(item_lengths, rank_cell, qt, kt, vt, members)
    heads_x = jnp.concatenate(
        [heads_t[0]] + [swap(heads_t[j], "tensor", j) for j in range(1, members)]
    )
    tokens_mine = lax.dynamic_slice_in_dim(tokens, rank * shard_rows, shard_rows).astype(f32)
    residual = tokens_mine + contract_rows(heads_x, output_x)
    normed_low = layer_norm(residual, second_gain, second_bias).astype(bf16)
    outgoing = jnp.dot(dispatch, normed_low, preferred_element_type=f32).astype(bf16)
    flat_in = exchange(outgoing)

    flat_grad, unused = lax.optimization_barrier((flat_grad, outgoing))
    grad_act = lax.dot_general(
        flat_grad, down_matrix, (((1,), (1,)), ((), ())), preferred_element_type=f32
    )
    gathered_grads = [flat_grad]
    for step in reversed(steps_of(members)):
        gathered_grads += [swap(a, "tensor", step) for a in gathered_grads]
    flat_in, grad_act = lax.optimization_barrier((flat_in, grad_act))
    act, grad_mid = expert(flat_in, grad_act, up_matrix)
    grad_back = exchange(grad_mid)
    gathered_rows = [flat_in]
    for step in reversed(steps_of(members)):
        gathered_rows += [swap(a, "tensor", step) for a in gathered_rows]

    gathered = list(zip(gathered_rows, gathered_grads))
    act, unused = lax.optimization_barrier((act, grad_mid))
    made = product(act, down_matrix)
    sums = expert_weights(rank_cell[0], gathered[0::2], up_matrix, down_matrix, members)
    grad_back, made, sums = lax.optimization_barrier((grad_back, made, sums))

    grad_normed = contract_rows(dispatch, grad_back)
    unused_mid, pull_mid = jax.vjp(layer_norm, residual, second_gain, second_bias)
    grad_res_norm, second_gain_part, second_bias_part = pull_mid(grad_normed)
    grad_res = cotangent.astype(f32) + grad_res_norm
    grad_low = grad_res.astype(bf16)
    places = rank * shard_rows + jnp.arange(shard_rows, dtype=jnp.int32)
    alive_mine = places < jnp.sum(item_lengths)
    grad_heads = (
        lax.dot_general(
            output_x, grad_low, (((1,), (1,)), ((), ())), preferred_element_type=f32
        )
        * alive_mine[None, :].astype(f32)
    ).astype(bf16)
    grad_parts = [grad_heads[:head_cols]] + [
        swap(grad_heads[j * head_cols : (j + 1) * head_cols], "tensor", j)
        for j in range(1, members)
    ]
    made, sums, grad_heads = lax.optimization_barrier((made, sums, grad_heads))
    returned = exchange(made)
    up_grad, down_grad = expert_weights(
        rank_cell[0], gathered[1::2], up_matrix, down_matrix, members, sums
    )
    output_part = jnp.dot(heads_x, grad_low, preferred_element_type=f32).astype(bf16)
    grad_parts, up_grad, down_grad, output_part = lax.optimization_barrier(
        (grad_parts, up_grad, down_grad, output_part)
    )

    groups = ((0, heads - 1), (heads - 1, 1)) if heads > 1 else ((0, heads),)
    joints = []
    pieces = []
    for first_head, count in groups:
        joint = attend_back(
            first_head, count, item_lengths, rank_cell, qt, kt, vt, heads_t, logs, grad_parts
        )
        weight_part = contract_rows(joint, normed_in).astype(bf16)
        weight_part, grad_parts = lax.optimization_barrier((weight_part, grad_parts))
        joints.append(joint)
        pieces.append(sum_halves(weight_part, "dp"))
    output_grad = sum_rows_over(
        pair_sums(
            [output_part[j * head_cols : (j + 1) * head_cols] for j in range(members)],
            "tensor", bf16,
        ),
        "dp",
    )

    partial, sums_first = input_grad(groups, normed_in, qw, kw, vw, joints, members)
    for step in steps_of(members):
        kept, sent = partial[: len(partial) // 2], partial[len(partial) // 2 :]
        partial = (kept.astype(f32) + swap(sent, "tensor", step).astype(f32)).astype(
            bf16 if 2 * step < members else f32
        )
    grad_in = partial[0]
    unused_first, pull_first = jax.vjp(
        lambda values: layer_norm(values, first_gain, first_bias), tokens_mine
    )
    token_grad = grad_res + pull_first(grad_in)[0]

    first_bias_part = sums_first[1]
    first_gain_part = (sums_first[0] - first_bias * first_bias_part) / first_gain
    norm_sums = sum_small(
        jnp.stack([first_gain_part, first_bias_part, second_gain_part, second_bias_part]),
        ("tensor", "dp"),
    )
    block_out = residual + contract_rows(dispatch, returned)
    bit_cell = (lax.axis_index("dp") & 1).astype(jnp.int32).reshape(1, 1)
    query_grad, key_grad, value_grad = finish(groups, bit_cell, pieces)
    return (
        block_out,
        token_grad,
        norm_sums[0],
        norm_sums[1],
        query_grad.T,
        key_grad.T,
        value_grad.T,
        output_grad,
        norm_sums[2],
        norm_sums[3],
        up_grad[None],
        down_grad[None],
    )


def solution(mesh):
    in_specs = (
        P("dp", None),
        P(),
        P(),
        P(None, "tensor"),
        P(None, "tensor"),
        P(None, "tensor"),
        P("tensor", None),
        P(),
        P(),
        P("dp", None, None),
        P("dp", None, None),
        P("dp", None),
        P(("dp", "tensor"), None),
        P(("dp", "tensor"), None),
        P(("dp", "tensor"), None),
    )
    out_specs = (
        P(("dp", "tensor"), None),
        P(("dp", "tensor"), None),
        P(),
        P(),
        P(None, "tensor"),
        P(None, "tensor"),
        P(None, "tensor"),
        P("tensor", None),
        P(),
        P(),
        P("dp", None, "tensor"),
        P("dp", "tensor", None),
    )
    return jax.shard_map(
        on_device, mesh=mesh, in_specs=in_specs, out_specs=out_specs, check_vma=False
    )
```

profile of v0, /device:TPU:0, one launch (start us, length us, event | category | flops | bytes accessed | tf_op | source)
XLA Modules:
  0.0 334.4 jit_solution(2816640453895531709)
XLA Ops:
  9.6 7.5 %project.1 = (bf16[2048,768]{1,0:T(8,128)(2,1)}, bf16[192,2048]{1,0:T(8,128)(2,1)}, bf16[192,2048]{1,0:T(8,128)(2,1)}, bf16[192,2048]{1,0:T(8,128)(2,1)}) custom-call(s32[1]{0:T(128)} %bitcast.2.rank_ref, bf16[2048,768]{1,0:T(8,128)(2,1)} %tokens_ref, f32[1,768]{1,0:T(1,128)} %broadcast_in_dim.18.gain_ref, f32[1,768]{1,0:T(1,128)} %broadcast_in_dim.19.bias_ref, ...), custom_call_target="tpu_custom_call" | custom-call | flops 1811939328 | bytes 9437184 | tf_op jit(solution)/shard_map/project/pallas_call | solution.py:76
  17.0 19.4 %attend.1 = (bf16[4,192,512]{2,1,0:T(8,128)(2,1)}, f32[3,1,2048]{2,1,0:T(1,128)}) custom-call(s32[1,5]{1,0:T(1,128)} %lens_ref.7, s32[1,1]{1,0:T(1,128)} %bitcast.rank_ref, bf16[192,2048]{1,0:T(8,128)(2,1)} %get-tuple-element.58.qt_ref, bf16[192,2048]{1,0:T(8,128)(2,1)} %get-tuple-element.59.kt_ref, bf16[192,2048]{1,0:T(8,128)(2,1)} %get-tuple-element.60.vt_ref), custom_call_target="tpu_custom_call" | custom-call | flops 2415919104 | bytes 2359296 | tf_op jit(solution)/shard_map/attend/pallas_call | solution.py:224
  39.6 14.1 %all-to-all-start.1 = ((bf16[8,64,768]{2,1,0:T(8,128)(2,1)}), bf16[8,64,768]{2,1,0:T(8,128)(2,1)S(1)}, u32[]{:S(2)}, u32[]{:S(2)}) async-start(bf16[8,64,768]{2,1,0:T(8,128)(2,1)} %bitcast.12), calls=%async_computation.1 | async-start | bytes 1572864 | tf_op jit(solution)/shard_map/all_to_all | solution.py:715
  63.2 10.7 %all-to-all-done.1 = bf16[8,64,768]{2,1,0:T(8,128)(2,1)S(1)} async-done(((bf16[8,64,768]{2,1,0:T(8,128)(2,1)}), bf16[8,64,768]{2,1,0:T(8,128)(2,1)S(1)}, u32[]{:S(2)}, u32[]{:S(2)}) %all-to-all-start.1) | async-done | bytes 786464 | tf_op jit(solution)/shard_map/all_to_all | solution.py:715
  73.9 3.6 %all-to-all-start = ((bf16[8,64,768]{2,1,0:T(8,128)(2,1)}), bf16[8,64,768]{2,1,0:T(8,128)(2,1)S(1)}, u32[]{:S(2)}, u32[]{:S(2)}) async-start(bf16[8,64,768]{2,1,0:T(8,128)(2,1)} %bitcast.71), calls=%async_computation | async-start | bytes 1572864 | tf_op jit(solution)/shard_map/all_to_all | solution.py:715
  77.5 6.9 %fusion.15.grad_act_ref = f32[512,3072]{1,0:T(8,128)} fusion(bf16[512,768]{1,0:T(8,128)(2,1)S(1)} %bitcast.62, bf16[1,3072,768]{2,1,0:T(8,128)(2,1)} %param.25), kind=kOutput, calls=%fused_computation.71 | convolution fusion | flops 2415919104 | bytes 11796480 | tf_op jit(solution)/shard_map/dot_general | solution.py:744
  84.4 13.5 %all-to-all-done = bf16[8,64,768]{2,1,0:T(8,128)(2,1)S(1)} async-done(((bf16[8,64,768]{2,1,0:T(8,128)(2,1)}), bf16[8,64,768]{2,1,0:T(8,128)(2,1)S(1)}, u32[]{:S(2)}, u32[]{:S(2)}) %all-to-all-start) | async-done | bytes 786464 | tf_op jit(solution)/shard_map/all_to_all | solution.py:715
  98.8 11.8 %expert.1 = (bf16[512,3072]{1,0:T(8,128)(2,1)}, bf16[512,768]{1,0:T(8,128)(2,1)}) custom-call(bf16[512,768]{1,0:T(8,128)(2,1)} %bitcast.66, f32[512,3072]{1,0:T(8,128)} %fusion.15.grad_act_ref, bf16[768,3072]{1,0:T(8,128)(2,1)} %bitcast.75), custom_call_target="tpu_custom_call" | custom-call | flops 4831838208 | bytes 9437184 | tf_op jit(solution)/shard_map/expert/pallas_call | solution.py:418
  110.6 4.5 %all-to-all-start.2 = ((bf16[8,64,768]{2,1,0:T(8,128)(2,1)}), bf16[8,64,768]{2,1,0:T(8,128)(2,1)}, u32[]{:S(2)}, u32[]{:S(2)}) async-start(bf16[8,64,768]{2,1,0:T(8,128)(2,1)} %bitcast.70), calls=%async_computation.2 | async-start | bytes 1572864 | tf_op jit(solution)/shard_map/all_to_all | solution.py:715
  120.3 6.7 %product.1 = bf16[512,768]{1,0:T(8,128)(2,1)} custom-call(bf16[512,3072]{1,0:T(8,128)(2,1)} %get-tuple-element.67.a_ref, bf16[3072,768]{1,0:T(8,128)(2,1)} %bitcast.72), custom_call_target="tpu_custom_call" | custom-call | flops 2415919104 | bytes 4718592 | tf_op jit(solution)/shard_map/product/pallas_call | solution.py:464
  127.0 8.8 %collective-permute-done.12.refs_1_ = bf16[512,768]{1,0:T(8,128)(2,1)} collective-permute-done((bf16[512,768]{1,0:T(8,128)(2,1)S(1)}, bf16[512,768]{1,0:T(8,128)(2,1)}, u32[]{:S(2)}, u32[]{:S(2)}) %collective-permute-start.12) | collective-permute-done | bytes 786464 | tf_op jit(solution)/shard_map/ppermute | solution.py:34
  135.8 14.6 %collective-permute-done.11.refs_0_ = bf16[512,768]{1,0:T(8,128)(2,1)} collective-permute-done((bf16[512,768]{1,0:T(8,128)(2,1)S(1)}, bf16[512,768]{1,0:T(8,128)(2,1)}, u32[]{:S(2)}, u32[]{:S(2)}) %collective-permute-start.11) | collective-permute-done | bytes 786464 | tf_op jit(solution)/shard_map/ppermute | solution.py:34
  150.4 9.4 %expert_weights.2 = (f32[768,768]{1,0:T(8,128)}, f32[768,768]{1,0:T(8,128)}) custom-call(s32[1]{0:T(128)} %bitcast.2.rank_ref, bf16[768,3072]{1,0:T(8,128)(2,1)} %bitcast.76, bf16[3072,768]{1,0:T(8,128)(2,1)} %bitcast.73, bf16[512,768]{1,0:T(8,128)(2,1)} %bitcast.67, bf16[512,768]{1,0:T(8,128)(2,1)} %bitcast.65, ...), custom_call_target="tpu_custom_call" | custom-call | flops 4831838208 | bytes 9437184 | tf_op jit(solution)/shard_map/expert_weights/pallas_call | solution.py:510
  169.8 10.0 %expert_weights.3 = (f32[768,768]{1,0:T(8,128)}, f32[768,768]{1,0:T(8,128)}) custom-call(s32[1]{0:T(128)} %bitcast.2.rank_ref, bf16[768,3072]{1,0:T(8,128)(2,1)} %bitcast.77, bf16[3072,768]{1,0:T(8,128)(2,1)} %bitcast.74, bf16[512,768]{1,0:T(8,128)(2,1)} %collective-permute-done.11.refs_0_, bf16[512,768]{1,0:T(8,128)(2,1)} %collective-permute-done.12.refs_1_, ...), custom_call_target="tpu_custom_call" | custom-call | flops 4831838208 | bytes 9437184 | tf_op jit(solution)/shard_map/expert_weights/pallas_call | solution.py:510
  179.9 19.5 %attend_back.2.refs_0_ = bf16[2048,384]{1,0:T(8,128)(2,1)} custom-call(s32[1,5]{1,0:T(1,128)} %lens_ref.7, s32[1,1]{1,0:T(1,128)} %bitcast.rank_ref, bf16[192,2048]{1,0:T(8,128)(2,1)} %get-tuple-element.58.qt_ref, bf16[192,2048]{1,0:T(8,128)(2,1)} %get-tuple-element.59.kt_ref, bf16[192,2048]{1,0:T(8,128)(2,1)} %get-tuple-element.60.vt_ref, ...), custom_call_target="tpu_custom_call" | custom-call | flops 4294967296 | bytes 3670016 | tf_op jit(solution)/shard_map/attend_back/pallas_call | solution.py:318
  199.3 4.6 %convolution_convert_fusion.2 = bf16[384,768]{1,0:T(8,128)(2,1)} fusion(bf16[2048,384]{1,0:T(8,128)(2,1)} %attend_back.2.refs_0_, bf16[2048,768]{1,0:T(8,128)(2,1)} %get-tuple-element.75.normed_ref), kind=kOutput, calls=%fused_computation.22 | convolution fusion | flops 1208254464 | bytes 5308416 | tf_op jit(solution)/shard_map/dot_general | solution.py:27
  203.9 12.9 %attend_back.3.refs_1_ = bf16[2048,192]{1,0:T(8,128)(2,1)} custom-call(s32[1,5]{1,0:T(1,128)} %lens_ref.7, s32[1,1]{1,0:T(1,128)} %bitcast.rank_ref, bf16[192,2048]{1,0:T(8,128)(2,1)} %get-tuple-element.58.qt_ref, bf16[192,2048]{1,0:T(8,128)(2,1)} %get-tuple-element.59.kt_ref, bf16[192,2048]{1,0:T(8,128)(2,1)} %get-tuple-element.60.vt_ref, ...), custom_call_target="tpu_custom_call" | custom-call | flops 2147483648 | bytes 1835008 | tf_op jit(solution)/shard_map/attend_back/pallas_call | solution.py:318
  216.9 6.9 %input_grad.1 = (bf16[4,512,768]{2,1,0:T(8,128)(2,1)}, f32[2,768]{1,0:T(2,128)}) custom-call(bf16[2048,768]{1,0:T(8,128)(2,1)} %get-tuple-element.75.normed_ref, bf16[192,768]{1,0:T(8,128)(2,1)} %bitcast.82, bf16[192,768]{1,0:T(8,128)(2,1)} %bitcast.84, bf16[192,768]{1,0:T(8,128)(2,1)} %bitcast.86, bf16[2048,384]{1,0:T(8,128)(2,1)} %attend_back.2.refs_0_, ...), custom_call_target="tpu_custom_call" | custom-call | flops 1811939328 | bytes 9437184 | tf_op jit(solution)/shard_map/input_grad/pallas_call | solution.py:584
  239.2 8.7 %collective-permute-start.20 = (f32[4,768]{1,0:T(4,128)S(1)}, f32[4,768]{1,0:T(4,128)S(1)}, u32[]{:S(2)}, u32[]{:S(2)}) collective-permute-start(f32[4,768]{1,0:T(4,128)S(1)} %add.129), channel_id=1, source_target_pairs={{0,8},{4,12},{8,0},{12,4},{16,24},{20,28},{24,16},{28,20},{1,9},{5... | collective-permute-start | bytes 36872 | tf_op jit(solution)/shard_map/ppermute | solution.py:34
  248.7 6.6 %all-to-all-start.4 = ((bf16[8,24,768]{2,1,0:T(8,128)(2,1)}), bf16[8,24,768]{2,1,0:T(8,128)(2,1)S(1)}, u32[]{:S(2)}, u32[]{:S(2)}) async-start(bf16[8,24,768]{2,1,0:T(8,128)(2,1)} %bitcast.60), calls=%async_computation.4 | async-start | bytes 589824 | tf_op jit(solution)/shard_map/all_to_all | solution.py:659
  265.0 4.2 %all-to-all-start.3 = ((bf16[8,64,768]{2,1,0:T(8,128)(2,1)}), bf16[8,64,768]{2,1,0:T(8,128)(2,1)}, u32[]{:S(2)}, u32[]{:S(2)}) async-start(bf16[8,64,768]{2,1,0:T(8,128)(2,1)} %bitcast.61), calls=%async_computation.3 | async-start | bytes 1572864 | tf_op jit(solution)/shard_map/all_to_all | solution.py:715
  276.4 18.1 %collective-permute-done.28 = bf16[96,768]{1,0:T(8,128)(2,1)S(1)} collective-permute-done((bf16[96,768]{1,0:T(8,128)(2,1)S(1)}, bf16[96,768]{1,0:T(8,128)(2,1)S(1)}, u32[]{:S(2)}, u32[]{:S(2)}) %collective-permute-start.28) | collective-permute-done | bytes 147488 | tf_op jit(solution)/shard_map/ppermute | solution.py:34
  304.2 4.3 %all-to-all-start.5 = ((bf16[8,24,768]{2,1,0:T(8,128)(2,1)}), bf16[8,24,768]{2,1,0:T(8,128)(2,1)}, u32[]{:S(2)}, u32[]{:S(2)}) async-start(bf16[8,24,768]{2,1,0:T(8,128)(2,1)} %broadcast_in_dim.47), calls=%async_computation.5 | async-start | bytes 589824 | tf_op jit(solution)/shard_map/all_to_all | solution.py:662
  315.7 6.0 %collective-permute-done.25.refs_1_ = bf16[192,768]{1,0:T(8,128)(2,1)S(1)} collective-permute-done((bf16[192,768]{1,0:T(8,128)(2,1)S(1)}, bf16[192,768]{1,0:T(8,128)(2,1)S(1)}, u32[]{:S(2)}, u32[]{:S(2)}) %collective-permute-start.25) | collective-permute-done | bytes 294944 | tf_op jit(solution)/shard_map/ppermute | solution.py:34
  (183 shorter events, 100.1 us)
Async XLA Ops:
  0.6 53.8 %collective-permute-start.3 = (bf16[192,768]{1,0:T(8,128)(2,1)}, bf16[192,768]{1,0:T(8,128)(2,1)S(1)}, u32[]{:S(2)}, u32[]{:S(2)}) collective-permute-start(bf16[192,768]{1,0:T(8,128)(2,1)} %param.21), channel_id=1, source_target_pairs={{0,1},{1,0},{2,3},{3,2},{4,5},{5,4},{6,7},{7,6},{8,9},{9,8},{10,11... | collective-permute-start | bytes 884744 | tf_op jit(solution)/shard_map/ppermute | solution.py:34
  1.2 54.0 %collective-permute-start.4 = (bf16[192,768]{1,0:T(8,128)(2,1)}, bf16[192,768]{1,0:T(8,128)(2,1)S(1)}, u32[]{:S(2)}, u32[]{:S(2)}) collective-permute-start(bf16[192,768]{1,0:T(8,128)(2,1)} %param.21), channel_id=1, source_target_pairs={{0,2},{1,3},{2,0},{3,1},{4,6},{5,7},{6,4},{7,5},{8,10},{9,11},{10,... | collective-permute-start | bytes 884744 | tf_op jit(solution)/shard_map/ppermute | solution.py:34
  3.7 52.2 %collective-permute-start.5 = (bf16[192,768]{1,0:T(8,128)(2,1)}, bf16[192,768]{1,0:T(8,128)(2,1)S(1)}, u32[]{:S(2)}, u32[]{:S(2)}) collective-permute-start(bf16[192,768]{1,0:T(8,128)(2,1)} %param.21), channel_id=1, source_target_pairs={{0,3},{1,2},{2,1},{3,0},{4,7},{5,6},{6,5},{7,4},{8,11},{9,10},{10,... | collective-permute-start | bytes 884744 | tf_op jit(solution)/shard_map/ppermute | solution.py:34
  37.7 18.9 %collective-permute-start.2 = (bf16[192,512]{1,0:T(8,128)(2,1)S(1)}, bf16[192,512]{1,0:T(8,128)(2,1)S(1)}, u32[]{:S(2)}, u32[]{:S(2)}) collective-permute-start(bf16[192,512]{1,0:T(8,128)(2,1)S(1)} %get-tuple-element.119), channel_id=1, source_target_pairs={{0,3},{1,2},{2,1},{3,0},{4,7},{5,6},{6,5},{7,4},{8,11},{9,10},{10,... | collective-permute-start | bytes 589832 | tf_op jit(solution)/shard_map/ppermute | solution.py:34
  39.5 17.2 %collective-permute-start.1 = (bf16[192,512]{1,0:T(8,128)(2,1)S(1)}, bf16[192,512]{1,0:T(8,128)(2,1)S(1)}, u32[]{:S(2)}, u32[]{:S(2)}) collective-permute-start(bf16[192,512]{1,0:T(8,128)(2,1)S(1)} %get-tuple-element.120), channel_id=1, source_target_pairs={{0,2},{1,3},{2,0},{3,1},{4,6},{5,7},{6,4},{7,5},{8,10},{9,11},{10,... | collective-permute-start | bytes 589832 | tf_op jit(solution)/shard_map/ppermute | solution.py:34
  39.6 34.3 %all-to-all-start.1 = ((bf16[8,64,768]{2,1,0:T(8,128)(2,1)}), bf16[8,64,768]{2,1,0:T(8,128)(2,1)S(1)}, u32[]{:S(2)}, u32[]{:S(2)}) async-start(bf16[8,64,768]{2,1,0:T(8,128)(2,1)} %bitcast.12), calls=%async_computation.1 | async-start | bytes 1572864 | tf_op jit(solution)/shard_map/all_to_all | solution.py:715
  73.9 24.0 %all-to-all-start = ((bf16[8,64,768]{2,1,0:T(8,128)(2,1)}), bf16[8,64,768]{2,1,0:T(8,128)(2,1)S(1)}, u32[]{:S(2)}, u32[]{:S(2)}) async-start(bf16[8,64,768]{2,1,0:T(8,128)(2,1)} %bitcast.71), calls=%async_computation | async-start | bytes 1572864 | tf_op jit(solution)/shard_map/all_to_all | solution.py:715
  110.6 49.3 %all-to-all-start.2 = ((bf16[8,64,768]{2,1,0:T(8,128)(2,1)}), bf16[8,64,768]{2,1,0:T(8,128)(2,1)}, u32[]{:S(2)}, u32[]{:S(2)}) async-start(bf16[8,64,768]{2,1,0:T(8,128)(2,1)} %bitcast.70), calls=%async_computation.2 | async-start | bytes 1572864 | tf_op jit(solution)/shard_map/all_to_all | solution.py:715
  115.1 20.7 %collective-permute-start.12 = (bf16[512,768]{1,0:T(8,128)(2,1)S(1)}, bf16[512,768]{1,0:T(8,128)(2,1)}, u32[]{:S(2)}, u32[]{:S(2)}) collective-permute-start(bf16[512,768]{1,0:T(8,128)(2,1)S(1)} %bitcast.63), channel_id=1, source_target_pairs={{0,2},{1,3},{2,0},{3,1},{4,6},{5,7},{6,4},{7,5},{8,10},{9,11},{10,... | collective-permute-start | bytes 2359304 | tf_op jit(solution)/shard_map/ppermute | solution.py:34
  116.7 33.7 %collective-permute-start.11 = (bf16[512,768]{1,0:T(8,128)(2,1)S(1)}, bf16[512,768]{1,0:T(8,128)(2,1)}, u32[]{:S(2)}, u32[]{:S(2)}) collective-permute-start(bf16[512,768]{1,0:T(8,128)(2,1)S(1)} %bitcast.68), channel_id=1, source_target_pairs={{0,2},{1,3},{2,0},{3,1},{4,6},{5,7},{6,4},{7,5},{8,10},{9,11},{10,... | collective-permute-start | bytes 2359304 | tf_op jit(solution)/shard_map/ppermute | solution.py:34
  117.2 33.2 %collective-permute-start.7 = (bf16[512,768]{1,0:T(8,128)(2,1)S(1)}, bf16[512,768]{1,0:T(8,128)(2,1)}, u32[]{:S(2)}, u32[]{:S(2)}) collective-permute-start(bf16[512,768]{1,0:T(8,128)(2,1)S(1)} %bitcast.64), channel_id=1, source_target_pairs={{0,1},{1,0},{2,3},{3,2},{4,5},{5,4},{6,7},{7,6},{8,9},{9,8},{10,11... | collective-permute-start | bytes 2359304 | tf_op jit(solution)/shard_map/ppermute | solution.py:34
  117.2 33.2 %collective-permute-start.6 = (bf16[512,768]{1,0:T(8,128)(2,1)S(1)}, bf16[512,768]{1,0:T(8,128)(2,1)}, u32[]{:S(2)}, u32[]{:S(2)}) collective-permute-start(bf16[512,768]{1,0:T(8,128)(2,1)S(1)} %bitcast.69), channel_id=1, source_target_pairs={{0,1},{1,0},{2,3},{3,2},{4,5},{5,4},{6,7},{7,6},{8,9},{9,8},{10,11... | collective-permute-start | bytes 2359304 | tf_op jit(solution)/shard_map/ppermute | solution.py:34
  135.8 34.1 %collective-permute-start.14 = (bf16[512,768]{1,0:T(8,128)(2,1)}, bf16[512,768]{1,0:T(8,128)(2,1)}, u32[]{:S(2)}, u32[]{:S(2)}) collective-permute-start(bf16[512,768]{1,0:T(8,128)(2,1)} %collective-permute-done.12.refs_1_), channel_id=1, source_target_pairs={{0,1},{1,0},{2,3},{3,2},{4,5},{5,4},{6,7},{7,6},{8,9},{9,8},{10,11... | collective-permute-start | bytes 2359304 | tf_op jit(solution)/shard_map/ppermute | solution.py:34
  150.4 19.4 %collective-permute-start.13 = (bf16[512,768]{1,0:T(8,128)(2,1)}, bf16[512,768]{1,0:T(8,128)(2,1)}, u32[]{:S(2)}, u32[]{:S(2)}) collective-permute-start(bf16[512,768]{1,0:T(8,128)(2,1)} %collective-permute-done.11.refs_0_), channel_id=1, source_target_pairs={{0,1},{1,0},{2,3},{3,2},{4,5},{5,4},{6,7},{7,6},{8,9},{9,8},{10,11... | collective-permute-start | bytes 2359304 | tf_op jit(solution)/shard_map/ppermute | solution.py:34
  231.0 66.8 %collective-permute-start.15 = (bf16[2,512,768]{2,1,0:T(8,128)(2,1)}, bf16[2,512,768]{2,1,0:T(8,128)(2,1)}, u32[]{:S(2)}, u32[]{:S(2)}) collective-permute-start(bf16[2,512,768]{2,1,0:T(8,128)(2,1)} %slice.75), channel_id=1, source_target_pairs={{0,1},{1,0},{2,3},{3,2},{4,5},{5,4},{6,7},{7,6},{8,9},{9,8},{10,11... | collective-permute-start | bytes 4718600 | tf_op jit(solution)/shard_map/ppermute | solution.py:34
  231.6 16.3 %collective-permute-start.30 = (bf16[192,768]{1,0:T(8,128)(2,1)S(1)}, bf16[192,768]{1,0:T(8,128)(2,1)S(1)}, u32[]{:S(2)}, u32[]{:S(2)}) collective-permute-start(bf16[192,768]{1,0:T(8,128)(2,1)S(1)} %get-tuple-element.112), channel_id=1, source_target_pairs={{0,1},{1,0},{2,3},{3,2},{4,5},{5,4},{6,7},{7,6},{8,9},{9,8},{10,11... | collective-permute-start | bytes 884744 | tf_op jit(solution)/shard_map/ppermute | solution.py:34
  236.6 24.9 %collective-permute-start.26 = (bf16[96,768]{1,0:T(8,128)(2,1)}, bf16[96,768]{1,0:T(8,128)(2,1)}, u32[]{:S(2)}, u32[]{:S(2)}) collective-permute-start(bf16[96,768]{1,0:T(8,128)(2,1)} %constant_dynamic-slice_fusion), channel_id=1, source_target_pairs={{0,4},{4,0},{8,12},{12,8},{16,20},{20,16},{24,28},{28,24},{1,5},{5... | collective-permute-start | bytes 442376 | tf_op jit(solution)/shard_map/ppermute | solution.py:34
  239.2 19.8 %collective-permute-start.20 = (f32[4,768]{1,0:T(4,128)S(1)}, f32[4,768]{1,0:T(4,128)S(1)}, u32[]{:S(2)}, u32[]{:S(2)}) collective-permute-start(f32[4,768]{1,0:T(4,128)S(1)} %add.129), channel_id=1, source_target_pairs={{0,8},{4,12},{8,0},{12,4},{16,24},{20,28},{24,16},{28,20},{1,9},{5... | collective-permute-start | bytes 36872 | tf_op jit(solution)/shard_map/ppermute | solution.py:34
  265.0 38.4 %all-to-all-start.3 = ((bf16[8,64,768]{2,1,0:T(8,128)(2,1)}), bf16[8,64,768]{2,1,0:T(8,128)(2,1)}, u32[]{:S(2)}, u32[]{:S(2)}) async-start(bf16[8,64,768]{2,1,0:T(8,128)(2,1)} %bitcast.61), calls=%async_computation.3 | async-start | bytes 1572864 | tf_op jit(solution)/shard_map/all_to_all | solution.py:715
  270.3 24.3 %collective-permute-start.28 = (bf16[96,768]{1,0:T(8,128)(2,1)S(1)}, bf16[96,768]{1,0:T(8,128)(2,1)S(1)}, u32[]{:S(2)}, u32[]{:S(2)}) collective-permute-start(bf16[96,768]{1,0:T(8,128)(2,1)S(1)} %add_convert_fusion.10), channel_id=1, source_target_pairs={{0,16},{4,20},{8,24},{12,28},{16,0},{20,4},{24,8},{28,12},{1,17},{... | collective-permute-start | bytes 442376 | tf_op jit(solution)/shard_map/ppermute | solution.py:34
  274.3 22.3 %collective-permute-start.23 = (bf16[192,768]{1,0:T(8,128)(2,1)S(1)}, bf16[192,768]{1,0:T(8,128)(2,1)S(1)}, u32[]{:S(2)}, u32[]{:S(2)}) collective-permute-start(bf16[192,768]{1,0:T(8,128)(2,1)S(1)} %add_convert_fusion.8), channel_id=1, source_target_pairs={{0,8},{4,12},{8,0},{12,4},{16,24},{20,28},{24,16},{28,20},{1,9},{5... | collective-permute-start | bytes 884744 | tf_op jit(solution)/shard_map/ppermute | solution.py:34
  295.3 20.4 %collective-permute-start.29 = (bf16[96,768]{1,0:T(8,128)(2,1)}, bf16[96,768]{1,0:T(8,128)(2,1)}, u32[]{:S(2)}, u32[]{:S(2)}) collective-permute-start(bf16[96,768]{1,0:T(8,128)(2,1)} %add_convert_fusion.9.refs_2_), channel_id=1, source_target_pairs={{0,4},{4,0},{8,12},{12,8},{16,20},{20,16},{24,28},{28,24},{1,5},{5... | collective-permute-start | bytes 442376 | tf_op jit(solution)/shard_map/ppermute | solution.py:34
  302.1 24.6 %collective-permute-start.16 = (bf16[1,512,768]{2,1,0:T(8,128)(2,1)}, bf16[1,512,768]{2,1,0:T(8,128)(2,1)}, u32[]{:S(2)}, u32[]{:S(2)}) collective-permute-start(bf16[1,512,768]{2,1,0:T(8,128)(2,1)} %slice.93), channel_id=1, source_target_pairs={{0,2},{1,3},{2,0},{3,1},{4,6},{5,7},{6,4},{7,5},{8,10},{9,11},{10,... | collective-permute-start | bytes 2359304 | tf_op jit(solution)/shard_map/ppermute | solution.py:34
  304.2 20.7 %all-to-all-start.5 = ((bf16[8,24,768]{2,1,0:T(8,128)(2,1)}), bf16[8,24,768]{2,1,0:T(8,128)(2,1)}, u32[]{:S(2)}, u32[]{:S(2)}) async-start(bf16[8,24,768]{2,1,0:T(8,128)(2,1)} %broadcast_in_dim.47), calls=%async_computation.5 | async-start | bytes 589824 | tf_op jit(solution)/shard_map/all_to_all | solution.py:662
  (43 other events, 326.5 us)
where the time goes:
time: 334 us
  Pallas kernels  110 us (33%)
  waiting for transfers between devices  77.5 us (23%)
  starting transfers between devices  74.7 us (22%)
  matrix products  26.4 us (8%)
  other arithmetic  23.1 us (7%)
  local copies, waits for them, and re-layouts  21.8 us (7%)
    ppermute x33, waiting for transfers between devices, swap(): return lax.ppermute(values, axis, [(i, i ^ step) for i in range(count)])  53.3 us
    ppermute x33, starting transfers between devices, swap(): return lax.ppermute(values, axis, [(i, i ^ step) for i in range(count)])  37.4 us
    pallas_call x2, Pallas kernels, attend_back(): pl.pallas_call(functools.partial(backward_kernel, first_head, heads), out...  32.4 us
    all_to_all x4, starting transfers between devices, exchange(): lax.all_to_all(rows.reshape(sources, -1, width), 'dp', split_axis=0, conc...  26.4 us
    all_to_all x4, waiting for transfers between devices, exchange(): lax.all_to_all(rows.reshape(sources, -1, width), 'dp', split_axis=0, conc...  24.2 us
    pallas_call x2, Pallas kernels, expert_weights(): pl.pallas_call(functools.partial(weight_kernel, len(group)), grid_spec=pl...  19.4 us
    pallas_call x1, Pallas kernels, attend(): pl.pallas_call(forward_kernel, out_shape=(jax.ShapeDtypeStruct((blocks, w...  19.4 us
    dot_general x5, matrix products, contract_rows(): lax.dot_general(left, right, (((0,), (0,)), ((), ())), preferred_element_...  15.3 us
  transfers between devices with their start and end apart: 39, of which 10 were waited for; matrix products, arithmetic and copies ran while one was open for 16% of the time, Pallas kernels for 18%

commit v1 on v0

--- a/solution.py
+++ b/solution.py
@@ -14,6 +14,7 @@
 bf16 = jnp.bfloat16
 VMEM = pl.BlockSpec(memory_space=pltpu.VMEM)
 SMEM = pl.BlockSpec(memory_space=pltpu.SMEM)
+COST = pl.CostEstimate(flops=2**20, bytes_accessed=2**20, transcendentals=0)
 
 
 def layer_norm(values, gain, shift):
@@ -96,11 +97,8 @@
         out_shape=(jax.ShapeDtypeStruct((slots, width), bf16),)
         + (jax.ShapeDtypeStruct((cols, slots), bf16),) * 3,
         name="project",
-        cost_estimate=pl.CostEstimate(
-            flops=6 * slots * width * cols, bytes_accessed=6 * slots * width,
-            transcendentals=slots,
-        ),
-    )(rank, tokens, gain[None], bias[None], qw, kw, vw)
+        cost_estimate=COST,
+    )(rank, tokens, gain.reshape(1, -1), bias.reshape(1, -1), qw, kw, vw)
 
 
 def item_ends(lens_ref):
@@ -151,8 +149,9 @@
 
 
 def forward_kernel(
-    lens_ref, rank_ref, qt_ref, kt_ref, vt_ref, out_ref, log_ref, masked_ref
+    lens_ref, rank_ref, qt_ref, kt_ref, vt_ref, *refs
 ):
+    *out_refs, log_ref, masked_ref, out_ref = refs
     blocks, width, shard = out_ref.shape
     heads = width // HEAD_DIM
     pair = 1
@@ -215,6 +214,8 @@
         return unused
 
     lax.fori_loop(0, blocks // pair, query_block, 0)
+    for b in range(blocks):
+        out_refs[b][...] = out_ref[b]
 
 
 def attend(lens, rank, qt, kt, vt, blocks):
@@ -223,30 +224,34 @@
     heads = width // HEAD_DIM
     return pl.pallas_call(
         forward_kernel,
-        out_shape=(
-            jax.ShapeDtypeStruct((blocks, width, size), bf16),
-            jax.ShapeDtypeStruct((heads, 1, slots), f32),
-        ),
+        out_shape=(jax.ShapeDtypeStruct((width, size), bf16),) * blocks
+        + (jax.ShapeDtypeStruct((heads, 1, slots), f32),),
         in_specs=[SMEM, SMEM, VMEM, VMEM, VMEM],
-        out_specs=(VMEM, VMEM),
-        scratch_shapes=[pltpu.VMEM((heads, slots, width), bf16)],
+        out_specs=(VMEM,) * (blocks + 1),
+        scratch_shapes=[
+            pltpu.VMEM((heads, slots, width), bf16),
+            pltpu.VMEM((blocks, width, size), bf16),
+        ],
         name="attend",
         compiler_params=pltpu.CompilerParams(vmem_limit_bytes=60 * 2**20),
-        cost_estimate=pl.CostEstimate(
-            flops=slots * slots * width * 3, bytes_accessed=6 * slots * width,
-            transcendentals=slots * slots * heads // 2,
-        ),
+        cost_estimate=COST,
     )(lens, rank, qt, kt, vt)
 
 
 def backward_kernel(
-    first_head, heads, lens_ref, rank_ref, qt_ref, kt_ref, vt_ref, out_ref, log_ref, *rest
+    first_head, heads, blocks, lens_ref, rank_ref, qt_ref, kt_ref, vt_ref, log_ref,
+    normed_ref, *rest
 ):
-    blocks, width, shard = out_ref.shape
+    width, slots = qt_ref.shape
+    shard = slots // blocks
     dim = HEAD_DIM
-    grad_refs = rest[:blocks]
-    joint_ref, kv_ref, q0_ref, og_ref, right_ref, inner_ref, dq_ref = rest[blocks:]
-    slots = blocks * shard
+    out_refs, grad_refs = rest[:blocks], rest[blocks : 2 * blocks]
+    joint_ref, weight_ref, kv_ref, q0_ref, og_ref, right_ref, inner_ref, dq_ref = rest[
+        2 * blocks : -3
+    ]
+    turned_ref, rows_ref, copied = rest[-3:]
+    fetch = pltpu.make_async_copy(normed_ref, rows_ref, copied)
+    fetch.start()
     unit = shard // 2
     rank = rank_ref[0, 0]
     ends = item_ends(lens_ref)
@@ -265,7 +270,7 @@
             og_ref[n, cols, :] = jnp.transpose(padded, (1, 0))
             right_ref[n, 1, :, cols] = padded
             inner_ref[n, :, cols] = jnp.sum(
-                out_ref[b, part, :].astype(f32) * grad.astype(f32), axis=0, keepdims=True
+                out_refs[b][part, :].astype(f32) * grad.astype(f32), axis=0, keepdims=True
             )
     dq_ref[...] = jnp.zeros_like(dq_ref)
 
@@ -303,36 +308,50 @@
         start = (jnp.zeros((unit, 2 * dim), f32),) * heads
         totals = lax.fori_loop(low, high, query_block, start)
         for n in range(heads):
-            joint_ref[rows, 2 * dim * n : 2 * dim * (n + 1)] = totals[n].astype(bf16)
+            part = slice(2 * dim * n, 2 * dim * (n + 1))
+            total = totals[n].astype(bf16)
+            joint_ref[rows, part] = total
+            turned_ref[part, rows] = jnp.transpose(total, (1, 0))
         return unused
 
     lax.fori_loop(0, 2 * blocks, key_block, 0)
     dq = (dq_ref[...] * dim ** (-0.5)).astype(bf16).reshape(heads * dim, slots)
+    turned_ref[2 * dim * heads :, :] = dq
     joint_ref[:, 2 * dim * heads :] = jnp.transpose(dq, (1, 0))
-
-
-def attend_back(first_head, heads, lens, rank, qt, kt, vt, out, logs, grads):
-    blocks, width, size = out.shape
-    slots = blocks * size
+    fetch.wait()
+    weight_ref[...] = jnp.dot(
+        turned_ref[...], rows_ref[...], preferred_element_type=f32
+    ).astype(bf16)
+
+
+def attend_back(first_head, heads, lens, rank, qt, kt, vt, logs, normed, outs, grads):
+    slots, width = normed.shape
+    blocks = len(outs)
     dim = HEAD_DIM
     return pl.pallas_call(
-        functools.partial(backward_kernel, first_head, heads),
-        out_shape=jax.ShapeDtypeStruct((slots, 3 * dim * heads), bf16),
-        in_specs=[SMEM, SMEM] + [VMEM] * (5 + blocks),
-        out_specs=VMEM,
+        functools.partial(backward_kernel, first_head, heads, blocks),
+        out_shape=(
+            jax.ShapeDtypeStruct((slots, 3 * dim * heads), bf16),
+            jax.ShapeDtypeStruct((3 * dim * heads, width), bf16),
+        ),
+        in_specs=[SMEM, SMEM]
+        + [VMEM] * 4
+        + [pl.BlockSpec(memory_space=pl.ANY)]
+        + [VMEM] * (2 * blocks),
+        out_specs=(VMEM, VMEM),
         scratch_shapes=[pltpu.VMEM((heads, slots, 2 * dim), bf16)] * 3
         + [
             pltpu.VMEM((heads, 2, 2 * dim, slots), bf16),
             pltpu.VMEM((heads, 1, slots), f32),
             pltpu.VMEM((heads, dim, slots), f32),
+            pltpu.VMEM((3 * dim * heads, slots), bf16),
+            pltpu.VMEM((slots, width), bf16),
+            pltpu.SemaphoreType.DMA,
         ],
         name="attend_back",
         compiler_params=pltpu.CompilerParams(vmem_limit_bytes=60 * 2**20),
-        cost_estimate=pl.CostEstimate(
-            flops=slots * slots * dim * heads * 8, bytes_accessed=14 * slots * dim * heads,
-            transcendentals=slots * slots * heads // 2,
-        ),
-    )(lens, rank, qt, kt, vt, out, logs, *grads)
+        cost_estimate=COST,
+    )(lens, rank, qt, kt, vt, logs, normed, *outs, *grads)
 
 
 def plan_kernel(capacity, lens_ref, rank_ref, routes_ref, order_ref, grad_ref,
@@ -375,11 +394,122 @@
         in_specs=[SMEM, SMEM, VMEM, VMEM, VMEM],
         out_specs=(VMEM, VMEM),
         name="plan",
-        cost_estimate=pl.CostEstimate(
-            flops=2 * count * shard * width, bytes_accessed=4 * shard * width,
-            transcendentals=0,
+        cost_estimate=COST,
+    )(lens, rank, routes.reshape(1, -1), order, grads)
+
+
+def across(left, right):
+    return lax.dot_general(
+        left, right, (((1,), (1,)), ((), ())), preferred_element_type=f32
+    )
+
+
+def middle_kernel(count, rank_ref, tokens_ref, gain_ref, bias_ref, dispatch_ref, *refs):
+    head_refs, weight_refs = refs[:count], refs[count : 2 * count]
+    residual_ref, rows_ref = refs[2 * count :]
+    residual = tokens_ref[...].astype(f32)
+    for head_ref, weight_ref in zip(head_refs, weight_refs):
+        residual = residual + contract_rows(head_ref[...], weight_ref[...])
+    residual_ref[...] = residual
+    normed = (normalized(residual) * gain_ref[...] + bias_ref[...]).astype(bf16)
+    rows_ref[...] = jnp.dot(
+        dispatch_ref[...], normed, preferred_element_type=f32
+    ).astype(bf16)
+
+
+def middle(rank, tokens, gain, bias, dispatch, heads, weights):
+    count, shard = dispatch.shape
+    width = tokens.shape[1]
+    fixed = lambda array: pl.BlockSpec(array.shape, lambda i, r: (0, 0))
+    small = [gain.reshape(1, -1), bias.reshape(1, -1), dispatch, *heads, *weights]
+    return pl.pallas_call(
+        functools.partial(middle_kernel, len(heads)),
+        grid_spec=pltpu.PrefetchScalarGridSpec(
+            num_scalar_prefetch=1,
+            grid=(1,),
+            in_specs=[pl.BlockSpec((shard, width), lambda i, r: (r[0], 0))]
+            + [fixed(array) for array in small],
+            out_specs=(
+                pl.BlockSpec((shard, width), lambda i, r: (0, 0)),
+                pl.BlockSpec((count, width), lambda i, r: (0, 0)),
+            ),
         ),
-    )(lens, rank, routes.reshape(1, -1), order, grads)
+        out_shape=(
+            jax.ShapeDtypeStruct((shard, width), f32),
+            jax.ShapeDtypeStruct((count, width), bf16),
+        ),
+        name="middle",
+        cost_estimate=COST,
+    )(rank, tokens, *small)
+
+
+def turn_kernel(
+    count, lens_ref, rank_ref, dispatch_ref, back_ref, residual_ref, cotangent_ref,
+    gain_ref, *refs
+):
+    weight_refs = refs[:count]
+    grad_ref, low_ref, sums_ref = refs[count : count + 3]
+    part_refs = refs[count + 3 :]
+    shard = residual_ref.shape[0]
+    grad_normed = contract_rows(dispatch_ref[...], back_ref[...])
+    values = residual_ref[...]
+    centred = values - jnp.mean(values, axis=-1, keepdims=True)
+    inverse = lax.rsqrt(jnp.mean(centred * centred, axis=-1, keepdims=True) + EPSILON)
+    normed = centred * inverse
+    sums_ref[0:1] = jnp.sum(grad_normed * normed, axis=0, keepdims=True)
+    sums_ref[1:2] = jnp.sum(grad_normed, axis=0, keepdims=True)
+    scaled = grad_normed * gain_ref[...]
+    grad = cotangent_ref[...].astype(f32) + inverse * (
+        scaled
+        - jnp.mean(scaled, axis=-1, keepdims=True)
+        - normed * jnp.mean(scaled * normed, axis=-1, keepdims=True)
+    )
+    grad_ref[...] = grad
+    low = grad.astype(bf16)
+    low_ref[...] = low
+    place = rank_ref[0, 0] * shard + lax.broadcasted_iota(jnp.int32, (1, shard), 1)
+    alive = place < item_ends(lens_ref)[-1]
+    for weight_ref, part_ref in zip(weight_refs, part_refs):
+        part_ref[...] = jnp.where(alive, across(weight_ref[...], low), 0.0).astype(bf16)
+
+
+def turn(lens, rank, dispatch, back, residual, cotangent, gain, weights):
+    shard, width = residual.shape
+    cols = weights[0].shape[0]
+    count = len(weights)
+    return pl.pallas_call(
+        functools.partial(turn_kernel, count),
+        out_shape=(
+            jax.ShapeDtypeStruct((shard, width), f32),
+            jax.ShapeDtypeStruct((shard, width), bf16),
+            jax.ShapeDtypeStruct((2, width), f32),
+        )
+        + (jax.ShapeDtypeStruct((cols, shard), bf16),) * count,
+        in_specs=[SMEM, SMEM] + [VMEM] * (5 + count),
+        out_specs=(VMEM,) * (3 + count),
+        name="turn",
+        cost_estimate=COST,
+    )(lens, rank, dispatch, back, residual, cotangent, gain.reshape(1, -1), *weights)
+
+
+def output_kernel(low_ref, *refs):
+    head_refs, (kept_ref, sent_ref) = refs[:-2], refs[-2:]
+    for j, head_ref in enumerate(head_refs):
+        made = jnp.dot(head_ref[...], low_ref[...], preferred_element_type=f32)
+        (kept_ref, sent_ref)[j % 2][j // 2] = made.astype(bf16)
+
+
+def output_products(low, heads):
+    cols = heads[0].shape[0]
+    shape = jax.ShapeDtypeStruct((len(heads) // 2, cols, low.shape[1]), bf16)
+    return pl.pallas_call(
+        output_kernel,
+        out_shape=(shape, shape),
+        in_specs=[VMEM] * (1 + len(heads)),
+        out_specs=(VMEM, VMEM),
+        name="output_products",
+        cost_estimate=COST,
+    )(low, *heads)
 
 
 def gelu_parts(values):
@@ -433,10 +563,7 @@
         ),
         scratch_shapes=[pltpu.VMEM((count, width), f32)],
         name="expert",
-        cost_estimate=pl.CostEstimate(
-            flops=4 * count * width * hidden, bytes_accessed=4 * width * hidden,
-            transcendentals=2 * count * hidden,
-        ),
+        cost_estimate=COST,
     )(rows, grad_act, up)
 
 
@@ -472,10 +599,7 @@
         out_specs=pl.BlockSpec((count, width), lambda i: (0, 0)),
         scratch_shapes=[pltpu.VMEM((count, width), f32)],
         name="product",
-        cost_estimate=pl.CostEstimate(
-            flops=2 * count * width * depth, bytes_accessed=2 * width * depth,
-            transcendentals=0,
-        ),
+        cost_estimate=COST,
     )(a, b)
 
 
@@ -525,17 +649,13 @@
             jax.ShapeDtypeStruct((hidden, width), f32),
         ),
         name="expert_weights",
-        cost_estimate=pl.CostEstimate(
-            flops=8 * count * width * hidden * len(group),
-            bytes_accessed=16 * width * hidden,
-            transcendentals=2 * count * hidden * len(group),
-        ),
+        cost_estimate=COST,
     )(rank, up, down, *rows, *earlier)
 
 
 def input_grad_kernel(groups, normed_ref, qw_ref, kw_ref, vw_ref, *refs):
     joint_refs = refs[: len(groups)]
-    part_ref, sums_ref, turned_ref = refs[len(groups) :]
+    kept_ref, sent_ref, sums_ref, turned_ref = refs[len(groups) :]
     step = pl.program_id(0)
     dim = HEAD_DIM
 
@@ -560,7 +680,14 @@
             joint_ref[...], turned_ref[rows, :], preferred_element_type=f32
         )
         at += joint_ref.shape[1]
-    part_ref[0] = total.astype(bf16)
+    @pl.when(step % 2 == 0)
+    def keep():
+        kept_ref[0] = total.astype(bf16)
+
+    @pl.when(step % 2 == 1)
+    def send():
+        sent_ref[0] = total.astype(bf16)
+
     gains = jnp.sum(total * normed_ref[...].astype(f32), axis=0, keepdims=True)
     shifts = jnp.sum(total, axis=0, keepdims=True)
 
@@ -580,38 +707,38 @@
     size = slots // blocks
     cols = qw.shape[0]
     fixed = pl.BlockSpec((cols, width), lambda i: (0, 0))
-    far = blocks // 2
     return pl.pallas_call(
         functools.partial(input_grad_kernel, groups),
         grid=(blocks,),
-        out_shape=(
-            jax.ShapeDtypeStruct((blocks, size, width), bf16),
-            jax.ShapeDtypeStruct((2, width), f32),
-        ),
+        out_shape=(jax.ShapeDtypeStruct((blocks // 2, size, width), bf16),) * 2
+        + (jax.ShapeDtypeStruct((2, width), f32),),
         in_specs=[pl.BlockSpec((size, width), lambda i: (i, 0)), fixed, fixed, fixed]
         + [pl.BlockSpec((size, joint.shape[1]), lambda i: (i, 0)) for joint in joints],
         out_specs=(
-            pl.BlockSpec((1, size, width), lambda i: ((i % 2) * far + i // 2, 0, 0)),
+            pl.BlockSpec((1, size, width), lambda i: (i // 2, 0, 0)),
+            pl.BlockSpec((1, size, width), lambda i: (i // 2, 0, 0)),
             pl.BlockSpec((2, width), lambda i: (0, 0)),
         ),
         scratch_shapes=[pltpu.VMEM((3 * cols, width), bf16)],
         name="input_grad",
-        cost_estimate=pl.CostEstimate(
-            flops=6 * slots * width * cols,
-            bytes_accessed=6 * slots * width, transcendentals=0,
-        ),
+        cost_estimate=COST,
     )(normed, qw, kw, vw, *joints)
 
 
-def sum_halves(values, axis):
+def start_halves(values, axis):
     low_bit = lax.axis_index(axis) & 1
     half = values.shape[0] // 2
     own = lax.dynamic_slice_in_dim(values, low_bit * half, half)
     away = lax.dynamic_slice_in_dim(values, (1 - low_bit) * half, half)
-    for step in steps_of(lax.axis_size(axis)):
-        arrived = swap(away if step == 1 else own, axis, step)
-        own = (own.astype(f32) + arrived.astype(f32)).astype(bf16)
-    return own, swap(own, axis, 1)
+    return add_low(own, swap(away, axis, 1))
+
+
+def add_low(a, b):
+    return (a.astype(f32) + b.astype(f32)).astype(bf16)
+
+
+def tie(*values):
+    return lax.optimization_barrier(values)
 
 
 def finish_kernel(groups, bit_ref, *refs):
@@ -661,17 +788,6 @@
     spread = jnp.broadcast_to(mine[None], parts.shape)
     full = lax.all_to_all(spread, axis, split_axis=0, concat_axis=0, tiled=True)
     return full.reshape(rows, cols).astype(f32)
-
-
-def pair_sums(parts, axis, last=f32):
-    count = len(parts)
-    for step in steps_of(count):
-        kind = bf16 if 2 * step < count else last
-        parts = [
-            (a.astype(f32) + swap(b, axis, step).astype(f32)).astype(kind)
-            for a, b in zip(parts[0::2], parts[1::2])
-        ]
-    return parts[0]
 
 
 def sum_small(values, axes):
@@ -722,106 +838,113 @@
         item_lengths, rank_cell, routes, slot_order, cotangent, capacity, experts_all
     )
     flat_grad = exchange(grad_slots)
-    tokens, grad_slots = lax.optimization_barrier((tokens, grad_slots))
+    tokens, grad_slots = tie(tokens, grad_slots)
     normed_in, qt, kt, vt = project(
         rank_cell[0], tokens, first_gain, first_bias, qw, kw, vw, members
     )
-    output_x = jnp.concatenate(
-        [output_weight]
-        + [swap(output_weight, "tensor", k) for k in range(1, members)]
-    )
-    heads_t, logs = attend(item_lengths, rank_cell, qt, kt, vt, members)
-    heads_x = jnp.concatenate(
-        [heads_t[0]] + [swap(heads_t[j], "tensor", j) for j in range(1, members)]
-    )
+    outputs = [output_weight] + [
+        swap(output_weight, "tensor", k) for k in range(1, members)
+    ]
+    *own_heads, logs = attend(item_lengths, rank_cell, qt, kt, vt, members)
+    own_heads, flat_grad, outputs = tie(own_heads, flat_grad, outputs)
+    all_heads = [own_heads[0]] + [
+        swap(own_heads[j], "tensor", j) for j in range(1, members)
+    ]
+    residual, outgoing = middle(
+        rank_cell[0], tokens, second_gain, second_bias, dispatch, all_heads, outputs
+    )
+    flat_in = exchange(outgoing)
+
+    flat_grad, outgoing = tie(flat_grad, outgoing)
+    grad_act = across(flat_grad, down_matrix)
+    gathered_grads = [flat_grad]
+    gathered_rows = [flat_in]
+    steps = steps_of(members)
+    for step in reversed(steps[1:]):
+        gathered_grads += [swap(a, "tensor", step) for a in gathered_grads]
+    flat_in, grad_act, gathered_grads = tie(flat_in, grad_act, gathered_grads)
+    gathered_rows = [flat_in]
+    for step in reversed(steps[1:]):
+        gathered_rows += [swap(a, "tensor", step) for a in gathered_rows]
+    near_grads = swap(gathered_grads[0], "tensor", 1)
+    near_rows = swap(flat_in, "tensor", 1)
+    far_grads = [swap(a, "tensor", 1) for a in gathered_grads[1:]]
+    act, grad_mid = expert(flat_in, grad_act, up_matrix)
+    act, grad_mid, near_rows, near_grads, far_grads = tie(
+        act, grad_mid, near_rows, near_grads, far_grads
+    )
+    grad_back = exchange(grad_mid)
+
+    act, near_rows, grad_mid = tie(act, near_rows, grad_mid)
+    made = product(act, down_matrix)
+    sums = expert_weights(
+        rank_cell[0],
+        [(flat_in, gathered_grads[0]), (near_rows, near_grads)],
+        up_matrix, down_matrix, members,
+    )
+    made, sums, gathered_rows = tie(made, sums, gathered_rows)
+    far_rows = [swap(a, "tensor", 1) for a in gathered_rows[1:]]
+    grad_back, made, sums = tie(grad_back, made, sums)
+
+    grad_res, grad_low, sums_second, *grad_heads = turn(
+        item_lengths, rank_cell, dispatch, grad_back, residual, cotangent,
+        second_gain, outputs,
+    )
+    grad_parts = [grad_heads[0]] + [
+        swap(grad_heads[j], "tensor", j) for j in range(1, members)
+    ]
+    made, sums, grad_low, grad_heads = tie(made, sums, grad_low, grad_heads)
+    returned = exchange(made)
+    kept, sent = output_products(grad_low, all_heads)
+    sums, kept, sent = tie(sums, kept, sent)
+    output_sum = add_low(kept, swap(sent, "tensor", 1))
+    sums = expert_weights(
+        rank_cell[0],
+        list(zip(gathered_rows[1:], gathered_grads[1:])) + list(zip(far_rows, far_grads)),
+        up_matrix, down_matrix, members, sums,
+    )
+    grad_parts, sums, output_sum = tie(grad_parts, sums, output_sum)
+    up_grad, down_grad = sums
+
+    back = functools.partial(
+        attend_back, lens=item_lengths, rank=rank_cell, qt=qt, kt=kt, vt=vt, logs=logs,
+        normed=normed_in, outs=own_heads,
+    )
+    groups = ((0, heads - 1), (heads - 1, 1))
+    joint_a, part_a = back(*groups[0], grads=grad_parts)
+    for step in steps[1:]:
+        output_sum = add_low(
+            output_sum[: len(output_sum) // 2],
+            swap(output_sum[len(output_sum) // 2 :], "tensor", step),
+        )
+    joint_a, part_a, output_sum, grad_parts = tie(joint_a, part_a, output_sum, grad_parts)
+    half_a = start_halves(part_a, "dp")
+    joint_b, part_b = back(*groups[1], grads=grad_parts)
+    joint_b, part_b, half_a, returned = tie(joint_b, part_b, half_a, returned)
+    output_grad = sum_rows_over(output_sum[0], "dp")
+
+    half_b = start_halves(part_b, "dp")
+    kept, sent, sums_first = input_grad(
+        groups, normed_in, qw, kw, vw, (joint_a, joint_b), members
+    )
+    for step in steps:
+        partial = kept.astype(f32) + swap(sent, "tensor", step).astype(f32)
+        count = partial.shape[0] // 2
+        kept, sent = partial[:count].astype(bf16), partial[count:].astype(bf16)
+    grad_in = partial[0]
+    for step in steps_of(sources)[1:]:
+        half_a = add_low(half_a, swap(half_a, "dp", step))
+        half_b = add_low(half_b, swap(half_b, "dp", step))
+    pieces = [(half_a, swap(half_a, "dp", 1)), (half_b, swap(half_b, "dp", 1))]
     tokens_mine = lax.dynamic_slice_in_dim(tokens, rank * shard_rows, shard_rows).astype(f32)
-    residual = tokens_mine + contract_rows(heads_x, output_x)
-    normed_low = layer_norm(residual, second_gain, second_bias).astype(bf16)
-    outgoing = jnp.dot(dispatch, normed_low, preferred_element_type=f32).astype(bf16)
-    flat_in = exchange(outgoing)
-
-    flat_grad, unused = lax.optimization_barrier((flat_grad, outgoing))
-    grad_act = lax.dot_general(
-        flat_grad, down_matrix, (((1,), (1,)), ((), ())), preferred_element_type=f32
-    )
-    gathered_grads = [flat_grad]
-    for step in reversed(steps_of(members)):
-        gathered_grads += [swap(a, "tensor", step) for a in gathered_grads]
-    flat_in, grad_act = lax.optimization_barrier((flat_in, grad_act))
-    act, grad_mid = expert(flat_in, grad_act, up_matrix)
-    grad_back = exchange(grad_mid)
-    gathered_rows = [flat_in]
-    for step in reversed(steps_of(members)):
-        gathered_rows += [swap(a, "tensor", step) for a in gathered_rows]
-
-    gathered = list(zip(gathered_rows, gathered_grads))
-    act, unused = lax.optimization_barrier((act, grad_mid))
-    made = product(act, down_matrix)
-    sums = expert_weights(rank_cell[0], gathered[0::2], up_matrix, down_matrix, members)
-    grad_back, made, sums = lax.optimization_barrier((grad_back, made, sums))
-
-    grad_normed = contract_rows(dispatch, grad_back)
-    unused_mid, pull_mid = jax.vjp(layer_norm, residual, second_gain, second_bias)
-    grad_res_norm, second_gain_part, second_bias_part = pull_mid(grad_normed)
-    grad_res = cotangent.astype(f32) + grad_res_norm
-    grad_low = grad_res.astype(bf16)
-    places = rank * shard_rows + jnp.arange(shard_rows, dtype=jnp.int32)
-    alive_mine = places < jnp.sum(item_lengths)
-    grad_heads = (
-        lax.dot_general(
-            output_x, grad_low, (((1,), (1,)), ((), ())), preferred_element_type=f32
-        )
-        * alive_mine[None, :].astype(f32)
-    ).astype(bf16)
-    grad_parts = [grad_heads[:head_cols]] + [
-        swap(grad_heads[j * head_cols : (j + 1) * head_cols], "tensor", j)
-        for j in range(1, members)
-    ]
-    made, sums, grad_heads = lax.optimization_barrier((made, sums, grad_heads))
-    returned = exchange(made)
-    up_grad, down_grad = expert_weights(
-        rank_cell[0], gathered[1::2], up_matrix, down_matrix, members, sums
-    )
-    output_part = jnp.dot(heads_x, grad_low, preferred_element_type=f32).astype(bf16)
-    grad_parts, up_grad, down_grad, output_part = lax.optimization_barrier(
-        (grad_parts, up_grad, down_grad, output_part)
-    )
-
-    groups = ((0, heads - 1), (heads - 1, 1)) if heads > 1 else ((0, heads),)
-    joints = []
-    pieces = []
-    for first_head, count in groups:
-        joint = attend_back(
-            first_head, count, item_lengths, rank_cell, qt, kt, vt, heads_t, logs, grad_parts
-        )
-        weight_part = contract_rows(joint, normed_in).astype(bf16)
-        weight_part, grad_parts = lax.optimization_barrier((weight_part, grad_parts))
-        joints.append(joint)
-        pieces.append(sum_halves(weight_part, "dp"))
-    output_grad = sum_rows_over(
-        pair_sums(
-            [output_part[j * head_cols : (j + 1) * head_cols] for j in range(members)],
-            "tensor", bf16,
-        ),
-        "dp",
-    )
-
-    partial, sums_first = input_grad(groups, normed_in, qw, kw, vw, joints, members)
-    for step in steps_of(members):
-        kept, sent = partial[: len(partial) // 2], partial[len(partial) // 2 :]
-        partial = (kept.astype(f32) + swap(sent, "tensor", step).astype(f32)).astype(
-            bf16 if 2 * step < members else f32
-        )
-    grad_in = partial[0]
     unused_first, pull_first = jax.vjp(
         lambda values: layer_norm(values, first_gain, first_bias), tokens_mine
     )
     token_grad = grad_res + pull_first(grad_in)[0]
 
-    first_bias_part = sums_first[1]
-    first_gain_part = (sums_first[0] - first_bias * first_bias_part) / first_gain
+    first_gain_part = (sums_first[0] - first_bias * sums_first[1]) / first_gain
     norm_sums = sum_small(
-        jnp.stack([first_gain_part, first_bias_part, second_gain_part, second_bias_part]),
+        jnp.stack([first_gain_part, sums_first[1], sums_second[0], sums_second[1]]),
         ("tensor", "dp"),
     )
     block_out = residual + contract_rows(dispatch, returned)

time: 334 us -> 292 us (0.87)
  waiting for transfers between devices: 77.5 us -> 44.9 us
  Pallas kernels: 110 us -> 128 us
  matrix products: 26.4 us -> 10.3 us
  local copies, waits for them, and re-layouts: 21.8 us -> 11.6 us
  other arithmetic: 23.1 us -> 17.4 us
  starting transfers between devices: 74.7 us -> 78.2 us
    all_to_all x4, waiting for transfers between devices: 24.2 us -> 2.19 us  [exchange(): lax.all_to_all(rows.reshape(sources, -1, width), 'dp', split_axis=0, conc...]
    pallas_call x3 -> x6, Pallas kernels: 51.7 us -> 68 us  [the longest x2 34.9 us: attend_back(): pl.pallas_call(functools.partial(backward_kernel, first_head, heads, bloc...]
    dot_general x5 -> x1, matrix products: 15.3 us -> 3.55 us  [contract_rows(): lax.dot_general(left, right, (((0,), (0,)), ((), ())), preferred_element_...]
    ppermute x33 -> x32, waiting for transfers between devices: 53.3 us -> 42.7 us  [swap(): return lax.ppermute(values, axis, [(i, i ^ step) for i in range(count)])]
    ppermute x33 -> x32, starting transfers between devices: 37.4 us -> 30.9 us  [swap(): return lax.ppermute(values, axis, [(i, i ^ step) for i in range(count)])]
    all_to_all x1, starting transfers between devices: 6.55 us -> 12.2 us  [sum_rows_over(): lax.all_to_all(parts, axis, split_axis=0, concat_axis=0, tiled=True)]
    unnamed x59 -> x60, local copies, waits for them, and re-layouts: 8.61 us -> 3.51 us
    convert_element_type x11 -> x8, other arithmetic: 9.7 us -> 4.92 us  [add_low(): return (a.astype(f32) + b.astype(f32)).astype(bf16)]
  transfers between devices with their start and end apart: 39 -> 38, of which waited for: 10 -> 11; matrix products, arithmetic and copies ran while one was open for 16% -> 10% of each run, Pallas kernels for 18% -> 38%
where the time goes in v1:
time: 292 us
  Pallas kernels  128 us (44%)
  starting transfers between devices  78.2 us (27%)
  waiting for transfers between devices  44.9 us (15%)
  other arithmetic  17.4 us (6%)
  local copies, waits for them, and re-layouts  11.6 us (4%)
  matrix products  10.3 us (4%)
    ppermute x32, waiting for transfers between devices, swap(): return lax.ppermute(values, axis, [(i, i ^ step) for i in range(count)])  42.7 us
    pallas_call x2, Pallas kernels, attend_back(): pl.pallas_call(functools.partial(backward_kernel, first_head, heads, bloc...  34.9 us
    ppermute x32, starting transfers between devices, swap(): return lax.ppermute(values, axis, [(i, i ^ step) for i in range(count)])  30.9 us
    all_to_all x4, starting transfers between devices, exchange(): lax.all_to_all(rows.reshape(sources, -1, width), 'dp', split_axis=0, conc...  30.7 us
    pallas_call x1, Pallas kernels, attend(): pl.pallas_call(forward_kernel, out_shape=(jax.ShapeDtypeStruct((width, si...  19.5 us
    pallas_call x2, Pallas kernels, expert_weights(): pl.pallas_call(functools.partial(weight_kernel, len(group)), grid_spec=pl...  19.4 us
    all_to_all x1, starting transfers between devices, sum_rows_over(): lax.all_to_all(parts, axis, split_axis=0, concat_axis=0, tiled=True)  12.2 us
    pallas_call x1, Pallas kernels, expert(): pl.pallas_call(expert_kernel, grid=(hidden // size,), out_shape=(jax.Shap...  11.8 us
  transfers between devices with their start and end apart: 38, of which 11 were waited for; matrix products, arithmetic and copies ran while one was open for 10% of the time, Pallas kernels for 38%

profile of v1, /device:TPU:0, one launch (start us, length us, event | category | flops | bytes accessed | tf_op | source)
XLA Modules:
  0.0 291.6 jit_solution(11198346463991374240)
XLA Ops:
  0.7 3.3 %plan.1 = (bf16[512,512]{1,0:T(8,128)(2,1)}, bf16[512,768]{1,0:T(8,128)(2,1)}) custom-call(s32[1,5]{1,0:T(1,128)} %lens_ref.9, s32[1,1]{1,0:T(1,128)} %bitcast.1.rank_ref, s32[1,512]{1,0:T(1,128)} %bitcast.63, s32[1,512]{1,0:T(1,128)} %order_ref.1, bf16[512,768]{1,0:T(8,128)(2,1)} %cotangent_ref.1), custom_call_target="tpu_custom_call" | custom-call | flops 1048576 | bytes 1048576 | tf_op jit(solution)/shard_map/plan/pallas_call | solution.py:388
  4.0 7.3 %all-to-all-start = ((bf16[8,64,768]{2,1,0:T(8,128)(2,1)}), bf16[8,64,768]{2,1,0:T(8,128)(2,1)S(1)}, u32[]{:S(2)}, u32[]{:S(2)}) async-start(bf16[8,64,768]{2,1,0:T(8,128)(2,1)} %bitcast.60), calls=%async_computation | async-start | bytes 1572864 | tf_op jit(solution)/shard_map/all_to_all | solution.py:831
  14.4 7.5 %project.1 = (bf16[2048,768]{1,0:T(8,128)(2,1)}, bf16[192,2048]{1,0:T(8,128)(2,1)}, bf16[192,2048]{1,0:T(8,128)(2,1)}, bf16[192,2048]{1,0:T(8,128)(2,1)}) custom-call(s32[1]{0:T(128)} %bitcast.rank_ref, bf16[2048,768]{1,0:T(8,128)(2,1)} %tokens_ref.1, f32[1,768]{1,0:T(1,128)} %reshape.103.gain_ref, f32[1,768]{1,0:T(1,128)} %reshape.104.bias_ref, ...), custom_call_target="tpu_custom_call" | custom-call | flops 1048576 | bytes 1048576 | tf_op jit(solution)/shard_map/project/pallas_call | solution.py:77
  21.8 19.5 %attend.1 = (bf16[192,512]{1,0:T(8,128)(2,1)}, bf16[192,512]{1,0:T(8,128)(2,1)}, bf16[192,512]{1,0:T(8,128)(2,1)}, bf16[192,512]{1,0:T(8,128)(2,1)}, f32[3,1,2048]{2,1,0:T(1,128)}) custom-call(s32[1,5]{1,0:T(1,128)} %lens_ref.9, s32[1,1]{1,0:T(1,128)} %bitcast.1.rank_ref, bf16[192,2048]{1,0:T(8,128)(2,1)} %get-tuple-element.109.qt_ref, ...), custom_call_target="tpu_custom_call" | custom-call | flops 1048576 | bytes 1048576 | tf_op jit(solution)/shard_map/attend/pallas_call | solution.py:225
  44.5 5.2 %collective-permute-done.4.refs_2_ = bf16[192,512]{1,0:T(8,128)(2,1)S(1)} collective-permute-done((bf16[192,512]{1,0:T(8,128)(2,1)}, bf16[192,512]{1,0:T(8,128)(2,1)S(1)}, u32[]{:S(2)}, u32[]{:S(2)}) %collective-permute-start.4) | collective-permute-done | bytes 196640 | tf_op jit(solution)/shard_map/ppermute | solution.py:35
  53.2 4.8 %middle.1 = (f32[512,768]{1,0:T(8,128)}, bf16[512,768]{1,0:T(8,128)(2,1)}) custom-call(s32[1]{0:T(128)} %bitcast.rank_ref, bf16[2048,768]{1,0:T(8,128)(2,1)} %tokens_ref.1, f32[1,768]{1,0:T(1,128)} %reshape.101.gain_ref, f32[1,768]{1,0:T(1,128)} %reshape.102.bias_ref, bf16[512,512]{1,0:T(8,128)(2,1)} %get-tuple-element.108.dispatch_ref, ...), custom_call_target="tpu_custom_call" | custom-call | flops 1048576 | bytes 1048576 | tf_op jit(solution)/shard_map/middle/pallas_call | solution.py:425
  58.0 13.7 %all-to-all-start.1 = ((bf16[8,64,768]{2,1,0:T(8,128)(2,1)}), bf16[8,64,768]{2,1,0:T(8,128)(2,1)}, u32[]{:S(2)}, u32[]{:S(2)}) async-start(bf16[8,64,768]{2,1,0:T(8,128)(2,1)} %bitcast.62), calls=%async_computation.1 | async-start | bytes 1572864 | tf_op jit(solution)/shard_map/all_to_all | solution.py:831
  73.2 6.8 %fusion.6.grad_act_ref = f32[512,3072]{1,0:T(8,128)} fusion(bf16[512,768]{1,0:T(8,128)(2,1)S(1)} %bitcast.48, bf16[1,3072,768]{2,1,0:T(8,128)(2,1)} %param.25), kind=kOutput, calls=%fused_computation.35 | convolution fusion | flops 2415919104 | bytes 11796480 | tf_op jit(solution)/shard_map/dot_general | solution.py:402
  80.0 11.5 %collective-permute-done.6.refs_1_ = bf16[512,768]{1,0:T(8,128)(2,1)S(1)} collective-permute-done((bf16[512,768]{1,0:T(8,128)(2,1)S(1)}, bf16[512,768]{1,0:T(8,128)(2,1)S(1)}, u32[]{:S(2)}, u32[]{:S(2)}) %collective-permute-start.6) | collective-permute-done | bytes 786464 | tf_op jit(solution)/shard_map/ppermute | solution.py:35
  93.3 11.8 %expert.1 = (bf16[512,3072]{1,0:T(8,128)(2,1)}, bf16[512,768]{1,0:T(8,128)(2,1)}) custom-call(bf16[512,768]{1,0:T(8,128)(2,1)} %bitcast.9.in_ref.refs_0_, f32[512,3072]{1,0:T(8,128)} %fusion.6.grad_act_ref, bf16[768,3072]{1,0:T(8,128)(2,1)} %bitcast.44), custom_call_target="tpu_custom_call" | custom-call | flops 1048576 | bytes 1048576 | tf_op jit(solution)/shard_map/expert/pallas_call | solution.py:548
  105.2 4.6 %all-to-all-start.2 = ((bf16[8,64,768]{2,1,0:T(8,128)(2,1)}), bf16[8,64,768]{2,1,0:T(8,128)(2,1)S(1)}, u32[]{:S(2)}, u32[]{:S(2)}) async-start(bf16[8,64,768]{2,1,0:T(8,128)(2,1)} %bitcast.61), calls=%async_computation.2 | async-start | bytes 1572864 | tf_op jit(solution)/shard_map/all_to_all | solution.py:831
  111.2 6.7 %product.1 = bf16[512,768]{1,0:T(8,128)(2,1)} custom-call(bf16[512,3072]{1,0:T(8,128)(2,1)} %get-tuple-element.139.a_ref, bf16[3072,768]{1,0:T(8,128)(2,1)} %bitcast.41), custom_call_target="tpu_custom_call" | custom-call | flops 1048576 | bytes 1048576 | tf_op jit(solution)/shard_map/product/pallas_call | solution.py:591
  117.9 9.4 %expert_weights.2 = (f32[768,768]{1,0:T(8,128)}, f32[768,768]{1,0:T(8,128)}) custom-call(s32[1]{0:T(128)} %bitcast.rank_ref, bf16[768,3072]{1,0:T(8,128)(2,1)} %bitcast.45, bf16[3072,768]{1,0:T(8,128)(2,1)} %bitcast.42, bf16[512,768]{1,0:T(8,128)(2,1)} %bitcast.9.in_ref.refs_0_, bf16[512,768]{1,0:T(8,128)(2,1)} %bitcast.50, bf16[512,768]{1,0:T(8,128)(2,1)} %copy-done.22, ...), custom_call_target="tpu_custom_call" | custom-call | flops 1048576 | bytes 1048576 | tf_op jit(solution)/shard_map/expert_weights/pallas_call | solution.py:634
  131.4 5.7 %turn.1 = (f32[512,768]{1,0:T(8,128)}, bf16[512,768]{1,0:T(8,128)(2,1)}, f32[2,768]{1,0:T(2,128)}, bf16[192,512]{1,0:T(8,128)(2,1)}, bf16[192,512]{1,0:T(8,128)(...) custom-call(s32[1,5]{1,0:T(1,128)} %lens_ref.9, s32[1,1]{1,0:T(1,128)} %bitcast.1.rank_ref, ...), custom_call_target="tpu_custom_call" | custom-call | flops 1048576 | bytes 1048576 | tf_op jit(solution)/shard_map/turn/pallas_call | solution.py:480
  142.1 5.1 %all-to-all-start.3 = ((bf16[8,64,768]{2,1,0:T(8,128)(2,1)}), bf16[8,64,768]{2,1,0:T(8,128)(2,1)S(1)}, u32[]{:S(2)}, u32[]{:S(2)}) async-start(bf16[8,64,768]{2,1,0:T(8,128)(2,1)} %bitcast.14), calls=%async_computation.3 | async-start | bytes 1572864 | tf_op jit(solution)/shard_map/all_to_all | solution.py:831
  148.2 10.0 %expert_weights.3 = (f32[768,768]{1,0:T(8,128)}, f32[768,768]{1,0:T(8,128)}) custom-call(s32[1]{0:T(128)} %bitcast.rank_ref, bf16[768,3072]{1,0:T(8,128)(2,1)} %bitcast.46, bf16[3072,768]{1,0:T(8,128)(2,1)} %bitcast.43, bf16[512,768]{1,0:T(8,128)(2,1)} %copy-done.14, bf16[512,768]{1,0:T(8,128)(2,1)} %copy-done.12, bf16[512,768]{1,0:T(8,128)(2,1)} %copy-done.15, ...), custom_call_target="tpu_custom_call" | custom-call | flops 1048576 | bytes 1048576 | tf_op jit(solution)/shard_map/expert_weights/pallas_call | solution.py:634
  161.1 20.9 %attend_back.2 = (bf16[2048,384]{1,0:T(8,128)(2,1)}, bf16[384,768]{1,0:T(8,128)(2,1)}) custom-call(s32[1,5]{1,0:T(1,128)} %lens_ref.9, s32[1,1]{1,0:T(1,128)} %bitcast.1.rank_ref, bf16[192,2048]{1,0:T(8,128)(2,1)} %get-tuple-element.109.qt_ref, bf16[192,2048]{1,0:T(8,128)(2,1)} %get-tuple-element.110.kt_ref, bf16[192,2048]{1,0:T(8,128)(2,1)} %get-tuple-element.111.vt_ref, ...), custom_call_target="tpu_custom_call" | custom-call | flops 1048576 | bytes 1048576 | tf_op jit(solution)/shard_map/attend_back/pallas_call | solution.py:331
  183.8 14.0 %attend_back.3 = (bf16[2048,192]{1,0:T(8,128)(2,1)}, bf16[192,768]{1,0:T(8,128)(2,1)}) custom-call(s32[1,5]{1,0:T(1,128)} %lens_ref.9, s32[1,1]{1,0:T(1,128)} %bitcast.1.rank_ref, bf16[192,2048]{1,0:T(8,128)(2,1)} %get-tuple-element.109.qt_ref, bf16[192,2048]{1,0:T(8,128)(2,1)} %get-tuple-element.110.kt_ref, bf16[192,2048]{1,0:T(8,128)(2,1)} %get-tuple-element.111.vt_ref, ...), custom_call_target="tpu_custom_call" | custom-call | flops 1048576 | bytes 1048576 | tf_op jit(solution)/shard_map/attend_back/pallas_call | solution.py:331
  198.9 8.8 %input_grad.1 = (bf16[2,512,768]{2,1,0:T(8,128)(2,1)}, bf16[2,512,768]{2,1,0:T(8,128)(2,1)}, f32[2,768]{1,0:T(2,128)}) custom-call(bf16[2048,768]{1,0:T(8,128)(2,1)} %get-tuple-element.126.normed_ref, bf16[192,768]{1,0:T(8,128)(2,1)} %bitcast.54, bf16[192,768]{1,0:T(8,128)(2,1)} %bitcast.56, bf16[192,768]{1,0:T(8,128)(2,1)} %bitcast.58, ...), custom_call_target="tpu_custom_call" | custom-call | flops 1048576 | bytes 1048576 | tf_op jit(solution)/shard_map/input_grad/pallas_call | solution.py:710
  212.7 12.2 %all-to-all-start.4 = ((bf16[8,24,768]{2,1,0:T(8,128)(2,1)}), bf16[8,24,768]{2,1,0:T(8,128)(2,1)}, u32[]{:S(2)}, u32[]{:S(2)}) async-start(bf16[8,24,768]{2,1,0:T(8,128)(2,1)} %bitcast.59), calls=%async_computation.4 | async-start | bytes 589824 | tf_op jit(solution)/shard_map/all_to_all | solution.py:786
  237.2 3.6 %convolution_add_fusion = f32[512,768]{1,0:T(8,128)} fusion(f32[512,768]{1,0:T(8,128)} %get-tuple-element.124.residual_ref, bf16[512,512]{1,0:T(8,128)(2,1)} %get-tuple-element.108.dispatch_ref, bf16[512,768]{1,0:T(8,128)(2,1)} %bitcast.51), kind=kOutput, calls=%fused_computation.11 | convolution fusion | flops 403046400 | bytes 4456448 | tf_op jit(solution)/shard_map/dot_general | solution.py:28
  242.5 4.3 %all-to-all-start.5 = ((bf16[8,24,768]{2,1,0:T(8,128)(2,1)}), bf16[8,24,768]{2,1,0:T(8,128)(2,1)}, u32[]{:S(2)}, u32[]{:S(2)}) async-start(bf16[8,24,768]{2,1,0:T(8,128)(2,1)} %broadcast_in_dim.23), calls=%async_computation.5 | async-start | bytes 589824 | tf_op jit(solution)/shard_map/all_to_all | solution.py:789
  260.7 10.3 %collective-permute-done.26 = bf16[192,768]{1,0:T(8,128)(2,1)S(1)} collective-permute-done((bf16[192,768]{1,0:T(8,128)(2,1)S(1)}, bf16[192,768]{1,0:T(8,128)(2,1)S(1)}, u32[]{:S(2)}, u32[]{:S(2)}) %collective-permute-start.26) | collective-permute-done | bytes 294944 | tf_op jit(solution)/shard_map/ppermute | solution.py:35
  277.3 4.5 %collective-permute-done.31.refs_3_ = bf16[96,768]{1,0:T(8,128)(2,1)} collective-permute-done((bf16[96,768]{1,0:T(8,128)(2,1)}, bf16[96,768]{1,0:T(8,128)(2,1)}, u32[]{:S(2)}, u32[]{:S(2)}) %collective-permute-start.31) | collective-permute-done | bytes 147488 | tf_op jit(solution)/shard_map/ppermute | solution.py:35
  (165 shorter events, 78.9 us)
Async XLA Ops:
  4.0 37.4 %all-to-all-start = ((bf16[8,64,768]{2,1,0:T(8,128)(2,1)}), bf16[8,64,768]{2,1,0:T(8,128)(2,1)S(1)}, u32[]{:S(2)}, u32[]{:S(2)}) async-start(bf16[8,64,768]{2,1,0:T(8,128)(2,1)} %bitcast.60), calls=%async_computation | async-start | bytes 1572864 | tf_op jit(solution)/shard_map/all_to_all | solution.py:831
  11.2 30.1 %collective-permute-start = (bf16[192,768]{1,0:T(8,128)(2,1)S(1)}, bf16[192,768]{1,0:T(8,128)(2,1)S(1)}, u32[]{:S(2)}, u32[]{:S(2)}) collective-permute-start(bf16[192,768]{1,0:T(8,128)(2,1)S(1)} %copy-done.7), channel_id=1, source_target_pairs={{0,1},{1,0},{2,3},{3,2},{4,5},{5,4},{6,7},{7,6},{8,9},{9,8},{10,11... | collective-permute-start | bytes 884744 | tf_op jit(solution)/shard_map/ppermute | solution.py:35
  11.3 30.0 %collective-permute-start.1 = (bf16[192,768]{1,0:T(8,128)(2,1)S(1)}, bf16[192,768]{1,0:T(8,128)(2,1)S(1)}, u32[]{:S(2)}, u32[]{:S(2)}) collective-permute-start(bf16[192,768]{1,0:T(8,128)(2,1)S(1)} %copy-done.7), channel_id=1, source_target_pairs={{0,2},{1,3},{2,0},{3,1},{4,6},{5,7},{6,4},{7,5},{8,10},{9,11},{10,... | collective-permute-start | bytes 884744 | tf_op jit(solution)/shard_map/ppermute | solution.py:35
  12.9 28.5 %collective-permute-start.2 = (bf16[192,768]{1,0:T(8,128)(2,1)S(1)}, bf16[192,768]{1,0:T(8,128)(2,1)S(1)}, u32[]{:S(2)}, u32[]{:S(2)}) collective-permute-start(bf16[192,768]{1,0:T(8,128)(2,1)S(1)} %copy-done.7), channel_id=1, source_target_pairs={{0,3},{1,2},{2,1},{3,0},{4,7},{5,6},{6,5},{7,4},{8,11},{9,10},{10,... | collective-permute-start | bytes 884744 | tf_op jit(solution)/shard_map/ppermute | solution.py:35
  58.0 34.8 %all-to-all-start.1 = ((bf16[8,64,768]{2,1,0:T(8,128)(2,1)}), bf16[8,64,768]{2,1,0:T(8,128)(2,1)}, u32[]{:S(2)}, u32[]{:S(2)}) async-start(bf16[8,64,768]{2,1,0:T(8,128)(2,1)} %bitcast.62), calls=%async_computation.1 | async-start | bytes 1572864 | tf_op jit(solution)/shard_map/all_to_all | solution.py:831
  71.7 19.8 %collective-permute-start.6 = (bf16[512,768]{1,0:T(8,128)(2,1)S(1)}, bf16[512,768]{1,0:T(8,128)(2,1)S(1)}, u32[]{:S(2)}, u32[]{:S(2)}) collective-permute-start(bf16[512,768]{1,0:T(8,128)(2,1)S(1)} %bitcast.47), channel_id=1, source_target_pairs={{0,2},{1,3},{2,0},{3,1},{4,6},{5,7},{6,4},{7,5},{8,10},{9,11},{10,... | collective-permute-start | bytes 2359304 | tf_op jit(solution)/shard_map/ppermute | solution.py:35
  105.2 25.3 %all-to-all-start.2 = ((bf16[8,64,768]{2,1,0:T(8,128)(2,1)}), bf16[8,64,768]{2,1,0:T(8,128)(2,1)S(1)}, u32[]{:S(2)}, u32[]{:S(2)}) async-start(bf16[8,64,768]{2,1,0:T(8,128)(2,1)} %bitcast.61), calls=%async_computation.2 | async-start | bytes 1572864 | tf_op jit(solution)/shard_map/all_to_all | solution.py:831
  109.7 19.8 %collective-permute-start.10 = (bf16[512,768]{1,0:T(8,128)(2,1)}, bf16[512,768]{1,0:T(8,128)(2,1)S(1)}, u32[]{:S(2)}, u32[]{:S(2)}) collective-permute-start(bf16[512,768]{1,0:T(8,128)(2,1)} %bitcast.9.in_ref.refs_0_), channel_id=1, source_target_pairs={{0,2},{1,3},{2,0},{3,1},{4,6},{5,7},{6,4},{7,5},{8,10},{9,11},{10,... | collective-permute-start | bytes 2359304 | tf_op jit(solution)/shard_map/ppermute | solution.py:35
  129.5 17.8 %collective-permute-start.14 = (bf16[512,768]{1,0:T(8,128)(2,1)S(1)}, bf16[512,768]{1,0:T(8,128)(2,1)S(1)}, u32[]{:S(2)}, u32[]{:S(2)}) collective-permute-start(bf16[512,768]{1,0:T(8,128)(2,1)S(1)} %collective-permute-done.10.refs_0_), channel_id=1, source_target_pairs={{0,1},{1,0},{2,3},{3,2},{4,5},{5,4},{6,7},{7,6},{8,9},{9,8},{10,11... | collective-permute-start | bytes 2359304 | tf_op jit(solution)/shard_map/ppermute | solution.py:35
  140.1 18.1 %collective-permute-start.15 = (bf16[2,192,768]{2,1,0:T(8,128)(2,1)}, bf16[2,192,768]{2,1,0:T(8,128)(2,1)}, u32[]{:S(2)}, u32[]{:S(2)}) collective-permute-start(bf16[2,192,768]{2,1,0:T(8,128)(2,1)} %get-tuple-element.168), channel_id=1, source_target_pairs={{0,1},{1,0},{2,3},{3,2},{4,5},{5,4},{6,7},{7,6},{8,9},{9,8},{10,11... | collective-permute-start | bytes 1769480 | tf_op jit(solution)/shard_map/ppermute | solution.py:35
  140.1 19.3 %collective-permute-start.11 = (bf16[192,512]{1,0:T(8,128)(2,1)}, bf16[192,512]{1,0:T(8,128)(2,1)S(1)}, u32[]{:S(2)}, u32[]{:S(2)}) collective-permute-start(bf16[192,512]{1,0:T(8,128)(2,1)} %get-tuple-element.149), channel_id=1, source_target_pairs={{0,1},{1,0},{2,3},{3,2},{4,5},{5,4},{6,7},{7,6},{8,9},{9,8},{10,11... | collective-permute-start | bytes 589832 | tf_op jit(solution)/shard_map/ppermute | solution.py:35
  140.6 18.8 %collective-permute-start.12 = (bf16[192,512]{1,0:T(8,128)(2,1)}, bf16[192,512]{1,0:T(8,128)(2,1)S(1)}, u32[]{:S(2)}, u32[]{:S(2)}) collective-permute-start(bf16[192,512]{1,0:T(8,128)(2,1)} %get-tuple-element.150), channel_id=1, source_target_pairs={{0,2},{1,3},{2,0},{3,1},{4,6},{5,7},{6,4},{7,5},{8,10},{9,11},{10,... | collective-permute-start | bytes 589832 | tf_op jit(solution)/shard_map/ppermute | solution.py:35
  142.1 17.3 %collective-permute-start.13 = (bf16[192,512]{1,0:T(8,128)(2,1)}, bf16[192,512]{1,0:T(8,128)(2,1)S(1)}, u32[]{:S(2)}, u32[]{:S(2)}) collective-permute-start(bf16[192,512]{1,0:T(8,128)(2,1)} %get-tuple-element.151), channel_id=1, source_target_pairs={{0,3},{1,2},{2,1},{3,0},{4,7},{5,6},{6,5},{7,4},{8,11},{9,10},{10,... | collective-permute-start | bytes 589832 | tf_op jit(solution)/shard_map/ppermute | solution.py:35
  142.1 55.8 %all-to-all-start.3 = ((bf16[8,64,768]{2,1,0:T(8,128)(2,1)}), bf16[8,64,768]{2,1,0:T(8,128)(2,1)S(1)}, u32[]{:S(2)}, u32[]{:S(2)}) async-start(bf16[8,64,768]{2,1,0:T(8,128)(2,1)} %bitcast.14), calls=%async_computation.3 | async-start | bytes 1572864 | tf_op jit(solution)/shard_map/all_to_all | solution.py:831
  159.5 22.5 %collective-permute-start.16 = (bf16[1,192,768]{2,1,0:T(8,128)(2,1)S(1)}, bf16[1,192,768]{2,1,0:T(8,128)(2,1)S(1)}, u32[]{:S(2)}, u32[]{:S(2)}) collective-permute-start(bf16[1,192,768]{2,1,0:T(8,128)(2,1)S(1)} %slice.37), channel_id=1, source_target_pairs={{0,2},{1,3},{2,0},{3,1},{4,6},{5,7},{6,4},{7,5},{8,10},{9,11},{10,... | collective-permute-start | bytes 884744 | tf_op jit(solution)/shard_map/ppermute | solution.py:35
  183.7 14.1 %collective-permute-start.17 = (bf16[192,768]{1,0:T(8,128)(2,1)S(1)}, bf16[192,768]{1,0:T(8,128)(2,1)S(1)}, u32[]{:S(2)}, u32[]{:S(2)}) collective-permute-start(bf16[192,768]{1,0:T(8,128)(2,1)S(1)} %constant_dynamic-slice_fusion.1), channel_id=1, source_target_pairs={{0,4},{4,0},{8,12},{12,8},{16,20},{20,16},{24,28},{28,24},{1,5},{5... | collective-permute-start | bytes 884744 | tf_op jit(solution)/shard_map/ppermute | solution.py:35
  208.5 45.2 %collective-permute-start.18 = (bf16[2,512,768]{2,1,0:T(8,128)(2,1)}, bf16[2,512,768]{2,1,0:T(8,128)(2,1)}, u32[]{:S(2)}, u32[]{:S(2)}) collective-permute-start(bf16[2,512,768]{2,1,0:T(8,128)(2,1)} %get-tuple-element.189), channel_id=1, source_target_pairs={{0,1},{1,0},{2,3},{3,2},{4,5},{5,4},{6,7},{7,6},{8,9},{9,8},{10,11... | collective-permute-start | bytes 4718600 | tf_op jit(solution)/shard_map/ppermute | solution.py:35
  212.7 28.1 %all-to-all-start.4 = ((bf16[8,24,768]{2,1,0:T(8,128)(2,1)}), bf16[8,24,768]{2,1,0:T(8,128)(2,1)}, u32[]{:S(2)}, u32[]{:S(2)}) async-start(bf16[8,24,768]{2,1,0:T(8,128)(2,1)} %bitcast.59), calls=%async_computation.4 | async-start | bytes 589824 | tf_op jit(solution)/shard_map/all_to_all | solution.py:786
  232.3 15.2 %collective-permute-start.28 = (bf16[96,768]{1,0:T(8,128)(2,1)}, bf16[96,768]{1,0:T(8,128)(2,1)}, u32[]{:S(2)}, u32[]{:S(2)}) collective-permute-start(bf16[96,768]{1,0:T(8,128)(2,1)} %constant_dynamic-slice_fusion), channel_id=1, source_target_pairs={{0,4},{4,0},{8,12},{12,8},{16,20},{20,16},{24,28},{28,24},{1,5},{5... | collective-permute-start | bytes 442376 | tf_op jit(solution)/shard_map/ppermute | solution.py:35
  233.7 16.5 %collective-permute-start.25 = (bf16[192,768]{1,0:T(8,128)(2,1)S(1)}, bf16[192,768]{1,0:T(8,128)(2,1)}, u32[]{:S(2)}, u32[]{:S(2)}) collective-permute-start(bf16[192,768]{1,0:T(8,128)(2,1)S(1)} %add_convert_fusion.4), channel_id=1, source_target_pairs={{0,8},{4,12},{8,0},{12,4},{16,24},{20,28},{24,16},{28,20},{1,9},{5... | collective-permute-start | bytes 884744 | tf_op jit(solution)/shard_map/ppermute | solution.py:35
  242.5 32.9 %all-to-all-start.5 = ((bf16[8,24,768]{2,1,0:T(8,128)(2,1)}), bf16[8,24,768]{2,1,0:T(8,128)(2,1)}, u32[]{:S(2)}, u32[]{:S(2)}) async-start(bf16[8,24,768]{2,1,0:T(8,128)(2,1)} %broadcast_in_dim.23), calls=%async_computation.5 | async-start | bytes 589824 | tf_op jit(solution)/shard_map/all_to_all | solution.py:789
  251.3 19.7 %collective-permute-start.26 = (bf16[192,768]{1,0:T(8,128)(2,1)S(1)}, bf16[192,768]{1,0:T(8,128)(2,1)S(1)}, u32[]{:S(2)}, u32[]{:S(2)}) collective-permute-start(bf16[192,768]{1,0:T(8,128)(2,1)S(1)} %add_convert_fusion.3), channel_id=1, source_target_pairs={{0,16},{4,20},{8,24},{12,28},{16,0},{20,4},{24,8},{28,12},{1,17},{... | collective-permute-start | bytes 884744 | tf_op jit(solution)/shard_map/ppermute | solution.py:35
  257.0 27.3 %collective-permute-start.19 = (bf16[1,512,768]{2,1,0:T(8,128)(2,1)}, bf16[1,512,768]{2,1,0:T(8,128)(2,1)}, u32[]{:S(2)}, u32[]{:S(2)}) collective-permute-start(bf16[1,512,768]{2,1,0:T(8,128)(2,1)} %slice.47), channel_id=1, source_target_pairs={{0,2},{1,3},{2,0},{3,1},{4,6},{5,7},{6,4},{7,5},{8,10},{9,11},{10,... | collective-permute-start | bytes 2359304 | tf_op jit(solution)/shard_map/ppermute | solution.py:35
  258.4 14.9 %collective-permute-start.30 = (bf16[96,768]{1,0:T(8,128)(2,1)S(1)}, bf16[96,768]{1,0:T(8,128)(2,1)S(1)}, u32[]{:S(2)}, u32[]{:S(2)}) collective-permute-start(bf16[96,768]{1,0:T(8,128)(2,1)S(1)} %add_convert_fusion.7), channel_id=1, source_target_pairs={{0,16},{4,20},{8,24},{12,28},{16,0},{20,4},{24,8},{28,12},{1,17},{... | collective-permute-start | bytes 442376 | tf_op jit(solution)/shard_map/ppermute | solution.py:35
  (44 other events, 445.1 us)

commit v2 on v1

--- a/solution.py
+++ b/solution.py
@@ -56,7 +56,7 @@
     normed_ref, qt_ref, kt_ref, vt_ref,
 ):
     values = tokens_ref[...].astype(f32)
-    normed = (normalized(values) * gain_ref[...] + bias_ref[...]).astype(bf16)
+    normed = (normalized(values) * gain_ref[...][None] + bias_ref[...][None]).astype(bf16)
     normed_ref[...] = normed
     for weight_ref, out_ref, factor in (
         (qw_ref, qt_ref, HEAD_DIM ** (-0.5)), (kw_ref, kt_ref, None), (vw_ref, vt_ref, None)
@@ -74,6 +74,7 @@
     cols = qw.shape[0]
     size = slots // blocks
     fixed = lambda i, r: (0, 0)
+    line = pl.BlockSpec((width,), lambda i, r: (0,))
     return pl.pallas_call(
         project_kernel,
         grid_spec=pltpu.PrefetchScalarGridSpec(
@@ -81,8 +82,8 @@
             grid=(blocks,),
             in_specs=[
                 pl.BlockSpec((size, width), lambda i, r: (i ^ r[0], 0)),
-                pl.BlockSpec((1, width), fixed),
-                pl.BlockSpec((1, width), fixed),
+                line,
+                line,
                 pl.BlockSpec((cols, width), fixed),
                 pl.BlockSpec((cols, width), fixed),
                 pl.BlockSpec((cols, width), fixed),
@@ -98,7 +99,7 @@
         + (jax.ShapeDtypeStruct((cols, slots), bf16),) * 3,
         name="project",
         cost_estimate=COST,
-    )(rank, tokens, gain.reshape(1, -1), bias.reshape(1, -1), qw, kw, vw)
+    )(rank, tokens, gain, bias, qw, kw, vw)
 
 
 def item_ends(lens_ref):
@@ -238,17 +239,25 @@
     )(lens, rank, qt, kt, vt)
 
 
+def stacked_parts(first_head, heads, query, key, value):
+    dim = HEAD_DIM
+    parts = []
+    for n in range(heads):
+        first = (first_head + n) * dim
+        parts += [(2 * n * dim, key, first, dim), ((2 * n + 1) * dim, value, first, dim)]
+    return parts + [(2 * heads * dim, query, first_head * dim, heads * dim)]
+
+
 def backward_kernel(
-    first_head, heads, blocks, lens_ref, rank_ref, qt_ref, kt_ref, vt_ref, log_ref,
-    normed_ref, *rest
+    first_head, heads, blocks, halves, lens_ref, rank_ref, bit_ref, qt_ref, kt_ref, vt_ref,
+    log_ref, qw_ref, kw_ref, vw_ref, normed_ref, *rest
 ):
     width, slots = qt_ref.shape
     shard = slots // blocks
     dim = HEAD_DIM
     out_refs, grad_refs = rest[:blocks], rest[blocks : 2 * blocks]
-    joint_ref, weight_ref, kv_ref, q0_ref, og_ref, right_ref, inner_ref, dq_ref = rest[
-        2 * blocks : -3
-    ]
+    joint_ref, sums_ref, *part_refs = rest[2 * blocks : 2 * blocks + 2 + halves]
+    kv_ref, q0_ref, og_ref, right_ref, inner_ref, dq_ref, made_ref = rest[-10:-3]
     turned_ref, rows_ref, copied = rest[-3:]
     fetch = pltpu.make_async_copy(normed_ref, rows_ref, copied)
     fetch.start()
@@ -319,39 +328,60 @@
     turned_ref[2 * dim * heads :, :] = dq
     joint_ref[:, 2 * dim * heads :] = jnp.transpose(dq, (1, 0))
     fetch.wait()
-    weight_ref[...] = jnp.dot(
-        turned_ref[...], rows_ref[...], preferred_element_type=f32
-    ).astype(bf16)
-
-
-def attend_back(first_head, heads, lens, rank, qt, kt, vt, logs, normed, outs, grads):
+    made_ref[...] = jnp.dot(turned_ref[...], rows_ref[...], preferred_element_type=f32)
+    gains = jnp.zeros((1, rows_ref.shape[1]), f32)
+    shifts = jnp.zeros((1, rows_ref.shape[1]), f32)
+    for at, weight_ref, first, size in stacked_parts(
+        first_head, heads, qw_ref, kw_ref, vw_ref
+    ):
+        weight = weight_ref[first : first + size, :].astype(f32)
+        gains += jnp.sum(weight * made_ref[at : at + size, :], axis=0, keepdims=True)
+        total = jnp.sum(turned_ref[at : at + size, :].astype(f32), axis=1, keepdims=True)
+        shifts += jnp.sum(weight * total, axis=0, keepdims=True)
+    sums_ref[0:1] = gains
+    sums_ref[1:2] = shifts
+    if halves == 2:
+        half = made_ref.shape[0] // 2
+        bit = bit_ref[0, 0]
+        part_refs[0][...] = made_ref[rows_at(bit, half), :].astype(bf16)
+        part_refs[1][...] = made_ref[rows_at(1 - bit, half), :].astype(bf16)
+    else:
+        part_refs[0][...] = made_ref[...].astype(bf16)
+
+
+def attend_back(
+    first_head, heads, halves, lens, rank, bit, qt, kt, vt, logs, weights, normed, outs, grads
+):
     slots, width = normed.shape
     blocks = len(outs)
     dim = HEAD_DIM
-    return pl.pallas_call(
-        functools.partial(backward_kernel, first_head, heads, blocks),
+    cols = 3 * dim * heads
+    return pl.pallas_call(
+        functools.partial(backward_kernel, first_head, heads, blocks, halves),
         out_shape=(
-            jax.ShapeDtypeStruct((slots, 3 * dim * heads), bf16),
-            jax.ShapeDtypeStruct((3 * dim * heads, width), bf16),
-        ),
-        in_specs=[SMEM, SMEM]
-        + [VMEM] * 4
+            jax.ShapeDtypeStruct((slots, cols), bf16),
+            jax.ShapeDtypeStruct((2, width), f32),
+        )
+        + (jax.ShapeDtypeStruct((cols // halves, width), bf16),) * halves,
+        in_specs=[SMEM, SMEM, SMEM]
+        + [VMEM] * 7
         + [pl.BlockSpec(memory_space=pl.ANY)]
         + [VMEM] * (2 * blocks),
-        out_specs=(VMEM, VMEM),
+        out_specs=(VMEM,) * (2 + halves),
         scratch_shapes=[pltpu.VMEM((heads, slots, 2 * dim), bf16)] * 3
         + [
             pltpu.VMEM((heads, 2, 2 * dim, slots), bf16),
             pltpu.VMEM((heads, 1, slots), f32),
             pltpu.VMEM((heads, dim, slots), f32),
-            pltpu.VMEM((3 * dim * heads, slots), bf16),
+            pltpu.VMEM((cols, width), f32),
+            pltpu.VMEM((cols, slots), bf16),
             pltpu.VMEM((slots, width), bf16),
             pltpu.SemaphoreType.DMA,
         ],
         name="attend_back",
         compiler_params=pltpu.CompilerParams(vmem_limit_bytes=60 * 2**20),
         cost_estimate=COST,
-    )(lens, rank, qt, kt, vt, logs, normed, *outs, *grads)
+    )(lens, rank, bit, qt, kt, vt, logs, *weights, normed, *outs, *grads)
 
 
 def plan_kernel(capacity, lens_ref, rank_ref, routes_ref, order_ref, grad_ref,
@@ -411,7 +441,7 @@
     for head_ref, weight_ref in zip(head_refs, weight_refs):
         residual = residual + contract_rows(head_ref[...], weight_ref[...])
     residual_ref[...] = residual
-    normed = (normalized(residual) * gain_ref[...] + bias_ref[...]).astype(bf16)
+    normed = (normalized(residual) * gain_ref[...][None] + bias_ref[...][None]).astype(bf16)
     rows_ref[...] = jnp.dot(
         dispatch_ref[...], normed, preferred_element_type=f32
     ).astype(bf16)
@@ -420,8 +450,8 @@
 def middle(rank, tokens, gain, bias, dispatch, heads, weights):
     count, shard = dispatch.shape
     width = tokens.shape[1]
-    fixed = lambda array: pl.BlockSpec(array.shape, lambda i, r: (0, 0))
-    small = [gain.reshape(1, -1), bias.reshape(1, -1), dispatch, *heads, *weights]
+    fixed = lambda array: pl.BlockSpec(array.shape, lambda i, r: (0,) * array.ndim)
+    small = [gain, bias, dispatch, *heads, *weights]
     return pl.pallas_call(
         functools.partial(middle_kernel, len(heads)),
         grid_spec=pltpu.PrefetchScalarGridSpec(
@@ -447,9 +477,9 @@
     count, lens_ref, rank_ref, dispatch_ref, back_ref, residual_ref, cotangent_ref,
     gain_ref, *refs
 ):
-    weight_refs = refs[:count]
-    grad_ref, low_ref, sums_ref = refs[count : count + 3]
-    part_refs = refs[count + 3 :]
+    head_refs, weight_refs = refs[:count], refs[count : 2 * count]
+    grad_ref, sums_ref, kept_ref, sent_ref = refs[2 * count : 2 * count + 4]
+    part_refs = refs[2 * count + 4 :]
     shard = residual_ref.shape[0]
     grad_normed = contract_rows(dispatch_ref[...], back_ref[...])
     values = residual_ref[...]
@@ -458,7 +488,7 @@
     normed = centred * inverse
     sums_ref[0:1] = jnp.sum(grad_normed * normed, axis=0, keepdims=True)
     sums_ref[1:2] = jnp.sum(grad_normed, axis=0, keepdims=True)
-    scaled = grad_normed * gain_ref[...]
+    scaled = grad_normed * gain_ref[...][None]
     grad = cotangent_ref[...].astype(f32) + inverse * (
         scaled
         - jnp.mean(scaled, axis=-1, keepdims=True)
@@ -466,14 +496,16 @@
     )
     grad_ref[...] = grad
     low = grad.astype(bf16)
-    low_ref[...] = low
     place = rank_ref[0, 0] * shard + lax.broadcasted_iota(jnp.int32, (1, shard), 1)
     alive = place < item_ends(lens_ref)[-1]
     for weight_ref, part_ref in zip(weight_refs, part_refs):
         part_ref[...] = jnp.where(alive, across(weight_ref[...], low), 0.0).astype(bf16)
-
-
-def turn(lens, rank, dispatch, back, residual, cotangent, gain, weights):
+    for j, head_ref in enumerate(head_refs):
+        made = jnp.dot(head_ref[...], low, preferred_element_type=f32)
+        (kept_ref, sent_ref)[j % 2][j // 2] = made.astype(bf16)
+
+
+def turn(lens, rank, dispatch, back, residual, cotangent, gain, heads, weights):
     shard, width = residual.shape
     cols = weights[0].shape[0]
     count = len(weights)
@@ -481,35 +513,16 @@
         functools.partial(turn_kernel, count),
         out_shape=(
             jax.ShapeDtypeStruct((shard, width), f32),
-            jax.ShapeDtypeStruct((shard, width), bf16),
             jax.ShapeDtypeStruct((2, width), f32),
+            jax.ShapeDtypeStruct((count // 2, cols, width), bf16),
+            jax.ShapeDtypeStruct((count // 2, cols, width), bf16),
         )
         + (jax.ShapeDtypeStruct((cols, shard), bf16),) * count,
-        in_specs=[SMEM, SMEM] + [VMEM] * (5 + count),
-        out_specs=(VMEM,) * (3 + count),
+        in_specs=[SMEM, SMEM] + [VMEM] * (5 + 2 * count),
+        out_specs=(VMEM,) * (4 + count),
         name="turn",
         cost_estimate=COST,
-    )(lens, rank, dispatch, back, residual, cotangent, gain.reshape(1, -1), *weights)
-
-
-def output_kernel(low_ref, *refs):
-    head_refs, (kept_ref, sent_ref) = refs[:-2], refs[-2:]
-    for j, head_ref in enumerate(head_refs):
-        made = jnp.dot(head_ref[...], low_ref[...], preferred_element_type=f32)
-        (kept_ref, sent_ref)[j % 2][j // 2] = made.astype(bf16)
-
-
-def output_products(low, heads):
-    cols = heads[0].shape[0]
-    shape = jax.ShapeDtypeStruct((len(heads) // 2, cols, low.shape[1]), bf16)
-    return pl.pallas_call(
-        output_kernel,
-        out_shape=(shape, shape),
-        in_specs=[VMEM] * (1 + len(heads)),
-        out_specs=(VMEM, VMEM),
-        name="output_products",
-        cost_estimate=COST,
-    )(low, *heads)
+    )(lens, rank, dispatch, back, residual, cotangent, gain, *heads, *weights)
 
 
 def gelu_parts(values):
@@ -653,24 +666,22 @@
     )(rank, up, down, *rows, *earlier)
 
 
-def input_grad_kernel(groups, normed_ref, qw_ref, kw_ref, vw_ref, *refs):
+def input_grad_kernel(groups, qw_ref, kw_ref, vw_ref, *refs):
     joint_refs = refs[: len(groups)]
-    kept_ref, sent_ref, sums_ref, turned_ref = refs[len(groups) :]
+    kept_ref, sent_ref, turned_ref = refs[len(groups) :]
     step = pl.program_id(0)
-    dim = HEAD_DIM
 
     @pl.when(step == 0)
     def stack():
-        at = 0
+        start = 0
         for first_head, heads in groups:
-            for n in range(first_head, first_head + heads):
-                part = slice(n * dim, (n + 1) * dim)
-                turned_ref[at : at + dim, :] = kw_ref[part, :]
-                turned_ref[at + dim : at + 2 * dim, :] = vw_ref[part, :]
-                at += 2 * dim
-            part = slice(first_head * dim, (first_head + heads) * dim)
-            turned_ref[at : at + heads * dim, :] = qw_ref[part, :]
-            at += heads * dim
+            for at, weight_ref, first, size in stacked_parts(
+                first_head, heads, qw_ref, kw_ref, vw_ref
+            ):
+                turned_ref[start + at : start + at + size, :] = weight_ref[
+                    first : first + size, :
+                ]
+            start += 3 * heads * HEAD_DIM
 
     total = 0.0
     at = 0
@@ -680,6 +691,7 @@
             joint_ref[...], turned_ref[rows, :], preferred_element_type=f32
         )
         at += joint_ref.shape[1]
+
     @pl.when(step % 2 == 0)
     def keep():
         kept_ref[0] = total.astype(bf16)
@@ -688,49 +700,64 @@
     def send():
         sent_ref[0] = total.astype(bf16)
 
-    gains = jnp.sum(total * normed_ref[...].astype(f32), axis=0, keepdims=True)
-    shifts = jnp.sum(total, axis=0, keepdims=True)
-
-    @pl.when(step == 0)
-    def first():
-        sums_ref[0:1] = gains
-        sums_ref[1:2] = shifts
-
-    @pl.when(step > 0)
-    def later():
-        sums_ref[0:1] += gains
-        sums_ref[1:2] += shifts
-
-
-def input_grad(groups, normed, qw, kw, vw, joints, blocks):
-    slots, width = normed.shape
-    size = slots // blocks
-    cols = qw.shape[0]
+
+def input_grad(groups, weights, joints, first, count, size):
+    cols, width = weights[0].shape
     fixed = pl.BlockSpec((cols, width), lambda i: (0, 0))
     return pl.pallas_call(
         functools.partial(input_grad_kernel, groups),
-        grid=(blocks,),
-        out_shape=(jax.ShapeDtypeStruct((blocks // 2, size, width), bf16),) * 2
-        + (jax.ShapeDtypeStruct((2, width), f32),),
-        in_specs=[pl.BlockSpec((size, width), lambda i: (i, 0)), fixed, fixed, fixed]
-        + [pl.BlockSpec((size, joint.shape[1]), lambda i: (i, 0)) for joint in joints],
-        out_specs=(
-            pl.BlockSpec((1, size, width), lambda i: (i // 2, 0, 0)),
-            pl.BlockSpec((1, size, width), lambda i: (i // 2, 0, 0)),
-            pl.BlockSpec((2, width), lambda i: (0, 0)),
-        ),
+        grid=(count,),
+        out_shape=(jax.ShapeDtypeStruct((count // 2, size, width), bf16),) * 2,
+        in_specs=[fixed] * 3
+        + [
+            pl.BlockSpec((size, joint.shape[1]), lambda i: (first + i, 0))
+            for joint in joints
+        ],
+        out_specs=(pl.BlockSpec((1, size, width), lambda i: (i // 2, 0, 0)),) * 2,
         scratch_shapes=[pltpu.VMEM((3 * cols, width), bf16)],
         name="input_grad",
         cost_estimate=COST,
-    )(normed, qw, kw, vw, *joints)
-
-
-def start_halves(values, axis):
-    low_bit = lax.axis_index(axis) & 1
-    half = values.shape[0] // 2
-    own = lax.dynamic_slice_in_dim(values, low_bit * half, half)
-    away = lax.dynamic_slice_in_dim(values, (1 - low_bit) * half, half)
-    return add_low(own, swap(away, axis, 1))
+    )(*weights, *joints)
+
+
+def close_kernel(rank_ref, tokens_ref, gain_ref, grad_ref, *refs):
+    *part_refs, out_ref = refs
+    grad_in = 0.0
+    for part_ref in part_refs:
+        grad_in = grad_in + part_ref[...].reshape(out_ref.shape).astype(f32)
+    values = tokens_ref[...].astype(f32)
+    centred = values - jnp.mean(values, axis=-1, keepdims=True)
+    inverse = lax.rsqrt(jnp.mean(centred * centred, axis=-1, keepdims=True) + EPSILON)
+    normed = centred * inverse
+    scaled = grad_in * gain_ref[...][None]
+    out_ref[...] = grad_ref[...] + inverse * (
+        scaled
+        - jnp.mean(scaled, axis=-1, keepdims=True)
+        - normed * jnp.mean(scaled * normed, axis=-1, keepdims=True)
+    )
+
+
+def close(rank, tokens, gain, grad, parts):
+    shard, width = grad.shape
+    size = shard // 2
+    rows = lambda i, r: (i, 0)
+    return pl.pallas_call(
+        close_kernel,
+        grid_spec=pltpu.PrefetchScalarGridSpec(
+            num_scalar_prefetch=1,
+            grid=(2,),
+            in_specs=[
+                pl.BlockSpec((size, width), lambda i, r: (2 * r[0] + i, 0)),
+                pl.BlockSpec((width,), lambda i, r: (0,)),
+                pl.BlockSpec((size, width), rows),
+            ]
+            + [pl.BlockSpec((1, size, width), lambda i, r: (0, i, 0))] * len(parts),
+            out_specs=pl.BlockSpec((size, width), rows),
+        ),
+        out_shape=jax.ShapeDtypeStruct((shard, width), f32),
+        name="close",
+        cost_estimate=COST,
+    )(rank, tokens, gain, grad, *parts)
 
 
 def add_low(a, b):
@@ -741,34 +768,30 @@
     return lax.optimization_barrier(values)
 
 
-def finish_kernel(groups, bit_ref, *refs):
-    pieces = refs[: 2 * len(groups)]
-    outs = refs[2 * len(groups) : 2 * len(groups) + 3]
-    whole_refs = refs[2 * len(groups) + 3 :]
-    query_ref, key_ref, value_ref = outs
-    dim = HEAD_DIM
+def finish_kernel(groups, counts, bit_ref, *refs):
+    pieces, refs = refs[: sum(counts)], refs[sum(counts) :]
+    query_ref, key_ref, value_ref = refs[:3]
     bit = bit_ref[0, 0]
-    for g, (first_head, heads) in enumerate(groups):
-        whole_ref = whole_refs[g]
-        half = whole_ref.shape[0] // 2
-        whole_ref[rows_at(bit, half), :] = pieces[2 * g][...].astype(f32)
-        whole_ref[rows_at(1 - bit, half), :] = pieces[2 * g + 1][...].astype(f32)
-        at = 0
-        for n in range(first_head, first_head + heads):
-            part = slice(n * dim, (n + 1) * dim)
-            key_ref[part, :] = whole_ref[at : at + dim, :]
-            value_ref[part, :] = whole_ref[at + dim : at + 2 * dim, :]
-            at += 2 * dim
-        part = slice(first_head * dim, (first_head + heads) * dim)
-        query_ref[part, :] = whole_ref[at : at + heads * dim, :]
+    for (first_head, heads), count, whole_ref in zip(groups, counts, refs[3:]):
+        own, pieces = pieces[:count], pieces[count:]
+        if count == 2:
+            half = whole_ref.shape[0] // 2
+            whole_ref[rows_at(bit, half), :] = own[0][...].astype(f32)
+            whole_ref[rows_at(1 - bit, half), :] = own[1][...].astype(f32)
+        else:
+            whole_ref[...] = own[0][...].astype(f32)
+        for at, target_ref, first, size in stacked_parts(
+            first_head, heads, query_ref, key_ref, value_ref
+        ):
+            target_ref[first : first + size, :] = whole_ref[at : at + size, :]
 
 
 def finish(groups, bit, pieces):
     width = pieces[0][0].shape[1]
     cols = sum(heads for first_head, heads in groups) * HEAD_DIM
-    flat = [half_piece for piece in pieces for half_piece in piece]
-    return pl.pallas_call(
-        functools.partial(finish_kernel, groups),
+    flat = [part for piece in pieces for part in piece]
+    return pl.pallas_call(
+        functools.partial(finish_kernel, groups, [len(piece) for piece in pieces]),
         out_shape=(jax.ShapeDtypeStruct((cols, width), f32),) * 3,
         in_specs=[SMEM] + [VMEM] * len(flat),
         out_specs=(VMEM,) * 3,
@@ -776,25 +799,32 @@
             pltpu.VMEM((3 * heads * HEAD_DIM, width), f32) for first_head, heads in groups
         ],
         name="finish",
+        cost_estimate=COST,
     )(bit, *flat)
 
 
-def sum_rows_over(values, axis):
+def scatter_rows(values, axis):
     count = lax.axis_size(axis)
     rows, cols = values.shape
     parts = values.reshape(count, rows // count, cols)
     arrived = lax.all_to_all(parts, axis, split_axis=0, concat_axis=0, tiled=True)
-    mine = jnp.sum(arrived.astype(f32), axis=0).astype(bf16)
-    spread = jnp.broadcast_to(mine[None], parts.shape)
+    return jnp.sum(arrived.astype(f32), axis=0).astype(bf16)
+
+
+def gather_rows(values, axis):
+    count = lax.axis_size(axis)
+    spread = jnp.broadcast_to(values[None], (count,) + values.shape)
     full = lax.all_to_all(spread, axis, split_axis=0, concat_axis=0, tiled=True)
-    return full.reshape(rows, cols).astype(f32)
-
-
-def sum_small(values, axes):
+    return full.reshape(count * values.shape[0], values.shape[1]).astype(f32)
+
+
+def sum_everywhere(values, axes):
+    count = 1
     for axis in axes:
-        for step in steps_of(lax.axis_size(axis)):
-            values = values + swap(values, axis, step)
-    return values
+        count *= lax.axis_size(axis)
+    spread = jnp.broadcast_to(values[None], (count,) + values.shape)
+    full = lax.all_to_all(spread, axes, split_axis=0, concat_axis=0, tiled=True)
+    return jnp.sum(full, axis=0)
 
 
 def on_device(
@@ -850,19 +880,20 @@
     all_heads = [own_heads[0]] + [
         swap(own_heads[j], "tensor", j) for j in range(1, members)
     ]
+    grad_act = across(flat_grad, down_matrix)
+    all_heads, grad_act = tie(all_heads, grad_act)
     residual, outgoing = middle(
         rank_cell[0], tokens, second_gain, second_bias, dispatch, all_heads, outputs
     )
     flat_in = exchange(outgoing)
 
     flat_grad, outgoing = tie(flat_grad, outgoing)
-    grad_act = across(flat_grad, down_matrix)
     gathered_grads = [flat_grad]
     gathered_rows = [flat_in]
     steps = steps_of(members)
     for step in reversed(steps[1:]):
         gathered_grads += [swap(a, "tensor", step) for a in gathered_grads]
-    flat_in, grad_act, gathered_grads = tie(flat_in, grad_act, gathered_grads)
+    flat_in, gathered_grads = tie(flat_in, gathered_grads)
     gathered_rows = [flat_in]
     for step in reversed(steps[1:]):
         gathered_rows += [swap(a, "tensor", step) for a in gathered_rows]
@@ -886,17 +917,14 @@
     far_rows = [swap(a, "tensor", 1) for a in gathered_rows[1:]]
     grad_back, made, sums = tie(grad_back, made, sums)
 
-    grad_res, grad_low, sums_second, *grad_heads = turn(
+    grad_res, sums_second, kept, sent, *grad_heads = turn(
         item_lengths, rank_cell, dispatch, grad_back, residual, cotangent,
-        second_gain, outputs,
+        second_gain, all_heads, outputs,
     )
     grad_parts = [grad_heads[0]] + [
         swap(grad_heads[j], "tensor", j) for j in range(1, members)
     ]
-    made, sums, grad_low, grad_heads = tie(made, sums, grad_low, grad_heads)
-    returned = exchange(made)
-    kept, sent = output_products(grad_low, all_heads)
-    sums, kept, sent = tie(sums, kept, sent)
+    sums, grad_heads = tie(sums, grad_heads)
     output_sum = add_low(kept, swap(sent, "tensor", 1))
     sums = expert_weights(
         rank_cell[0],
@@ -905,50 +933,61 @@
     )
     grad_parts, sums, output_sum = tie(grad_parts, sums, output_sum)
     up_grad, down_grad = sums
-
+    made, up_grad = tie(made, up_grad)
+    returned = exchange(made)
+
+    bit_cell = (lax.axis_index("dp") & 1).astype(jnp.int32).reshape(1, 1)
+    weights = (qw, kw, vw)
     back = functools.partial(
-        attend_back, lens=item_lengths, rank=rank_cell, qt=qt, kt=kt, vt=vt, logs=logs,
-        normed=normed_in, outs=own_heads,
+        attend_back, lens=item_lengths, rank=rank_cell, bit=bit_cell, qt=qt, kt=kt, vt=vt,
+        logs=logs, weights=weights, normed=normed_in, outs=own_heads,
     )
     groups = ((0, heads - 1), (heads - 1, 1))
-    joint_a, part_a = back(*groups[0], grads=grad_parts)
+    joint_a, sums_a, own_a, away_a = back(*groups[0], halves=2, grads=grad_parts)
     for step in steps[1:]:
         output_sum = add_low(
             output_sum[: len(output_sum) // 2],
             swap(output_sum[len(output_sum) // 2 :], "tensor", step),
         )
-    joint_a, part_a, output_sum, grad_parts = tie(joint_a, part_a, output_sum, grad_parts)
-    half_a = start_halves(part_a, "dp")
-    joint_b, part_b = back(*groups[1], grads=grad_parts)
-    joint_b, part_b, half_a, returned = tie(joint_b, part_b, half_a, returned)
-    output_grad = sum_rows_over(output_sum[0], "dp")
-
-    half_b = start_halves(part_b, "dp")
-    kept, sent, sums_first = input_grad(
-        groups, normed_in, qw, kw, vw, (joint_a, joint_b), members
-    )
-    for step in steps:
-        partial = kept.astype(f32) + swap(sent, "tensor", step).astype(f32)
-        count = partial.shape[0] // 2
-        kept, sent = partial[:count].astype(bf16), partial[count:].astype(bf16)
-    grad_in = partial[0]
-    for step in steps_of(sources)[1:]:
+    joint_a, away_a, output_sum, grad_parts, returned = tie(
+        joint_a, away_a, output_sum, grad_parts, returned
+    )
+    half_a = add_low(own_a, swap(away_a, "dp", 1))
+    joint_b, sums_b, part_b = back(*groups[1], halves=1, grads=grad_parts)
+    output_part = scatter_rows(output_sum[0], "dp")
+    joint_b, part_b, half_a, output_part = tie(joint_b, part_b, half_a, output_part)
+
+    dp_steps = steps_of(sources)
+    far = members // 2
+    far_kept, far_sent = input_grad(
+        groups, weights, (joint_a, joint_b), far, members - far, shard_rows
+    )
+    near_kept, near_sent = input_grad(
+        groups, weights, (joint_a, joint_b), 0, far, shard_rows
+    )
+    part_b = add_low(part_b, swap(part_b, "dp", dp_steps[0]))
+    far_kept = add_low(far_kept, swap(far_sent, "tensor", 1))
+    near_core = swap(near_sent, "tensor", 1)
+    sums_first = sums_a + sums_b
+    far_kept, part_b, sums_first, output_part = tie(
+        far_kept, part_b, sums_first, output_part
+    )
+    near_far = swap(far_kept, "tensor", 2)
+    for step in dp_steps[1:]:
         half_a = add_low(half_a, swap(half_a, "dp", step))
-        half_b = add_low(half_b, swap(half_b, "dp", step))
-    pieces = [(half_a, swap(half_a, "dp", 1)), (half_b, swap(half_b, "dp", 1))]
-    tokens_mine = lax.dynamic_slice_in_dim(tokens, rank * shard_rows, shard_rows).astype(f32)
-    unused_first, pull_first = jax.vjp(
-        lambda values: layer_norm(values, first_gain, first_bias), tokens_mine
-    )
-    token_grad = grad_res + pull_first(grad_in)[0]
+        part_b = add_low(part_b, swap(part_b, "dp", step))
+    pieces = [(half_a, swap(half_a, "dp", 1)), (part_b,)]
+    token_grad = close(
+        rank_cell[0], tokens, first_gain, grad_res, (near_kept, near_core, near_far)
+    )
 
     first_gain_part = (sums_first[0] - first_bias * sums_first[1]) / first_gain
-    norm_sums = sum_small(
+    norm_sums = sum_everywhere(
         jnp.stack([first_gain_part, sums_first[1], sums_second[0], sums_second[1]]),
-        ("tensor", "dp"),
-    )
+        ("dp", "tensor"),
+    )
+    output_grad = gather_rows(output_part, "dp")
     block_out = residual + contract_rows(dispatch, returned)
-    bit_cell = (lax.axis_index("dp") & 1).astype(jnp.int32).reshape(1, 1)
     query_grad, key_grad, value_grad = finish(groups, bit_cell, pieces)
     return (
         block_out,

time: 292 us -> 287 us (0.983)
  starting transfers between devices: 78.2 us -> 60.2 us
  Pallas kernels: 128 us -> 144 us
  waiting for transfers between devices: 44.9 us -> 57.7 us
  other arithmetic: 17.4 us -> 6.46 us
  local copies, waits for them, and re-layouts: 11.6 us -> 7.41 us
    all_to_all x2 -> x3, waiting for transfers between devices: 0.01 us -> 12.4 us  [the longest x1 12.4 us: gather_rows(): full = lax.all_to_all(spread, axis, split_axis=0, concat_axis=0, tiled=True)]
    pallas_call x1, Pallas kernels: 19.5 us -> 27.3 us  [attend(): pl.pallas_call(forward_kernel, out_shape=(jax.ShapeDtypeStruct((width, si...]
    all_to_all x4, starting transfers between devices: 30.7 us -> 23 us  [exchange(): lax.all_to_all(rows.reshape(sources, -1, width), 'dp', split_axis=0, conc...]
    ppermute x32 -> x27, starting transfers between devices: 30.9 us -> 23.6 us  [swap(): return lax.ppermute(values, axis, [(i, i ^ step) for i in range(count)])]
    pallas_call x2, Pallas kernels: 34.9 us -> 42.1 us  [attend_back(): pl.pallas_call(functools.partial(backward_kernel, first_head, heads, bloc...]
    reduce_sum x4 -> x2, other arithmetic: 5.4 us -> 0.13 us  [the longest x1 0.08 us: sum_everywhere(): return jnp.sum(full, axis=0)]
    add x6 -> x1, other arithmetic: 3.01 us -> 0.01 us  [on_device(): sums_first = sums_a + sums_b]
    all_to_all x2 -> x3, starting transfers between devices: 16.6 us -> 13.6 us  [the longest x1 6.56 us: scatter_rows(): lax.all_to_all(parts, axis, split_axis=0, concat_axis=0, tiled=True)]
  transfers between devices with their start and end apart: 38 -> 34, of which waited for: 11 -> 8; matrix products, arithmetic and copies ran while one was open for 10% -> 6% of each run, Pallas kernels for 38% -> 46%
where the time goes in v2:
time: 287 us; the launch traced here: 286 us
  Pallas kernels  144 us (50%)
  starting transfers between devices  60.2 us (21%)
  waiting for transfers between devices  57.7 us (20%)
  matrix products  8.6 us (3%)
  local copies, waits for them, and re-layouts  7.41 us (3%)
  other arithmetic  6.46 us (2%)
    ppermute x27, waiting for transfers between devices, swap(): return lax.ppermute(values, axis, [(i, i ^ step) for i in range(count)])  43.3 us
    pallas_call x2, Pallas kernels, attend_back(): pl.pallas_call(functools.partial(backward_kernel, first_head, heads, bloc...  42.1 us
    pallas_call x1, Pallas kernels, attend(): pl.pallas_call(forward_kernel, out_shape=(jax.ShapeDtypeStruct((width, si...  27.3 us
    ppermute x27, starting transfers between devices, swap(): return lax.ppermute(values, axis, [(i, i ^ step) for i in range(count)])  23.6 us
    all_to_all x4, starting transfers between devices, exchange(): lax.all_to_all(rows.reshape(sources, -1, width), 'dp', split_axis=0, conc...  23 us
    pallas_call x2, Pallas kernels, expert_weights(): pl.pallas_call(functools.partial(weight_kernel, len(group)), grid_spec=pl...  19.4 us
    all_to_all x1, waiting for transfers between devices, gather_rows(): full = lax.all_to_all(spread, axis, split_axis=0, concat_axis=0, tiled=True)  12.4 us
    pallas_call x1, Pallas kernels, expert(): pl.pallas_call(expert_kernel, grid=(hidden // size,), out_shape=(jax.Shap...  11.8 us
  transfers between devices with their start and end apart: 34, of which 8 were waited for; matrix products, arithmetic and copies ran while one was open for 6% of the time, Pallas kernels for 46%

profile of v2, /device:TPU:0, one launch (start us, length us, event | category | flops | bytes accessed | tf_op | source)
XLA Modules:
  0.0 286.0 jit_solution(13852808238156388731)
XLA Ops:
  3.9 7.3 %all-to-all-start = ((bf16[8,64,768]{2,1,0:T(8,128)(2,1)}), bf16[8,64,768]{2,1,0:T(8,128)(2,1)S(1)}, u32[]{:S(2)}, u32[]{:S(2)}) async-start(bf16[8,64,768]{2,1,0:T(8,128)(2,1)} %bitcast.62), calls=%async_computation | async-start | bytes 1572864 | tf_op jit(solution)/shard_map/all_to_all | solution.py:861
  13.2 7.5 %project.1 = (bf16[2048,768]{1,0:T(8,128)(2,1)}, bf16[192,2048]{1,0:T(8,128)(2,1)}, bf16[192,2048]{1,0:T(8,128)(2,1)}, bf16[192,2048]{1,0:T(8,128)(2,1)}) custom-call(s32[1]{0:T(128)} %bitcast.rank_ref, bf16[2048,768]{1,0:T(8,128)(2,1)} %tokens_ref.2, f32[768]{0:T(1024)} %gain_ref.7, f32[768]{0:T(1024)} %bias_ref.2, bf16[192,768]{1,0:T(8,128)(2,1)} %bitcast.37, ...), custom_call_target="tpu_custom_call" | custom-call | flops 1048576 | bytes 1048576 | tf_op jit(solution)/shard_map/project/pallas_call | solution.py:78
  20.6 27.3 %attend.1 = (bf16[192,512]{1,0:T(8,128)(2,1)}, bf16[192,512]{1,0:T(8,128)(2,1)}, bf16[192,512]{1,0:T(8,128)(2,1)}, bf16[192,512]{1,0:T(8,128)(2,1)}, f32[3,1,2048]{2,1,0:T(1,128)}) custom-call(s32[1,5]{1,0:T(1,128)} %lens_ref.9, s32[1,1]{1,0:T(1,128)} %bitcast.1.rank_ref, bf16[192,2048]{1,0:T(8,128)(2,1)} %get-tuple-element.117.qt_ref, ...), custom_call_target="tpu_custom_call" | custom-call | flops 1048576 | bytes 1048576 | tf_op jit(solution)/shard_map/attend/pallas_call | solution.py:226
  49.9 6.9 %fusion.grad_act_ref = f32[512,3072]{1,0:T(8,128)} fusion(bf16[512,768]{1,0:T(8,128)(2,1)S(1)} %bitcast.56, bf16[1,3072,768]{2,1,0:T(8,128)(2,1)} %param.25), kind=kOutput, calls=%fused_computation.18 | convolution fusion | flops 2415919104 | bytes 11796480 | tf_op jit(solution)/shard_map/dot_general | solution.py:432
  59.7 4.8 %middle.1 = (f32[512,768]{1,0:T(8,128)}, bf16[512,768]{1,0:T(8,128)(2,1)}) custom-call(s32[1]{0:T(128)} %bitcast.rank_ref, bf16[2048,768]{1,0:T(8,128)(2,1)} %tokens_ref.2, f32[768]{0:T(1024)} %gain_ref.6, f32[768]{0:T(1024)} %bias_ref.3, bf16[512,512]{1,0:T(8,128)(2,1)} %get-tuple-element.116.dispatch_ref, ...), custom_call_target="tpu_custom_call" | custom-call | flops 1048576 | bytes 1048576 | tf_op jit(solution)/shard_map/middle/pallas_call | solution.py:455
  64.5 5.9 %all-to-all-start.1 = ((bf16[8,64,768]{2,1,0:T(8,128)(2,1)}), bf16[8,64,768]{2,1,0:T(8,128)(2,1)S(1)}, u32[]{:S(2)}, u32[]{:S(2)}) async-start(bf16[8,64,768]{2,1,0:T(8,128)(2,1)} %bitcast.64), calls=%async_computation.1 | async-start | bytes 1572864 | tf_op jit(solution)/shard_map/all_to_all | solution.py:861
  72.0 18.2 %collective-permute-done.6.refs_1_ = bf16[512,768]{1,0:T(8,128)(2,1)S(1)} collective-permute-done((bf16[512,768]{1,0:T(8,128)(2,1)S(1)}, bf16[512,768]{1,0:T(8,128)(2,1)S(1)}, u32[]{:S(2)}, u32[]{:S(2)}) %collective-permute-start.6) | collective-permute-done | bytes 786464 | tf_op jit(solution)/shard_map/ppermute | solution.py:35
  92.2 11.8 %expert.1 = (bf16[512,3072]{1,0:T(8,128)(2,1)}, bf16[512,768]{1,0:T(8,128)(2,1)}) custom-call(bf16[512,768]{1,0:T(8,128)(2,1)} %bitcast.53, f32[512,3072]{1,0:T(8,128)} %fusion.grad_act_ref, bf16[768,3072]{1,0:T(8,128)(2,1)} %bitcast.34), custom_call_target="tpu_custom_call" | custom-call | flops 1048576 | bytes 1048576 | tf_op jit(solution)/shard_map/expert/pallas_call | solution.py:561
  104.1 4.6 %all-to-all-start.2 = ((bf16[8,64,768]{2,1,0:T(8,128)(2,1)}), bf16[8,64,768]{2,1,0:T(8,128)(2,1)S(1)}, u32[]{:S(2)}, u32[]{:S(2)}) async-start(bf16[8,64,768]{2,1,0:T(8,128)(2,1)} %bitcast.63), calls=%async_computation.2 | async-start | bytes 1572864 | tf_op jit(solution)/shard_map/all_to_all | solution.py:861
  110.2 6.6 %product.1 = bf16[512,768]{1,0:T(8,128)(2,1)} custom-call(bf16[512,3072]{1,0:T(8,128)(2,1)} %get-tuple-element.151.a_ref, bf16[3072,768]{1,0:T(8,128)(2,1)} %bitcast.31), custom_call_target="tpu_custom_call" | custom-call | flops 1048576 | bytes 1048576 | tf_op jit(solution)/shard_map/product/pallas_call | solution.py:604
  116.8 9.4 %expert_weights.2 = (f32[768,768]{1,0:T(8,128)}, f32[768,768]{1,0:T(8,128)}) custom-call(s32[1]{0:T(128)} %bitcast.rank_ref, bf16[768,3072]{1,0:T(8,128)(2,1)} %bitcast.35, bf16[3072,768]{1,0:T(8,128)(2,1)} %bitcast.32, bf16[512,768]{1,0:T(8,128)(2,1)} %bitcast.55, bf16[512,768]{1,0:T(8,128)(2,1)} %bitcast.59, ...), custom_call_target="tpu_custom_call" | custom-call | flops 1048576 | bytes 1048576 | tf_op jit(solution)/shard_map/expert_weights/pallas_call | solution.py:647
  130.1 6.5 %turn.1 = (f32[512,768]{1,0:T(8,128)}, f32[2,768]{1,0:T(2,128)}, bf16[2,192,768]{2,1,0:T(8,128)(2,1)}, bf16[2,192,768]{2,1,0:T(8,128)(2,1)}, bf16[192,512]{1,0:T...) custom-call(s32[1,5]{1,0:T(1,128)} %lens_ref.9, ...), custom_call_target="tpu_custom_call" | custom-call | flops 1048576 | bytes 1048576 | tf_op jit(solution)/shard_map/turn/pallas_call | solution.py:512
  139.5 10.0 %expert_weights.3 = (f32[768,768]{1,0:T(8,128)}, f32[768,768]{1,0:T(8,128)}) custom-call(s32[1]{0:T(128)} %bitcast.rank_ref, bf16[768,3072]{1,0:T(8,128)(2,1)} %bitcast.36, bf16[3072,768]{1,0:T(8,128)(2,1)} %bitcast.33, bf16[512,768]{1,0:T(8,128)(2,1)} %copy-done.12, bf16[512,768]{1,0:T(8,128)(2,1)} %copy-done.10, bf16[512,768]{1,0:T(8,128)(2,1)} %copy-done.13, ...), custom_call_target="tpu_custom_call" | custom-call | flops 1048576 | bytes 1048576 | tf_op jit(solution)/shard_map/expert_weights/pallas_call | solution.py:647
  149.7 5.2 %all-to-all-start.3 = ((bf16[8,64,768]{2,1,0:T(8,128)(2,1)}), bf16[8,64,768]{2,1,0:T(8,128)(2,1)S(1)}, u32[]{:S(2)}, u32[]{:S(2)}) async-start(bf16[8,64,768]{2,1,0:T(8,128)(2,1)} %bitcast.15), calls=%async_computation.3 | async-start | bytes 1572864 | tf_op jit(solution)/shard_map/all_to_all | solution.py:861
  156.5 25.4 %attend_back.2 = (bf16[2048,384]{1,0:T(8,128)(2,1)}, f32[2,768]{1,0:T(2,128)}, bf16[192,768]{1,0:T(8,128)(2,1)}, bf16[192,768]{1,0:T(8,128)(2,1)}) custom-call(s32[1,5]{1,0:T(1,128)} %lens_ref.9, s32[1,1]{1,0:T(1,128)} %bitcast.1.rank_ref, s32[1,1]{1,0:T(1,128)} %bitcast.9.bit_ref, bf16[192,2048]{1,0:T(8,128)(2,1)} %get-tuple-element.117.qt_ref, ...), custom_call_target="tpu_custom_call" | custom-call | flops 1048576 | bytes 1048576 | tf_op jit(solution)/shard_map/attend_back/pallas_call | solution.py:359
  182.7 6.6 %all-to-all-start.4 = ((bf16[8,24,768]{2,1,0:T(8,128)(2,1)}), bf16[8,24,768]{2,1,0:T(8,128)(2,1)S(1)}, u32[]{:S(2)}, u32[]{:S(2)}) async-start(bf16[8,24,768]{2,1,0:T(8,128)(2,1)} %bitcast.17), calls=%async_computation.4 | async-start | bytes 589824 | tf_op jit(solution)/shard_map/all_to_all | solution.py:810
  189.3 16.7 %attend_back.3 = (bf16[2048,192]{1,0:T(8,128)(2,1)}, f32[2,768]{1,0:T(2,128)}, bf16[192,768]{1,0:T(8,128)(2,1)}) custom-call(s32[1,5]{1,0:T(1,128)} %lens_ref.9, s32[1,1]{1,0:T(1,128)} %bitcast.1.rank_ref, s32[1,1]{1,0:T(1,128)} %bitcast.9.bit_ref, bf16[192,2048]{1,0:T(8,128)(2,1)} %get-tuple-element.117.qt_ref, ...), custom_call_target="tpu_custom_call" | custom-call | flops 1048576 | bytes 1048576 | tf_op jit(solution)/shard_map/attend_back/pallas_call | solution.py:359
  208.0 4.4 %input_grad.3 = (bf16[1,512,768]{2,1,0:T(8,128)(2,1)}, bf16[1,512,768]{2,1,0:T(8,128)(2,1)}) custom-call(bf16[192,768]{1,0:T(8,128)(2,1)} %bitcast.40, bf16[192,768]{1,0:T(8,128)(2,1)} %bitcast.45, bf16[192,768]{1,0:T(8,128)(2,1)} %bitcast.50, bf16[2048,384]{1,0:T(8,128)(2,1)} %get-tuple-element.186.refs_0_, bf16[2048,192]{1,0:T(8,128)(2,1)} %get-tuple-element.196.refs_1_), custom_call_target="tpu_custom_call" | custom-call | flops 1048576 | bytes 1048576 | tf_op jit(solution)/shard_map/input_grad/pallas_call | solution.py:707
  212.5 3.5 %collective-permute-start.22 = (bf16[192,768]{1,0:T(8,128)(2,1)S(1)}, bf16[192,768]{1,0:T(8,128)(2,1)}, u32[]{:S(2)}, u32[]{:S(2)}) collective-permute-start(bf16[192,768]{1,0:T(8,128)(2,1)S(1)} %add_convert_fusion.7), channel_id=1, source_target_pairs={{0,8},{4,12},{8,0},{12,4},{16,24},{20,28},{24,16},{28,20},{1,9},{5... | collective-permute-start | bytes 884744 | tf_op jit(solution)/shard_map/ppermute | solution.py:35
  217.8 4.4 %input_grad.2 = (bf16[1,512,768]{2,1,0:T(8,128)(2,1)}, bf16[1,512,768]{2,1,0:T(8,128)(2,1)}) custom-call(bf16[192,768]{1,0:T(8,128)(2,1)} %bitcast.41, bf16[192,768]{1,0:T(8,128)(2,1)} %bitcast.46, bf16[192,768]{1,0:T(8,128)(2,1)} %bitcast.51, bf16[2048,384]{1,0:T(8,128)(2,1)} %get-tuple-element.186.refs_0_, bf16[2048,192]{1,0:T(8,128)(2,1)} %get-tuple-element.196.refs_1_), custom_call_target="tpu_custom_call" | custom-call | flops 1048576 | bytes 1048576 | tf_op jit(solution)/shard_map/input_grad/pallas_call | solution.py:707
  234.8 12.4 %all-to-all-done.6 = bf16[8,24,768]{2,1,0:T(8,128)(2,1)S(1)} async-done(((bf16[8,24,768]{2,1,0:T(8,128)(2,1)}), bf16[8,24,768]{2,1,0:T(8,128)(2,1)S(1)}, u32[]{:S(2)}, u32[]{:S(2)}) %all-to-all-start.6) | async-done | bytes 294944 | tf_op jit(solution)/shard_map/all_to_all | solution.py:817
  248.0 3.6 %all-to-all-start.5 = ((f32[32,4,768]{2,1,0:T(4,128)}), f32[32,4,768]{2,1,0:T(4,128)S(1)}, u32[]{:S(2)}, u32[]{:S(2)}) async-start(f32[32,4,768]{2,1,0:T(4,128)} %broadcast_in_dim.8), calls=%async_computation.5 | async-start | bytes 786432 | tf_op jit(solution)/shard_map/all_to_all | solution.py:826
  257.0 19.5 %collective-permute-done.26 = bf16[192,768]{1,0:T(8,128)(2,1)S(1)} collective-permute-done((bf16[192,768]{1,0:T(8,128)(2,1)S(1)}, bf16[192,768]{1,0:T(8,128)(2,1)S(1)}, u32[]{:S(2)}, u32[]{:S(2)}) %collective-permute-start.26) | collective-permute-done | bytes 294944 | tf_op jit(solution)/shard_map/ppermute | solution.py:35
  282.1 3.9 %close.1 = f32[512,768]{1,0:T(8,128)} custom-call(s32[1]{0:T(128)} %bitcast.rank_ref, bf16[2048,768]{1,0:T(8,128)(2,1)} %tokens_ref.2, f32[768]{0:T(1024)} %gain_ref.7, f32[512,768]{1,0:T(8,128)} %get-tuple-element.185.grad_ref, bf16[1,512,768]{2,1,0:T(8,128)(2,1)} %get-tuple-element.197.refs_0_, bf16[1,512,768]{2,1,0:T(8,128)(2,1)} %collective-permute-done.18.refs_1_, ...), custom_call_target="tpu_custom_call" | custom-call | flops 1048576 | bytes 1048576 | tf_op jit(solution)/shard_map/close/pallas_call | solution.py:744
  (146 shorter events, 52.6 us)
Async XLA Ops:
  3.9 44.0 %all-to-all-start = ((bf16[8,64,768]{2,1,0:T(8,128)(2,1)}), bf16[8,64,768]{2,1,0:T(8,128)(2,1)S(1)}, u32[]{:S(2)}, u32[]{:S(2)}) async-start(bf16[8,64,768]{2,1,0:T(8,128)(2,1)} %bitcast.62), calls=%async_computation | async-start | bytes 1572864 | tf_op jit(solution)/shard_map/all_to_all | solution.py:861
  11.2 36.7 %collective-permute-start = (bf16[192,768]{1,0:T(8,128)(2,1)S(1)}, bf16[192,768]{1,0:T(8,128)(2,1)S(1)}, u32[]{:S(2)}, u32[]{:S(2)}) collective-permute-start(bf16[192,768]{1,0:T(8,128)(2,1)S(1)} %copy-done.6), channel_id=1, source_target_pairs={{0,1},{1,0},{2,3},{3,2},{4,5},{5,4},{6,7},{7,6},{8,9},{9,8},{10,11... | collective-permute-start | bytes 884744 | tf_op jit(solution)/shard_map/ppermute | solution.py:35
  11.3 36.6 %collective-permute-start.1 = (bf16[192,768]{1,0:T(8,128)(2,1)S(1)}, bf16[192,768]{1,0:T(8,128)(2,1)S(1)}, u32[]{:S(2)}, u32[]{:S(2)}) collective-permute-start(bf16[192,768]{1,0:T(8,128)(2,1)S(1)} %copy-done.6), channel_id=1, source_target_pairs={{0,2},{1,3},{2,0},{3,1},{4,6},{5,7},{6,4},{7,5},{8,10},{9,11},{10,... | collective-permute-start | bytes 884744 | tf_op jit(solution)/shard_map/ppermute | solution.py:35
  12.9 35.1 %collective-permute-start.2 = (bf16[192,768]{1,0:T(8,128)(2,1)S(1)}, bf16[192,768]{1,0:T(8,128)(2,1)S(1)}, u32[]{:S(2)}, u32[]{:S(2)}) collective-permute-start(bf16[192,768]{1,0:T(8,128)(2,1)S(1)} %copy-done.6), channel_id=1, source_target_pairs={{0,3},{1,2},{2,1},{3,0},{4,7},{5,6},{6,5},{7,4},{8,11},{9,10},{10,... | collective-permute-start | bytes 884744 | tf_op jit(solution)/shard_map/ppermute | solution.py:35
  64.5 26.8 %all-to-all-start.1 = ((bf16[8,64,768]{2,1,0:T(8,128)(2,1)}), bf16[8,64,768]{2,1,0:T(8,128)(2,1)S(1)}, u32[]{:S(2)}, u32[]{:S(2)}) async-start(bf16[8,64,768]{2,1,0:T(8,128)(2,1)} %bitcast.64), calls=%async_computation.1 | async-start | bytes 1572864 | tf_op jit(solution)/shard_map/all_to_all | solution.py:861
  70.5 19.8 %collective-permute-start.6 = (bf16[512,768]{1,0:T(8,128)(2,1)S(1)}, bf16[512,768]{1,0:T(8,128)(2,1)S(1)}, u32[]{:S(2)}, u32[]{:S(2)}) collective-permute-start(bf16[512,768]{1,0:T(8,128)(2,1)S(1)} %bitcast.57), channel_id=1, source_target_pairs={{0,2},{1,3},{2,0},{3,1},{4,6},{5,7},{6,4},{7,5},{8,10},{9,11},{10,... | collective-permute-start | bytes 2359304 | tf_op jit(solution)/shard_map/ppermute | solution.py:35
  104.1 25.1 %all-to-all-start.2 = ((bf16[8,64,768]{2,1,0:T(8,128)(2,1)}), bf16[8,64,768]{2,1,0:T(8,128)(2,1)S(1)}, u32[]{:S(2)}, u32[]{:S(2)}) async-start(bf16[8,64,768]{2,1,0:T(8,128)(2,1)} %bitcast.63), calls=%async_computation.2 | async-start | bytes 1572864 | tf_op jit(solution)/shard_map/all_to_all | solution.py:861
  108.7 19.6 %collective-permute-start.10 = (bf16[512,768]{1,0:T(8,128)(2,1)}, bf16[512,768]{1,0:T(8,128)(2,1)S(1)}, u32[]{:S(2)}, u32[]{:S(2)}) collective-permute-start(bf16[512,768]{1,0:T(8,128)(2,1)} %bitcast.54), channel_id=1, source_target_pairs={{0,2},{1,3},{2,0},{3,1},{4,6},{5,7},{6,4},{7,5},{8,10},{9,11},{10,... | collective-permute-start | bytes 2359304 | tf_op jit(solution)/shard_map/ppermute | solution.py:35
  136.6 13.0 %collective-permute-start.15 = (bf16[2,192,768]{2,1,0:T(8,128)(2,1)}, bf16[2,192,768]{2,1,0:T(8,128)(2,1)S(1)}, u32[]{:S(2)}, u32[]{:S(2)}) collective-permute-start(bf16[2,192,768]{2,1,0:T(8,128)(2,1)} %get-tuple-element.173), channel_id=1, source_target_pairs={{0,1},{1,0},{2,3},{3,2},{4,5},{5,4},{6,7},{7,6},{8,9},{9,8},{10,11... | collective-permute-start | bytes 1769480 | tf_op jit(solution)/shard_map/ppermute | solution.py:35
  136.6 13.0 %collective-permute-start.11 = (bf16[192,512]{1,0:T(8,128)(2,1)}, bf16[192,512]{1,0:T(8,128)(2,1)S(1)}, u32[]{:S(2)}, u32[]{:S(2)}) collective-permute-start(bf16[192,512]{1,0:T(8,128)(2,1)} %get-tuple-element.161), channel_id=1, source_target_pairs={{0,1},{1,0},{2,3},{3,2},{4,5},{5,4},{6,7},{7,6},{8,9},{9,8},{10,11... | collective-permute-start | bytes 589832 | tf_op jit(solution)/shard_map/ppermute | solution.py:35
  149.7 33.0 %all-to-all-start.3 = ((bf16[8,64,768]{2,1,0:T(8,128)(2,1)}), bf16[8,64,768]{2,1,0:T(8,128)(2,1)S(1)}, u32[]{:S(2)}, u32[]{:S(2)}) async-start(bf16[8,64,768]{2,1,0:T(8,128)(2,1)} %bitcast.15), calls=%async_computation.3 | async-start | bytes 1572864 | tf_op jit(solution)/shard_map/all_to_all | solution.py:861
  154.9 27.0 %collective-permute-start.16 = (bf16[1,192,768]{2,1,0:T(8,128)(2,1)S(1)}, bf16[1,192,768]{2,1,0:T(8,128)(2,1)S(1)}, u32[]{:S(2)}, u32[]{:S(2)}) collective-permute-start(bf16[1,192,768]{2,1,0:T(8,128)(2,1)S(1)} %slice.29), channel_id=1, source_target_pairs={{0,2},{1,3},{2,0},{3,1},{4,6},{5,7},{6,4},{7,5},{8,10},{9,11},{10,... | collective-permute-start | bytes 884744 | tf_op jit(solution)/shard_map/ppermute | solution.py:35
  182.7 23.2 %collective-permute-start.17 = (bf16[192,768]{1,0:T(8,128)(2,1)}, bf16[192,768]{1,0:T(8,128)(2,1)S(1)}, u32[]{:S(2)}, u32[]{:S(2)}) collective-permute-start(bf16[192,768]{1,0:T(8,128)(2,1)} %get-tuple-element.194), channel_id=1, source_target_pairs={{0,4},{4,0},{8,12},{12,8},{16,20},{20,16},{24,28},{28,24},{1,5},{5... | collective-permute-start | bytes 884744 | tf_op jit(solution)/shard_map/ppermute | solution.py:35
  182.7 25.2 %all-to-all-start.4 = ((bf16[8,24,768]{2,1,0:T(8,128)(2,1)}), bf16[8,24,768]{2,1,0:T(8,128)(2,1)S(1)}, u32[]{:S(2)}, u32[]{:S(2)}) async-start(bf16[8,24,768]{2,1,0:T(8,128)(2,1)} %bitcast.17), calls=%async_computation.4 | async-start | bytes 589824 | tf_op jit(solution)/shard_map/all_to_all | solution.py:810
  207.9 18.8 %collective-permute-start.20 = (bf16[192,768]{1,0:T(8,128)(2,1)}, bf16[192,768]{1,0:T(8,128)(2,1)S(1)}, u32[]{:S(2)}, u32[]{:S(2)}) collective-permute-start(bf16[192,768]{1,0:T(8,128)(2,1)} %get-tuple-element.201), channel_id=1, source_target_pairs={{0,4},{4,0},{8,12},{12,8},{16,20},{20,16},{24,28},{28,24},{1,5},{5... | collective-permute-start | bytes 884744 | tf_op jit(solution)/shard_map/ppermute | solution.py:35
  212.5 14.4 %collective-permute-start.19 = (bf16[1,512,768]{2,1,0:T(8,128)(2,1)}, bf16[1,512,768]{2,1,0:T(8,128)(2,1)}, u32[]{:S(2)}, u32[]{:S(2)}) collective-permute-start(bf16[1,512,768]{2,1,0:T(8,128)(2,1)} %get-tuple-element.200), channel_id=1, source_target_pairs={{0,1},{1,0},{2,3},{3,2},{4,5},{5,4},{6,7},{7,6},{8,9},{9,8},{10,11... | collective-permute-start | bytes 2359304 | tf_op jit(solution)/shard_map/ppermute | solution.py:35
  222.3 58.9 %collective-permute-start.18 = (bf16[1,512,768]{2,1,0:T(8,128)(2,1)}, bf16[1,512,768]{2,1,0:T(8,128)(2,1)}, u32[]{:S(2)}, u32[]{:S(2)}) collective-permute-start(bf16[1,512,768]{2,1,0:T(8,128)(2,1)} %get-tuple-element.198), channel_id=1, source_target_pairs={{0,1},{1,0},{2,3},{3,2},{4,5},{5,4},{6,7},{7,6},{8,9},{9,8},{10,11... | collective-permute-start | bytes 2359304 | tf_op jit(solution)/shard_map/ppermute | solution.py:35
  224.8 29.7 %collective-permute-start.23 = (bf16[192,768]{1,0:T(8,128)(2,1)S(1)}, bf16[192,768]{1,0:T(8,128)(2,1)S(1)}, u32[]{:S(2)}, u32[]{:S(2)}) collective-permute-start(bf16[192,768]{1,0:T(8,128)(2,1)S(1)} %add_convert_fusion.5), channel_id=1, source_target_pairs={{0,16},{4,20},{8,24},{12,28},{16,0},{20,4},{24,8},{28,12},{1,17},{... | collective-permute-start | bytes 884744 | tf_op jit(solution)/shard_map/ppermute | solution.py:35
  228.2 23.5 %collective-permute-start.25 = (bf16[192,768]{1,0:T(8,128)(2,1)S(1)}, bf16[192,768]{1,0:T(8,128)(2,1)S(1)}, u32[]{:S(2)}, u32[]{:S(2)}) collective-permute-start(bf16[192,768]{1,0:T(8,128)(2,1)S(1)} %add_convert_fusion.6), channel_id=1, source_target_pairs={{0,8},{4,12},{8,0},{12,4},{16,24},{20,28},{24,16},{28,20},{1,9},{5... | collective-permute-start | bytes 884744 | tf_op jit(solution)/shard_map/ppermute | solution.py:35
  230.7 16.5 %all-to-all-start.6 = ((bf16[8,24,768]{2,1,0:T(8,128)(2,1)}), bf16[8,24,768]{2,1,0:T(8,128)(2,1)S(1)}, u32[]{:S(2)}, u32[]{:S(2)}) async-start(bf16[8,24,768]{2,1,0:T(8,128)(2,1)} %broadcast_in_dim.9), calls=%async_computation.6 | async-start | bytes 589824 | tf_op jit(solution)/shard_map/all_to_all | solution.py:817
  234.2 47.0 %collective-permute-start.21 = (bf16[1,512,768]{2,1,0:T(8,128)(2,1)S(1)}, bf16[1,512,768]{2,1,0:T(8,128)(2,1)S(1)}, u32[]{:S(2)}, u32[]{:S(2)}) collective-permute-start(bf16[1,512,768]{2,1,0:T(8,128)(2,1)S(1)} %add_convert_fusion), channel_id=1, source_target_pairs={{0,2},{1,3},{2,0},{3,1},{4,6},{5,7},{6,4},{7,5},{8,10},{9,11},{10,... | collective-permute-start | bytes 2359304 | tf_op jit(solution)/shard_map/ppermute | solution.py:35
  248.0 32.4 %all-to-all-start.5 = ((f32[32,4,768]{2,1,0:T(4,128)}), f32[32,4,768]{2,1,0:T(4,128)S(1)}, u32[]{:S(2)}, u32[]{:S(2)}) async-start(f32[32,4,768]{2,1,0:T(4,128)} %broadcast_in_dim.8), calls=%async_computation.5 | async-start | bytes 786432 | tf_op jit(solution)/shard_map/all_to_all | solution.py:826
  251.7 24.7 %collective-permute-start.26 = (bf16[192,768]{1,0:T(8,128)(2,1)S(1)}, bf16[192,768]{1,0:T(8,128)(2,1)S(1)}, u32[]{:S(2)}, u32[]{:S(2)}) collective-permute-start(bf16[192,768]{1,0:T(8,128)(2,1)S(1)} %add_convert_fusion.3), channel_id=1, source_target_pairs={{0,16},{4,20},{8,24},{12,28},{16,0},{20,4},{24,8},{28,12},{1,17},{... | collective-permute-start | bytes 884744 | tf_op jit(solution)/shard_map/ppermute | solution.py:35
  254.5 22.7 %collective-permute-start.24 = (bf16[192,768]{1,0:T(8,128)(2,1)S(1)}, bf16[192,768]{1,0:T(8,128)(2,1)S(1)}, u32[]{:S(2)}, u32[]{:S(2)}) collective-permute-start(bf16[192,768]{1,0:T(8,128)(2,1)S(1)} %add_convert_fusion.4.refs_0_), channel_id=1, source_target_pairs={{0,4},{4,0},{8,12},{12,8},{16,20},{20,16},{24,28},{28,24},{1,5},{5... | collective-permute-start | bytes 884744 | tf_op jit(solution)/shard_map/ppermute | solution.py:35
  (42 other events, 404.7 us)

commit v3 on v2

--- a/solution.py
+++ b/solution.py
@@ -14,6 +14,7 @@
 bf16 = jnp.bfloat16
 VMEM = pl.BlockSpec(memory_space=pltpu.VMEM)
 SMEM = pl.BlockSpec(memory_space=pltpu.SMEM)
+SUM_ROWS = 16
 COST = pl.CostEstimate(flops=2**20, bytes_accessed=2**20, transcendentals=0)
 
 
@@ -249,14 +250,15 @@
 
 
 def backward_kernel(
-    first_head, heads, blocks, halves, lens_ref, rank_ref, bit_ref, qt_ref, kt_ref, vt_ref,
+    first_head, heads, blocks, extras, lens_ref, rank_ref, bit_ref, qt_ref, kt_ref, vt_ref,
     log_ref, qw_ref, kw_ref, vw_ref, normed_ref, *rest
 ):
+    extra_refs, rest = rest[:extras], rest[extras:]
     width, slots = qt_ref.shape
     shard = slots // blocks
     dim = HEAD_DIM
     out_refs, grad_refs = rest[:blocks], rest[blocks : 2 * blocks]
-    joint_ref, sums_ref, *part_refs = rest[2 * blocks : 2 * blocks + 2 + halves]
+    joint_ref, sums_ref, own_ref, away_ref = rest[2 * blocks : 2 * blocks + 4]
     kv_ref, q0_ref, og_ref, right_ref, inner_ref, dq_ref, made_ref = rest[-10:-3]
     turned_ref, rows_ref, copied = rest[-3:]
     fetch = pltpu.make_async_copy(normed_ref, rows_ref, copied)
@@ -340,34 +342,36 @@
         shifts += jnp.sum(weight * total, axis=0, keepdims=True)
     sums_ref[0:1] = gains
     sums_ref[1:2] = shifts
-    if halves == 2:
-        half = made_ref.shape[0] // 2
-        bit = bit_ref[0, 0]
-        part_refs[0][...] = made_ref[rows_at(bit, half), :].astype(bf16)
-        part_refs[1][...] = made_ref[rows_at(1 - bit, half), :].astype(bf16)
-    else:
-        part_refs[0][...] = made_ref[...].astype(bf16)
+    half = made_ref.shape[0] // 2
+    bit = bit_ref[0, 0]
+    for part_ref, at in ((own_ref, bit), (away_ref, 1 - bit)):
+        part_ref[0:half, :] = made_ref[rows_at(at, half), :].astype(bf16)
+        if extras:
+            lines = [sums_ref[...] + extra_refs[0][...], extra_refs[1][...]]
+            lines.append(jnp.zeros((SUM_ROWS - 4, gains.shape[1]), f32))
+            part_ref[half:, :] = jnp.concatenate(lines, axis=0).astype(bf16)
 
 
 def attend_back(
-    first_head, heads, halves, lens, rank, bit, qt, kt, vt, logs, weights, normed, outs, grads
+    first_head, heads, extras, lens, rank, bit, qt, kt, vt, logs, weights, normed, outs, grads
 ):
     slots, width = normed.shape
     blocks = len(outs)
     dim = HEAD_DIM
     cols = 3 * dim * heads
-    return pl.pallas_call(
-        functools.partial(backward_kernel, first_head, heads, blocks, halves),
+    rows = cols // 2 + (SUM_ROWS if extras else 0)
+    return pl.pallas_call(
+        functools.partial(backward_kernel, first_head, heads, blocks, len(extras)),
         out_shape=(
             jax.ShapeDtypeStruct((slots, cols), bf16),
             jax.ShapeDtypeStruct((2, width), f32),
         )
-        + (jax.ShapeDtypeStruct((cols // halves, width), bf16),) * halves,
+        + (jax.ShapeDtypeStruct((rows, width), bf16),) * 2,
         in_specs=[SMEM, SMEM, SMEM]
         + [VMEM] * 7
         + [pl.BlockSpec(memory_space=pl.ANY)]
-        + [VMEM] * (2 * blocks),
-        out_specs=(VMEM,) * (2 + halves),
+        + [VMEM] * (len(extras) + 2 * blocks),
+        out_specs=(VMEM,) * 4,
         scratch_shapes=[pltpu.VMEM((heads, slots, 2 * dim), bf16)] * 3
         + [
             pltpu.VMEM((heads, 2, 2 * dim, slots), bf16),
@@ -381,7 +385,7 @@
         name="attend_back",
         compiler_params=pltpu.CompilerParams(vmem_limit_bytes=60 * 2**20),
         cost_estimate=COST,
-    )(lens, rank, bit, qt, kt, vt, logs, *weights, normed, *outs, *grads)
+    )(lens, rank, bit, qt, kt, vt, logs, *weights, normed, *extras, *outs, *grads)
 
 
 def plan_kernel(capacity, lens_ref, rank_ref, routes_ref, order_ref, grad_ref,
@@ -768,18 +772,14 @@
     return lax.optimization_barrier(values)
 
 
-def finish_kernel(groups, counts, bit_ref, *refs):
-    pieces, refs = refs[: sum(counts)], refs[sum(counts) :]
+def finish_kernel(groups, bit_ref, *refs):
+    pieces, refs = refs[: 2 * len(groups)], refs[2 * len(groups) :]
     query_ref, key_ref, value_ref = refs[:3]
     bit = bit_ref[0, 0]
-    for (first_head, heads), count, whole_ref in zip(groups, counts, refs[3:]):
-        own, pieces = pieces[:count], pieces[count:]
-        if count == 2:
-            half = whole_ref.shape[0] // 2
-            whole_ref[rows_at(bit, half), :] = own[0][...].astype(f32)
-            whole_ref[rows_at(1 - bit, half), :] = own[1][...].astype(f32)
-        else:
-            whole_ref[...] = own[0][...].astype(f32)
+    for g, ((first_head, heads), whole_ref) in enumerate(zip(groups, refs[3:])):
+        half = whole_ref.shape[0] // 2
+        for piece_ref, at in ((pieces[2 * g], bit), (pieces[2 * g + 1], 1 - bit)):
+            whole_ref[rows_at(at, half), :] = piece_ref[0:half, :].astype(f32)
         for at, target_ref, first, size in stacked_parts(
             first_head, heads, query_ref, key_ref, value_ref
         ):
@@ -787,44 +787,19 @@
 
 
 def finish(groups, bit, pieces):
-    width = pieces[0][0].shape[1]
+    width = pieces[0].shape[1]
     cols = sum(heads for first_head, heads in groups) * HEAD_DIM
-    flat = [part for piece in pieces for part in piece]
-    return pl.pallas_call(
-        functools.partial(finish_kernel, groups, [len(piece) for piece in pieces]),
+    return pl.pallas_call(
+        functools.partial(finish_kernel, groups),
         out_shape=(jax.ShapeDtypeStruct((cols, width), f32),) * 3,
-        in_specs=[SMEM] + [VMEM] * len(flat),
+        in_specs=[SMEM] + [VMEM] * len(pieces),
         out_specs=(VMEM,) * 3,
         scratch_shapes=[
             pltpu.VMEM((3 * heads * HEAD_DIM, width), f32) for first_head, heads in groups
         ],
         name="finish",
         cost_estimate=COST,
-    )(bit, *flat)
-
-
-def scatter_rows(values, axis):
-    count = lax.axis_size(axis)
-    rows, cols = values.shape
-    parts = values.reshape(count, rows // count, cols)
-    arrived = lax.all_to_all(parts, axis, split_axis=0, concat_axis=0, tiled=True)
-    return jnp.sum(arrived.astype(f32), axis=0).astype(bf16)
-
-
-def gather_rows(values, axis):
-    count = lax.axis_size(axis)
-    spread = jnp.broadcast_to(values[None], (count,) + values.shape)
-    full = lax.all_to_all(spread, axis, split_axis=0, concat_axis=0, tiled=True)
-    return full.reshape(count * values.shape[0], values.shape[1]).astype(f32)
-
-
-def sum_everywhere(values, axes):
-    count = 1
-    for axis in axes:
-        count *= lax.axis_size(axis)
-    spread = jnp.broadcast_to(values[None], (count,) + values.shape)
-    full = lax.all_to_all(spread, axes, split_axis=0, concat_axis=0, tiled=True)
-    return jnp.sum(full, axis=0)
+    )(bit, *pieces)
 
 
 def on_device(
@@ -924,40 +899,37 @@
     grad_parts = [grad_heads[0]] + [
         swap(grad_heads[j], "tensor", j) for j in range(1, members)
     ]
-    sums, grad_heads = tie(sums, grad_heads)
+    made, grad_heads = tie(made, grad_heads)
+    returned = exchange(made)
     output_sum = add_low(kept, swap(sent, "tensor", 1))
-    sums = expert_weights(
-        rank_cell[0],
-        list(zip(gathered_rows[1:], gathered_grads[1:])) + list(zip(far_rows, far_grads)),
-        up_matrix, down_matrix, members, sums,
-    )
-    grad_parts, sums, output_sum = tie(grad_parts, sums, output_sum)
-    up_grad, down_grad = sums
-    made, up_grad = tie(made, up_grad)
-    returned = exchange(made)
+    grad_parts, output_sum = tie(grad_parts, output_sum)
 
     bit_cell = (lax.axis_index("dp") & 1).astype(jnp.int32).reshape(1, 1)
     weights = (qw, kw, vw)
+    dp_steps = steps_of(sources)
     back = functools.partial(
         attend_back, lens=item_lengths, rank=rank_cell, bit=bit_cell, qt=qt, kt=kt, vt=vt,
         logs=logs, weights=weights, normed=normed_in, outs=own_heads,
     )
     groups = ((0, heads - 1), (heads - 1, 1))
-    joint_a, sums_a, own_a, away_a = back(*groups[0], halves=2, grads=grad_parts)
+    joint_a, sums_a, own_a, away_a = back(*groups[0], extras=(), grads=grad_parts)
     for step in steps[1:]:
         output_sum = add_low(
             output_sum[: len(output_sum) // 2],
             swap(output_sum[len(output_sum) // 2 :], "tensor", step),
         )
-    joint_a, away_a, output_sum, grad_parts, returned = tie(
-        joint_a, away_a, output_sum, grad_parts, returned
-    )
-    half_a = add_low(own_a, swap(away_a, "dp", 1))
-    joint_b, sums_b, part_b = back(*groups[1], halves=1, grads=grad_parts)
-    output_part = scatter_rows(output_sum[0], "dp")
-    joint_b, part_b, half_a, output_part = tie(joint_b, part_b, half_a, output_part)
-
-    dp_steps = steps_of(sources)
+    joint_a, own_a, away_a, output_sum, grad_parts = tie(
+        joint_a, own_a, away_a, output_sum, grad_parts
+    )
+    own_a = add_low(own_a, swap(away_a, "dp", 1))
+    output_sum = add_low(output_sum[0], swap(output_sum[0], "dp", dp_steps[-1]))
+    joint_b, unused, own_b, away_b = back(
+        *groups[1], extras=(sums_a, sums_second), grads=grad_parts
+    )
+    joint_b, own_a, own_b, away_b, output_sum, returned = tie(
+        joint_b, own_a, own_b, away_b, output_sum, returned
+    )
+
     far = members // 2
     far_kept, far_sent = input_grad(
         groups, weights, (joint_a, joint_b), far, members - far, shard_rows
@@ -965,39 +937,43 @@
     near_kept, near_sent = input_grad(
         groups, weights, (joint_a, joint_b), 0, far, shard_rows
     )
-    part_b = add_low(part_b, swap(part_b, "dp", dp_steps[0]))
+    own_b = add_low(own_b, swap(away_b, "dp", 1))
     far_kept = add_low(far_kept, swap(far_sent, "tensor", 1))
+    far_kept, own_b, output_sum, near_sent = tie(far_kept, own_b, output_sum, near_sent)
     near_core = swap(near_sent, "tensor", 1)
-    sums_first = sums_a + sums_b
-    far_kept, part_b, sums_first, output_part = tie(
-        far_kept, part_b, sums_first, output_part
-    )
     near_far = swap(far_kept, "tensor", 2)
     for step in dp_steps[1:]:
-        half_a = add_low(half_a, swap(half_a, "dp", step))
-        part_b = add_low(part_b, swap(part_b, "dp", step))
-    pieces = [(half_a, swap(half_a, "dp", 1)), (part_b,)]
+        own_a = add_low(own_a, swap(own_a, "dp", step))
+        own_b = add_low(own_b, swap(own_b, "dp", step))
+        if step == dp_steps[1]:
+            own_b, sums, gathered_rows, far_rows = tie(own_b, sums, gathered_rows, far_rows)
+    up_grad, down_grad = expert_weights(
+        rank_cell[0],
+        list(zip(gathered_rows[1:], gathered_grads[1:])) + list(zip(far_rows, far_grads)),
+        up_matrix, down_matrix, members, sums,
+    )
+    own_b, up_grad, down_grad, near_far = tie(own_b, up_grad, down_grad, near_far)
+    norm_sums = own_b[3 * HEAD_DIM * groups[1][1] // 2 :][:8].astype(f32)
+    for step in steps:
+        norm_sums = norm_sums + swap(norm_sums, "tensor", step)
+    pieces = (own_a, swap(own_a, "dp", 1), own_b, swap(own_b, "dp", 1))
     token_grad = close(
         rank_cell[0], tokens, first_gain, grad_res, (near_kept, near_core, near_far)
     )
-
-    first_gain_part = (sums_first[0] - first_bias * sums_first[1]) / first_gain
-    norm_sums = sum_everywhere(
-        jnp.stack([first_gain_part, sums_first[1], sums_second[0], sums_second[1]]),
-        ("dp", "tensor"),
-    )
-    output_grad = gather_rows(output_part, "dp")
+    for step in dp_steps[:-1]:
+        output_sum = add_low(output_sum, swap(output_sum, "dp", step))
+
     block_out = residual + contract_rows(dispatch, returned)
     query_grad, key_grad, value_grad = finish(groups, bit_cell, pieces)
     return (
         block_out,
         token_grad,
-        norm_sums[0],
+        (norm_sums[0] - first_bias * norm_sums[1]) / first_gain,
         norm_sums[1],
         query_grad.T,
         key_grad.T,
         value_grad.T,
-        output_grad,
+        output_sum.astype(f32),
         norm_sums[2],
         norm_sums[3],
         up_grad[None],

time: 287 us -> 253 us (0.88)
  waiting for transfers between devices: 57.7 us -> 40.4 us
  starting transfers between devices: 60.2 us -> 48.6 us
  local copies, waits for them, and re-layouts: 7.41 us -> 3.38 us
    all_to_all x3 -> x0, starting transfers between devices: 13.6 us -> none  [the longest x1 6.56 us: scatter_rows(): lax.all_to_all(parts, axis, split_axis=0, concat_axis=0, tiled=True)]
    all_to_all x3 -> x0, waiting for transfers between devices: 12.4 us -> none  [the longest x1 12.4 us: gather_rows(): full = lax.all_to_all(spread, axis, split_axis=0, concat_axis=0, tiled=True)]
    ppermute x27 -> x33, waiting for transfers between devices: 43.3 us -> 38.3 us  [swap(): return lax.ppermute(values, axis, [(i, i ^ step) for i in range(count)])]
    ppermute x27 -> x33, starting transfers between devices: 23.6 us -> 26 us  [swap(): return lax.ppermute(values, axis, [(i, i ^ step) for i in range(count)])]
  transfers between devices with their start and end apart: 34 -> 37, of which waited for: 8 -> 13; matrix products, arithmetic and copies ran while one was open for 6% -> 6% of each run, Pallas kernels for 46% -> 49%
where the time goes in v3:
time: 253 us
  Pallas kernels  145 us (57%)
  starting transfers between devices  48.6 us (19%)
  waiting for transfers between devices  40.4 us (16%)
  matrix products  8.59 us (3%)
  other arithmetic  6.46 us (3%)
  local copies, waits for them, and re-layouts  3.38 us (1%)
    pallas_call x2, Pallas kernels, attend_back(): pl.pallas_call(functools.partial(backward_kernel, first_head, heads, bloc...  42.1 us
    ppermute x33, waiting for transfers between devices, swap(): return lax.ppermute(values, axis, [(i, i ^ step) for i in range(count)])  38.3 us
    pallas_call x1, Pallas kernels, attend(): pl.pallas_call(forward_kernel, out_shape=(jax.ShapeDtypeStruct((width, si...  27.2 us
    ppermute x33, starting transfers between devices, swap(): return lax.ppermute(values, axis, [(i, i ^ step) for i in range(count)])  26 us
    all_to_all x4, starting transfers between devices, exchange(): lax.all_to_all(rows.reshape(sources, -1, width), 'dp', split_axis=0, conc...  22.7 us
    pallas_call x2, Pallas kernels, expert_weights(): pl.pallas_call(functools.partial(weight_kernel, len(group)), grid_spec=pl...  19.4 us
    pallas_call x1, Pallas kernels, expert(): pl.pallas_call(expert_kernel, grid=(hidden // size,), out_shape=(jax.Shap...  11.8 us
    pallas_call x2, Pallas kernels, input_grad(): pl.pallas_call(functools.partial(input_grad_kernel, groups), grid=(count,...  8.75 us
  transfers between devices with their start and end apart: 37, of which 13 were waited for; matrix products, arithmetic and copies ran while one was open for 6% of the time, Pallas kernels for 49%

profile of v3, /device:TPU:0, one launch (start us, length us, event | category | flops | bytes accessed | tf_op | source)
XLA Modules:
  0.0 253.2 jit_solution(3038781933055831949)
XLA Ops:
  0.7 3.3 %plan.1 = (bf16[512,512]{1,0:T(8,128)(2,1)}, bf16[512,768]{1,0:T(8,128)(2,1)}) custom-call(s32[1,5]{1,0:T(1,128)} %lens_ref.9, s32[1,1]{1,0:T(1,128)} %bitcast.1.rank_ref, s32[1,512]{1,0:T(1,128)} %bitcast.64, s32[1,512]{1,0:T(1,128)} %order_ref.1, bf16[512,768]{1,0:T(8,128)(2,1)} %cotangent_ref.1), custom_call_target="tpu_custom_call" | custom-call | flops 1048576 | bytes 1048576 | tf_op jit(solution)/shard_map/plan/pallas_call | solution.py:422
  3.9 7.3 %all-to-all-start = ((bf16[8,64,768]{2,1,0:T(8,128)(2,1)}), bf16[8,64,768]{2,1,0:T(8,128)(2,1)S(1)}, u32[]{:S(2)}, u32[]{:S(2)}) async-start(bf16[8,64,768]{2,1,0:T(8,128)(2,1)} %bitcast.61), calls=%async_computation | async-start | bytes 1572864 | tf_op jit(solution)/shard_map/all_to_all | solution.py:836
  13.2 7.5 %project.1 = (bf16[2048,768]{1,0:T(8,128)(2,1)}, bf16[192,2048]{1,0:T(8,128)(2,1)}, bf16[192,2048]{1,0:T(8,128)(2,1)}, bf16[192,2048]{1,0:T(8,128)(2,1)}) custom-call(s32[1]{0:T(128)} %bitcast.rank_ref, bf16[2048,768]{1,0:T(8,128)(2,1)} %tokens_ref.2, f32[768]{0:T(1024)} %gain_ref.7, f32[768]{0:T(1024)} %bias_ref.2, bf16[192,768]{1,0:T(8,128)(2,1)} %bitcast.35, ...), custom_call_target="tpu_custom_call" | custom-call | flops 1048576 | bytes 1048576 | tf_op jit(solution)/shard_map/project/pallas_call | solution.py:79
  20.6 27.2 %attend.1 = (bf16[192,512]{1,0:T(8,128)(2,1)}, bf16[192,512]{1,0:T(8,128)(2,1)}, bf16[192,512]{1,0:T(8,128)(2,1)}, bf16[192,512]{1,0:T(8,128)(2,1)}, f32[3,1,2048]{2,1,0:T(1,128)}) custom-call(s32[1,5]{1,0:T(1,128)} %lens_ref.9, s32[1,1]{1,0:T(1,128)} %bitcast.1.rank_ref, bf16[192,2048]{1,0:T(8,128)(2,1)} %get-tuple-element.123.qt_ref, ...), custom_call_target="tpu_custom_call" | custom-call | flops 1048576 | bytes 1048576 | tf_op jit(solution)/shard_map/attend/pallas_call | solution.py:227
  49.9 6.8 %fusion.2.grad_act_ref = f32[512,3072]{1,0:T(8,128)} fusion(bf16[512,768]{1,0:T(8,128)(2,1)S(1)} %bitcast.54, bf16[1,3072,768]{2,1,0:T(8,128)(2,1)} %param.25), kind=kOutput, calls=%fused_computation.21 | convolution fusion | flops 2415919104 | bytes 11796480 | tf_op jit(solution)/shard_map/dot_general | solution.py:436
  59.6 4.8 %middle.1 = (f32[512,768]{1,0:T(8,128)}, bf16[512,768]{1,0:T(8,128)(2,1)}) custom-call(s32[1]{0:T(128)} %bitcast.rank_ref, bf16[2048,768]{1,0:T(8,128)(2,1)} %tokens_ref.2, f32[768]{0:T(1024)} %gain_ref.6, f32[768]{0:T(1024)} %bias_ref.3, bf16[512,512]{1,0:T(8,128)(2,1)} %get-tuple-element.122.dispatch_ref, ...), custom_call_target="tpu_custom_call" | custom-call | flops 1048576 | bytes 1048576 | tf_op jit(solution)/shard_map/middle/pallas_call | solution.py:459
  64.5 5.9 %all-to-all-start.1 = ((bf16[8,64,768]{2,1,0:T(8,128)(2,1)}), bf16[8,64,768]{2,1,0:T(8,128)(2,1)S(1)}, u32[]{:S(2)}, u32[]{:S(2)}) async-start(bf16[8,64,768]{2,1,0:T(8,128)(2,1)} %bitcast.63), calls=%async_computation.1 | async-start | bytes 1572864 | tf_op jit(solution)/shard_map/all_to_all | solution.py:836
  71.8 18.3 %collective-permute-done.6.refs_1_ = bf16[512,768]{1,0:T(8,128)(2,1)S(1)} collective-permute-done((bf16[512,768]{1,0:T(8,128)(2,1)S(1)}, bf16[512,768]{1,0:T(8,128)(2,1)S(1)}, u32[]{:S(2)}, u32[]{:S(2)}) %collective-permute-start.6) | collective-permute-done | bytes 786464 | tf_op jit(solution)/shard_map/ppermute | solution.py:36
  92.2 11.8 %expert.1 = (bf16[512,3072]{1,0:T(8,128)(2,1)}, bf16[512,768]{1,0:T(8,128)(2,1)}) custom-call(bf16[512,768]{1,0:T(8,128)(2,1)} %bitcast.51, f32[512,3072]{1,0:T(8,128)} %fusion.2.grad_act_ref, bf16[768,3072]{1,0:T(8,128)(2,1)} %bitcast.32), custom_call_target="tpu_custom_call" | custom-call | flops 1048576 | bytes 1048576 | tf_op jit(solution)/shard_map/expert/pallas_call | solution.py:565
  104.0 4.6 %all-to-all-start.2 = ((bf16[8,64,768]{2,1,0:T(8,128)(2,1)}), bf16[8,64,768]{2,1,0:T(8,128)(2,1)S(1)}, u32[]{:S(2)}, u32[]{:S(2)}) async-start(bf16[8,64,768]{2,1,0:T(8,128)(2,1)} %bitcast.62), calls=%async_computation.2 | async-start | bytes 1572864 | tf_op jit(solution)/shard_map/all_to_all | solution.py:836
  110.1 6.6 %product.1 = bf16[512,768]{1,0:T(8,128)(2,1)} custom-call(bf16[512,3072]{1,0:T(8,128)(2,1)} %get-tuple-element.157.a_ref, bf16[3072,768]{1,0:T(8,128)(2,1)} %bitcast.29), custom_call_target="tpu_custom_call" | custom-call | flops 1048576 | bytes 1048576 | tf_op jit(solution)/shard_map/product/pallas_call | solution.py:608
  116.8 9.4 %expert_weights.2 = (f32[768,768]{1,0:T(8,128)}, f32[768,768]{1,0:T(8,128)}) custom-call(s32[1]{0:T(128)} %bitcast.rank_ref, bf16[768,3072]{1,0:T(8,128)(2,1)} %bitcast.33, bf16[3072,768]{1,0:T(8,128)(2,1)} %bitcast.30, bf16[512,768]{1,0:T(8,128)(2,1)} %bitcast.53, bf16[512,768]{1,0:T(8,128)(2,1)} %bitcast.57, ...), custom_call_target="tpu_custom_call" | custom-call | flops 1048576 | bytes 1048576 | tf_op jit(solution)/shard_map/expert_weights/pallas_call | solution.py:651
  130.0 6.5 %turn.1 = (f32[512,768]{1,0:T(8,128)}, f32[2,768]{1,0:T(2,128)}, bf16[2,192,768]{2,1,0:T(8,128)(2,1)}, bf16[2,192,768]{2,1,0:T(8,128)(2,1)}, bf16[192,512]{1,0:T...) custom-call(s32[1,5]{1,0:T(1,128)} %lens_ref.9, ...), custom_call_target="tpu_custom_call" | custom-call | flops 1048576 | bytes 1048576 | tf_op jit(solution)/shard_map/turn/pallas_call | solution.py:516
  138.6 4.9 %all-to-all-start.3 = ((bf16[8,64,768]{2,1,0:T(8,128)(2,1)}), bf16[8,64,768]{2,1,0:T(8,128)(2,1)S(1)}, u32[]{:S(2)}, u32[]{:S(2)}) async-start(bf16[8,64,768]{2,1,0:T(8,128)(2,1)} %bitcast.16), calls=%async_computation.3 | async-start | bytes 1572864 | tf_op jit(solution)/shard_map/all_to_all | solution.py:836
  149.1 25.4 %attend_back.2 = (bf16[2048,384]{1,0:T(8,128)(2,1)}, f32[2,768]{1,0:T(2,128)}, bf16[192,768]{1,0:T(8,128)(2,1)}, bf16[192,768]{1,0:T(8,128)(2,1)}) custom-call(s32[1,5]{1,0:T(1,128)} %lens_ref.9, s32[1,1]{1,0:T(1,128)} %bitcast.1.rank_ref, s32[1,1]{1,0:T(1,128)} %bitcast.9.bit_ref, bf16[192,2048]{1,0:T(8,128)(2,1)} %get-tuple-element.123.qt_ref, ...), custom_call_target="tpu_custom_call" | custom-call | flops 1048576 | bytes 1048576 | tf_op jit(solution)/shard_map/attend_back/pallas_call | solution.py:363
  174.9 3.1 %collective-permute-start.16 = (bf16[192,768]{1,0:T(8,128)(2,1)}, bf16[192,768]{1,0:T(8,128)(2,1)S(1)}, u32[]{:S(2)}, u32[]{:S(2)}) collective-permute-start(bf16[192,768]{1,0:T(8,128)(2,1)} %get-tuple-element.188), channel_id=1, source_target_pairs={{0,4},{4,0},{8,12},{12,8},{16,20},{20,16},{24,28},{28,24},{1,5},{5... | collective-permute-start | bytes 884744 | tf_op jit(solution)/shard_map/ppermute | solution.py:36
  178.0 16.7 %attend_back.3 = (bf16[2048,192]{1,0:T(8,128)(2,1)}, f32[2,768]{1,0:T(2,128)}, bf16[112,768]{1,0:T(8,128)(2,1)}, bf16[112,768]{1,0:T(8,128)(2,1)}) custom-call(s32[1,5]{1,0:T(1,128)} %lens_ref.9, s32[1,1]{1,0:T(1,128)} %bitcast.1.rank_ref, s32[1,1]{1,0:T(1,128)} %bitcast.9.bit_ref, bf16[192,2048]{1,0:T(8,128)(2,1)} %get-tuple-element.123.qt_ref, ...), custom_call_target="tpu_custom_call" | custom-call | flops 1048576 | bytes 1048576 | tf_op jit(solution)/shard_map/attend_back/pallas_call | solution.py:363
  194.9 4.3 %input_grad.3 = (bf16[1,512,768]{2,1,0:T(8,128)(2,1)}, bf16[1,512,768]{2,1,0:T(8,128)(2,1)}) custom-call(bf16[192,768]{1,0:T(8,128)(2,1)} %bitcast.38, bf16[192,768]{1,0:T(8,128)(2,1)} %bitcast.43, bf16[192,768]{1,0:T(8,128)(2,1)} %bitcast.48, bf16[2048,384]{1,0:T(8,128)(2,1)} %get-tuple-element.196.refs_0_, bf16[2048,192]{1,0:T(8,128)(2,1)} %get-tuple-element.197.refs_1_), custom_call_target="tpu_custom_call" | custom-call | flops 1048576 | bytes 1048576 | tf_op jit(solution)/shard_map/input_grad/pallas_call | solution.py:711
  199.8 4.4 %input_grad.2 = (bf16[1,512,768]{2,1,0:T(8,128)(2,1)}, bf16[1,512,768]{2,1,0:T(8,128)(2,1)}) custom-call(bf16[192,768]{1,0:T(8,128)(2,1)} %bitcast.39, bf16[192,768]{1,0:T(8,128)(2,1)} %bitcast.44, bf16[192,768]{1,0:T(8,128)(2,1)} %bitcast.49, bf16[2048,384]{1,0:T(8,128)(2,1)} %get-tuple-element.196.refs_0_, bf16[2048,192]{1,0:T(8,128)(2,1)} %get-tuple-element.197.refs_1_), custom_call_target="tpu_custom_call" | custom-call | flops 1048576 | bytes 1048576 | tf_op jit(solution)/shard_map/input_grad/pallas_call | solution.py:711
  217.2 10.0 %expert_weights.3 = (f32[768,768]{1,0:T(8,128)}, f32[768,768]{1,0:T(8,128)}) custom-call(s32[1]{0:T(128)} %bitcast.rank_ref, bf16[768,3072]{1,0:T(8,128)(2,1)} %bitcast.34, bf16[3072,768]{1,0:T(8,128)(2,1)} %bitcast.31, bf16[512,768]{1,0:T(8,128)(2,1)} %copy-done.13, bf16[512,768]{1,0:T(8,128)(2,1)} %copy-done.11, ...), custom_call_target="tpu_custom_call" | custom-call | flops 1048576 | bytes 1048576 | tf_op jit(solution)/shard_map/expert_weights/pallas_call | solution.py:651
  227.3 2.6 %collective-permute-start.32 = (bf16[192,768]{1,0:T(8,128)(2,1)S(1)}, bf16[192,768]{1,0:T(8,128)(2,1)S(1)}, u32[]{:S(2)}, u32[]{:S(2)}) collective-permute-start(bf16[192,768]{1,0:T(8,128)(2,1)S(1)} %add_convert_fusion.3), channel_id=1, source_target_pairs={{0,8},{4,12},{8,0},{12,4},{16,24},{20,28},{24,16},{28,20},{1,9},{5... | collective-permute-start | bytes 884744 | tf_op jit(solution)/shard_map/ppermute | solution.py:36
  229.9 6.6 %collective-permute-done.23 = bf16[112,768]{1,0:T(8,128)(2,1)S(1)} collective-permute-done((bf16[112,768]{1,0:T(8,128)(2,1)S(1)}, bf16[112,768]{1,0:T(8,128)(2,1)S(1)}, u32[]{:S(2)}, u32[]{:S(2)}) %collective-permute-start.23) | collective-permute-done | bytes 172064 | tf_op jit(solution)/shard_map/ppermute | solution.py:36
  239.0 3.7 %collective-permute-done.32 = bf16[192,768]{1,0:T(8,128)(2,1)S(1)} collective-permute-done((bf16[192,768]{1,0:T(8,128)(2,1)S(1)}, bf16[192,768]{1,0:T(8,128)(2,1)S(1)}, u32[]{:S(2)}, u32[]{:S(2)}) %collective-permute-start.32) | collective-permute-done | bytes 294944 | tf_op jit(solution)/shard_map/ppermute | solution.py:36
  243.9 4.1 %close.1 = f32[512,768]{1,0:T(8,128)} custom-call(s32[1]{0:T(128)} %bitcast.rank_ref, bf16[2048,768]{1,0:T(8,128)(2,1)} %tokens_ref.2, f32[768]{0:T(1024)} %gain_ref.7, f32[512,768]{1,0:T(8,128)} %get-tuple-element.195.grad_ref, bf16[1,512,768]{2,1,0:T(8,128)(2,1)} %get-tuple-element.198.refs_0_, bf16[1,512,768]{2,1,0:T(8,128)(2,1)} %collective-permute-done.20.refs_1_, ...), custom_call_target="tpu_custom_call" | custom-call | flops 1048576 | bytes 1048576 | tf_op jit(solution)/shard_map/close/pallas_call | solution.py:748
  (143 shorter events, 46.2 us)
Async XLA Ops:
  3.9 44.0 %all-to-all-start = ((bf16[8,64,768]{2,1,0:T(8,128)(2,1)}), bf16[8,64,768]{2,1,0:T(8,128)(2,1)S(1)}, u32[]{:S(2)}, u32[]{:S(2)}) async-start(bf16[8,64,768]{2,1,0:T(8,128)(2,1)} %bitcast.61), calls=%async_computation | async-start | bytes 1572864 | tf_op jit(solution)/shard_map/all_to_all | solution.py:836
  11.2 36.6 %collective-permute-start = (bf16[192,768]{1,0:T(8,128)(2,1)S(1)}, bf16[192,768]{1,0:T(8,128)(2,1)S(1)}, u32[]{:S(2)}, u32[]{:S(2)}) collective-permute-start(bf16[192,768]{1,0:T(8,128)(2,1)S(1)} %copy-done.6), channel_id=1, source_target_pairs={{0,1},{1,0},{2,3},{3,2},{4,5},{5,4},{6,7},{7,6},{8,9},{9,8},{10,11... | collective-permute-start | bytes 884744 | tf_op jit(solution)/shard_map/ppermute | solution.py:36
  11.3 36.5 %collective-permute-start.1 = (bf16[192,768]{1,0:T(8,128)(2,1)S(1)}, bf16[192,768]{1,0:T(8,128)(2,1)S(1)}, u32[]{:S(2)}, u32[]{:S(2)}) collective-permute-start(bf16[192,768]{1,0:T(8,128)(2,1)S(1)} %copy-done.6), channel_id=1, source_target_pairs={{0,2},{1,3},{2,0},{3,1},{4,6},{5,7},{6,4},{7,5},{8,10},{9,11},{10,... | collective-permute-start | bytes 884744 | tf_op jit(solution)/shard_map/ppermute | solution.py:36
  12.9 35.0 %collective-permute-start.2 = (bf16[192,768]{1,0:T(8,128)(2,1)S(1)}, bf16[192,768]{1,0:T(8,128)(2,1)S(1)}, u32[]{:S(2)}, u32[]{:S(2)}) collective-permute-start(bf16[192,768]{1,0:T(8,128)(2,1)S(1)} %copy-done.6), channel_id=1, source_target_pairs={{0,3},{1,2},{2,1},{3,0},{4,7},{5,6},{6,5},{7,4},{8,11},{9,10},{10,... | collective-permute-start | bytes 884744 | tf_op jit(solution)/shard_map/ppermute | solution.py:36
  64.5 26.8 %all-to-all-start.1 = ((bf16[8,64,768]{2,1,0:T(8,128)(2,1)}), bf16[8,64,768]{2,1,0:T(8,128)(2,1)S(1)}, u32[]{:S(2)}, u32[]{:S(2)}) async-start(bf16[8,64,768]{2,1,0:T(8,128)(2,1)} %bitcast.63), calls=%async_computation.1 | async-start | bytes 1572864 | tf_op jit(solution)/shard_map/all_to_all | solution.py:836
  70.4 19.8 %collective-permute-start.6 = (bf16[512,768]{1,0:T(8,128)(2,1)S(1)}, bf16[512,768]{1,0:T(8,128)(2,1)S(1)}, u32[]{:S(2)}, u32[]{:S(2)}) collective-permute-start(bf16[512,768]{1,0:T(8,128)(2,1)S(1)} %bitcast.55), channel_id=1, source_target_pairs={{0,2},{1,3},{2,0},{3,1},{4,6},{5,7},{6,4},{7,5},{8,10},{9,11},{10,... | collective-permute-start | bytes 2359304 | tf_op jit(solution)/shard_map/ppermute | solution.py:36
  91.3 12.7 %collective-permute-start.7 = (bf16[512,768]{1,0:T(8,128)(2,1)S(1)}, bf16[512,768]{1,0:T(8,128)(2,1)}, u32[]{:S(2)}, u32[]{:S(2)}) collective-permute-start(bf16[512,768]{1,0:T(8,128)(2,1)S(1)} %bitcast.50), channel_id=1, source_target_pairs={{0,1},{1,0},{2,3},{3,2},{4,5},{5,4},{6,7},{7,6},{8,9},{9,8},{10,11... | collective-permute-start | bytes 2359304 | tf_op jit(solution)/shard_map/ppermute | solution.py:36
  91.3 12.7 %collective-permute-start.8 = (bf16[512,768]{1,0:T(8,128)(2,1)S(1)}, bf16[512,768]{1,0:T(8,128)(2,1)}, u32[]{:S(2)}, u32[]{:S(2)}) collective-permute-start(bf16[512,768]{1,0:T(8,128)(2,1)S(1)} %bitcast.56), channel_id=1, source_target_pairs={{0,1},{1,0},{2,3},{3,2},{4,5},{5,4},{6,7},{7,6},{8,9},{9,8},{10,11... | collective-permute-start | bytes 2359304 | tf_op jit(solution)/shard_map/ppermute | solution.py:36
  91.8 12.2 %collective-permute-start.9 = (bf16[512,768]{1,0:T(8,128)(2,1)S(1)}, bf16[512,768]{1,0:T(8,128)(2,1)S(1)}, u32[]{:S(2)}, u32[]{:S(2)}) collective-permute-start(bf16[512,768]{1,0:T(8,128)(2,1)S(1)} %collective-permute-done.6.refs_1_), channel_id=1, source_target_pairs={{0,1},{1,0},{2,3},{3,2},{4,5},{5,4},{6,7},{7,6},{8,9},{9,8},{10,11... | collective-permute-start | bytes 2359304 | tf_op jit(solution)/shard_map/ppermute | solution.py:36
  104.0 25.1 %all-to-all-start.2 = ((bf16[8,64,768]{2,1,0:T(8,128)(2,1)}), bf16[8,64,768]{2,1,0:T(8,128)(2,1)S(1)}, u32[]{:S(2)}, u32[]{:S(2)}) async-start(bf16[8,64,768]{2,1,0:T(8,128)(2,1)} %bitcast.62), calls=%async_computation.2 | async-start | bytes 1572864 | tf_op jit(solution)/shard_map/all_to_all | solution.py:836
  108.6 19.6 %collective-permute-start.10 = (bf16[512,768]{1,0:T(8,128)(2,1)}, bf16[512,768]{1,0:T(8,128)(2,1)S(1)}, u32[]{:S(2)}, u32[]{:S(2)}) collective-permute-start(bf16[512,768]{1,0:T(8,128)(2,1)} %bitcast.52), channel_id=1, source_target_pairs={{0,2},{1,3},{2,0},{3,1},{4,6},{5,7},{6,4},{7,5},{8,10},{9,11},{10,... | collective-permute-start | bytes 2359304 | tf_op jit(solution)/shard_map/ppermute | solution.py:36
  138.6 56.3 %all-to-all-start.3 = ((bf16[8,64,768]{2,1,0:T(8,128)(2,1)}), bf16[8,64,768]{2,1,0:T(8,128)(2,1)S(1)}, u32[]{:S(2)}, u32[]{:S(2)}) async-start(bf16[8,64,768]{2,1,0:T(8,128)(2,1)} %bitcast.16), calls=%async_computation.3 | async-start | bytes 1572864 | tf_op jit(solution)/shard_map/all_to_all | solution.py:836
  147.5 27.0 %collective-permute-start.15 = (bf16[1,192,768]{2,1,0:T(8,128)(2,1)S(1)}, bf16[1,192,768]{2,1,0:T(8,128)(2,1)S(1)}, u32[]{:S(2)}, u32[]{:S(2)}) collective-permute-start(bf16[1,192,768]{2,1,0:T(8,128)(2,1)S(1)} %slice.25), channel_id=1, source_target_pairs={{0,2},{1,3},{2,0},{3,1},{4,6},{5,7},{6,4},{7,5},{8,10},{9,11},{10,... | collective-permute-start | bytes 884744 | tf_op jit(solution)/shard_map/ppermute | solution.py:36
  174.6 20.0 %collective-permute-start.17 = (bf16[192,768]{1,0:T(8,128)(2,1)S(1)}, bf16[192,768]{1,0:T(8,128)(2,1)S(1)}, u32[]{:S(2)}, u32[]{:S(2)}) collective-permute-start(bf16[192,768]{1,0:T(8,128)(2,1)S(1)} %bitcast.60), channel_id=1, source_target_pairs={{0,16},{4,20},{8,24},{12,28},{16,0},{20,4},{24,8},{28,12},{1,17},{... | collective-permute-start | bytes 884744 | tf_op jit(solution)/shard_map/ppermute | solution.py:36
  174.9 19.9 %collective-permute-start.16 = (bf16[192,768]{1,0:T(8,128)(2,1)}, bf16[192,768]{1,0:T(8,128)(2,1)S(1)}, u32[]{:S(2)}, u32[]{:S(2)}) collective-permute-start(bf16[192,768]{1,0:T(8,128)(2,1)} %get-tuple-element.188), channel_id=1, source_target_pairs={{0,4},{4,0},{8,12},{12,8},{16,20},{20,16},{24,28},{28,24},{1,5},{5... | collective-permute-start | bytes 884744 | tf_op jit(solution)/shard_map/ppermute | solution.py:36
  199.5 15.4 %collective-permute-start.22 = (bf16[512,768]{1,0:T(8,128)(2,1)}, bf16[512,768]{1,0:T(8,128)(2,1)}, u32[]{:S(2)}, u32[]{:S(2)}) collective-permute-start(bf16[512,768]{1,0:T(8,128)(2,1)} %copy-done.13), channel_id=1, source_target_pairs={{0,1},{1,0},{2,3},{3,2},{4,5},{5,4},{6,7},{7,6},{8,9},{9,8},{10,11... | collective-permute-start | bytes 2359304 | tf_op jit(solution)/shard_map/ppermute | solution.py:36
  199.8 13.1 %collective-permute-start.27 = (bf16[192,768]{1,0:T(8,128)(2,1)S(1)}, bf16[192,768]{1,0:T(8,128)(2,1)}, u32[]{:S(2)}, u32[]{:S(2)}) collective-permute-start(bf16[192,768]{1,0:T(8,128)(2,1)S(1)} %add_convert_fusion.7), channel_id=1, source_target_pairs={{0,8},{4,12},{8,0},{12,4},{16,24},{20,28},{24,16},{28,20},{1,9},{5... | collective-permute-start | bytes 884744 | tf_op jit(solution)/shard_map/ppermute | solution.py:36
  210.3 26.2 %collective-permute-start.24 = (bf16[1,512,768]{2,1,0:T(8,128)(2,1)S(1)}, bf16[1,512,768]{2,1,0:T(8,128)(2,1)S(1)}, u32[]{:S(2)}, u32[]{:S(2)}) collective-permute-start(bf16[1,512,768]{2,1,0:T(8,128)(2,1)S(1)} %add_convert_fusion), channel_id=1, source_target_pairs={{0,2},{1,3},{2,0},{3,1},{4,6},{5,7},{6,4},{7,5},{8,10},{9,11},{10,... | collective-permute-start | bytes 2359304 | tf_op jit(solution)/shard_map/ppermute | solution.py:36
  210.9 16.3 %collective-permute-start.31 = (bf16[192,768]{1,0:T(8,128)(2,1)S(1)}, bf16[192,768]{1,0:T(8,128)(2,1)S(1)}, u32[]{:S(2)}, u32[]{:S(2)}) collective-permute-start(bf16[192,768]{1,0:T(8,128)(2,1)S(1)} %add_convert_fusion.6), channel_id=1, source_target_pairs={{0,4},{4,0},{8,12},{12,8},{16,20},{20,16},{24,28},{28,24},{1,5},{5... | collective-permute-start | bytes 884744 | tf_op jit(solution)/shard_map/ppermute | solution.py:36
  214.0 22.7 %collective-permute-start.28 = (bf16[192,768]{1,0:T(8,128)(2,1)S(1)}, bf16[192,768]{1,0:T(8,128)(2,1)S(1)}, u32[]{:S(2)}, u32[]{:S(2)}) collective-permute-start(bf16[192,768]{1,0:T(8,128)(2,1)S(1)} %add_convert_fusion.5), channel_id=1, source_target_pairs={{0,16},{4,20},{8,24},{12,28},{16,0},{20,4},{24,8},{28,12},{1,17},{... | collective-permute-start | bytes 884744 | tf_op jit(solution)/shard_map/ppermute | solution.py:36
  214.8 29.1 %collective-permute-start.20 = (bf16[1,512,768]{2,1,0:T(8,128)(2,1)}, bf16[1,512,768]{2,1,0:T(8,128)(2,1)}, u32[]{:S(2)}, u32[]{:S(2)}) collective-permute-start(bf16[1,512,768]{2,1,0:T(8,128)(2,1)} %get-tuple-element.205), channel_id=1, source_target_pairs={{0,1},{1,0},{2,3},{3,2},{4,5},{5,4},{6,7},{7,6},{8,9},{9,8},{10,11... | collective-permute-start | bytes 2359304 | tf_op jit(solution)/shard_map/ppermute | solution.py:36
  214.9 21.6 %collective-permute-start.23 = (bf16[112,768]{1,0:T(8,128)(2,1)S(1)}, bf16[112,768]{1,0:T(8,128)(2,1)S(1)}, u32[]{:S(2)}, u32[]{:S(2)}) collective-permute-start(bf16[112,768]{1,0:T(8,128)(2,1)S(1)} %add_convert_fusion.10), channel_id=1, source_target_pairs={{0,16},{4,20},{8,24},{12,28},{16,0},{20,4},{24,8},{28,12},{1,17},{... | collective-permute-start | bytes 516104 | tf_op jit(solution)/shard_map/ppermute | solution.py:36
  227.3 15.4 %collective-permute-start.32 = (bf16[192,768]{1,0:T(8,128)(2,1)S(1)}, bf16[192,768]{1,0:T(8,128)(2,1)S(1)}, u32[]{:S(2)}, u32[]{:S(2)}) collective-permute-start(bf16[192,768]{1,0:T(8,128)(2,1)S(1)} %add_convert_fusion.3), channel_id=1, source_target_pairs={{0,8},{4,12},{8,0},{12,4},{16,24},{20,28},{24,16},{28,20},{1,9},{5... | collective-permute-start | bytes 884744 | tf_op jit(solution)/shard_map/ppermute | solution.py:36
  236.7 12.6 %collective-permute-start.29 = (bf16[192,768]{1,0:T(8,128)(2,1)S(1)}, bf16[192,768]{1,0:T(8,128)(2,1)S(1)}, u32[]{:S(2)}, u32[]{:S(2)}) collective-permute-start(bf16[192,768]{1,0:T(8,128)(2,1)S(1)} %add_convert_fusion.4.refs_0_), channel_id=1, source_target_pairs={{0,4},{4,0},{8,12},{12,8},{16,20},{20,16},{24,28},{28,24},{1,5},{5... | collective-permute-start | bytes 884744 | tf_op jit(solution)/shard_map/ppermute | solution.py:36
  (42 other events, 358.6 us)

commit v4 on v3

--- a/solution.py
+++ b/solution.py
@@ -137,11 +137,17 @@
     return pl.ds(pl.multiple_of(block * size, size), size)
 
 
-def memory_segments(block, size, shard, rank, ends, axis):
-    shape = (1, size) if axis else (size, 1)
-    at = block * size + lax.broadcasted_iota(jnp.int32, shape, axis)
+def fill_segments(row_ref, col_ref, shard, rank, ends):
+    slots = row_ref.shape[1]
+    at = lax.broadcasted_iota(jnp.int32, (1, slots), 1)
     place = ((at // shard) ^ rank) * shard + at % shard
-    return segments_at(place, ends)
+    segments = segments_at(place, ends)
+    row_ref[...] = segments
+    col_ref[...] = jnp.transpose(jnp.broadcast_to(segments, (128, slots)), (1, 0))
+
+
+def block_bias(row_ref, col_ref, rows, cols):
+    return jnp.where(col_ref[rows, 0:1] == row_ref[:, cols], 0.0, NEGATIVE)
 
 
 def lane_masked(values, head):
@@ -151,93 +157,124 @@
 
 
 def forward_kernel(
-    lens_ref, rank_ref, qt_ref, kt_ref, vt_ref, *refs
+    first, blocks, lens_ref, rank_ref, qt_ref, kt_ref, vt_ref, *refs
 ):
-    *out_refs, log_ref, masked_ref, out_ref = refs
-    blocks, width, shard = out_ref.shape
+    *out_refs, log_ref, masked_ref, out_ref, row_ref, col_ref, score_ref = refs
+    count, width, size = out_ref.shape
     heads = width // HEAD_DIM
-    pair = 1
-    size = shard * pair
+    shard = size
     rank = rank_ref[0, 0]
     ends = item_ends(lens_ref)
+    fill_segments(row_ref, col_ref, shard, rank, ends)
     keys = jnp.transpose(kt_ref[...], (1, 0))
     for h in range(heads):
         masked_ref[h] = lane_masked(keys, h)
 
-    def query_block(i, unused):
-        at = i ^ (rank // pair)
+    def query_block(b, unused):
+        at = first + b
+        i = at ^ rank
         cols = rows_at(at, size)
-        seg_q = memory_segments(at, size, shard, rank, ends, 1)
         queries = qt_ref[:, cols]
 
-        def key_block(j, carry):
+        def score_block(j, carry):
             rows = rows_at(j ^ rank, shard)
-            seg_k = memory_segments(j ^ rank, shard, shard, rank, ends, 0)
-            same = seg_k == seg_q
+            bias = block_bias(row_ref, col_ref, rows, cols)
             result = []
             for h in range(heads):
-                highest, summed, total = carry[h]
                 scores = jnp.dot(
                     masked_ref[h, rows, :], queries, preferred_element_type=f32
                 )
-                scores = jnp.where(same, scores, NEGATIVE)
-                raised = jnp.maximum(highest, jnp.max(scores, axis=0, keepdims=True))
-                shrink = jnp.exp(highest - raised)
-                soft = jnp.exp(scores - raised)
-                summed = summed * shrink + jnp.sum(soft, axis=0, keepdims=True)
-                total = total * shrink + jnp.dot(
+                scores = scores + bias
+                score_ref[h, rows_at(j, shard), :] = scores
+                part = jnp.max(scores.reshape(-1, 8, size), axis=0)
+                result.append(jnp.maximum(carry[h], part))
+            return tuple(result)
+
+        low, high = block_span(i * size, size, shard, ends)
+        peaks = lax.fori_loop(
+            low, high, score_block, (jnp.full((8, size), NEGATIVE, f32),) * heads
+        )
+        peaks = [jnp.max(peak, axis=0, keepdims=True) for peak in peaks]
+
+        def key_block(j, carry):
+            rows = rows_at(j ^ rank, shard)
+            result = []
+            for h in range(heads):
+                summed, total = carry[h]
+                soft = jnp.exp(score_ref[h, rows_at(j, shard), :] - peaks[h])
+                summed = summed + jnp.sum(soft.reshape(-1, 8, size), axis=0)
+                total = total + jnp.dot(
                     vt_ref[pl.ds(h * HEAD_DIM, HEAD_DIM), rows],
                     soft.astype(bf16),
                     preferred_element_type=f32,
                 )
-                result.append((raised, summed, total))
+                result.append((summed, total))
             return tuple(result)
 
-        start = tuple(
-            (
-                jnp.full((1, size), NEGATIVE, f32),
-                jnp.zeros((1, size), f32),
-                jnp.zeros((HEAD_DIM, size), f32),
-            )
-            for h in range(heads)
-        )
-        low, high = block_span(i * size, size, shard, ends)
+        start = ((jnp.zeros((8, size), f32), jnp.zeros((HEAD_DIM, size), f32)),) * heads
         done = lax.fori_loop(low, high, key_block, start)
-        live = seg_q < len(ends)
+        live = row_ref[:, cols] < len(ends)
         for h in range(heads):
-            highest, summed, total = done[h]
+            summed, total = done[h]
+            summed = jnp.sum(summed, axis=0, keepdims=True)
+            highest = peaks[h]
             summed = jnp.where(live, summed, 1.0)
             result = jnp.where(live, total / summed, 0.0).astype(bf16)
             logs = jnp.where(live, highest + jnp.log(summed), -NEGATIVE)
-            for p in range(pair):
-                part = slice(p * shard, (p + 1) * shard)
-                out_ref[at * pair + p, pl.ds(h * HEAD_DIM, HEAD_DIM), :] = result[:, part]
-            log_ref[h, :, cols] = logs
+            out_ref[b, pl.ds(h * HEAD_DIM, HEAD_DIM), :] = result
+            log_ref[h, :, rows_at(b, size)] = logs
         return unused
 
-    lax.fori_loop(0, blocks // pair, query_block, 0)
-    for b in range(blocks):
+    lax.fori_loop(0, count, query_block, 0)
+    for b in range(count):
         out_refs[b][...] = out_ref[b]
 
 
-def attend(lens, rank, qt, kt, vt, blocks):
+def attend(lens, rank, qt, kt, vt, blocks, first, count):
     width, slots = qt.shape
     size = slots // blocks
     heads = width // HEAD_DIM
     return pl.pallas_call(
-        forward_kernel,
-        out_shape=(jax.ShapeDtypeStruct((width, size), bf16),) * blocks
-        + (jax.ShapeDtypeStruct((heads, 1, slots), f32),),
+        functools.partial(forward_kernel, first, blocks),
+        out_shape=(jax.ShapeDtypeStruct((width, size), bf16),) * count
+        + (jax.ShapeDtypeStruct((heads, 1, count * size), f32),),
         in_specs=[SMEM, SMEM, VMEM, VMEM, VMEM],
-        out_specs=(VMEM,) * (blocks + 1),
+        out_specs=(VMEM,) * (count + 1),
         scratch_shapes=[
             pltpu.VMEM((heads, slots, width), bf16),
-            pltpu.VMEM((blocks, width, size), bf16),
+            pltpu.VMEM((count, width, size), bf16),
+            pltpu.VMEM((1, slots), jnp.int32),
+            pltpu.VMEM((slots, 128), jnp.int32),
+            pltpu.VMEM((heads, slots, size), f32),
         ],
         name="attend",
         compiler_params=pltpu.CompilerParams(vmem_limit_bytes=60 * 2**20),
         cost_estimate=COST,
     )(lens, rank, qt, kt, vt)
+
+
+def split_rows(values):
+    high = values.astype(bf16)
+    return jnp.concatenate([high, (values - high.astype(f32)).astype(bf16)], axis=0)
+
+
+def add_kernel(a_ref, b_ref, out_ref):
+    half = out_ref.shape[0] - SUM_ROWS
+    line = SUM_ROWS // 2
+    total = a_ref[...].astype(f32) + b_ref[...].astype(f32)
+    out_ref[:half, :] = total[:half].astype(bf16)
+    out_ref[half:, :] = split_rows(total[half : half + line] + total[half + line :])
+
+
+def add_parts(a, b):
+    return pl.pallas_call(
+        add_kernel,
+        out_shape=jax.ShapeDtypeStruct(a.shape, bf16),
+        in_specs=[VMEM, VMEM],
+        out_specs=VMEM,
+        name="add_parts",
+        cost_estimate=COST,
+    )(a, b)
 
 
 def stacked_parts(first_head, heads, query, key, value):
@@ -251,7 +288,7 @@
 
 def backward_kernel(
     first_head, heads, blocks, extras, lens_ref, rank_ref, bit_ref, qt_ref, kt_ref, vt_ref,
-    log_ref, qw_ref, kw_ref, vw_ref, normed_ref, *rest
+    near_ref, far_ref, qw_ref, kw_ref, vw_ref, normed_ref, *rest
 ):
     extra_refs, rest = rest[:extras], rest[extras:]
     width, slots = qt_ref.shape
@@ -259,13 +296,19 @@
     dim = HEAD_DIM
     out_refs, grad_refs = rest[:blocks], rest[blocks : 2 * blocks]
     joint_ref, sums_ref, own_ref, away_ref = rest[2 * blocks : 2 * blocks + 4]
-    kv_ref, q0_ref, og_ref, right_ref, inner_ref, dq_ref, made_ref = rest[-10:-3]
+    kv_ref, q0_ref, og_ref, right_ref, inner_ref, dq_ref, made_ref = rest[-13:-6]
+    log_ref = rest[-6]
+    row_ref, col_ref = rest[-5:-3]
     turned_ref, rows_ref, copied = rest[-3:]
     fetch = pltpu.make_async_copy(normed_ref, rows_ref, copied)
     fetch.start()
     unit = shard // 2
     rank = rank_ref[0, 0]
     ends = item_ends(lens_ref)
+    fill_segments(row_ref, col_ref, shard, rank, ends)
+    near = near_ref.shape[2]
+    log_ref[:, :, :near] = near_ref[...]
+    log_ref[:, :, near:] = far_ref[...]
     zero = jnp.zeros((dim, slots), bf16)
     for n in range(heads):
         part = slice((first_head + n) * dim, (first_head + n + 1) * dim)
@@ -288,12 +331,11 @@
     def key_block(j, unused):
         at_key = ((j // 2) ^ rank) * 2 + j % 2
         rows = rows_at(at_key, unit)
-        seg_k = memory_segments(at_key, unit, shard, rank, ends, 0)
 
         def query_block(i, totals):
             at = i ^ rank
             cols = rows_at(at, shard)
-            same = seg_k == memory_segments(at, shard, shard, rank, ends, 1)
+            same = col_ref[rows, 0:1] == row_ref[:, cols]
             result = []
             for n in range(heads):
                 head = first_head + n
@@ -348,8 +390,8 @@
         part_ref[0:half, :] = made_ref[rows_at(at, half), :].astype(bf16)
         if extras:
             lines = [sums_ref[...] + extra_refs[0][...], extra_refs[1][...]]
-            lines.append(jnp.zeros((SUM_ROWS - 4, gains.shape[1]), f32))
-            part_ref[half:, :] = jnp.concatenate(lines, axis=0).astype(bf16)
+            lines.append(jnp.zeros((SUM_ROWS // 2 - 4, gains.shape[1]), f32))
+            part_ref[half:, :] = split_rows(jnp.concatenate(lines, axis=0))
 
 
 def attend_back(
@@ -368,7 +410,7 @@
         )
         + (jax.ShapeDtypeStruct((rows, width), bf16),) * 2,
         in_specs=[SMEM, SMEM, SMEM]
-        + [VMEM] * 7
+        + [VMEM] * 8
         + [pl.BlockSpec(memory_space=pl.ANY)]
         + [VMEM] * (len(extras) + 2 * blocks),
         out_specs=(VMEM,) * 4,
@@ -378,6 +420,9 @@
             pltpu.VMEM((heads, 1, slots), f32),
             pltpu.VMEM((heads, dim, slots), f32),
             pltpu.VMEM((cols, width), f32),
+            pltpu.VMEM((qt.shape[0] // dim, 1, slots), f32),
+            pltpu.VMEM((1, slots), jnp.int32),
+            pltpu.VMEM((slots, 128), jnp.int32),
             pltpu.VMEM((cols, slots), bf16),
             pltpu.VMEM((slots, width), bf16),
             pltpu.SemaphoreType.DMA,
@@ -385,7 +430,7 @@
         name="attend_back",
         compiler_params=pltpu.CompilerParams(vmem_limit_bytes=60 * 2**20),
         cost_estimate=COST,
-    )(lens, rank, bit, qt, kt, vt, logs, *weights, normed, *extras, *outs, *grads)
+    )(lens, rank, bit, qt, kt, vt, *logs, *weights, normed, *extras, *outs, *grads)
 
 
 def plan_kernel(capacity, lens_ref, rank_ref, routes_ref, order_ref, grad_ref,
@@ -850,25 +895,34 @@
     outputs = [output_weight] + [
         swap(output_weight, "tensor", k) for k in range(1, members)
     ]
-    *own_heads, logs = attend(item_lengths, rank_cell, qt, kt, vt, members)
-    own_heads, flat_grad, outputs = tie(own_heads, flat_grad, outputs)
-    all_heads = [own_heads[0]] + [
-        swap(own_heads[j], "tensor", j) for j in range(1, members)
-    ]
-    grad_act = across(flat_grad, down_matrix)
-    all_heads, grad_act = tie(all_heads, grad_act)
+    far = members // 2
+    *far_heads, far_logs = attend(
+        item_lengths, rank_cell, qt, kt, vt, members, far, members - far
+    )
+    far_heads, kt = tie(far_heads, kt)
+    far_arrived = [swap(far_heads[j - far], "tensor", j) for j in range(far, members)]
+    *near_heads, near_logs = attend(item_lengths, rank_cell, qt, kt, vt, members, 0, far)
+    near_heads, far_arrived, outputs = tie(near_heads, far_arrived, outputs)
+    own_heads = near_heads + far_heads
+    logs = (near_logs, far_logs)
+    all_heads = (
+        near_heads[:1]
+        + [swap(near_heads[j], "tensor", j) for j in range(1, far)]
+        + far_arrived
+    )
     residual, outgoing = middle(
         rank_cell[0], tokens, second_gain, second_bias, dispatch, all_heads, outputs
     )
     flat_in = exchange(outgoing)
 
     flat_grad, outgoing = tie(flat_grad, outgoing)
+    grad_act = across(flat_grad, down_matrix)
     gathered_grads = [flat_grad]
     gathered_rows = [flat_in]
     steps = steps_of(members)
     for step in reversed(steps[1:]):
         gathered_grads += [swap(a, "tensor", step) for a in gathered_grads]
-    flat_in, gathered_grads = tie(flat_in, gathered_grads)
+    flat_in, grad_act, gathered_grads = tie(flat_in, grad_act, gathered_grads)
     gathered_rows = [flat_in]
     for step in reversed(steps[1:]):
         gathered_rows += [swap(a, "tensor", step) for a in gathered_rows]
@@ -930,21 +984,20 @@
         joint_b, own_a, own_b, away_b, output_sum, returned
     )
 
-    far = members // 2
     far_kept, far_sent = input_grad(
         groups, weights, (joint_a, joint_b), far, members - far, shard_rows
     )
     near_kept, near_sent = input_grad(
         groups, weights, (joint_a, joint_b), 0, far, shard_rows
     )
-    own_b = add_low(own_b, swap(away_b, "dp", 1))
+    own_b = add_parts(own_b, swap(away_b, "dp", 1))
     far_kept = add_low(far_kept, swap(far_sent, "tensor", 1))
     far_kept, own_b, output_sum, near_sent = tie(far_kept, own_b, output_sum, near_sent)
     near_core = swap(near_sent, "tensor", 1)
     near_far = swap(far_kept, "tensor", 2)
     for step in dp_steps[1:]:
         own_a = add_low(own_a, swap(own_a, "dp", step))
-        own_b = add_low(own_b, swap(own_b, "dp", step))
+        own_b = add_parts(own_b, swap(own_b, "dp", step))
         if step == dp_steps[1]:
             own_b, sums, gathered_rows, far_rows = tie(own_b, sums, gathered_rows, far_rows)
     up_grad, down_grad = expert_weights(
@@ -953,7 +1006,8 @@
         up_matrix, down_matrix, members, sums,
     )
     own_b, up_grad, down_grad, near_far = tie(own_b, up_grad, down_grad, near_far)
-    norm_sums = own_b[3 * HEAD_DIM * groups[1][1] // 2 :][:8].astype(f32)
+    norm_sums = own_b[-SUM_ROWS:].astype(f32)
+    norm_sums = norm_sums[: SUM_ROWS // 2] + norm_sums[SUM_ROWS // 2 :]
     for step in steps:
         norm_sums = norm_sums + swap(norm_sums, "tensor", step)
     pieces = (own_a, swap(own_a, "dp", 1), own_b, swap(own_b, "dp", 1))

time: 253 us -> 242 us (0.957)
  waiting for transfers between devices: 40.4 us -> 29.9 us
  Pallas kernels: 145 us -> 136 us
  starting transfers between devices: 48.6 us -> 53.2 us
    ppermute x33, waiting for transfers between devices: 38.3 us -> 16.6 us  [swap(): return lax.ppermute(values, axis, [(i, i ^ step) for i in range(count)])]
    all_to_all x4, waiting for transfers between devices: 2.09 us -> 13.3 us  [exchange(): lax.all_to_all(rows.reshape(sources, -1, width), 'dp', split_axis=0, conc...]
    pallas_call x2, Pallas kernels: 42.1 us -> 35.9 us  [attend_back(): pl.pallas_call(functools.partial(backward_kernel, first_head, heads, bloc...]
    pallas_call x1 -> x5, Pallas kernels: 27.2 us -> 24.7 us  [the longest x2 19.5 us: attend(): pl.pallas_call(functools.partial(forward_kernel, first, blocks), out_shap...]
    convert_element_type x11 -> x8, other arithmetic: 4.97 us -> 6.06 us  [add_low(): return (a.astype(f32) + b.astype(f32)).astype(bf16)]
  transfers between devices with their start and end apart: 37 -> 37, of which waited for: 13 -> 10; matrix products, arithmetic and copies ran while one was open for 6% -> 7% of each run, Pallas kernels for 49% -> 49%
where the time goes in v4:
time: 242 us
  Pallas kernels  136 us (56%)
  starting transfers between devices  53.2 us (22%)
  waiting for transfers between devices  29.9 us (12%)
  matrix products  8.59 us (4%)
  other arithmetic  8.3 us (3%)
  local copies, waits for them, and re-layouts  5.44 us (2%)
    pallas_call x2, Pallas kernels, attend_back(): pl.pallas_call(functools.partial(backward_kernel, first_head, heads, bloc...  35.9 us
    ppermute x33, starting transfers between devices, swap(): return lax.ppermute(values, axis, [(i, i ^ step) for i in range(count)])  28.3 us
    all_to_all x4, starting transfers between devices, exchange(): lax.all_to_all(rows.reshape(sources, -1, width), 'dp', split_axis=0, conc...  24.9 us
    pallas_call x2, Pallas kernels, attend(): pl.pallas_call(functools.partial(forward_kernel, first, blocks), out_shap...  19.5 us
    pallas_call x2, Pallas kernels, expert_weights(): pl.pallas_call(functools.partial(weight_kernel, len(group)), grid_spec=pl...  19.4 us
    ppermute x33, waiting for transfers between devices, swap(): return lax.ppermute(values, axis, [(i, i ^ step) for i in range(count)])  16.6 us
    all_to_all x4, waiting for transfers between devices, exchange(): lax.all_to_all(rows.reshape(sources, -1, width), 'dp', split_axis=0, conc...  13.3 us
    pallas_call x1, Pallas kernels, expert(): pl.pallas_call(expert_kernel, grid=(hidden // size,), out_shape=(jax.Shap...  11.8 us
  transfers between devices with their start and end apart: 37, of which 10 were waited for; matrix products, arithmetic and copies ran while one was open for 7% of the time, Pallas kernels for 49%

profile of v4, /device:TPU:0, one launch (start us, length us, event | category | flops | bytes accessed | tf_op | source)
XLA Modules:
  0.0 242.4 jit_solution(18319708925226008790)
XLA Ops:
  0.7 3.3 %plan.1 = (bf16[512,512]{1,0:T(8,128)(2,1)}, bf16[512,768]{1,0:T(8,128)(2,1)}) custom-call(s32[1,5]{1,0:T(1,128)} %lens_ref.11, s32[1,1]{1,0:T(1,128)} %bitcast.1.rank_ref, s32[1,512]{1,0:T(1,128)} %bitcast.64, s32[1,512]{1,0:T(1,128)} %order_ref.1, bf16[512,768]{1,0:T(8,128)(2,1)} %cotangent_ref.1), custom_call_target="tpu_custom_call" | custom-call | flops 1048576 | bytes 1048576 | tf_op jit(solution)/shard_map/plan/pallas_call | solution.py:467
  3.9 7.3 %all-to-all-start.1 = ((bf16[8,64,768]{2,1,0:T(8,128)(2,1)}), bf16[8,64,768]{2,1,0:T(8,128)(2,1)S(1)}, u32[]{:S(2)}, u32[]{:S(2)}) async-start(bf16[8,64,768]{2,1,0:T(8,128)(2,1)} %bitcast.61), calls=%async_computation.1 | async-start | bytes 1572864 | tf_op jit(solution)/shard_map/all_to_all | solution.py:881
  13.2 7.5 %project.1 = (bf16[2048,768]{1,0:T(8,128)(2,1)}, bf16[192,2048]{1,0:T(8,128)(2,1)}, bf16[192,2048]{1,0:T(8,128)(2,1)}, bf16[192,2048]{1,0:T(8,128)(2,1)}) custom-call(s32[1]{0:T(128)} %bitcast.rank_ref, bf16[2048,768]{1,0:T(8,128)(2,1)} %tokens_ref.2, f32[768]{0:T(1024)} %gain_ref.7, f32[768]{0:T(1024)} %bias_ref.2, bf16[192,768]{1,0:T(8,128)(2,1)} %bitcast.35, ...), custom_call_target="tpu_custom_call" | custom-call | flops 1048576 | bytes 1048576 | tf_op jit(solution)/shard_map/project/pallas_call | solution.py:79
  20.6 9.8 %attend.2 = (bf16[192,512]{1,0:T(8,128)(2,1)}, bf16[192,512]{1,0:T(8,128)(2,1)}, f32[3,1,1024]{2,1,0:T(1,128)}) custom-call(s32[1,5]{1,0:T(1,128)} %lens_ref.11, s32[1,1]{1,0:T(1,128)} %bitcast.1.rank_ref, bf16[192,2048]{1,0:T(8,128)(2,1)} %get-tuple-element.122.qt_ref, bf16[192,2048]{1,0:T(8,128)(2,1)} %get-tuple-element.127.kt_ref, ...), custom_call_target="tpu_custom_call" | custom-call | flops 1048576 | bytes 1048576 | tf_op jit(solution)/shard_map/attend/pallas_call | solution.py:237
  32.1 9.8 %attend.3 = (bf16[192,512]{1,0:T(8,128)(2,1)}, bf16[192,512]{1,0:T(8,128)(2,1)}, f32[3,1,1024]{2,1,0:T(1,128)}) custom-call(s32[1,5]{1,0:T(1,128)} %lens_ref.11, s32[1,1]{1,0:T(1,128)} %bitcast.1.rank_ref, bf16[192,2048]{1,0:T(8,128)(2,1)} %get-tuple-element.122.qt_ref, bf16[192,2048]{1,0:T(8,128)(2,1)} %get-tuple-element.127.kt_ref, ...), custom_call_target="tpu_custom_call" | custom-call | flops 1048576 | bytes 1048576 | tf_op jit(solution)/shard_map/attend/pallas_call | solution.py:237
  44.5 4.8 %middle.1 = (f32[512,768]{1,0:T(8,128)}, bf16[512,768]{1,0:T(8,128)(2,1)}) custom-call(s32[1]{0:T(128)} %bitcast.rank_ref, bf16[2048,768]{1,0:T(8,128)(2,1)} %tokens_ref.2, f32[768]{0:T(1024)} %gain_ref.6, f32[768]{0:T(1024)} %bias_ref.3, bf16[512,512]{1,0:T(8,128)(2,1)} %get-tuple-element.121.dispatch_ref, ...), custom_call_target="tpu_custom_call" | custom-call | flops 1048576 | bytes 1048576 | tf_op jit(solution)/shard_map/middle/pallas_call | solution.py:504
  49.3 8.5 %all-to-all-start = ((bf16[8,64,768]{2,1,0:T(8,128)(2,1)}), bf16[8,64,768]{2,1,0:T(8,128)(2,1)S(1)}, u32[]{:S(2)}, u32[]{:S(2)}) async-start(bf16[8,64,768]{2,1,0:T(8,128)(2,1)} %bitcast.63), calls=%async_computation | async-start | bytes 1572864 | tf_op jit(solution)/shard_map/all_to_all | solution.py:881
  59.3 6.8 %fusion.1.grad_act_ref = f32[512,3072]{1,0:T(8,128)} fusion(bf16[512,768]{1,0:T(8,128)(2,1)S(1)} %bitcast.55, bf16[1,3072,768]{2,1,0:T(8,128)(2,1)} %param.25), kind=kOutput, calls=%fused_computation.18 | convolution fusion | flops 2415919104 | bytes 11796480 | tf_op jit(solution)/shard_map/dot_general | solution.py:481
  66.1 12.3 %all-to-all-done = bf16[8,64,768]{2,1,0:T(8,128)(2,1)S(1)} async-done(((bf16[8,64,768]{2,1,0:T(8,128)(2,1)}), bf16[8,64,768]{2,1,0:T(8,128)(2,1)S(1)}, u32[]{:S(2)}, u32[]{:S(2)}) %all-to-all-start) | async-done | bytes 786464 | tf_op jit(solution)/shard_map/all_to_all | solution.py:881
  79.4 11.8 %expert.1 = (bf16[512,3072]{1,0:T(8,128)(2,1)}, bf16[512,768]{1,0:T(8,128)(2,1)}) custom-call(bf16[512,768]{1,0:T(8,128)(2,1)} %bitcast.51, f32[512,3072]{1,0:T(8,128)} %fusion.1.grad_act_ref, bf16[768,3072]{1,0:T(8,128)(2,1)} %bitcast.32), custom_call_target="tpu_custom_call" | custom-call | flops 1048576 | bytes 1048576 | tf_op jit(solution)/shard_map/expert/pallas_call | solution.py:610
  91.2 4.3 %all-to-all-start.2 = ((bf16[8,64,768]{2,1,0:T(8,128)(2,1)}), bf16[8,64,768]{2,1,0:T(8,128)(2,1)S(1)}, u32[]{:S(2)}, u32[]{:S(2)}) async-start(bf16[8,64,768]{2,1,0:T(8,128)(2,1)} %bitcast.62), calls=%async_computation.2 | async-start | bytes 1572864 | tf_op jit(solution)/shard_map/all_to_all | solution.py:881
  97.0 6.6 %product.1 = bf16[512,768]{1,0:T(8,128)(2,1)} custom-call(bf16[512,3072]{1,0:T(8,128)(2,1)} %get-tuple-element.155.a_ref, bf16[3072,768]{1,0:T(8,128)(2,1)} %bitcast.29), custom_call_target="tpu_custom_call" | custom-call | flops 1048576 | bytes 1048576 | tf_op jit(solution)/shard_map/product/pallas_call | solution.py:653
  103.6 9.4 %expert_weights.2 = (f32[768,768]{1,0:T(8,128)}, f32[768,768]{1,0:T(8,128)}) custom-call(s32[1]{0:T(128)} %bitcast.rank_ref, bf16[768,3072]{1,0:T(8,128)(2,1)} %bitcast.33, bf16[3072,768]{1,0:T(8,128)(2,1)} %bitcast.30, bf16[512,768]{1,0:T(8,128)(2,1)} %bitcast.53, bf16[512,768]{1,0:T(8,128)(2,1)} %bitcast.57, ...), custom_call_target="tpu_custom_call" | custom-call | flops 1048576 | bytes 1048576 | tf_op jit(solution)/shard_map/expert_weights/pallas_call | solution.py:696
  117.1 6.5 %turn.1 = (f32[512,768]{1,0:T(8,128)}, f32[2,768]{1,0:T(2,128)}, bf16[2,192,768]{2,1,0:T(8,128)(2,1)}, bf16[2,192,768]{2,1,0:T(8,128)(2,1)}, bf16[192,512]{1,0:T...) custom-call(s32[1,5]{1,0:T(1,128)} %lens_ref.11, ...), custom_call_target="tpu_custom_call" | custom-call | flops 1048576 | bytes 1048576 | tf_op jit(solution)/shard_map/turn/pallas_call | solution.py:561
  125.7 4.8 %all-to-all-start.3 = ((bf16[8,64,768]{2,1,0:T(8,128)(2,1)}), bf16[8,64,768]{2,1,0:T(8,128)(2,1)S(1)}, u32[]{:S(2)}, u32[]{:S(2)}) async-start(bf16[8,64,768]{2,1,0:T(8,128)(2,1)} %bitcast.16), calls=%async_computation.3 | async-start | bytes 1572864 | tf_op jit(solution)/shard_map/all_to_all | solution.py:881
  136.2 21.6 %attend_back.2 = (bf16[2048,384]{1,0:T(8,128)(2,1)}, f32[2,768]{1,0:T(2,128)}, bf16[192,768]{1,0:T(8,128)(2,1)}, bf16[192,768]{1,0:T(8,128)(2,1)}) custom-call(s32[1,5]{1,0:T(1,128)} %lens_ref.11, s32[1,1]{1,0:T(1,128)} %bitcast.1.rank_ref, s32[1,1]{1,0:T(1,128)} %bitcast.6.bit_ref, bf16[192,2048]{1,0:T(8,128)(2,1)} %get-tuple-element.122.qt_ref, ...), custom_call_target="tpu_custom_call" | custom-call | flops 1048576 | bytes 1048576 | tf_op jit(solution)/shard_map/attend_back/pallas_call | solution.py:405
  160.4 14.3 %attend_back.3 = (bf16[2048,192]{1,0:T(8,128)(2,1)}, f32[2,768]{1,0:T(2,128)}, bf16[112,768]{1,0:T(8,128)(2,1)}, bf16[112,768]{1,0:T(8,128)(2,1)}) custom-call(s32[1,5]{1,0:T(1,128)} %lens_ref.11, s32[1,1]{1,0:T(1,128)} %bitcast.1.rank_ref, s32[1,1]{1,0:T(1,128)} %bitcast.6.bit_ref, bf16[192,2048]{1,0:T(8,128)(2,1)} %get-tuple-element.122.qt_ref, ...), custom_call_target="tpu_custom_call" | custom-call | flops 1048576 | bytes 1048576 | tf_op jit(solution)/shard_map/attend_back/pallas_call | solution.py:405
  175.0 4.4 %input_grad.3 = (bf16[1,512,768]{2,1,0:T(8,128)(2,1)}, bf16[1,512,768]{2,1,0:T(8,128)(2,1)}) custom-call(bf16[192,768]{1,0:T(8,128)(2,1)} %bitcast.38, bf16[192,768]{1,0:T(8,128)(2,1)} %bitcast.43, bf16[192,768]{1,0:T(8,128)(2,1)} %bitcast.48, bf16[2048,384]{1,0:T(8,128)(2,1)} %get-tuple-element.194.refs_0_, bf16[2048,192]{1,0:T(8,128)(2,1)} %get-tuple-element.195.refs_1_), custom_call_target="tpu_custom_call" | custom-call | flops 1048576 | bytes 1048576 | tf_op jit(solution)/shard_map/input_grad/pallas_call | solution.py:756
  181.2 4.4 %collective-permute-start.27 = (bf16[192,768]{1,0:T(8,128)(2,1)S(1)}, bf16[192,768]{1,0:T(8,128)(2,1)}, u32[]{:S(2)}, u32[]{:S(2)}) collective-permute-start(bf16[192,768]{1,0:T(8,128)(2,1)S(1)} %add_convert_fusion.7), channel_id=1, source_target_pairs={{0,8},{4,12},{8,0},{12,4},{16,24},{20,28},{24,16},{28,20},{1,9},{5... | collective-permute-start | bytes 884744 | tf_op jit(solution)/shard_map/ppermute | solution.py:36
  185.6 4.3 %input_grad.2 = (bf16[1,512,768]{2,1,0:T(8,128)(2,1)}, bf16[1,512,768]{2,1,0:T(8,128)(2,1)}) custom-call(bf16[192,768]{1,0:T(8,128)(2,1)} %bitcast.39, bf16[192,768]{1,0:T(8,128)(2,1)} %bitcast.44, bf16[192,768]{1,0:T(8,128)(2,1)} %bitcast.49, bf16[2048,384]{1,0:T(8,128)(2,1)} %get-tuple-element.194.refs_0_, bf16[2048,192]{1,0:T(8,128)(2,1)} %get-tuple-element.195.refs_1_), custom_call_target="tpu_custom_call" | custom-call | flops 1048576 | bytes 1048576 | tf_op jit(solution)/shard_map/input_grad/pallas_call | solution.py:756
  201.2 5.1 %collective-permute-done.21.b_ref = bf16[112,768]{1,0:T(8,128)(2,1)S(1)} collective-permute-done((bf16[112,768]{1,0:T(8,128)(2,1)S(1)}, bf16[112,768]{1,0:T(8,128)(2,1)S(1)}, u32[]{:S(2)}, u32[]{:S(2)}) %collective-permute-start.21) | collective-permute-done | bytes 172064 | tf_op jit(solution)/shard_map/ppermute | solution.py:36
  208.7 10.0 %expert_weights.3 = (f32[768,768]{1,0:T(8,128)}, f32[768,768]{1,0:T(8,128)}) custom-call(s32[1]{0:T(128)} %bitcast.rank_ref, bf16[768,3072]{1,0:T(8,128)(2,1)} %bitcast.34, bf16[3072,768]{1,0:T(8,128)(2,1)} %bitcast.31, bf16[512,768]{1,0:T(8,128)(2,1)} %copy-done.12, bf16[512,768]{1,0:T(8,128)(2,1)} %copy-done.10, ...), custom_call_target="tpu_custom_call" | custom-call | flops 1048576 | bytes 1048576 | tf_op jit(solution)/shard_map/expert_weights/pallas_call | solution.py:696
  219.8 2.9 %collective-permute-done.23.b_ref = bf16[112,768]{1,0:T(8,128)(2,1)S(1)} collective-permute-done((bf16[112,768]{1,0:T(8,128)(2,1)}, bf16[112,768]{1,0:T(8,128)(2,1)S(1)}, u32[]{:S(2)}, u32[]{:S(2)}) %collective-permute-start.23) | collective-permute-done | bytes 172064 | tf_op jit(solution)/shard_map/ppermute | solution.py:36
  231.9 4.1 %close.1 = f32[512,768]{1,0:T(8,128)} custom-call(s32[1]{0:T(128)} %bitcast.rank_ref, bf16[2048,768]{1,0:T(8,128)(2,1)} %tokens_ref.2, f32[768]{0:T(1024)} %gain_ref.7, f32[512,768]{1,0:T(8,128)} %get-tuple-element.193.grad_ref, bf16[1,512,768]{2,1,0:T(8,128)(2,1)} %get-tuple-element.196.refs_0_, bf16[1,512,768]{2,1,0:T(8,128)(2,1)} %copy-done.16, ...), custom_call_target="tpu_custom_call" | custom-call | flops 1048576 | bytes 1048576 | tf_op jit(solution)/shard_map/close/pallas_call | solution.py:793
  (145 shorter events, 56.6 us)
Async XLA Ops:
  3.9 45.4 %all-to-all-start.1 = ((bf16[8,64,768]{2,1,0:T(8,128)(2,1)}), bf16[8,64,768]{2,1,0:T(8,128)(2,1)S(1)}, u32[]{:S(2)}, u32[]{:S(2)}) async-start(bf16[8,64,768]{2,1,0:T(8,128)(2,1)} %bitcast.61), calls=%async_computation.1 | async-start | bytes 1572864 | tf_op jit(solution)/shard_map/all_to_all | solution.py:881
  11.2 30.7 %collective-permute-start.2 = (bf16[192,768]{1,0:T(8,128)(2,1)S(1)}, bf16[192,768]{1,0:T(8,128)(2,1)S(1)}, u32[]{:S(2)}, u32[]{:S(2)}) collective-permute-start(bf16[192,768]{1,0:T(8,128)(2,1)S(1)} %copy-done.6), channel_id=1, source_target_pairs={{0,1},{1,0},{2,3},{3,2},{4,5},{5,4},{6,7},{7,6},{8,9},{9,8},{10,11... | collective-permute-start | bytes 884744 | tf_op jit(solution)/shard_map/ppermute | solution.py:36
  11.3 30.6 %collective-permute-start.3 = (bf16[192,768]{1,0:T(8,128)(2,1)S(1)}, bf16[192,768]{1,0:T(8,128)(2,1)S(1)}, u32[]{:S(2)}, u32[]{:S(2)}) collective-permute-start(bf16[192,768]{1,0:T(8,128)(2,1)S(1)} %copy-done.6), channel_id=1, source_target_pairs={{0,2},{1,3},{2,0},{3,1},{4,6},{5,7},{6,4},{7,5},{8,10},{9,11},{10,... | collective-permute-start | bytes 884744 | tf_op jit(solution)/shard_map/ppermute | solution.py:36
  12.9 29.1 %collective-permute-start.4 = (bf16[192,768]{1,0:T(8,128)(2,1)S(1)}, bf16[192,768]{1,0:T(8,128)(2,1)S(1)}, u32[]{:S(2)}, u32[]{:S(2)}) collective-permute-start(bf16[192,768]{1,0:T(8,128)(2,1)S(1)} %copy-done.6), channel_id=1, source_target_pairs={{0,3},{1,2},{2,1},{3,0},{4,7},{5,6},{6,5},{7,4},{8,11},{9,10},{10,... | collective-permute-start | bytes 884744 | tf_op jit(solution)/shard_map/ppermute | solution.py:36
  30.4 11.5 %collective-permute-start = (bf16[192,512]{1,0:T(8,128)(2,1)}, bf16[192,512]{1,0:T(8,128)(2,1)S(1)}, u32[]{:S(2)}, u32[]{:S(2)}) collective-permute-start(bf16[192,512]{1,0:T(8,128)(2,1)} %get-tuple-element.130.rest_2_.rest_4_), channel_id=1, source_target_pairs={{0,2},{1,3},{2,0},{3,1},{4,6},{5,7},{6,4},{7,5},{8,10},{9,11},{10,... | collective-permute-start | bytes 589832 | tf_op jit(solution)/shard_map/ppermute | solution.py:36
  49.3 29.2 %all-to-all-start = ((bf16[8,64,768]{2,1,0:T(8,128)(2,1)}), bf16[8,64,768]{2,1,0:T(8,128)(2,1)S(1)}, u32[]{:S(2)}, u32[]{:S(2)}) async-start(bf16[8,64,768]{2,1,0:T(8,128)(2,1)} %bitcast.63), calls=%async_computation | async-start | bytes 1572864 | tf_op jit(solution)/shard_map/all_to_all | solution.py:881
  57.8 20.7 %collective-permute-start.6 = (bf16[512,768]{1,0:T(8,128)(2,1)S(1)}, bf16[512,768]{1,0:T(8,128)(2,1)S(1)}, u32[]{:S(2)}, u32[]{:S(2)}) collective-permute-start(bf16[512,768]{1,0:T(8,128)(2,1)S(1)} %bitcast.54), channel_id=1, source_target_pairs={{0,2},{1,3},{2,0},{3,1},{4,6},{5,7},{6,4},{7,5},{8,10},{9,11},{10,... | collective-permute-start | bytes 2359304 | tf_op jit(solution)/shard_map/ppermute | solution.py:36
  78.5 12.7 %collective-permute-start.7 = (bf16[512,768]{1,0:T(8,128)(2,1)S(1)}, bf16[512,768]{1,0:T(8,128)(2,1)}, u32[]{:S(2)}, u32[]{:S(2)}) collective-permute-start(bf16[512,768]{1,0:T(8,128)(2,1)S(1)} %bitcast.50), channel_id=1, source_target_pairs={{0,1},{1,0},{2,3},{3,2},{4,5},{5,4},{6,7},{7,6},{8,9},{9,8},{10,11... | collective-permute-start | bytes 2359304 | tf_op jit(solution)/shard_map/ppermute | solution.py:36
  78.6 12.6 %collective-permute-start.8 = (bf16[512,768]{1,0:T(8,128)(2,1)S(1)}, bf16[512,768]{1,0:T(8,128)(2,1)}, u32[]{:S(2)}, u32[]{:S(2)}) collective-permute-start(bf16[512,768]{1,0:T(8,128)(2,1)S(1)} %bitcast.56), channel_id=1, source_target_pairs={{0,1},{1,0},{2,3},{3,2},{4,5},{5,4},{6,7},{7,6},{8,9},{9,8},{10,11... | collective-permute-start | bytes 2359304 | tf_op jit(solution)/shard_map/ppermute | solution.py:36
  79.1 12.1 %collective-permute-start.9 = (bf16[512,768]{1,0:T(8,128)(2,1)S(1)}, bf16[512,768]{1,0:T(8,128)(2,1)S(1)}, u32[]{:S(2)}, u32[]{:S(2)}) collective-permute-start(bf16[512,768]{1,0:T(8,128)(2,1)S(1)} %collective-permute-done.6.refs_1_), channel_id=1, source_target_pairs={{0,1},{1,0},{2,3},{3,2},{4,5},{5,4},{6,7},{7,6},{8,9},{9,8},{10,11... | collective-permute-start | bytes 2359304 | tf_op jit(solution)/shard_map/ppermute | solution.py:36
  91.2 25.0 %all-to-all-start.2 = ((bf16[8,64,768]{2,1,0:T(8,128)(2,1)}), bf16[8,64,768]{2,1,0:T(8,128)(2,1)S(1)}, u32[]{:S(2)}, u32[]{:S(2)}) async-start(bf16[8,64,768]{2,1,0:T(8,128)(2,1)} %bitcast.62), calls=%async_computation.2 | async-start | bytes 1572864 | tf_op jit(solution)/shard_map/all_to_all | solution.py:881
  95.5 19.8 %collective-permute-start.10 = (bf16[512,768]{1,0:T(8,128)(2,1)}, bf16[512,768]{1,0:T(8,128)(2,1)S(1)}, u32[]{:S(2)}, u32[]{:S(2)}) collective-permute-start(bf16[512,768]{1,0:T(8,128)(2,1)} %bitcast.52), channel_id=1, source_target_pairs={{0,2},{1,3},{2,0},{3,1},{4,6},{5,7},{6,4},{7,5},{8,10},{9,11},{10,... | collective-permute-start | bytes 2359304 | tf_op jit(solution)/shard_map/ppermute | solution.py:36
  125.7 49.3 %all-to-all-start.3 = ((bf16[8,64,768]{2,1,0:T(8,128)(2,1)}), bf16[8,64,768]{2,1,0:T(8,128)(2,1)S(1)}, u32[]{:S(2)}, u32[]{:S(2)}) async-start(bf16[8,64,768]{2,1,0:T(8,128)(2,1)} %bitcast.16), calls=%async_computation.3 | async-start | bytes 1572864 | tf_op jit(solution)/shard_map/all_to_all | solution.py:881
  134.7 23.2 %collective-permute-start.15 = (bf16[1,192,768]{2,1,0:T(8,128)(2,1)S(1)}, bf16[1,192,768]{2,1,0:T(8,128)(2,1)S(1)}, u32[]{:S(2)}, u32[]{:S(2)}) collective-permute-start(bf16[1,192,768]{2,1,0:T(8,128)(2,1)S(1)} %slice.29), channel_id=1, source_target_pairs={{0,2},{1,3},{2,0},{3,1},{4,6},{5,7},{6,4},{7,5},{8,10},{9,11},{10,... | collective-permute-start | bytes 884744 | tf_op jit(solution)/shard_map/ppermute | solution.py:36
  157.9 16.9 %collective-permute-start.17 = (bf16[192,768]{1,0:T(8,128)(2,1)S(1)}, bf16[192,768]{1,0:T(8,128)(2,1)S(1)}, u32[]{:S(2)}, u32[]{:S(2)}) collective-permute-start(bf16[192,768]{1,0:T(8,128)(2,1)S(1)} %bitcast.60), channel_id=1, source_target_pairs={{0,16},{4,20},{8,24},{12,28},{16,0},{20,4},{24,8},{28,12},{1,17},{... | collective-permute-start | bytes 884744 | tf_op jit(solution)/shard_map/ppermute | solution.py:36
  158.0 16.9 %collective-permute-start.16 = (bf16[192,768]{1,0:T(8,128)(2,1)}, bf16[192,768]{1,0:T(8,128)(2,1)S(1)}, u32[]{:S(2)}, u32[]{:S(2)}) collective-permute-start(bf16[192,768]{1,0:T(8,128)(2,1)} %get-tuple-element.186), channel_id=1, source_target_pairs={{0,4},{4,0},{8,12},{12,8},{16,20},{20,16},{24,28},{28,24},{1,5},{5... | collective-permute-start | bytes 884744 | tf_op jit(solution)/shard_map/ppermute | solution.py:36
  179.5 12.2 %collective-permute-start.18 = (bf16[1,512,768]{2,1,0:T(8,128)(2,1)}, bf16[1,512,768]{2,1,0:T(8,128)(2,1)}, u32[]{:S(2)}, u32[]{:S(2)}) collective-permute-start(bf16[1,512,768]{2,1,0:T(8,128)(2,1)} %get-tuple-element.198), channel_id=1, source_target_pairs={{0,1},{1,0},{2,3},{3,2},{4,5},{5,4},{6,7},{7,6},{8,9},{9,8},{10,11... | collective-permute-start | bytes 2359304 | tf_op jit(solution)/shard_map/ppermute | solution.py:36
  181.0 27.7 %collective-permute-start.22 = (bf16[512,768]{1,0:T(8,128)(2,1)}, bf16[512,768]{1,0:T(8,128)(2,1)}, u32[]{:S(2)}, u32[]{:S(2)}) collective-permute-start(bf16[512,768]{1,0:T(8,128)(2,1)} %copy-done.12), channel_id=1, source_target_pairs={{0,1},{1,0},{2,3},{3,2},{4,5},{5,4},{6,7},{7,6},{8,9},{9,8},{10,11... | collective-permute-start | bytes 2359304 | tf_op jit(solution)/shard_map/ppermute | solution.py:36
  181.2 17.8 %collective-permute-start.27 = (bf16[192,768]{1,0:T(8,128)(2,1)S(1)}, bf16[192,768]{1,0:T(8,128)(2,1)}, u32[]{:S(2)}, u32[]{:S(2)}) collective-permute-start(bf16[192,768]{1,0:T(8,128)(2,1)S(1)} %add_convert_fusion.7), channel_id=1, source_target_pairs={{0,8},{4,12},{8,0},{12,4},{16,24},{20,28},{24,16},{28,20},{1,9},{5... | collective-permute-start | bytes 884744 | tf_op jit(solution)/shard_map/ppermute | solution.py:36
  194.1 31.0 %collective-permute-start.24 = (bf16[1,512,768]{2,1,0:T(8,128)(2,1)}, bf16[1,512,768]{2,1,0:T(8,128)(2,1)}, u32[]{:S(2)}, u32[]{:S(2)}) collective-permute-start(bf16[1,512,768]{2,1,0:T(8,128)(2,1)} %add_convert_fusion), channel_id=1, source_target_pairs={{0,2},{1,3},{2,0},{3,1},{4,6},{5,7},{6,4},{7,5},{8,10},{9,11},{10,... | collective-permute-start | bytes 2359304 | tf_op jit(solution)/shard_map/ppermute | solution.py:36
  194.7 24.0 %collective-permute-start.31 = (bf16[192,768]{1,0:T(8,128)(2,1)S(1)}, bf16[192,768]{1,0:T(8,128)(2,1)}, u32[]{:S(2)}, u32[]{:S(2)}) collective-permute-start(bf16[192,768]{1,0:T(8,128)(2,1)S(1)} %add_convert_fusion.6), channel_id=1, source_target_pairs={{0,4},{4,0},{8,12},{12,8},{16,20},{20,16},{24,28},{28,24},{1,5},{5... | collective-permute-start | bytes 884744 | tf_op jit(solution)/shard_map/ppermute | solution.py:36
  200.0 26.0 %collective-permute-start.28 = (bf16[192,768]{1,0:T(8,128)(2,1)S(1)}, bf16[192,768]{1,0:T(8,128)(2,1)S(1)}, u32[]{:S(2)}, u32[]{:S(2)}) collective-permute-start(bf16[192,768]{1,0:T(8,128)(2,1)S(1)} %add_convert_fusion.5), channel_id=1, source_target_pairs={{0,16},{4,20},{8,24},{12,28},{16,0},{20,4},{24,8},{28,12},{1,17},{... | collective-permute-start | bytes 884744 | tf_op jit(solution)/shard_map/ppermute | solution.py:36
  206.3 24.7 %collective-permute-start.20 = (bf16[1,512,768]{2,1,0:T(8,128)(2,1)}, bf16[1,512,768]{2,1,0:T(8,128)(2,1)S(1)}, u32[]{:S(2)}, u32[]{:S(2)}) collective-permute-start(bf16[1,512,768]{2,1,0:T(8,128)(2,1)} %get-tuple-element.203), channel_id=1, source_target_pairs={{0,1},{1,0},{2,3},{3,2},{4,5},{5,4},{6,7},{7,6},{8,9},{9,8},{10,11... | collective-permute-start | bytes 2359304 | tf_op jit(solution)/shard_map/ppermute | solution.py:36
  208.7 14.1 %collective-permute-start.23 = (bf16[112,768]{1,0:T(8,128)(2,1)}, bf16[112,768]{1,0:T(8,128)(2,1)S(1)}, u32[]{:S(2)}, u32[]{:S(2)}) collective-permute-start(bf16[112,768]{1,0:T(8,128)(2,1)} %add_parts.4.a_ref), channel_id=1, source_target_pairs={{0,16},{4,20},{8,24},{12,28},{16,0},{20,4},{24,8},{28,12},{1,17},{... | collective-permute-start | bytes 516104 | tf_op jit(solution)/shard_map/ppermute | solution.py:36
  (42 other events, 314.3 us)

commit v5 on v4

--- a/solution.py
+++ b/solution.py
@@ -16,6 +16,7 @@
 SMEM = pl.BlockSpec(memory_space=pltpu.SMEM)
 SUM_ROWS = 16
 COST = pl.CostEstimate(flops=2**20, bytes_accessed=2**20, transcendentals=0)
+LONG = pl.CostEstimate(flops=2**34, bytes_accessed=2**24, transcendentals=0)
 
 
 def layer_norm(values, gain, shift):
@@ -574,21 +575,64 @@
     )(lens, rank, dispatch, back, residual, cotangent, gain, *heads, *weights)
 
 
+def output_sum_kernel(kept_ref, core_ref, first_ref, near_ref, far_ref):
+    cols = near_ref.shape[0]
+    total = [
+        (kept_ref[j].astype(f32) + core_ref[j].astype(f32)).astype(bf16) for j in range(2)
+    ]
+    near_ref[...] = total[0]
+    far_ref[:cols, :] = total[1]
+    far_ref[cols:, :] = first_ref[...]
+
+
+def output_sums(kept, core, first):
+    slots, cols, width = kept.shape
+    return pl.pallas_call(
+        output_sum_kernel,
+        out_shape=(
+            jax.ShapeDtypeStruct((cols, width), bf16),
+            jax.ShapeDtypeStruct((cols + first.shape[0], width), bf16),
+        ),
+        in_specs=[VMEM] * 3,
+        out_specs=(VMEM, VMEM),
+        name="output_sums",
+        cost_estimate=LONG,
+    )(kept, core, first)
+
+
 def gelu_parts(values):
     below = 0.5 + 0.5 * lax.erf(values * (0.5**0.5))
     density = jnp.exp(-0.5 * values * values) * (0.5 / jnp.pi) ** 0.5
     return values * below, below + values * density
 
 
-def expert_kernel(in_ref, grad_act_ref, up_ref, act_ref, mid_ref, sum_ref):
+def part_at(step, parts, rank):
+    half = parts // 2
+    return (2 * (step % half) + step // half) ^ rank
+
+
+def expert_kernel(
+    rank_ref, in_ref, grad_act_ref, up_ref,
+    act_kept_ref, pre_kept_ref, act_sent_ref, pre_sent_ref, mid_ref, sum_ref,
+):
     step = pl.program_id(0)
     pre = jnp.dot(in_ref[...], up_ref[...], preferred_element_type=f32)
     act, slope = gelu_parts(pre)
-    act_ref[...] = act.astype(bf16)
+    act = act.astype(bf16)
     grad_pre = (grad_act_ref[...] * slope).astype(bf16)
-    mid = lax.dot_general(
-        grad_pre, up_ref[...], (((1,), (1,)), ((), ())), preferred_element_type=f32
-    )
+    half = pl.num_programs(0) // 2
+
+    @pl.when(step < half)
+    def keep():
+        act_kept_ref[...] = act
+        pre_kept_ref[...] = grad_pre
+
+    @pl.when(step >= half)
+    def send():
+        act_sent_ref[...] = act
+        pre_sent_ref[...] = grad_pre
+
+    mid = across(grad_pre, up_ref[...])
 
     @pl.when(step == 0)
     def first():
@@ -603,35 +647,41 @@
         mid_ref[...] = sum_ref[...].astype(bf16)
 
 
-def expert(rows, grad_act, up):
+def expert(rank, rows, grad_act, up, parts):
     count, width = rows.shape
     hidden = up.shape[1]
-    size = min(512, hidden)
+    size = min(256, hidden // parts)
+    cuts = hidden // parts // size
+    steps = parts * cuts
+    column = lambda i, r: (0, part_at(i // cuts, parts, r[0]) * cuts + i % cuts)
+    kept = pl.BlockSpec((count, size), lambda i, r: (0, jnp.minimum(i, steps // 2 - 1)))
+    sent = pl.BlockSpec((count, size), lambda i, r: (0, jnp.maximum(i - steps // 2, 0)))
+    fixed = pl.BlockSpec((count, width), lambda i, r: (0, 0))
     return pl.pallas_call(
         expert_kernel,
-        grid=(hidden // size,),
-        out_shape=(
-            jax.ShapeDtypeStruct((count, hidden), bf16),
-            jax.ShapeDtypeStruct((count, width), bf16),
+        grid_spec=pltpu.PrefetchScalarGridSpec(
+            num_scalar_prefetch=1,
+            grid=(steps,),
+            in_specs=[
+                fixed,
+                pl.BlockSpec((count, size), column),
+                pl.BlockSpec((width, size), column),
+            ],
+            out_specs=(kept, kept, sent, sent, fixed),
+            scratch_shapes=[pltpu.VMEM((count, width), f32)],
         ),
-        in_specs=[
-            pl.BlockSpec((count, width), lambda i: (0, 0)),
-            pl.BlockSpec((count, size), lambda i: (0, i)),
-            pl.BlockSpec((width, size), lambda i: (0, i)),
-        ],
-        out_specs=(
-            pl.BlockSpec((count, size), lambda i: (0, i)),
-            pl.BlockSpec((count, width), lambda i: (0, 0)),
-        ),
-        scratch_shapes=[pltpu.VMEM((count, width), f32)],
+        out_shape=(jax.ShapeDtypeStruct((count, hidden // 2), bf16),) * 4
+        + (jax.ShapeDtypeStruct((count, width), bf16),),
         name="expert",
         cost_estimate=COST,
-    )(rows, grad_act, up)
-
-
-def product_kernel(a_ref, b_ref, out_ref, sum_ref):
+    )(rank, rows, grad_act, up)
+
+
+def product_kernel(rank_ref, kept_ref, sent_ref, down_ref, out_ref, sum_ref):
     step = pl.program_id(0)
-    made = jnp.dot(a_ref[...], b_ref[...], preferred_element_type=f32)
+    steps = pl.num_programs(0)
+    act = jnp.where(step < steps // 2, kept_ref[...], sent_ref[...])
+    made = jnp.dot(act, down_ref[...], preferred_element_type=f32)
 
     @pl.when(step == 0)
     def first():
@@ -641,78 +691,115 @@
     def later():
         sum_ref[...] += made
 
-    @pl.when(step == pl.num_programs(0) - 1)
+    @pl.when(step == steps - 1)
     def last():
         out_ref[...] = sum_ref[...].astype(bf16)
 
 
-def product(a, b):
-    count, depth = a.shape
-    width = b.shape[1]
-    size = min(1024, depth)
+def product(rank, kept, sent, down, parts):
+    count = kept.shape[0]
+    hidden, width = down.shape
+    size = hidden // parts
     return pl.pallas_call(
         product_kernel,
-        grid=(depth // size,),
+        grid_spec=pltpu.PrefetchScalarGridSpec(
+            num_scalar_prefetch=1,
+            grid=(parts,),
+            in_specs=[
+                pl.BlockSpec((count, size), lambda i, r: (0, jnp.minimum(i, parts // 2 - 1))),
+                pl.BlockSpec((count, size), lambda i, r: (0, jnp.maximum(i - parts // 2, 0))),
+                pl.BlockSpec((size, width), lambda i, r: (part_at(i, parts, r[0]), 0)),
+            ],
+            out_specs=pl.BlockSpec((count, width), lambda i, r: (0, 0)),
+            scratch_shapes=[pltpu.VMEM((count, width), f32)],
+        ),
         out_shape=jax.ShapeDtypeStruct((count, width), bf16),
-        in_specs=[
-            pl.BlockSpec((count, size), lambda i: (0, i)),
-            pl.BlockSpec((size, width), lambda i: (i, 0)),
-        ],
-        out_specs=pl.BlockSpec((count, width), lambda i: (0, 0)),
-        scratch_shapes=[pltpu.VMEM((count, width), f32)],
         name="product",
         cost_estimate=COST,
-    )(a, b)
-
-
-def weight_kernel(groups, rank_ref, up_ref, down_ref, *refs):
-    dup_ref, ddown_ref = refs[-2:]
+    )(rank, kept, sent, down)
+
+
+def weight_kernel(groups, *refs):
+    first_ref, rest_ref, up_ref, down_ref = refs[-4:]
     dup = ddown = 0.0
     for g in range(groups):
-        in_ref, grad_ref = refs[2 * g : 2 * g + 2]
-        pre = jnp.dot(in_ref[...], up_ref[...], preferred_element_type=f32)
-        grad_act = lax.dot_general(
-            grad_ref[...], down_ref[...], (((1,), (1,)), ((), ())),
-            preferred_element_type=f32,
-        )
-        act, slope = gelu_parts(pre)
-        dup = dup + contract_rows(in_ref[...], (grad_act * slope).astype(bf16))
-        ddown = ddown + contract_rows(act.astype(bf16), grad_ref[...])
-    if len(refs) > 2 * groups + 2:
-        dup = dup + refs[2 * groups][...]
-        ddown = ddown + refs[2 * groups + 1][...]
-    dup_ref[...] = dup
-    ddown_ref[...] = ddown
-
-
-def expert_weights(rank, group, up, down, parts, earlier=()):
-    count, width = group[0][0].shape
-    hidden = up.shape[1] // parts
-    size = min(256, hidden)
-    blocks = hidden // size
-    up_block = pl.BlockSpec((width, size), lambda i, r: (0, i))
-    down_block = pl.BlockSpec((size, width), lambda i, r: (i, 0))
-    rows = [values for both in group for values in both]
-    return pl.pallas_call(
-        functools.partial(weight_kernel, len(group)),
-        grid_spec=pltpu.PrefetchScalarGridSpec(
-            num_scalar_prefetch=1,
-            grid=(blocks,),
-            in_specs=[
-                pl.BlockSpec((width, size), lambda i, r: (0, r[0] * blocks + i)),
-                pl.BlockSpec((size, width), lambda i, r: (r[0] * blocks + i, 0)),
-            ]
-            + [pl.BlockSpec((count, width), lambda i, r: (0, 0))] * len(rows)
-            + ([up_block, down_block] if earlier else []),
-            out_specs=(up_block, down_block),
-        ),
-        out_shape=(
-            jax.ShapeDtypeStruct((width, hidden), f32),
-            jax.ShapeDtypeStruct((hidden, width), f32),
+        in_ref, grad_ref, act_ref, pre_ref = refs[4 * g : 4 * g + 4]
+        dup = dup + contract_rows(in_ref[...], pre_ref[...])
+        ddown = ddown + contract_rows(act_ref[...], grad_ref[...])
+    cut = first_ref.shape[0]
+
+    @pl.when(pl.program_id(0) == 0)
+    def far():
+        first_ref[...] = dup[:cut].astype(bf16)
+        rest_ref[: dup.shape[0] - cut, :] = dup[cut:].astype(bf16)
+        rest_ref[dup.shape[0] - cut :, :] = ddown.astype(bf16)
+
+    @pl.when(pl.program_id(0) == 1)
+    def near():
+        up_ref[...] = dup
+        down_ref[...] = ddown
+
+
+def expert_weights(groups):
+    count, width = groups[0][0].shape
+    size = groups[0][2].shape[1] // 2
+    fixed = pl.BlockSpec((count, width), lambda i: (0, 0))
+    columns = pl.BlockSpec((count, size), lambda i: (0, 1 - i))
+    cut = (width + size) // 4
+    shapes = ((cut, size), (width + size - cut, size), (width, size), (size, width))
+    return pl.pallas_call(
+        functools.partial(weight_kernel, len(groups)),
+        grid=(2,),
+        in_specs=[fixed, fixed, columns, columns] * len(groups),
+        out_specs=tuple(pl.BlockSpec(shape, lambda i: (0, 0)) for shape in shapes),
+        out_shape=tuple(
+            jax.ShapeDtypeStruct(shape, bf16 if k < 2 else f32)
+            for k, shape in enumerate(shapes)
         ),
         name="expert_weights",
-        cost_estimate=COST,
-    )(rank, up, down, *rows, *earlier)
+        compiler_params=pltpu.CompilerParams(vmem_limit_bytes=60 * 2**20),
+        cost_estimate=COST,
+    )(*[values for group in groups for values in group])
+
+
+def expert_sum_kernel(near_up_ref, near_down_ref, first_ref, rest_ref, up_ref, down_ref):
+    step = pl.program_id(0)
+    half = pl.num_programs(0) // 2
+    far = jnp.where(step < half // 2, first_ref[...], rest_ref[...]).astype(f32)
+
+    @pl.when(step < half)
+    def upper():
+        up_ref[...] = near_up_ref[...] + far
+
+    @pl.when(step >= half)
+    def lower():
+        down_ref[...] = near_down_ref[...] + far
+
+
+def expert_sums(near_up, near_down, first, rest):
+    count, width = near_up.shape
+    steps = 8
+    half = steps // 2
+    size = count // half
+    head = steps // 4
+    skip = first.shape[0] // size - head
+    block = lambda place: pl.BlockSpec((size, width), lambda i: (place(i), 0))
+    upper = block(lambda i: jnp.minimum(i, half - 1))
+    lower = block(lambda i: jnp.maximum(i - half, 0))
+    return pl.pallas_call(
+        expert_sum_kernel,
+        grid=(steps,),
+        out_shape=(jax.ShapeDtypeStruct((count, width), f32),) * 2,
+        in_specs=[
+            upper,
+            lower,
+            block(lambda i: jnp.minimum(i, head - 1) + skip),
+            block(lambda i: jnp.maximum(i - head, 0)),
+        ],
+        out_specs=(upper, lower),
+        name="expert_sums",
+        cost_estimate=COST,
+    )(near_up, near_down, first, rest)
 
 
 def input_grad_kernel(groups, qw_ref, kw_ref, vw_ref, *refs):
@@ -917,35 +1004,26 @@
 
     flat_grad, outgoing = tie(flat_grad, outgoing)
     grad_act = across(flat_grad, down_matrix)
-    gathered_grads = [flat_grad]
-    gathered_rows = [flat_in]
+    near_grads = swap(flat_grad, "tensor", 1)
+    flat_in, grad_act, near_grads = tie(flat_in, grad_act, near_grads)
+    near_rows = swap(flat_in, "tensor", 1)
+    act, grad_pre, act_sent, pre_sent, grad_mid = expert(
+        rank_cell[0], flat_in, grad_act, up_matrix, members
+    )
+    grad_mid, act, near_rows = tie(grad_mid, act, near_rows)
+    grad_back = exchange(grad_mid)
+
+    act, act_sent, pre_sent, grad_mid = tie(act, act_sent, pre_sent, grad_mid)
+    near_act = swap(act_sent, "tensor", 1)
+    near_pre = swap(pre_sent, "tensor", 1)
+    made = product(rank_cell[0], act, act_sent, down_matrix, members)
+    made, near_act, near_pre = tie(made, near_act, near_pre)
+    *expert_far, expert_up_near, expert_down_near = expert_weights(
+        [(flat_in, flat_grad, act, grad_pre), (near_rows, near_grads, near_act, near_pre)]
+    )
+    grad_back, made, expert_far = tie(grad_back, made, expert_far)
+
     steps = steps_of(members)
-    for step in reversed(steps[1:]):
-        gathered_grads += [swap(a, "tensor", step) for a in gathered_grads]
-    flat_in, grad_act, gathered_grads = tie(flat_in, grad_act, gathered_grads)
-    gathered_rows = [flat_in]
-    for step in reversed(steps[1:]):
-        gathered_rows += [swap(a, "tensor", step) for a in gathered_rows]
-    near_grads = swap(gathered_grads[0], "tensor", 1)
-    near_rows = swap(flat_in, "tensor", 1)
-    far_grads = [swap(a, "tensor", 1) for a in gathered_grads[1:]]
-    act, grad_mid = expert(flat_in, grad_act, up_matrix)
-    act, grad_mid, near_rows, near_grads, far_grads = tie(
-        act, grad_mid, near_rows, near_grads, far_grads
-    )
-    grad_back = exchange(grad_mid)
-
-    act, near_rows, grad_mid = tie(act, near_rows, grad_mid)
-    made = product(act, down_matrix)
-    sums = expert_weights(
-        rank_cell[0],
-        [(flat_in, gathered_grads[0]), (near_rows, near_grads)],
-        up_matrix, down_matrix, members,
-    )
-    made, sums, gathered_rows = tie(made, sums, gathered_rows)
-    far_rows = [swap(a, "tensor", 1) for a in gathered_rows[1:]]
-    grad_back, made, sums = tie(grad_back, made, sums)
-
     grad_res, sums_second, kept, sent, *grad_heads = turn(
         item_lengths, rank_cell, dispatch, grad_back, residual, cotangent,
         second_gain, all_heads, outputs,
@@ -953,10 +1031,10 @@
     grad_parts = [grad_heads[0]] + [
         swap(grad_heads[j], "tensor", j) for j in range(1, members)
     ]
+    output_near, output_far = output_sums(kept, swap(sent, "tensor", 1), expert_far[0])
     made, grad_heads = tie(made, grad_heads)
     returned = exchange(made)
-    output_sum = add_low(kept, swap(sent, "tensor", 1))
-    grad_parts, output_sum = tie(grad_parts, output_sum)
+    grad_parts, output_near, output_far = tie(grad_parts, output_near, output_far)
 
     bit_cell = (lax.axis_index("dp") & 1).astype(jnp.int32).reshape(1, 1)
     weights = (qw, kw, vw)
@@ -967,21 +1045,19 @@
     )
     groups = ((0, heads - 1), (heads - 1, 1))
     joint_a, sums_a, own_a, away_a = back(*groups[0], extras=(), grads=grad_parts)
-    for step in steps[1:]:
-        output_sum = add_low(
-            output_sum[: len(output_sum) // 2],
-            swap(output_sum[len(output_sum) // 2 :], "tensor", step),
-        )
-    joint_a, own_a, away_a, output_sum, grad_parts = tie(
-        joint_a, own_a, away_a, output_sum, grad_parts
-    )
+    output_got = swap(output_far, "tensor", 2)
+    joint_a, own_a, away_a, output_got, grad_parts, expert_rest, returned = tie(
+        joint_a, own_a, away_a, output_got, grad_parts, expert_far[1], returned
+    )
+    expert_got = swap(expert_rest, "tensor", 2)
+    output_sum = add_low(output_near, output_got[: output_near.shape[0]])
     own_a = add_low(own_a, swap(away_a, "dp", 1))
-    output_sum = add_low(output_sum[0], swap(output_sum[0], "dp", dp_steps[-1]))
+    output_sum = add_low(output_sum, swap(output_sum, "dp", dp_steps[-1]))
     joint_b, unused, own_b, away_b = back(
         *groups[1], extras=(sums_a, sums_second), grads=grad_parts
     )
-    joint_b, own_a, own_b, away_b, output_sum, returned = tie(
-        joint_b, own_a, own_b, away_b, output_sum, returned
+    joint_b, own_a, own_b, away_b, output_sum = tie(
+        joint_b, own_a, own_b, away_b, output_sum
     )
 
     far_kept, far_sent = input_grad(
@@ -999,11 +1075,9 @@
         own_a = add_low(own_a, swap(own_a, "dp", step))
         own_b = add_parts(own_b, swap(own_b, "dp", step))
         if step == dp_steps[1]:
-            own_b, sums, gathered_rows, far_rows = tie(own_b, sums, gathered_rows, far_rows)
-    up_grad, down_grad = expert_weights(
-        rank_cell[0],
-        list(zip(gathered_rows[1:], gathered_grads[1:])) + list(zip(far_rows, far_grads)),
-        up_matrix, down_matrix, members, sums,
+            own_b, expert_got = tie(own_b, expert_got)
+    up_grad, down_grad = expert_sums(
+        expert_up_near, expert_down_near, output_got, expert_got
     )
     own_b, up_grad, down_grad, near_far = tie(own_b, up_grad, down_grad, near_far)
     norm_sums = own_b[-SUM_ROWS:].astype(f32)

time: 242 us -> 255 us (1.054)
  starting transfers between devices: 53.2 us -> 61.5 us
  local copies, waits for them, and re-layouts: 5.44 us -> 8.27 us
    pallas_call x4 -> x5, Pallas kernels: 37.8 us -> 50.2 us  [the longest x1 21 us: expert(): pl.pallas_call(expert_kernel, grid_spec=pltpu.PrefetchScalarGridSpec(num_...]
    pallas_call x2, Pallas kernels: 35.9 us -> 27.1 us  [attend_back(): pl.pallas_call(functools.partial(backward_kernel, first_head, heads, bloc...]
    ppermute x33 -> x32, starting transfers between devices: 28.3 us -> 36 us  [swap(): return lax.ppermute(values, axis, [(i, i ^ step) for i in range(count)])]
    pallas_call x2, Pallas kernels: 19.5 us -> 15.7 us  [attend(): pl.pallas_call(functools.partial(forward_kernel, first, blocks), out_shap...]
    unnamed x58 -> x66, local copies, waits for them, and re-layouts: 4.8 us -> 7.65 us
    convert_element_type x8 -> x7, other arithmetic: 6.06 us -> 4.78 us  [add_low(): return (a.astype(f32) + b.astype(f32)).astype(bf16)]
    ppermute x33 -> x32, waiting for transfers between devices: 16.6 us -> 17.9 us  [swap(): return lax.ppermute(values, axis, [(i, i ^ step) for i in range(count)])]
  transfers between devices with their start and end apart: 37 -> 36, of which waited for: 10 -> 9; matrix products, arithmetic and copies ran while one was open for 7% -> 6% of each run, Pallas kernels for 49% -> 49%
where the time goes in v5:
time: 255 us; the launch traced here: 254 us
  Pallas kernels  136 us (53%)
  starting transfers between devices  61.5 us (24%)
  waiting for transfers between devices  31.8 us (12%)
  matrix products  8.6 us (3%)
  local copies, waits for them, and re-layouts  8.27 us (3%)
  other arithmetic  7.09 us (3%)
    ppermute x32, starting transfers between devices, swap(): return lax.ppermute(values, axis, [(i, i ^ step) for i in range(count)])  36 us
    pallas_call x2, Pallas kernels, attend_back(): pl.pallas_call(functools.partial(backward_kernel, first_head, heads, bloc...  27.1 us
    all_to_all x4, starting transfers between devices, exchange(): lax.all_to_all(rows.reshape(sources, -1, width), 'dp', split_axis=0, conc...  25.5 us
    pallas_call x1, Pallas kernels, expert(): pl.pallas_call(expert_kernel, grid_spec=pltpu.PrefetchScalarGridSpec(num_...  21 us
    ppermute x32, waiting for transfers between devices, swap(): return lax.ppermute(values, axis, [(i, i ^ step) for i in range(count)])  17.9 us
    pallas_call x2, Pallas kernels, attend(): pl.pallas_call(functools.partial(forward_kernel, first, blocks), out_shap...  15.7 us
    all_to_all x4, waiting for transfers between devices, exchange(): lax.all_to_all(rows.reshape(sources, -1, width), 'dp', split_axis=0, conc...  13.9 us
    pallas_call x1, Pallas kernels, expert_weights(): pl.pallas_call(functools.partial(weight_kernel, len(groups)), grid=(2,),...  11.9 us
  transfers between devices with their start and end apart: 36, of which 9 were waited for; matrix products, arithmetic and copies ran while one was open for 6% of the time, Pallas kernels for 49%

profile of v5, /device:TPU:0, one launch (start us, length us, event | category | flops | bytes accessed | tf_op | source)
XLA Modules:
  0.0 254.1 jit_solution(12124435679220752412)
XLA Ops:
  3.9 7.3 %all-to-all-start.1 = ((bf16[8,64,768]{2,1,0:T(8,128)(2,1)}), bf16[8,64,768]{2,1,0:T(8,128)(2,1)S(1)}, u32[]{:S(2)}, u32[]{:S(2)}) async-start(bf16[8,64,768]{2,1,0:T(8,128)(2,1)} %bitcast.52), calls=%async_computation.1 | async-start | bytes 1572864 | tf_op jit(solution)/shard_map/all_to_all | solution.py:968
  13.4 7.5 %project.1 = (bf16[2048,768]{1,0:T(8,128)(2,1)}, bf16[192,2048]{1,0:T(8,128)(2,1)}, bf16[192,2048]{1,0:T(8,128)(2,1)}, bf16[192,2048]{1,0:T(8,128)(2,1)}) custom-call(s32[1]{0:T(128)} %bitcast.rank_ref, bf16[2048,768]{1,0:T(8,128)(2,1)} %tokens_ref.2, f32[768]{0:T(1024)} %gain_ref.7, f32[768]{0:T(1024)} %bias_ref.2, bf16[192,768]{1,0:T(8,128)(2,1)} %bitcast.27, ...), custom_call_target="tpu_custom_call" | custom-call | flops 1048576 | bytes 1048576 | tf_op jit(solution)/shard_map/project/pallas_call | solution.py:80
  20.9 5.9 %attend.2 = (bf16[192,512]{1,0:T(8,128)(2,1)}, bf16[192,512]{1,0:T(8,128)(2,1)}, f32[3,1,1024]{2,1,0:T(1,128)}) custom-call(s32[1,5]{1,0:T(1,128)} %lens_ref.11, s32[1,1]{1,0:T(1,128)} %bitcast.1.rank_ref, bf16[192,2048]{1,0:T(8,128)(2,1)} %get-tuple-element.125.qt_ref, bf16[192,2048]{1,0:T(8,128)(2,1)} %get-tuple-element.130.kt_ref, ...), custom_call_target="tpu_custom_call" | custom-call | flops 1048576 | bytes 1048576 | tf_op jit(solution)/shard_map/attend/pallas_call | solution.py:238
  26.9 5.3 %collective-permute-start = (bf16[192,512]{1,0:T(8,128)(2,1)}, bf16[192,512]{1,0:T(8,128)(2,1)S(1)}, u32[]{:S(2)}, u32[]{:S(2)}) collective-permute-start(bf16[192,512]{1,0:T(8,128)(2,1)} %get-tuple-element.133.rest_2_.rest_4_), channel_id=1, source_target_pairs={{0,2},{1,3},{2,0},{3,1},{4,6},{5,7},{6,4},{7,5},{8,10},{9,11},{10,... | collective-permute-start | bytes 589832 | tf_op jit(solution)/shard_map/ppermute | solution.py:37
  32.2 9.8 %attend.3 = (bf16[192,512]{1,0:T(8,128)(2,1)}, bf16[192,512]{1,0:T(8,128)(2,1)}, f32[3,1,1024]{2,1,0:T(1,128)}) custom-call(s32[1,5]{1,0:T(1,128)} %lens_ref.11, s32[1,1]{1,0:T(1,128)} %bitcast.1.rank_ref, bf16[192,2048]{1,0:T(8,128)(2,1)} %get-tuple-element.125.qt_ref, bf16[192,2048]{1,0:T(8,128)(2,1)} %get-tuple-element.130.kt_ref, ...), custom_call_target="tpu_custom_call" | custom-call | flops 1048576 | bytes 1048576 | tf_op jit(solution)/shard_map/attend/pallas_call | solution.py:238
  44.4 4.9 %middle.1 = (f32[512,768]{1,0:T(8,128)}, bf16[512,768]{1,0:T(8,128)(2,1)}) custom-call(s32[1]{0:T(128)} %bitcast.rank_ref, bf16[2048,768]{1,0:T(8,128)(2,1)} %tokens_ref.2, f32[768]{0:T(1024)} %gain_ref.6, f32[768]{0:T(1024)} %bias_ref.3, bf16[512,512]{1,0:T(8,128)(2,1)} %get-tuple-element.124.dispatch_ref, ...), custom_call_target="tpu_custom_call" | custom-call | flops 1048576 | bytes 1048576 | tf_op jit(solution)/shard_map/middle/pallas_call | solution.py:505
  49.3 8.8 %all-to-all-start = ((bf16[8,64,768]{2,1,0:T(8,128)(2,1)}), bf16[8,64,768]{2,1,0:T(8,128)(2,1)S(1)}, u32[]{:S(2)}, u32[]{:S(2)}) async-start(bf16[8,64,768]{2,1,0:T(8,128)(2,1)} %bitcast.54), calls=%async_computation | async-start | bytes 1572864 | tf_op jit(solution)/shard_map/all_to_all | solution.py:968
  58.1 6.9 %fusion.1.grad_act_ref = f32[512,3072]{1,0:T(8,128)} fusion(bf16[512,768]{1,0:T(8,128)(2,1)S(1)} %bitcast.48, bf16[1,3072,768]{2,1,0:T(8,128)(2,1)} %param.25), kind=kOutput, calls=%fused_computation.17 | convolution fusion | flops 2415919104 | bytes 11796480 | tf_op jit(solution)/shard_map/dot_general | solution.py:482
  65.0 13.7 %all-to-all-done = bf16[8,64,768]{2,1,0:T(8,128)(2,1)S(1)} async-done(((bf16[8,64,768]{2,1,0:T(8,128)(2,1)}), bf16[8,64,768]{2,1,0:T(8,128)(2,1)S(1)}, u32[]{:S(2)}, u32[]{:S(2)}) %all-to-all-start) | async-done | bytes 786464 | tf_op jit(solution)/shard_map/all_to_all | solution.py:968
  79.6 21.0 %expert.1 = (bf16[512,1536]{1,0:T(8,128)(2,1)}, bf16[512,1536]{1,0:T(8,128)(2,1)}, bf16[512,1536]{1,0:T(8,128)(2,1)}, bf16[512,1536]{1,0:T(8,128)(2,1)}, bf16[512,768]{1,0:T(8,128)(2,1)}) custom-call(s32[1]{0:T(128)} %bitcast.rank_ref, bf16[512,768]{1,0:T(8,128)(2,1)} %bitcast.43, f32[512,3072]{1,0:T(8,128)} %fusion.1.grad_act_ref, bf16[768,3072]{1,0:T(8,128)(2,1)} %bitcast.45), custom_call_target="tpu_custom_call" | custom-call | flops 1048576 | bytes 1048576 | tf_op jit(solution)/shard_map/expert/pallas_call | solution.py:660
  105.3 7.1 %product.1 = bf16[512,768]{1,0:T(8,128)(2,1)} custom-call(s32[1]{0:T(128)} %bitcast.rank_ref, bf16[512,1536]{1,0:T(8,128)(2,1)} %get-tuple-element.157.kept_ref.refs_2_, bf16[512,1536]{1,0:T(8,128)(2,1)} %get-tuple-element.158.sent_ref, bf16[3072,768]{1,0:T(8,128)(2,1)} %bitcast.46), custom_call_target="tpu_custom_call" | custom-call | flops 1048576 | bytes 1048576 | tf_op jit(solution)/shard_map/product/pallas_call | solution.py:703
  113.6 11.9 %expert_weights.1 = (bf16[384,768]{1,0:T(8,128)(2,1)}, bf16[1152,768]{1,0:T(8,128)(2,1)}, f32[768,768]{1,0:T(8,128)}, f32[768,768]{1,0:T(8,128)}) custom-call(bf16[512,768]{1,0:T(8,128)(2,1)} %bitcast.44, bf16[512,768]{1,0:T(8,128)(2,1)} %bitcast.49, bf16[512,1536]{1,0:T(8,128)(2,1)} %get-tuple-element.157.kept_ref.refs_2_, ...), custom_call_target="tpu_custom_call" | custom-call | flops 1048576 | bytes 1048576 | tf_op jit(solution)/shard_map/expert_weights/pallas_call | solution.py:750
  126.5 6.5 %turn.1 = (f32[512,768]{1,0:T(8,128)}, f32[2,768]{1,0:T(2,128)}, bf16[2,192,768]{2,1,0:T(8,128)(2,1)}, bf16[2,192,768]{2,1,0:T(8,128)(2,1)}, bf16[192,512]{1,0:T...) custom-call(s32[1,5]{1,0:T(1,128)} %lens_ref.11, ...), custom_call_target="tpu_custom_call" | custom-call | flops 1048576 | bytes 1048576 | tf_op jit(solution)/shard_map/turn/pallas_call | solution.py:562
  135.0 5.8 %all-to-all-start.3 = ((bf16[8,64,768]{2,1,0:T(8,128)(2,1)}), bf16[8,64,768]{2,1,0:T(8,128)(2,1)S(1)}, u32[]{:S(2)}, u32[]{:S(2)}) async-start(bf16[8,64,768]{2,1,0:T(8,128)(2,1)} %bitcast.15), calls=%async_computation.3 | async-start | bytes 1572864 | tf_op jit(solution)/shard_map/all_to_all | solution.py:968
  145.6 16.1 %attend_back.2 = (bf16[2048,384]{1,0:T(8,128)(2,1)}, f32[2,768]{1,0:T(2,128)}, bf16[192,768]{1,0:T(8,128)(2,1)}, bf16[192,768]{1,0:T(8,128)(2,1)}) custom-call(s32[1,5]{1,0:T(1,128)} %lens_ref.11, s32[1,1]{1,0:T(1,128)} %bitcast.1.rank_ref, s32[1,1]{1,0:T(1,128)} %bitcast.6.bit_ref, bf16[192,2048]{1,0:T(8,128)(2,1)} %get-tuple-element.125.qt_ref, ...), custom_call_target="tpu_custom_call" | custom-call | flops 1048576 | bytes 1048576 | tf_op jit(solution)/shard_map/attend_back/pallas_call | solution.py:406
  161.7 5.0 %collective-permute-done.14.first_ref = bf16[576,768]{1,0:T(8,128)(2,1)S(1)} collective-permute-done((bf16[576,768]{1,0:T(8,128)(2,1)}, bf16[576,768]{1,0:T(8,128)(2,1)S(1)}, u32[]{:S(2)}, u32[]{:S(2)}) %collective-permute-start.14) | collective-permute-done | bytes 884768 | tf_op jit(solution)/shard_map/ppermute | solution.py:37
  166.8 4.4 %collective-permute-start.16 = (bf16[192,768]{1,0:T(8,128)(2,1)S(1)}, bf16[192,768]{1,0:T(8,128)(2,1)S(1)}, u32[]{:S(2)}, u32[]{:S(2)}) collective-permute-start(bf16[192,768]{1,0:T(8,128)(2,1)S(1)} %add_convert_fusion.6), channel_id=1, source_target_pairs={{0,16},{4,20},{8,24},{12,28},{16,0},{20,4},{24,8},{28,12},{1,17},{... | collective-permute-start | bytes 884744 | tf_op jit(solution)/shard_map/ppermute | solution.py:37
  172.5 11.0 %attend_back.3 = (bf16[2048,192]{1,0:T(8,128)(2,1)}, f32[2,768]{1,0:T(2,128)}, bf16[112,768]{1,0:T(8,128)(2,1)}, bf16[112,768]{1,0:T(8,128)(2,1)}) custom-call(s32[1,5]{1,0:T(1,128)} %lens_ref.11, s32[1,1]{1,0:T(1,128)} %bitcast.1.rank_ref, s32[1,1]{1,0:T(1,128)} %bitcast.6.bit_ref, bf16[192,2048]{1,0:T(8,128)(2,1)} %get-tuple-element.125.qt_ref, ...), custom_call_target="tpu_custom_call" | custom-call | flops 1048576 | bytes 1048576 | tf_op jit(solution)/shard_map/attend_back/pallas_call | solution.py:406
  185.1 4.4 %input_grad.3 = (bf16[1,512,768]{2,1,0:T(8,128)(2,1)}, bf16[1,512,768]{2,1,0:T(8,128)(2,1)}) custom-call(bf16[192,768]{1,0:T(8,128)(2,1)} %bitcast.30, bf16[192,768]{1,0:T(8,128)(2,1)} %bitcast.35, bf16[192,768]{1,0:T(8,128)(2,1)} %bitcast.40, bf16[2048,384]{1,0:T(8,128)(2,1)} %get-tuple-element.191.refs_0_, bf16[2048,192]{1,0:T(8,128)(2,1)} %get-tuple-element.205.refs_1_), custom_call_target="tpu_custom_call" | custom-call | flops 1048576 | bytes 1048576 | tf_op jit(solution)/shard_map/input_grad/pallas_call | solution.py:843
  191.9 4.8 %collective-permute-start.26 = (bf16[192,768]{1,0:T(8,128)(2,1)S(1)}, bf16[192,768]{1,0:T(8,128)(2,1)}, u32[]{:S(2)}, u32[]{:S(2)}) collective-permute-start(bf16[192,768]{1,0:T(8,128)(2,1)S(1)} %add_convert_fusion.7), channel_id=1, source_target_pairs={{0,8},{4,12},{8,0},{12,4},{16,24},{20,28},{24,16},{28,20},{1,9},{5... | collective-permute-start | bytes 884744 | tf_op jit(solution)/shard_map/ppermute | solution.py:37
  196.7 4.4 %input_grad.2 = (bf16[1,512,768]{2,1,0:T(8,128)(2,1)}, bf16[1,512,768]{2,1,0:T(8,128)(2,1)}) custom-call(bf16[192,768]{1,0:T(8,128)(2,1)} %bitcast.31, bf16[192,768]{1,0:T(8,128)(2,1)} %bitcast.36, bf16[192,768]{1,0:T(8,128)(2,1)} %bitcast.41, bf16[2048,384]{1,0:T(8,128)(2,1)} %get-tuple-element.191.refs_0_, bf16[2048,192]{1,0:T(8,128)(2,1)} %get-tuple-element.205.refs_1_), custom_call_target="tpu_custom_call" | custom-call | flops 1048576 | bytes 1048576 | tf_op jit(solution)/shard_map/input_grad/pallas_call | solution.py:843
  222.7 7.7 %expert_sums.1 = (f32[768,768]{1,0:T(8,128)}, f32[768,768]{1,0:T(8,128)}) custom-call(f32[768,768]{1,0:T(8,128)} %get-tuple-element.217.near_up_ref, f32[768,768]{1,0:T(8,128)} %get-tuple-element.218.near_down_ref, bf16[576,768]{1,0:T(8,128)(2,1)} %copy-done.6, bf16[1152,768]{1,0:T(8,128)(2,1)} %collective-permute-done.21.rest_ref), custom_call_target="tpu_custom_call" | custom-call | flops 1048576 | bytes 1048576 | tf_op jit(solution)/shard_map/expert_sums/pallas_call | solution.py:789
  230.4 3.9 %collective-permute-done.22.b_ref = bf16[112,768]{1,0:T(8,128)(2,1)S(1)} collective-permute-done((bf16[112,768]{1,0:T(8,128)(2,1)}, bf16[112,768]{1,0:T(8,128)(2,1)S(1)}, u32[]{:S(2)}, u32[]{:S(2)}) %collective-permute-start.22) | collective-permute-done | bytes 172064 | tf_op jit(solution)/shard_map/ppermute | solution.py:37
  242.4 4.2 %close.1 = f32[512,768]{1,0:T(8,128)} custom-call(s32[1]{0:T(128)} %bitcast.rank_ref, bf16[2048,768]{1,0:T(8,128)(2,1)} %tokens_ref.2, f32[768]{0:T(1024)} %gain_ref.7, f32[512,768]{1,0:T(8,128)} %get-tuple-element.190.grad_ref, bf16[1,512,768]{2,1,0:T(8,128)(2,1)} %get-tuple-element.206.refs_0_, bf16[1,512,768]{2,1,0:T(8,128)(2,1)} %copy-done.18, ...), custom_call_target="tpu_custom_call" | custom-call | flops 1048576 | bytes 1048576 | tf_op jit(solution)/shard_map/close/pallas_call | solution.py:880
  (150 shorter events, 65.0 us)
Async XLA Ops:
  3.9 45.3 %all-to-all-start.1 = ((bf16[8,64,768]{2,1,0:T(8,128)(2,1)}), bf16[8,64,768]{2,1,0:T(8,128)(2,1)S(1)}, u32[]{:S(2)}, u32[]{:S(2)}) async-start(bf16[8,64,768]{2,1,0:T(8,128)(2,1)} %bitcast.52), calls=%async_computation.1 | async-start | bytes 1572864 | tf_op jit(solution)/shard_map/all_to_all | solution.py:968
  11.2 30.8 %collective-permute-start.3 = (bf16[192,768]{1,0:T(8,128)(2,1)S(1)}, bf16[192,768]{1,0:T(8,128)(2,1)S(1)}, u32[]{:S(2)}, u32[]{:S(2)}) collective-permute-start(bf16[192,768]{1,0:T(8,128)(2,1)S(1)} %copy-done.8), channel_id=1, source_target_pairs={{0,2},{1,3},{2,0},{3,1},{4,6},{5,7},{6,4},{7,5},{8,10},{9,11},{10,... | collective-permute-start | bytes 884744 | tf_op jit(solution)/shard_map/ppermute | solution.py:37
  12.8 29.2 %collective-permute-start.2 = (bf16[192,768]{1,0:T(8,128)(2,1)S(1)}, bf16[192,768]{1,0:T(8,128)(2,1)S(1)}, u32[]{:S(2)}, u32[]{:S(2)}) collective-permute-start(bf16[192,768]{1,0:T(8,128)(2,1)S(1)} %copy-done.8), channel_id=1, source_target_pairs={{0,1},{1,0},{2,3},{3,2},{4,5},{5,4},{6,7},{7,6},{8,9},{9,8},{10,11... | collective-permute-start | bytes 884744 | tf_op jit(solution)/shard_map/ppermute | solution.py:37
  12.8 29.3 %collective-permute-start.4 = (bf16[192,768]{1,0:T(8,128)(2,1)S(1)}, bf16[192,768]{1,0:T(8,128)(2,1)S(1)}, u32[]{:S(2)}, u32[]{:S(2)}) collective-permute-start(bf16[192,768]{1,0:T(8,128)(2,1)S(1)} %copy-done.8), channel_id=1, source_target_pairs={{0,3},{1,2},{2,1},{3,0},{4,7},{5,6},{6,5},{7,4},{8,11},{9,10},{10,... | collective-permute-start | bytes 884744 | tf_op jit(solution)/shard_map/ppermute | solution.py:37
  26.9 15.1 %collective-permute-start = (bf16[192,512]{1,0:T(8,128)(2,1)}, bf16[192,512]{1,0:T(8,128)(2,1)S(1)}, u32[]{:S(2)}, u32[]{:S(2)}) collective-permute-start(bf16[192,512]{1,0:T(8,128)(2,1)} %get-tuple-element.133.rest_2_.rest_4_), channel_id=1, source_target_pairs={{0,2},{1,3},{2,0},{3,1},{4,6},{5,7},{6,4},{7,5},{8,10},{9,11},{10,... | collective-permute-start | bytes 589832 | tf_op jit(solution)/shard_map/ppermute | solution.py:37
  49.3 29.4 %all-to-all-start = ((bf16[8,64,768]{2,1,0:T(8,128)(2,1)}), bf16[8,64,768]{2,1,0:T(8,128)(2,1)S(1)}, u32[]{:S(2)}, u32[]{:S(2)}) async-start(bf16[8,64,768]{2,1,0:T(8,128)(2,1)} %bitcast.54), calls=%async_computation | async-start | bytes 1572864 | tf_op jit(solution)/shard_map/all_to_all | solution.py:968
  58.1 20.7 %collective-permute-start.6 = (bf16[512,768]{1,0:T(8,128)(2,1)S(1)}, bf16[512,768]{1,0:T(8,128)(2,1)S(1)}, u32[]{:S(2)}, u32[]{:S(2)}) collective-permute-start(bf16[512,768]{1,0:T(8,128)(2,1)S(1)} %bitcast.47), channel_id=1, source_target_pairs={{0,1},{1,0},{2,3},{3,2},{4,5},{5,4},{6,7},{7,6},{8,9},{9,8},{10,11... | collective-permute-start | bytes 2359304 | tf_op jit(solution)/shard_map/ppermute | solution.py:37
  78.7 21.9 %collective-permute-start.7 = (bf16[512,768]{1,0:T(8,128)(2,1)S(1)}, bf16[512,768]{1,0:T(8,128)(2,1)S(1)}, u32[]{:S(2)}, u32[]{:S(2)}) collective-permute-start(bf16[512,768]{1,0:T(8,128)(2,1)S(1)} %bitcast.42), channel_id=1, source_target_pairs={{0,1},{1,0},{2,3},{3,2},{4,5},{5,4},{6,7},{7,6},{8,9},{9,8},{10,11... | collective-permute-start | bytes 2359304 | tf_op jit(solution)/shard_map/ppermute | solution.py:37
  100.7 11.8 %collective-permute-start.9 = (bf16[512,1536]{1,0:T(8,128)(2,1)}, bf16[512,1536]{1,0:T(8,128)(2,1)S(1)}, u32[]{:S(2)}, u32[]{:S(2)}) collective-permute-start(bf16[512,1536]{1,0:T(8,128)(2,1)} %get-tuple-element.159), channel_id=1, source_target_pairs={{0,1},{1,0},{2,3},{3,2},{4,5},{5,4},{6,7},{7,6},{8,9},{9,8},{10,11... | collective-permute-start | bytes 4718600 | tf_op jit(solution)/shard_map/ppermute | solution.py:37
  100.7 11.7 %collective-permute-start.8 = (bf16[512,1536]{1,0:T(8,128)(2,1)}, bf16[512,1536]{1,0:T(8,128)(2,1)}, u32[]{:S(2)}, u32[]{:S(2)}) collective-permute-start(bf16[512,1536]{1,0:T(8,128)(2,1)} %get-tuple-element.158.sent_ref), channel_id=1, source_target_pairs={{0,1},{1,0},{2,3},{3,2},{4,5},{5,4},{6,7},{7,6},{8,9},{9,8},{10,11... | collective-permute-start | bytes 4718600 | tf_op jit(solution)/shard_map/ppermute | solution.py:37
  101.6 24.0 %all-to-all-start.2 = ((bf16[8,64,768]{2,1,0:T(8,128)(2,1)}), bf16[8,64,768]{2,1,0:T(8,128)(2,1)S(1)}, u32[]{:S(2)}, u32[]{:S(2)}) async-start(bf16[8,64,768]{2,1,0:T(8,128)(2,1)} %bitcast.53), calls=%async_computation.2 | async-start | bytes 1572864 | tf_op jit(solution)/shard_map/all_to_all | solution.py:968
  135.0 26.7 %all-to-all-start.3 = ((bf16[8,64,768]{2,1,0:T(8,128)(2,1)}), bf16[8,64,768]{2,1,0:T(8,128)(2,1)S(1)}, u32[]{:S(2)}, u32[]{:S(2)}) async-start(bf16[8,64,768]{2,1,0:T(8,128)(2,1)} %bitcast.15), calls=%async_computation.3 | async-start | bytes 1572864 | tf_op jit(solution)/shard_map/all_to_all | solution.py:968
  144.1 22.6 %collective-permute-start.14 = (bf16[576,768]{1,0:T(8,128)(2,1)}, bf16[576,768]{1,0:T(8,128)(2,1)S(1)}, u32[]{:S(2)}, u32[]{:S(2)}) collective-permute-start(bf16[576,768]{1,0:T(8,128)(2,1)} %get-tuple-element.185), channel_id=1, source_target_pairs={{0,2},{1,3},{2,0},{3,1},{4,6},{5,7},{6,4},{7,5},{8,10},{9,11},{10,... | collective-permute-start | bytes 2654216 | tf_op jit(solution)/shard_map/ppermute | solution.py:37
  166.8 18.2 %collective-permute-start.16 = (bf16[192,768]{1,0:T(8,128)(2,1)S(1)}, bf16[192,768]{1,0:T(8,128)(2,1)S(1)}, u32[]{:S(2)}, u32[]{:S(2)}) collective-permute-start(bf16[192,768]{1,0:T(8,128)(2,1)S(1)} %add_convert_fusion.6), channel_id=1, source_target_pairs={{0,16},{4,20},{8,24},{12,28},{16,0},{20,4},{24,8},{28,12},{1,17},{... | collective-permute-start | bytes 884744 | tf_op jit(solution)/shard_map/ppermute | solution.py:37
  171.2 13.9 %collective-permute-start.15 = (bf16[192,768]{1,0:T(8,128)(2,1)}, bf16[192,768]{1,0:T(8,128)(2,1)S(1)}, u32[]{:S(2)}, u32[]{:S(2)}) collective-permute-start(bf16[192,768]{1,0:T(8,128)(2,1)} %get-tuple-element.200), channel_id=1, source_target_pairs={{0,4},{4,0},{8,12},{12,8},{16,20},{20,16},{24,28},{28,24},{1,5},{5... | collective-permute-start | bytes 884744 | tf_op jit(solution)/shard_map/ppermute | solution.py:37
  171.2 46.9 %collective-permute-start.21 = (bf16[1152,768]{1,0:T(8,128)(2,1)}, bf16[1152,768]{1,0:T(8,128)(2,1)}, u32[]{:S(2)}, u32[]{:S(2)}) collective-permute-start(bf16[1152,768]{1,0:T(8,128)(2,1)} %get-tuple-element.215), channel_id=1, source_target_pairs={{0,2},{1,3},{2,0},{3,1},{4,6},{5,7},{6,4},{7,5},{8,10},{9,11},{10,... | collective-permute-start | bytes 5308424 | tf_op jit(solution)/shard_map/ppermute | solution.py:37
  189.5 13.5 %collective-permute-start.17 = (bf16[1,512,768]{2,1,0:T(8,128)(2,1)}, bf16[1,512,768]{2,1,0:T(8,128)(2,1)}, u32[]{:S(2)}, u32[]{:S(2)}) collective-permute-start(bf16[1,512,768]{2,1,0:T(8,128)(2,1)} %get-tuple-element.208), channel_id=1, source_target_pairs={{0,1},{1,0},{2,3},{3,2},{4,5},{5,4},{6,7},{7,6},{8,9},{9,8},{10,11... | collective-permute-start | bytes 2359304 | tf_op jit(solution)/shard_map/ppermute | solution.py:37
  191.9 19.1 %collective-permute-start.26 = (bf16[192,768]{1,0:T(8,128)(2,1)S(1)}, bf16[192,768]{1,0:T(8,128)(2,1)}, u32[]{:S(2)}, u32[]{:S(2)}) collective-permute-start(bf16[192,768]{1,0:T(8,128)(2,1)S(1)} %add_convert_fusion.7), channel_id=1, source_target_pairs={{0,8},{4,12},{8,0},{12,4},{16,24},{20,28},{24,16},{28,20},{1,9},{5... | collective-permute-start | bytes 884744 | tf_op jit(solution)/shard_map/ppermute | solution.py:37
  205.4 14.6 %collective-permute-start.30 = (bf16[192,768]{1,0:T(8,128)(2,1)S(1)}, bf16[192,768]{1,0:T(8,128)(2,1)}, u32[]{:S(2)}, u32[]{:S(2)}) collective-permute-start(bf16[192,768]{1,0:T(8,128)(2,1)S(1)} %add_convert_fusion.5), channel_id=1, source_target_pairs={{0,4},{4,0},{8,12},{12,8},{16,20},{20,16},{24,28},{28,24},{1,5},{5... | collective-permute-start | bytes 884744 | tf_op jit(solution)/shard_map/ppermute | solution.py:37
  205.5 31.2 %collective-permute-start.23 = (bf16[1,512,768]{2,1,0:T(8,128)(2,1)}, bf16[1,512,768]{2,1,0:T(8,128)(2,1)}, u32[]{:S(2)}, u32[]{:S(2)}) collective-permute-start(bf16[1,512,768]{2,1,0:T(8,128)(2,1)} %add_convert_fusion), channel_id=1, source_target_pairs={{0,2},{1,3},{2,0},{3,1},{4,6},{5,7},{6,4},{7,5},{8,10},{9,11},{10,... | collective-permute-start | bytes 2359304 | tf_op jit(solution)/shard_map/ppermute | solution.py:37
  212.0 25.6 %collective-permute-start.27 = (bf16[192,768]{1,0:T(8,128)(2,1)S(1)}, bf16[192,768]{1,0:T(8,128)(2,1)S(1)}, u32[]{:S(2)}, u32[]{:S(2)}) collective-permute-start(bf16[192,768]{1,0:T(8,128)(2,1)S(1)} %add_convert_fusion.4), channel_id=1, source_target_pairs={{0,16},{4,20},{8,24},{12,28},{16,0},{20,4},{24,8},{28,12},{1,17},{... | collective-permute-start | bytes 884744 | tf_op jit(solution)/shard_map/ppermute | solution.py:37
  215.7 25.8 %collective-permute-start.19 = (bf16[1,512,768]{2,1,0:T(8,128)(2,1)}, bf16[1,512,768]{2,1,0:T(8,128)(2,1)S(1)}, u32[]{:S(2)}, u32[]{:S(2)}) collective-permute-start(bf16[1,512,768]{2,1,0:T(8,128)(2,1)} %get-tuple-element.213), channel_id=1, source_target_pairs={{0,1},{1,0},{2,3},{3,2},{4,5},{5,4},{6,7},{7,6},{8,9},{9,8},{10,11... | collective-permute-start | bytes 2359304 | tf_op jit(solution)/shard_map/ppermute | solution.py:37
  218.1 16.2 %collective-permute-start.22 = (bf16[112,768]{1,0:T(8,128)(2,1)}, bf16[112,768]{1,0:T(8,128)(2,1)S(1)}, u32[]{:S(2)}, u32[]{:S(2)}) collective-permute-start(bf16[112,768]{1,0:T(8,128)(2,1)} %add_parts.4.a_ref), channel_id=1, source_target_pairs={{0,16},{4,20},{8,24},{12,28},{16,0},{20,4},{24,8},{28,12},{1,17},{... | collective-permute-start | bytes 516104 | tf_op jit(solution)/shard_map/ppermute | solution.py:37
  221.1 18.4 %collective-permute-start.31 = (bf16[192,768]{1,0:T(8,128)(2,1)S(1)}, bf16[192,768]{1,0:T(8,128)(2,1)S(1)}, u32[]{:S(2)}, u32[]{:S(2)}) collective-permute-start(bf16[192,768]{1,0:T(8,128)(2,1)S(1)} %add_convert_fusion.2), channel_id=1, source_target_pairs={{0,8},{4,12},{8,0},{12,4},{16,24},{20,28},{24,16},{28,20},{1,9},{5... | collective-permute-start | bytes 884744 | tf_op jit(solution)/shard_map/ppermute | solution.py:37
  (45 other events, 265.5 us)

commit v6 on v5

--- a/solution.py
+++ b/solution.py
@@ -100,6 +100,7 @@
         out_shape=(jax.ShapeDtypeStruct((slots, width), bf16),)
         + (jax.ShapeDtypeStruct((cols, slots), bf16),) * 3,
         name="project",
+        compiler_params=pltpu.CompilerParams(vmem_limit_bytes=12 * 2**20),
         cost_estimate=COST,
     )(rank, tokens, gain, bias, qw, kw, vw)
 
@@ -249,7 +250,7 @@
             pltpu.VMEM((heads, slots, size), f32),
         ],
         name="attend",
-        compiler_params=pltpu.CompilerParams(vmem_limit_bytes=60 * 2**20),
+        compiler_params=pltpu.CompilerParams(vmem_limit_bytes=26 * 2**20),
         cost_estimate=COST,
     )(lens, rank, qt, kt, vt)
 
@@ -274,6 +275,7 @@
         in_specs=[VMEM, VMEM],
         out_specs=VMEM,
         name="add_parts",
+        compiler_params=pltpu.CompilerParams(vmem_limit_bytes=4 * 2**20),
         cost_estimate=COST,
     )(a, b)
 
@@ -429,7 +431,7 @@
             pltpu.SemaphoreType.DMA,
         ],
         name="attend_back",
-        compiler_params=pltpu.CompilerParams(vmem_limit_bytes=60 * 2**20),
+        compiler_params=pltpu.CompilerParams(vmem_limit_bytes=28 * 2**20),
         cost_estimate=COST,
     )(lens, rank, bit, qt, kt, vt, *logs, *weights, normed, *extras, *outs, *grads)
 
@@ -474,6 +476,7 @@
         in_specs=[SMEM, SMEM, VMEM, VMEM, VMEM],
         out_specs=(VMEM, VMEM),
         name="plan",
+        compiler_params=pltpu.CompilerParams(vmem_limit_bytes=6 * 2**20),
         cost_estimate=COST,
     )(lens, rank, routes.reshape(1, -1), order, grads)
 
@@ -519,6 +522,7 @@
             jax.ShapeDtypeStruct((count, width), bf16),
         ),
         name="middle",
+        compiler_params=pltpu.CompilerParams(vmem_limit_bytes=10 * 2**20),
         cost_estimate=COST,
     )(rank, tokens, *small)
 
@@ -571,6 +575,7 @@
         in_specs=[SMEM, SMEM] + [VMEM] * (5 + 2 * count),
         out_specs=(VMEM,) * (4 + count),
         name="turn",
+        compiler_params=pltpu.CompilerParams(vmem_limit_bytes=16 * 2**20),
         cost_estimate=COST,
     )(lens, rank, dispatch, back, residual, cotangent, gain, *heads, *weights)
 
@@ -596,6 +601,7 @@
         in_specs=[VMEM] * 3,
         out_specs=(VMEM, VMEM),
         name="output_sums",
+        compiler_params=pltpu.CompilerParams(vmem_limit_bytes=6 * 2**20),
         cost_estimate=LONG,
     )(kept, core, first)
 
@@ -650,7 +656,7 @@
 def expert(rank, rows, grad_act, up, parts):
     count, width = rows.shape
     hidden = up.shape[1]
-    size = min(256, hidden // parts)
+    size = min(768, hidden // parts)
     cuts = hidden // parts // size
     steps = parts * cuts
     column = lambda i, r: (0, part_at(i // cuts, parts, r[0]) * cuts + i % cuts)
@@ -673,6 +679,7 @@
         out_shape=(jax.ShapeDtypeStruct((count, hidden // 2), bf16),) * 4
         + (jax.ShapeDtypeStruct((count, width), bf16),),
         name="expert",
+        compiler_params=pltpu.CompilerParams(vmem_limit_bytes=40 * 2**20),
         cost_estimate=COST,
     )(rank, rows, grad_act, up)
 
@@ -715,6 +722,7 @@
         ),
         out_shape=jax.ShapeDtypeStruct((count, width), bf16),
         name="product",
+        compiler_params=pltpu.CompilerParams(vmem_limit_bytes=14 * 2**20),
         cost_estimate=COST,
     )(rank, kept, sent, down)
 
@@ -757,7 +765,7 @@
             for k, shape in enumerate(shapes)
         ),
         name="expert_weights",
-        compiler_params=pltpu.CompilerParams(vmem_limit_bytes=60 * 2**20),
+        compiler_params=pltpu.CompilerParams(vmem_limit_bytes=28 * 2**20),
         cost_estimate=COST,
     )(*[values for group in groups for values in group])
 
@@ -798,6 +806,7 @@
         ],
         out_specs=(upper, lower),
         name="expert_sums",
+        compiler_params=pltpu.CompilerParams(vmem_limit_bytes=10 * 2**20),
         cost_estimate=COST,
     )(near_up, near_down, first, rest)
 
@@ -852,6 +861,7 @@
         out_specs=(pl.BlockSpec((1, size, width), lambda i: (i // 2, 0, 0)),) * 2,
         scratch_shapes=[pltpu.VMEM((3 * cols, width), bf16)],
         name="input_grad",
+        compiler_params=pltpu.CompilerParams(vmem_limit_bytes=12 * 2**20),
         cost_estimate=COST,
     )(*weights, *joints)
 
@@ -892,6 +902,7 @@
         ),
         out_shape=jax.ShapeDtypeStruct((shard, width), f32),
         name="close",
+        compiler_params=pltpu.CompilerParams(vmem_limit_bytes=12 * 2**20),
         cost_estimate=COST,
     )(rank, tokens, gain, grad, *parts)
 
@@ -930,6 +941,7 @@
             pltpu.VMEM((3 * heads * HEAD_DIM, width), f32) for first_head, heads in groups
         ],
         name="finish",
+        compiler_params=pltpu.CompilerParams(vmem_limit_bytes=8 * 2**20),
         cost_estimate=COST,
     )(bit, *pieces)
 

time: 255 us -> 285 us (1.12)
  local copies, waits for them, and re-layouts: 8.27 us -> 74.2 us
  Pallas kernels: 136 us -> 110 us
  starting transfers between devices: 61.5 us -> 47.1 us
  waiting for transfers between devices: 31.8 us -> 37.8 us
  other arithmetic: 7.09 us -> 3.16 us
    unnamed x66 -> x192, local copies, waits for them, and re-layouts: 7.65 us -> 73.6 us
    ppermute x32, starting transfers between devices: 36 us -> 24 us  [swap(): return lax.ppermute(values, axis, [(i, i ^ step) for i in range(count)])]
    pallas_call x1, Pallas kernels: 21 us -> 13.4 us  [expert(): pl.pallas_call(expert_kernel, grid_spec=pltpu.PrefetchScalarGridSpec(num_...]
    ppermute x32, waiting for transfers between devices: 17.9 us -> 24.9 us  [swap(): return lax.ppermute(values, axis, [(i, i ^ step) for i in range(count)])]
    pallas_call x2, Pallas kernels: 27.1 us -> 34.1 us  [attend_back(): pl.pallas_call(functools.partial(backward_kernel, first_head, heads, bloc...]
    pallas_call x2, Pallas kernels: 8.75 us -> 3.55 us  [input_grad(): pl.pallas_call(functools.partial(input_grad_kernel, groups), grid=(count,...]
    pallas_call x3, Pallas kernels: 5.32 us -> 0.15 us  [add_parts(): pl.pallas_call(add_kernel, out_shape=jax.ShapeDtypeStruct(a.shape, bf16),...]
    pallas_call x1, Pallas kernels: 11.9 us -> 8.09 us  [expert_weights(): pl.pallas_call(functools.partial(weight_kernel, len(groups)), grid=(2,),...]
  transfers between devices with their start and end apart: 36 -> 36, of which waited for: 9 -> 7; matrix products, arithmetic and copies ran while one was open for 6% -> 5% of each run, Pallas kernels for 49% -> 35%
where the time goes in v6:
time: 285 us; the launch traced here: 284 us
  Pallas kernels  110 us (39%)
  local copies, waits for them, and re-layouts  74.2 us (26%)
  starting transfers between devices  47.1 us (17%)
  waiting for transfers between devices  37.8 us (13%)
  matrix products  10.8 us (4%)
  other arithmetic  3.16 us (1%)
    unnamed x192, local copies, waits for them, and re-layouts  73.6 us
    pallas_call x2, Pallas kernels, attend_back(): pl.pallas_call(functools.partial(backward_kernel, first_head, heads, bloc...  34.1 us
    ppermute x32, waiting for transfers between devices, swap(): return lax.ppermute(values, axis, [(i, i ^ step) for i in range(count)])  24.9 us
    ppermute x32, starting transfers between devices, swap(): return lax.ppermute(values, axis, [(i, i ^ step) for i in range(count)])  24 us
    all_to_all x4, starting transfers between devices, exchange(): lax.all_to_all(rows.reshape(sources, -1, width), 'dp', split_axis=0, conc...  23.2 us
    pallas_call x2, Pallas kernels, attend(): pl.pallas_call(functools.partial(forward_kernel, first, blocks), out_shap...  18.4 us
    pallas_call x1, Pallas kernels, expert(): pl.pallas_call(expert_kernel, grid_spec=pltpu.PrefetchScalarGridSpec(num_...  13.4 us
    all_to_all x4, waiting for transfers between devices, exchange(): lax.all_to_all(rows.reshape(sources, -1, width), 'dp', split_axis=0, conc...  12.9 us
  transfers between devices with their start and end apart: 36, of which 7 were waited for; matrix products, arithmetic and copies ran while one was open for 5% of the time, Pallas kernels for 35%

profile of v6, /device:TPU:0, one launch (start us, length us, event | category | flops | bytes accessed | tf_op | source)
XLA Modules:
  0.0 284.1 jit_solution(6703452863785013824)
XLA Ops:
  3.9 2.6 plan.1
  6.5 7.3 %all-to-all-start.1 = ((bf16[8,64,768]{2,1,0:T(8,128)(2,1)}), bf16[8,64,768]{2,1,0:T(8,128)(2,1)}, u32[]{:S(2)}, u32[]{:S(2)}) async-start(bf16[8,64,768]{2,1,0:T(8,128)(2,1)} %bitcast.9), calls=%async_computation.1 | async-start | bytes 1572864 | tf_op jit(solution)/shard_map/all_to_all | solution.py:980
  17.9 5.4 %project.1 = (bf16[2048,768]{1,0:T(8,128)(2,1)S(1)}, bf16[192,2048]{1,0:T(8,128)(2,1)S(1)}, bf16[192,2048]{1,0:T(8,128)(2,1)S(1)}, bf16[192,2048]{1,0:T(8,128)(2,1)S(1)}) custom-call(s32[1]{0:T(128)} %bitcast.rank_ref, bf16[2048,768]{1,0:T(8,128)(2,1)S(1)} %copy-done, f32[768]{0:T(1024)S(1)} %copy-done.81, f32[768]{0:T(1024)S(1)} %copy-done.84, ...), custom_call_target="tpu_custom_call" | custom-call | flops 1048576 | bytes 1048576 | tf_op jit(solution)/shard_map/project/pallas_call | solution.py:80
  25.0 9.2 %attend.2 = (bf16[192,512]{1,0:T(8,128)(2,1)S(1)}, bf16[192,512]{1,0:T(8,128)(2,1)S(1)}, f32[3,1,1024]{2,1,0:T(1,128)S(1)}) custom-call(s32[1,5]{1,0:T(1,128)S(1)} %copy-done.83, s32[1,1]{1,0:T(1,128)} %bitcast.1.rank_ref, bf16[192,2048]{1,0:T(8,128)(2,1)S(1)} %get-tuple-element.125.qt_ref, bf16[192,2048]{1,0:T(8,128)(2,1)S(1)} %get-tuple-element.130.kt_ref, ...), custom_call_target="tpu_custom_call" | custom-call | flops 1048576 | bytes 1048576 | tf_op jit(solution)/shard_map/attend/pallas_call | solution.py:239
  35.8 9.2 %attend.3 = (bf16[192,512]{1,0:T(8,128)(2,1)S(1)}, bf16[192,512]{1,0:T(8,128)(2,1)S(1)}, f32[3,1,1024]{2,1,0:T(1,128)S(1)}) custom-call(s32[1,5]{1,0:T(1,128)S(1)} %copy-done.83, s32[1,1]{1,0:T(1,128)} %bitcast.1.rank_ref, bf16[192,2048]{1,0:T(8,128)(2,1)S(1)} %get-tuple-element.125.qt_ref, bf16[192,2048]{1,0:T(8,128)(2,1)S(1)} %get-tuple-element.130.kt_ref, ...), custom_call_target="tpu_custom_call" | custom-call | flops 1048576 | bytes 1048576 | tf_op jit(solution)/shard_map/attend/pallas_call | solution.py:239
  47.0 3.0 %middle.1 = (f32[512,768]{1,0:T(8,128)S(1)}, bf16[512,768]{1,0:T(8,128)(2,1)S(1)}) custom-call(s32[1]{0:T(128)} %bitcast.rank_ref, bf16[2048,768]{1,0:T(8,128)(2,1)S(1)} %copy-done.1, f32[768]{0:T(1024)S(1)} %copy-done.85, f32[768]{0:T(1024)S(1)} %copy-done.86, bf16[512,512]{1,0:T(8,128)(2,1)S(1)} %copy-done.32, ...), custom_call_target="tpu_custom_call" | custom-call | flops 1048576 | bytes 1048576 | tf_op jit(solution)/shard_map/middle/pallas_call | solution.py:508
  56.9 6.0 %all-to-all-start = ((bf16[8,64,768]{2,1,0:T(8,128)(2,1)}), bf16[8,64,768]{2,1,0:T(8,128)(2,1)}, u32[]{:S(2)}, u32[]{:S(2)}) async-start(bf16[8,64,768]{2,1,0:T(8,128)(2,1)} %bitcast.46), calls=%async_computation | async-start | bytes 1572864 | tf_op jit(solution)/shard_map/all_to_all | solution.py:980
  63.0 7.8 %fusion.1.grad_act_ref = f32[512,3072]{1,0:T(8,128)} fusion(bf16[512,768]{1,0:T(8,128)(2,1)} %bitcast.10.refs_1_, bf16[1,3072,768]{2,1,0:T(8,128)(2,1)} %param.25), kind=kOutput, calls=%fused_computation.17 | convolution fusion | flops 2415919104 | bytes 11796480 | tf_op jit(solution)/shard_map/dot_general | solution.py:485
  70.8 12.9 %all-to-all-done = bf16[8,64,768]{2,1,0:T(8,128)(2,1)} async-done(((bf16[8,64,768]{2,1,0:T(8,128)(2,1)}), bf16[8,64,768]{2,1,0:T(8,128)(2,1)}, u32[]{:S(2)}, u32[]{:S(2)}) %all-to-all-start) | async-done | bytes 786464 | tf_op jit(solution)/shard_map/all_to_all | solution.py:980
  86.1 13.4 %expert.1 = (bf16[512,1536]{1,0:T(8,128)(2,1)S(1)}, bf16[512,1536]{1,0:T(8,128)(2,1)S(1)}, bf16[512,1536]{1,0:T(8,128)(2,1)}, bf16[512,1536]{1,0:T(8,128)(2,1)}, bf16[512,768]{1,0:T(8,128)(2,1)S(1)}) custom-call(s32[1]{0:T(128)} %bitcast.rank_ref, bf16[512,768]{1,0:T(8,128)(2,1)} %bitcast.8.in_ref.refs_0_, f32[512,3072]{1,0:T(8,128)} %fusion.1.grad_act_ref, ...), custom_call_target="tpu_custom_call" | custom-call | flops 1048576 | bytes 1048576 | tf_op jit(solution)/shard_map/expert/pallas_call | solution.py:666
  104.2 4.2 %all-to-all-start.2 = ((bf16[8,64,768]{2,1,0:T(8,128)(2,1)}), bf16[8,64,768]{2,1,0:T(8,128)(2,1)}, u32[]{:S(2)}, u32[]{:S(2)}) async-start(bf16[8,64,768]{2,1,0:T(8,128)(2,1)} %bitcast.45), calls=%async_computation.2 | async-start | bytes 1572864 | tf_op jit(solution)/shard_map/all_to_all | solution.py:980
  112.2 5.4 %product.1 = bf16[512,768]{1,0:T(8,128)(2,1)S(1)} custom-call(s32[1]{0:T(128)} %bitcast.rank_ref, bf16[512,1536]{1,0:T(8,128)(2,1)S(1)} %copy-done.27, bf16[512,1536]{1,0:T(8,128)(2,1)} %get-tuple-element.158.sent_ref, bf16[3072,768]{1,0:T(8,128)(2,1)S(1)} %bitcast.43), custom_call_target="tpu_custom_call" | custom-call | flops 1048576 | bytes 1048576 | tf_op jit(solution)/shard_map/product/pallas_call | solution.py:710
  118.5 8.1 %expert_weights.1 = (bf16[384,768]{1,0:T(8,128)(2,1)S(1)}, bf16[1152,768]{1,0:T(8,128)(2,1)S(1)}, f32[768,768]{1,0:T(8,128)S(1)}, f32[768,768]{1,0:T(8,128)S(1)}) custom-call(bf16[512,768]{1,0:T(8,128)(2,1)} %bitcast.8.in_ref.refs_0_, bf16[512,768]{1,0:T(8,128)(2,1)} %bitcast.10.refs_1_, bf16[512,1536]{1,0:T(8,128)(2,1)S(1)} %copy-done.28, ...), custom_call_target="tpu_custom_call" | custom-call | flops 1048576 | bytes 1048576 | tf_op jit(solution)/shard_map/expert_weights/pallas_call | solution.py:758
  141.6 5.0 %turn.1 = (f32[512,768]{1,0:T(8,128)S(1)}, f32[2,768]{1,0:T(2,128)S(1)}, bf16[2,192,768]{2,1,0:T(8,128)(2,1)S(1)}, bf16[2,192,768]{2,1,0:T(8,128)(2,1)}, bf16[19...) custom-call(s32[1,5]{1,0:T(1,128)S(1)} %copy-done.83, ...), custom_call_target="tpu_custom_call" | custom-call | flops 1048576 | bytes 1048576 | tf_op jit(solution)/shard_map/turn/pallas_call | solution.py:566
  151.6 5.6 %all-to-all-start.3 = ((bf16[8,64,768]{2,1,0:T(8,128)(2,1)}), bf16[8,64,768]{2,1,0:T(8,128)(2,1)}, u32[]{:S(2)}, u32[]{:S(2)}) async-start(bf16[8,64,768]{2,1,0:T(8,128)(2,1)} %bitcast.44), calls=%async_computation.3 | async-start | bytes 1572864 | tf_op jit(solution)/shard_map/all_to_all | solution.py:980
  175.6 20.6 %attend_back.2 = (bf16[2048,384]{1,0:T(8,128)(2,1)S(1)}, f32[2,768]{1,0:T(2,128)S(1)}, bf16[192,768]{1,0:T(8,128)(2,1)S(1)}, bf16[192,768]{1,0:T(8,128)(2,1)S(1)}) custom-call(s32[1,5]{1,0:T(1,128)S(1)} %copy-done.83, s32[1,1]{1,0:T(1,128)} %bitcast.1.rank_ref, s32[1,1]{1,0:T(1,128)} %bitcast.6.bit_ref, bf16[192,2048]{1,0:T(8,128)(2,1)S(1)} %copy-done.6, ...), custom_call_target="tpu_custom_call" | custom-call | flops 1048576 | bytes 1048576 | tf_op jit(solution)/shard_map/attend_back/pallas_call | solution.py:408
  199.9 5.2 %collective-permute-start.15 = (bf16[192,768]{1,0:T(8,128)(2,1)}, bf16[192,768]{1,0:T(8,128)(2,1)S(1)}, u32[]{:S(2)}, u32[]{:S(2)}) collective-permute-start(bf16[192,768]{1,0:T(8,128)(2,1)} %copy-done.94), channel_id=1, source_target_pairs={{0,4},{4,0},{8,12},{12,8},{16,20},{20,16},{24,28},{28,24},{1,5},{5... | collective-permute-start | bytes 884744 | tf_op jit(solution)/shard_map/ppermute | solution.py:37
  217.5 13.5 %attend_back.3 = (bf16[2048,192]{1,0:T(8,128)(2,1)S(1)}, f32[2,768]{1,0:T(2,128)}, bf16[112,768]{1,0:T(8,128)(2,1)S(1)}, bf16[112,768]{1,0:T(8,128)(2,1)S(1)}) custom-call(s32[1,5]{1,0:T(1,128)S(1)} %copy-done.83, s32[1,1]{1,0:T(1,128)} %bitcast.1.rank_ref, s32[1,1]{1,0:T(1,128)} %bitcast.6.bit_ref, bf16[192,2048]{1,0:T(8,128)(2,1)S(1)} %copy-done.7, ...), custom_call_target="tpu_custom_call" | custom-call | flops 1048576 | bytes 1048576 | tf_op jit(solution)/shard_map/attend_back/pallas_call | solution.py:408
  236.5 4.6 %collective-permute-done.18.b_ref = bf16[112,768]{1,0:T(8,128)(2,1)S(1)} collective-permute-done((bf16[112,768]{1,0:T(8,128)(2,1)S(1)}, bf16[112,768]{1,0:T(8,128)(2,1)S(1)}, u32[]{:S(2)}, u32[]{:S(2)}) %collective-permute-start.18) | collective-permute-done | bytes 172064 | tf_op jit(solution)/shard_map/ppermute | solution.py:37
  243.2 3.0 %convolution_add_fusion = f32[512,768]{1,0:T(8,128)} fusion(f32[512,768]{1,0:T(8,128)S(1)} %copy-done.25, bf16[512,512]{1,0:T(8,128)(2,1)S(1)} %copy-done.34, bf16[512,768]{1,0:T(8,128)(2,1)} %bitcast.16), kind=kOutput, calls=%fused_computation.1 | convolution fusion | flops 403046400 | bytes 4456448 | tf_op jit(solution)/shard_map/dot_general | solution.py:30
  247.4 6.6 %collective-permute-done.20.b_ref = bf16[112,768]{1,0:T(8,128)(2,1)S(1)} collective-permute-done((bf16[112,768]{1,0:T(8,128)(2,1)S(1)}, bf16[112,768]{1,0:T(8,128)(2,1)S(1)}, u32[]{:S(2)}, u32[]{:S(2)}) %collective-permute-start.20) | collective-permute-done | bytes 172064 | tf_op jit(solution)/shard_map/ppermute | solution.py:37
  256.2 4.9 %expert_sums.1 = (f32[768,768]{1,0:T(8,128)}, f32[768,768]{1,0:T(8,128)}) custom-call(f32[768,768]{1,0:T(8,128)S(1)} %copy-done.43, f32[768,768]{1,0:T(8,128)S(1)} %copy-done.45, bf16[576,768]{1,0:T(8,128)(2,1)} %collective-permute-done.14.first_ref, bf16[1152,768]{1,0:T(8,128)(2,1)S(1)} %collective-permute-done.21.rest_ref), custom_call_target="tpu_custom_call" | custom-call | flops 1048576 | bytes 1048576 | tf_op jit(solution)/shard_map/expert_sums/pallas_call | solution.py:797
  261.1 8.2 %collective-permute-done.22.b_ref = bf16[112,768]{1,0:T(8,128)(2,1)S(1)} collective-permute-done((bf16[112,768]{1,0:T(8,128)(2,1)S(1)}, bf16[112,768]{1,0:T(8,128)(2,1)S(1)}, u32[]{:S(2)}, u32[]{:S(2)}) %collective-permute-start.22) | collective-permute-done | bytes 172064 | tf_op jit(solution)/shard_map/ppermute | solution.py:37
  279.5 3.3 %collective-permute-done.29.refs_3_ = bf16[112,768]{1,0:T(8,128)(2,1)S(1)} collective-permute-done((bf16[112,768]{1,0:T(8,128)(2,1)S(1)}, bf16[112,768]{1,0:T(8,128)(2,1)S(1)}, u32[]{:S(2)}, u32[]{:S(2)}) %collective-permute-start.29) | collective-permute-done | bytes 172064 | tf_op jit(solution)/shard_map/ppermute | solution.py:37
  (276 shorter events, 107.8 us)
Async XLA Ops:
  6.5 50.4 %all-to-all-start.1 = ((bf16[8,64,768]{2,1,0:T(8,128)(2,1)}), bf16[8,64,768]{2,1,0:T(8,128)(2,1)}, u32[]{:S(2)}, u32[]{:S(2)}) async-start(bf16[8,64,768]{2,1,0:T(8,128)(2,1)} %bitcast.9), calls=%async_computation.1 | async-start | bytes 1572864 | tf_op jit(solution)/shard_map/all_to_all | solution.py:980
  13.8 31.3 %collective-permute-start.3 = (bf16[192,768]{1,0:T(8,128)(2,1)}, bf16[192,768]{1,0:T(8,128)(2,1)S(1)}, u32[]{:S(2)}, u32[]{:S(2)}) collective-permute-start(bf16[192,768]{1,0:T(8,128)(2,1)} %refs_4_.1), channel_id=1, source_target_pairs={{0,2},{1,3},{2,0},{3,1},{4,6},{5,7},{6,4},{7,5},{8,10},{9,11},{10,... | collective-permute-start | bytes 884744 | tf_op jit(solution)/shard_map/ppermute | solution.py:37
  15.3 29.8 %collective-permute-start.2 = (bf16[192,768]{1,0:T(8,128)(2,1)}, bf16[192,768]{1,0:T(8,128)(2,1)S(1)}, u32[]{:S(2)}, u32[]{:S(2)}) collective-permute-start(bf16[192,768]{1,0:T(8,128)(2,1)} %refs_4_.1), channel_id=1, source_target_pairs={{0,1},{1,0},{2,3},{3,2},{4,5},{5,4},{6,7},{7,6},{8,9},{9,8},{10,11... | collective-permute-start | bytes 884744 | tf_op jit(solution)/shard_map/ppermute | solution.py:37
  15.3 29.8 %collective-permute-start.4 = (bf16[192,768]{1,0:T(8,128)(2,1)}, bf16[192,768]{1,0:T(8,128)(2,1)S(1)}, u32[]{:S(2)}, u32[]{:S(2)}) collective-permute-start(bf16[192,768]{1,0:T(8,128)(2,1)} %refs_4_.1), channel_id=1, source_target_pairs={{0,3},{1,2},{2,1},{3,0},{4,7},{5,6},{6,5},{7,4},{8,11},{9,10},{10,... | collective-permute-start | bytes 884744 | tf_op jit(solution)/shard_map/ppermute | solution.py:37
  56.9 26.8 %all-to-all-start = ((bf16[8,64,768]{2,1,0:T(8,128)(2,1)}), bf16[8,64,768]{2,1,0:T(8,128)(2,1)}, u32[]{:S(2)}, u32[]{:S(2)}) async-start(bf16[8,64,768]{2,1,0:T(8,128)(2,1)} %bitcast.46), calls=%async_computation | async-start | bytes 1572864 | tf_op jit(solution)/shard_map/all_to_all | solution.py:980
  62.9 20.8 %collective-permute-start.6 = (bf16[512,768]{1,0:T(8,128)(2,1)}, bf16[512,768]{1,0:T(8,128)(2,1)}, u32[]{:S(2)}, u32[]{:S(2)}) collective-permute-start(bf16[512,768]{1,0:T(8,128)(2,1)} %bitcast.10.refs_1_), channel_id=1, source_target_pairs={{0,1},{1,0},{2,3},{3,2},{4,5},{5,4},{6,7},{7,6},{8,9},{9,8},{10,11... | collective-permute-start | bytes 2359304 | tf_op jit(solution)/shard_map/ppermute | solution.py:37
  83.7 19.0 %collective-permute-start.7 = (bf16[512,768]{1,0:T(8,128)(2,1)}, bf16[512,768]{1,0:T(8,128)(2,1)S(1)}, u32[]{:S(2)}, u32[]{:S(2)}) collective-permute-start(bf16[512,768]{1,0:T(8,128)(2,1)} %bitcast.8.in_ref.refs_0_), channel_id=1, source_target_pairs={{0,1},{1,0},{2,3},{3,2},{4,5},{5,4},{6,7},{7,6},{8,9},{9,8},{10,11... | collective-permute-start | bytes 2359304 | tf_op jit(solution)/shard_map/ppermute | solution.py:37
  103.6 14.8 %collective-permute-start.9 = (bf16[512,1536]{1,0:T(8,128)(2,1)}, bf16[512,1536]{1,0:T(8,128)(2,1)}, u32[]{:S(2)}, u32[]{:S(2)}) collective-permute-start(bf16[512,1536]{1,0:T(8,128)(2,1)} %get-tuple-element.159), channel_id=1, source_target_pairs={{0,1},{1,0},{2,3},{3,2},{4,5},{5,4},{6,7},{7,6},{8,9},{9,8},{10,11... | collective-permute-start | bytes 4718600 | tf_op jit(solution)/shard_map/ppermute | solution.py:37
  104.2 14.3 %collective-permute-start.8 = (bf16[512,1536]{1,0:T(8,128)(2,1)}, bf16[512,1536]{1,0:T(8,128)(2,1)}, u32[]{:S(2)}, u32[]{:S(2)}) collective-permute-start(bf16[512,1536]{1,0:T(8,128)(2,1)} %get-tuple-element.158.sent_ref), channel_id=1, source_target_pairs={{0,1},{1,0},{2,3},{3,2},{4,5},{5,4},{6,7},{7,6},{8,9},{9,8},{10,11... | collective-permute-start | bytes 4718600 | tf_op jit(solution)/shard_map/ppermute | solution.py:37
  104.2 27.2 %all-to-all-start.2 = ((bf16[8,64,768]{2,1,0:T(8,128)(2,1)}), bf16[8,64,768]{2,1,0:T(8,128)(2,1)}, u32[]{:S(2)}, u32[]{:S(2)}) async-start(bf16[8,64,768]{2,1,0:T(8,128)(2,1)} %bitcast.45), calls=%async_computation.2 | async-start | bytes 1572864 | tf_op jit(solution)/shard_map/all_to_all | solution.py:980
  149.7 12.4 %collective-permute-start.10 = (bf16[192,512]{1,0:T(8,128)(2,1)}, bf16[192,512]{1,0:T(8,128)(2,1)}, u32[]{:S(2)}, u32[]{:S(2)}) collective-permute-start(bf16[192,512]{1,0:T(8,128)(2,1)} %get-tuple-element.170), channel_id=1, source_target_pairs={{0,1},{1,0},{2,3},{3,2},{4,5},{5,4},{6,7},{7,6},{8,9},{9,8},{10,11... | collective-permute-start | bytes 589832 | tf_op jit(solution)/shard_map/ppermute | solution.py:37
  149.7 12.4 %collective-permute-start.11 = (bf16[192,512]{1,0:T(8,128)(2,1)}, bf16[192,512]{1,0:T(8,128)(2,1)}, u32[]{:S(2)}, u32[]{:S(2)}) collective-permute-start(bf16[192,512]{1,0:T(8,128)(2,1)} %get-tuple-element.171), channel_id=1, source_target_pairs={{0,2},{1,3},{2,0},{3,1},{4,6},{5,7},{6,4},{7,5},{8,10},{9,11},{10,... | collective-permute-start | bytes 589832 | tf_op jit(solution)/shard_map/ppermute | solution.py:37
  151.6 47.1 %all-to-all-start.3 = ((bf16[8,64,768]{2,1,0:T(8,128)(2,1)}), bf16[8,64,768]{2,1,0:T(8,128)(2,1)}, u32[]{:S(2)}, u32[]{:S(2)}) async-start(bf16[8,64,768]{2,1,0:T(8,128)(2,1)} %bitcast.44), calls=%async_computation.3 | async-start | bytes 1572864 | tf_op jit(solution)/shard_map/all_to_all | solution.py:980
  162.2 36.6 %collective-permute-start.14 = (bf16[576,768]{1,0:T(8,128)(2,1)}, bf16[576,768]{1,0:T(8,128)(2,1)}, u32[]{:S(2)}, u32[]{:S(2)}) collective-permute-start(bf16[576,768]{1,0:T(8,128)(2,1)} %get-tuple-element.185), channel_id=1, source_target_pairs={{0,2},{1,3},{2,0},{3,1},{4,6},{5,7},{6,4},{7,5},{8,10},{9,11},{10,... | collective-permute-start | bytes 2654216 | tf_op jit(solution)/shard_map/ppermute | solution.py:37
  199.9 31.2 %collective-permute-start.16 = (bf16[192,768]{1,0:T(8,128)(2,1)S(1)}, bf16[192,768]{1,0:T(8,128)(2,1)S(1)}, u32[]{:S(2)}, u32[]{:S(2)}) collective-permute-start(bf16[192,768]{1,0:T(8,128)(2,1)S(1)} %add_convert_fusion.6), channel_id=1, source_target_pairs={{0,16},{4,20},{8,24},{12,28},{16,0},{20,4},{24,8},{28,12},{1,17},{... | collective-permute-start | bytes 884744 | tf_op jit(solution)/shard_map/ppermute | solution.py:37
  199.9 31.2 %collective-permute-start.15 = (bf16[192,768]{1,0:T(8,128)(2,1)}, bf16[192,768]{1,0:T(8,128)(2,1)S(1)}, u32[]{:S(2)}, u32[]{:S(2)}) collective-permute-start(bf16[192,768]{1,0:T(8,128)(2,1)} %copy-done.94), channel_id=1, source_target_pairs={{0,4},{4,0},{8,12},{12,8},{16,20},{20,16},{24,28},{28,24},{1,5},{5... | collective-permute-start | bytes 884744 | tf_op jit(solution)/shard_map/ppermute | solution.py:37
  205.1 49.0 %collective-permute-start.21 = (bf16[1152,768]{1,0:T(8,128)(2,1)}, bf16[1152,768]{1,0:T(8,128)(2,1)S(1)}, u32[]{:S(2)}, u32[]{:S(2)}) collective-permute-start(bf16[1152,768]{1,0:T(8,128)(2,1)} %copy-done.89), channel_id=1, source_target_pairs={{0,2},{1,3},{2,0},{3,1},{4,6},{5,7},{6,4},{7,5},{8,10},{9,11},{10,... | collective-permute-start | bytes 5308424 | tf_op jit(solution)/shard_map/ppermute | solution.py:37
  234.4 11.9 %collective-permute-start.26 = (bf16[192,768]{1,0:T(8,128)(2,1)S(1)}, bf16[192,768]{1,0:T(8,128)(2,1)S(1)}, u32[]{:S(2)}, u32[]{:S(2)}) collective-permute-start(bf16[192,768]{1,0:T(8,128)(2,1)S(1)} %add_convert_fusion.7), channel_id=1, source_target_pairs={{0,8},{4,12},{8,0},{12,4},{16,24},{20,28},{24,16},{28,20},{1,9},{5... | collective-permute-start | bytes 884744 | tf_op jit(solution)/shard_map/ppermute | solution.py:37
  241.4 12.8 %collective-permute-start.30 = (bf16[192,768]{1,0:T(8,128)(2,1)S(1)}, bf16[192,768]{1,0:T(8,128)(2,1)S(1)}, u32[]{:S(2)}, u32[]{:S(2)}) collective-permute-start(bf16[192,768]{1,0:T(8,128)(2,1)S(1)} %add_convert_fusion.5), channel_id=1, source_target_pairs={{0,4},{4,0},{8,12},{12,8},{16,20},{20,16},{24,28},{28,24},{1,5},{5... | collective-permute-start | bytes 884744 | tf_op jit(solution)/shard_map/ppermute | solution.py:37
  241.7 27.7 %collective-permute-start.23 = (bf16[1,512,768]{2,1,0:T(8,128)(2,1)S(1)}, bf16[1,512,768]{2,1,0:T(8,128)(2,1)S(1)}, u32[]{:S(2)}, u32[]{:S(2)}) collective-permute-start(bf16[1,512,768]{2,1,0:T(8,128)(2,1)S(1)} %add_convert_fusion), channel_id=1, source_target_pairs={{0,2},{1,3},{2,0},{3,1},{4,6},{5,7},{6,4},{7,5},{8,10},{9,11},{10,... | collective-permute-start | bytes 2359304 | tf_op jit(solution)/shard_map/ppermute | solution.py:37
  246.4 23.1 %collective-permute-start.27 = (bf16[192,768]{1,0:T(8,128)(2,1)S(1)}, bf16[192,768]{1,0:T(8,128)(2,1)S(1)}, u32[]{:S(2)}, u32[]{:S(2)}) collective-permute-start(bf16[192,768]{1,0:T(8,128)(2,1)S(1)} %add_convert_fusion.4), channel_id=1, source_target_pairs={{0,16},{4,20},{8,24},{12,28},{16,0},{20,4},{24,8},{28,12},{1,17},{... | collective-permute-start | bytes 884744 | tf_op jit(solution)/shard_map/ppermute | solution.py:37
  254.0 20.3 %collective-permute-start.19 = (bf16[1,512,768]{2,1,0:T(8,128)(2,1)S(1)}, bf16[1,512,768]{2,1,0:T(8,128)(2,1)S(1)}, u32[]{:S(2)}, u32[]{:S(2)}) collective-permute-start(bf16[1,512,768]{2,1,0:T(8,128)(2,1)S(1)} %get-tuple-element.213), channel_id=1, source_target_pairs={{0,1},{1,0},{2,3},{3,2},{4,5},{5,4},{6,7},{7,6},{8,9},{9,8},{10,11... | collective-permute-start | bytes 2359304 | tf_op jit(solution)/shard_map/ppermute | solution.py:37
  254.1 15.2 %collective-permute-start.22 = (bf16[112,768]{1,0:T(8,128)(2,1)S(1)}, bf16[112,768]{1,0:T(8,128)(2,1)S(1)}, u32[]{:S(2)}, u32[]{:S(2)}) collective-permute-start(bf16[112,768]{1,0:T(8,128)(2,1)S(1)} %add_parts.4.a_ref), channel_id=1, source_target_pairs={{0,16},{4,20},{8,24},{12,28},{16,0},{20,4},{24,8},{28,12},{1,17},{... | collective-permute-start | bytes 516104 | tf_op jit(solution)/shard_map/ppermute | solution.py:37
  254.3 17.6 %collective-permute-start.31 = (bf16[192,768]{1,0:T(8,128)(2,1)S(1)}, bf16[192,768]{1,0:T(8,128)(2,1)S(1)}, u32[]{:S(2)}, u32[]{:S(2)}) collective-permute-start(bf16[192,768]{1,0:T(8,128)(2,1)S(1)} %add_convert_fusion.2), channel_id=1, source_target_pairs={{0,8},{4,12},{8,0},{12,4},{16,24},{20,28},{24,16},{28,20},{1,9},{5... | collective-permute-start | bytes 884744 | tf_op jit(solution)/shard_map/ppermute | solution.py:37
  (108 other events, 494.5 us)

commit v7 on v5

--- a/solution.py
+++ b/solution.py
@@ -13,6 +13,7 @@
 f32 = jnp.float32
 bf16 = jnp.bfloat16
 VMEM = pl.BlockSpec(memory_space=pltpu.VMEM)
+HBM = pl.BlockSpec(memory_space=pltpu.MemorySpace.HBM)
 SMEM = pl.BlockSpec(memory_space=pltpu.SMEM)
 SUM_ROWS = 16
 COST = pl.CostEstimate(flops=2**20, bytes_accessed=2**20, transcendentals=0)
@@ -274,6 +275,7 @@
         in_specs=[VMEM, VMEM],
         out_specs=VMEM,
         name="add_parts",
+        compiler_params=pltpu.CompilerParams(vmem_limit_bytes=5 * 2**20),
         cost_estimate=COST,
     )(a, b)
 
@@ -612,88 +614,112 @@
 
 
 def expert_kernel(
-    rank_ref, in_ref, grad_act_ref, up_ref,
-    act_kept_ref, pre_kept_ref, act_sent_ref, pre_sent_ref, mid_ref, sum_ref,
+    parts, rank_ref, in_ref, grad_act_ref, up_ref,
+    act_kept_ref, pre_kept_ref, act_sent_ref, pre_sent_ref, mid_ref,
+    grads_ref, ups_ref, acts_ref, pres_ref, sum_ref, fetched, stored,
 ):
-    step = pl.program_id(0)
-    pre = jnp.dot(in_ref[...], up_ref[...], preferred_element_type=f32)
-    act, slope = gelu_parts(pre)
-    act = act.astype(bf16)
-    grad_pre = (grad_act_ref[...] * slope).astype(bf16)
-    half = pl.num_programs(0) // 2
-
-    @pl.when(step < half)
-    def keep():
-        act_kept_ref[...] = act
-        pre_kept_ref[...] = grad_pre
-
-    @pl.when(step >= half)
-    def send():
-        act_sent_ref[...] = act
-        pre_sent_ref[...] = grad_pre
-
-    mid = across(grad_pre, up_ref[...])
-
-    @pl.when(step == 0)
-    def first():
-        sum_ref[...] = mid
-
-    @pl.when(step > 0)
-    def later():
-        sum_ref[...] += mid
-
-    @pl.when(step == pl.num_programs(0) - 1)
-    def last():
-        mid_ref[...] = sum_ref[...].astype(bf16)
+    rank = rank_ref[0, 0]
+    size = ups_ref.shape[2]
+    half = parts // 2
+
+    def fetch(p):
+        cols = rows_at(part_at(p, parts, rank), size)
+        return (
+            pltpu.make_async_copy(up_ref.at[:, cols], ups_ref.at[p], fetched.at[0, p]),
+            pltpu.make_async_copy(grad_act_ref.at[:, cols], grads_ref.at[p], fetched.at[1, p]),
+        )
+
+    def store(p, act_out_ref, pre_out_ref):
+        cols = rows_at(p % half, size)
+        return (
+            pltpu.make_async_copy(acts_ref.at[p], act_out_ref.at[:, cols], stored.at[0, p]),
+            pltpu.make_async_copy(pres_ref.at[p], pre_out_ref.at[:, cols], stored.at[1, p]),
+        )
+
+    for p in range(parts):
+        for copy in fetch(p):
+            copy.start()
+    sum_ref[...] = jnp.zeros_like(sum_ref)
+
+    def part(p, unused):
+        for copy in fetch(p):
+            copy.wait()
+        pre = jnp.dot(in_ref[...], ups_ref[p], preferred_element_type=f32)
+        act, slope = gelu_parts(pre)
+        acts_ref[p] = act.astype(bf16)
+        grad_pre = (grads_ref[p].astype(f32) * slope).astype(bf16)
+        pres_ref[p] = grad_pre
+        sum_ref[...] += across(grad_pre, ups_ref[p])
+
+        @pl.when(p < half)
+        def keep():
+            for copy in store(p, act_kept_ref, pre_kept_ref):
+                copy.start()
+
+        @pl.when(p >= half)
+        def send():
+            for copy in store(p, act_sent_ref, pre_sent_ref):
+                copy.start()
+
+        return unused
+
+    lax.fori_loop(0, parts, part, 0)
+    mid_ref[...] = sum_ref[...].astype(bf16)
+    for p in range(parts):
+        outs = (act_kept_ref, pre_kept_ref) if p < half else (act_sent_ref, pre_sent_ref)
+        for copy in store(p, *outs):
+            copy.wait()
 
 
 def expert(rank, rows, grad_act, up, parts):
     count, width = rows.shape
     hidden = up.shape[1]
-    size = min(256, hidden // parts)
-    cuts = hidden // parts // size
-    steps = parts * cuts
-    column = lambda i, r: (0, part_at(i // cuts, parts, r[0]) * cuts + i % cuts)
-    kept = pl.BlockSpec((count, size), lambda i, r: (0, jnp.minimum(i, steps // 2 - 1)))
-    sent = pl.BlockSpec((count, size), lambda i, r: (0, jnp.maximum(i - steps // 2, 0)))
-    fixed = pl.BlockSpec((count, width), lambda i, r: (0, 0))
-    return pl.pallas_call(
-        expert_kernel,
-        grid_spec=pltpu.PrefetchScalarGridSpec(
-            num_scalar_prefetch=1,
-            grid=(steps,),
-            in_specs=[
-                fixed,
-                pl.BlockSpec((count, size), column),
-                pl.BlockSpec((width, size), column),
-            ],
-            out_specs=(kept, kept, sent, sent, fixed),
-            scratch_shapes=[pltpu.VMEM((count, width), f32)],
-        ),
+    size = hidden // parts
+    return pl.pallas_call(
+        functools.partial(expert_kernel, parts),
         out_shape=(jax.ShapeDtypeStruct((count, hidden // 2), bf16),) * 4
         + (jax.ShapeDtypeStruct((count, width), bf16),),
+        in_specs=[SMEM, VMEM, HBM, HBM],
+        out_specs=(HBM,) * 4 + (VMEM,),
+        scratch_shapes=[
+            pltpu.VMEM((parts, count, size), grad_act.dtype),
+            pltpu.VMEM((parts, width, size), bf16),
+            pltpu.VMEM((parts, count, size), bf16),
+            pltpu.VMEM((parts, count, size), bf16),
+            pltpu.VMEM((count, width), f32),
+            pltpu.SemaphoreType.DMA((2, parts)),
+            pltpu.SemaphoreType.DMA((2, parts)),
+        ],
         name="expert",
-        cost_estimate=COST,
-    )(rank, rows, grad_act, up)
-
-
-def product_kernel(rank_ref, kept_ref, sent_ref, down_ref, out_ref, sum_ref):
-    step = pl.program_id(0)
-    steps = pl.num_programs(0)
-    act = jnp.where(step < steps // 2, kept_ref[...], sent_ref[...])
-    made = jnp.dot(act, down_ref[...], preferred_element_type=f32)
-
-    @pl.when(step == 0)
-    def first():
-        sum_ref[...] = made
-
-    @pl.when(step > 0)
-    def later():
-        sum_ref[...] += made
-
-    @pl.when(step == steps - 1)
-    def last():
-        out_ref[...] = sum_ref[...].astype(bf16)
+        compiler_params=pltpu.CompilerParams(vmem_limit_bytes=60 * 2**20),
+        cost_estimate=COST,
+    )(rank.reshape(1, 1), rows, grad_act, up)
+
+
+def product_kernel(parts, rank_ref, kept_ref, sent_ref, down_ref, out_ref,
+                   acts_ref, downs_ref, sum_ref, fetched):
+    rank = rank_ref[0, 0]
+    size = downs_ref.shape[1]
+    half = parts // 2
+
+    def fetch(p):
+        rows = rows_at(part_at(p, parts, rank), size)
+        source = kept_ref if p < half else sent_ref
+        cols = slice((p % half) * size, (p % half + 1) * size)
+        return (
+            pltpu.make_async_copy(down_ref.at[rows, :], downs_ref.at[p], fetched.at[0, p]),
+            pltpu.make_async_copy(source.at[:, cols], acts_ref.at[p], fetched.at[1, p]),
+        )
+
+    for p in range(parts):
+        for copy in fetch(p):
+            copy.start()
+    sum_ref[...] = jnp.zeros_like(sum_ref)
+    for p in range(parts):
+        for copy in fetch(p):
+            copy.wait()
+        sum_ref[...] += jnp.dot(acts_ref[p], downs_ref[p], preferred_element_type=f32)
+    out_ref[...] = sum_ref[...].astype(bf16)
 
 
 def product(rank, kept, sent, down, parts):
@@ -701,22 +727,19 @@
     hidden, width = down.shape
     size = hidden // parts
     return pl.pallas_call(
-        product_kernel,
-        grid_spec=pltpu.PrefetchScalarGridSpec(
-            num_scalar_prefetch=1,
-            grid=(parts,),
-            in_specs=[
-                pl.BlockSpec((count, size), lambda i, r: (0, jnp.minimum(i, parts // 2 - 1))),
-                pl.BlockSpec((count, size), lambda i, r: (0, jnp.maximum(i - parts // 2, 0))),
-                pl.BlockSpec((size, width), lambda i, r: (part_at(i, parts, r[0]), 0)),
-            ],
-            out_specs=pl.BlockSpec((count, width), lambda i, r: (0, 0)),
-            scratch_shapes=[pltpu.VMEM((count, width), f32)],
-        ),
+        functools.partial(product_kernel, parts),
         out_shape=jax.ShapeDtypeStruct((count, width), bf16),
+        in_specs=[SMEM, HBM, HBM, HBM],
+        out_specs=VMEM,
+        scratch_shapes=[
+            pltpu.VMEM((parts, count, size), bf16),
+            pltpu.VMEM((parts, size, width), bf16),
+            pltpu.VMEM((count, width), f32),
+            pltpu.SemaphoreType.DMA((2, parts)),
+        ],
         name="product",
         cost_estimate=COST,
-    )(rank, kept, sent, down)
+    )(rank.reshape(1, 1), kept, sent, down)
 
 
 def weight_kernel(groups, *refs):
@@ -798,6 +821,7 @@
         ],
         out_specs=(upper, lower),
         name="expert_sums",
+        compiler_params=pltpu.CompilerParams(vmem_limit_bytes=10 * 2**20),
         cost_estimate=COST,
     )(near_up, near_down, first, rest)
 
@@ -852,6 +876,7 @@
         out_specs=(pl.BlockSpec((1, size, width), lambda i: (i // 2, 0, 0)),) * 2,
         scratch_shapes=[pltpu.VMEM((3 * cols, width), bf16)],
         name="input_grad",
+        compiler_params=pltpu.CompilerParams(vmem_limit_bytes=12 * 2**20),
         cost_estimate=COST,
     )(*weights, *joints)
 
@@ -892,6 +917,7 @@
         ),
         out_shape=jax.ShapeDtypeStruct((shard, width), f32),
         name="close",
+        compiler_params=pltpu.CompilerParams(vmem_limit_bytes=12 * 2**20),
         cost_estimate=COST,
     )(rank, tokens, gain, grad, *parts)
 
@@ -930,6 +956,7 @@
             pltpu.VMEM((3 * heads * HEAD_DIM, width), f32) for first_head, heads in groups
         ],
         name="finish",
+        compiler_params=pltpu.CompilerParams(vmem_limit_bytes=10 * 2**20),
         cost_estimate=COST,
     )(bit, *pieces)
 
@@ -1003,7 +1030,7 @@
     flat_in = exchange(outgoing)
 
     flat_grad, outgoing = tie(flat_grad, outgoing)
-    grad_act = across(flat_grad, down_matrix)
+    grad_act = across(flat_grad, down_matrix).astype(bf16)
     near_grads = swap(flat_grad, "tensor", 1)
     flat_in, grad_act, near_grads = tie(flat_in, grad_act, near_grads)
     near_rows = swap(flat_in, "tensor", 1)

time: 255 us -> 237 us (0.929)
  Pallas kernels: 136 us -> 115 us
  waiting for transfers between devices: 31.8 us -> 41.9 us
  starting transfers between devices: 61.5 us -> 57.2 us
    pallas_call x2, Pallas kernels: 28.1 us -> 18.2 us  [the longest x1 11.8 us: expert(): pl.pallas_call(functools.partial(expert_kernel, parts), out_shape=(jax.Sh...]
    ppermute x32, waiting for transfers between devices: 17.9 us -> 26.6 us  [swap(): return lax.ppermute(values, axis, [(i, i ^ step) for i in range(count)])]
    ppermute x32, starting transfers between devices: 36 us -> 30.6 us  [swap(): return lax.ppermute(values, axis, [(i, i ^ step) for i in range(count)])]
    pallas_call x2, Pallas kernels: 8.75 us -> 3.54 us  [input_grad(): pl.pallas_call(functools.partial(input_grad_kernel, groups), grid=(count,...]
    pallas_call x2, Pallas kernels: 27.1 us -> 32.3 us  [attend_back(): pl.pallas_call(functools.partial(backward_kernel, first_head, heads, bloc...]
    pallas_call x3, Pallas kernels: 5.32 us -> 0.15 us  [add_parts(): pl.pallas_call(add_kernel, out_shape=jax.ShapeDtypeStruct(a.shape, bf16),...]
    pallas_call x1, Pallas kernels: 7.68 us -> 4.01 us  [expert_sums(): pl.pallas_call(expert_sum_kernel, grid=(steps,), out_shape=(jax.ShapeDtyp...]
    unnamed x66 -> x72, local copies, waits for them, and re-layouts: 7.65 us -> 6.57 us
  transfers between devices with their start and end apart: 36 -> 36, of which waited for: 9 -> 14; matrix products, arithmetic and copies ran while one was open for 6% -> 5% of each run, Pallas kernels for 49% -> 44%
where the time goes in v7:
time: 237 us; the launch traced here: 236 us
  Pallas kernels  115 us (49%)
  starting transfers between devices  57.2 us (24%)
  waiting for transfers between devices  41.9 us (18%)
  matrix products  8.08 us (3%)
  local copies, waits for them, and re-layouts  7.19 us (3%)
  other arithmetic  5.03 us (2%)
    pallas_call x2, Pallas kernels, attend_back(): pl.pallas_call(functools.partial(backward_kernel, first_head, heads, bloc...  32.3 us
    ppermute x32, starting transfers between devices, swap(): return lax.ppermute(values, axis, [(i, i ^ step) for i in range(count)])  30.6 us
    ppermute x32, waiting for transfers between devices, swap(): return lax.ppermute(values, axis, [(i, i ^ step) for i in range(count)])  26.6 us
    all_to_all x4, starting transfers between devices, exchange(): lax.all_to_all(rows.reshape(sources, -1, width), 'dp', split_axis=0, conc...  26.6 us
    pallas_call x2, Pallas kernels, attend(): pl.pallas_call(functools.partial(forward_kernel, first, blocks), out_shap...  17 us
    all_to_all x4, waiting for transfers between devices, exchange(): lax.all_to_all(rows.reshape(sources, -1, width), 'dp', split_axis=0, conc...  15.3 us
    pallas_call x1, Pallas kernels, expert_weights(): pl.pallas_call(functools.partial(weight_kernel, len(groups)), grid=(2,),...  11.9 us
    pallas_call x1, Pallas kernels, expert(): pl.pallas_call(functools.partial(expert_kernel, parts), out_shape=(jax.Sh...  11.8 us
  transfers between devices with their start and end apart: 36, of which 14 were waited for; matrix products, arithmetic and copies ran while one was open for 5% of the time, Pallas kernels for 44%

profile of v7, /device:TPU:0, one launch (start us, length us, event | category | flops | bytes accessed | tf_op | source)
XLA Modules:
  0.0 235.7 jit_solution(5453693462244230008)
XLA Ops:
  0.7 3.3 %plan.1 = (bf16[512,512]{1,0:T(8,128)(2,1)}, bf16[512,768]{1,0:T(8,128)(2,1)}) custom-call(s32[1,5]{1,0:T(1,128)} %lens_ref.11, s32[1,1]{1,0:T(1,128)} %bitcast.1.rank_ref, s32[1,512]{1,0:T(1,128)} %bitcast.55, s32[1,512]{1,0:T(1,128)} %order_ref.1, bf16[512,768]{1,0:T(8,128)(2,1)} %cotangent_ref.1), custom_call_target="tpu_custom_call" | custom-call | flops 1048576 | bytes 1048576 | tf_op jit(solution)/shard_map/plan/pallas_call | solution.py:470
  3.9 7.3 %all-to-all-start.1 = ((bf16[8,64,768]{2,1,0:T(8,128)(2,1)}), bf16[8,64,768]{2,1,0:T(8,128)(2,1)S(1)}, u32[]{:S(2)}, u32[]{:S(2)}) async-start(bf16[8,64,768]{2,1,0:T(8,128)(2,1)} %bitcast.52), calls=%async_computation.1 | async-start | bytes 1572864 | tf_op jit(solution)/shard_map/all_to_all | solution.py:995
  13.4 7.5 %project.1 = (bf16[2048,768]{1,0:T(8,128)(2,1)}, bf16[192,2048]{1,0:T(8,128)(2,1)}, bf16[192,2048]{1,0:T(8,128)(2,1)}, bf16[192,2048]{1,0:T(8,128)(2,1)}) custom-call(s32[1]{0:T(128)} %bitcast.rank_ref, bf16[2048,768]{1,0:T(8,128)(2,1)} %tokens_ref.2, f32[768]{0:T(1024)} %gain_ref.7, f32[768]{0:T(1024)} %bias_ref.2, bf16[192,768]{1,0:T(8,128)(2,1)} %bitcast.27, ...), custom_call_target="tpu_custom_call" | custom-call | flops 1048576 | bytes 1048576 | tf_op jit(solution)/shard_map/project/pallas_call | solution.py:81
  20.9 8.5 %attend.2 = (bf16[192,512]{1,0:T(8,128)(2,1)}, bf16[192,512]{1,0:T(8,128)(2,1)}, f32[3,1,1024]{2,1,0:T(1,128)}) custom-call(s32[1,5]{1,0:T(1,128)} %lens_ref.11, s32[1,1]{1,0:T(1,128)} %bitcast.1.rank_ref, bf16[192,2048]{1,0:T(8,128)(2,1)} %get-tuple-element.125.qt_ref, bf16[192,2048]{1,0:T(8,128)(2,1)} %get-tuple-element.130.kt_ref, ...), custom_call_target="tpu_custom_call" | custom-call | flops 1048576 | bytes 1048576 | tf_op jit(solution)/shard_map/attend/pallas_call | solution.py:239
  30.9 8.5 %attend.3 = (bf16[192,512]{1,0:T(8,128)(2,1)}, bf16[192,512]{1,0:T(8,128)(2,1)}, f32[3,1,1024]{2,1,0:T(1,128)}) custom-call(s32[1,5]{1,0:T(1,128)} %lens_ref.11, s32[1,1]{1,0:T(1,128)} %bitcast.1.rank_ref, bf16[192,2048]{1,0:T(8,128)(2,1)} %get-tuple-element.125.qt_ref, bf16[192,2048]{1,0:T(8,128)(2,1)} %get-tuple-element.130.kt_ref, ...), custom_call_target="tpu_custom_call" | custom-call | flops 1048576 | bytes 1048576 | tf_op jit(solution)/shard_map/attend/pallas_call | solution.py:239
  42.6 4.9 %middle.1 = (f32[512,768]{1,0:T(8,128)}, bf16[512,768]{1,0:T(8,128)(2,1)}) custom-call(s32[1]{0:T(128)} %bitcast.rank_ref, bf16[2048,768]{1,0:T(8,128)(2,1)} %tokens_ref.2, f32[768]{0:T(1024)} %gain_ref.6, f32[768]{0:T(1024)} %bias_ref.3, bf16[512,512]{1,0:T(8,128)(2,1)} %get-tuple-element.124.dispatch_ref, ...), custom_call_target="tpu_custom_call" | custom-call | flops 1048576 | bytes 1048576 | tf_op jit(solution)/shard_map/middle/pallas_call | solution.py:507
  47.4 10.7 %all-to-all-start = ((bf16[8,64,768]{2,1,0:T(8,128)(2,1)}), bf16[8,64,768]{2,1,0:T(8,128)(2,1)S(1)}, u32[]{:S(2)}, u32[]{:S(2)}) async-start(bf16[8,64,768]{2,1,0:T(8,128)(2,1)} %bitcast.54), calls=%async_computation | async-start | bytes 1572864 | tf_op jit(solution)/shard_map/all_to_all | solution.py:995
  58.1 6.3 %convolution_convert_fusion.grad_act_ref = bf16[512,3072]{1,0:T(8,128)(2,1)} fusion(bf16[512,768]{1,0:T(8,128)(2,1)S(1)} %bitcast.48, bf16[1,3072,768]{2,1,0:T(8,128)(2,1)} %param.25), kind=kOutput, calls=%fused_computation | convolution fusion | flops 2417491968 | bytes 8650752 | tf_op jit(solution)/shard_map/dot_general | solution.py:484
  64.5 14.3 %all-to-all-done = bf16[8,64,768]{2,1,0:T(8,128)(2,1)S(1)} async-done(((bf16[8,64,768]{2,1,0:T(8,128)(2,1)}), bf16[8,64,768]{2,1,0:T(8,128)(2,1)S(1)}, u32[]{:S(2)}, u32[]{:S(2)}) %all-to-all-start) | async-done | bytes 786464 | tf_op jit(solution)/shard_map/all_to_all | solution.py:995
  79.6 11.8 %expert.1 = (bf16[512,1536]{1,0:T(8,128)(2,1)}, bf16[512,1536]{1,0:T(8,128)(2,1)}, bf16[512,1536]{1,0:T(8,128)(2,1)}, bf16[512,1536]{1,0:T(8,128)(2,1)}, bf16[512,768]{1,0:T(8,128)(2,1)}) custom-call(s32[1,1]{1,0:T(1,128)} %bitcast.1.rank_ref, bf16[512,768]{1,0:T(8,128)(2,1)} %bitcast.43, bf16[512,3072]{1,0:T(8,128)(2,1)} %convolution_convert_fusion.grad_act_ref, ...), custom_call_target="tpu_custom_call" | custom-call | flops 1048576 | bytes 1048576 | tf_op jit(solution)/shard_map/expert/pallas_call | solution.py:678
  92.8 3.7 %all-to-all-start.2 = ((bf16[8,64,768]{2,1,0:T(8,128)(2,1)}), bf16[8,64,768]{2,1,0:T(8,128)(2,1)S(1)}, u32[]{:S(2)}, u32[]{:S(2)}) async-start(bf16[8,64,768]{2,1,0:T(8,128)(2,1)} %bitcast.53), calls=%async_computation.2 | async-start | bytes 1572864 | tf_op jit(solution)/shard_map/all_to_all | solution.py:995
  96.6 6.5 %product.1 = bf16[512,768]{1,0:T(8,128)(2,1)} custom-call(s32[1,1]{1,0:T(1,128)} %bitcast.1.rank_ref, bf16[512,1536]{1,0:T(8,128)(2,1)} %get-tuple-element.157.kept_ref.refs_2_, bf16[512,1536]{1,0:T(8,128)(2,1)} %get-tuple-element.158.sent_ref, bf16[3072,768]{1,0:T(8,128)(2,1)} %bitcast.46), custom_call_target="tpu_custom_call" | custom-call | flops 1048576 | bytes 1048576 | tf_op jit(solution)/shard_map/product/pallas_call | solution.py:729
  104.2 11.9 %expert_weights.1 = (bf16[384,768]{1,0:T(8,128)(2,1)}, bf16[1152,768]{1,0:T(8,128)(2,1)}, f32[768,768]{1,0:T(8,128)}, f32[768,768]{1,0:T(8,128)}) custom-call(bf16[512,768]{1,0:T(8,128)(2,1)} %bitcast.44, bf16[512,768]{1,0:T(8,128)(2,1)} %bitcast.49, bf16[512,1536]{1,0:T(8,128)(2,1)} %get-tuple-element.157.kept_ref.refs_2_, ...), custom_call_target="tpu_custom_call" | custom-call | flops 1048576 | bytes 1048576 | tf_op jit(solution)/shard_map/expert_weights/pallas_call | solution.py:773
  118.0 6.5 %turn.1 = (f32[512,768]{1,0:T(8,128)}, f32[2,768]{1,0:T(2,128)}, bf16[2,192,768]{2,1,0:T(8,128)(2,1)}, bf16[2,192,768]{2,1,0:T(8,128)(2,1)}, bf16[192,512]{1,0:T...) custom-call(s32[1,5]{1,0:T(1,128)} %lens_ref.11, ...), custom_call_target="tpu_custom_call" | custom-call | flops 1048576 | bytes 1048576 | tf_op jit(solution)/shard_map/turn/pallas_call | solution.py:564
  126.5 4.9 %all-to-all-start.3 = ((bf16[8,64,768]{2,1,0:T(8,128)(2,1)}), bf16[8,64,768]{2,1,0:T(8,128)(2,1)S(1)}, u32[]{:S(2)}, u32[]{:S(2)}) async-start(bf16[8,64,768]{2,1,0:T(8,128)(2,1)} %bitcast.15), calls=%async_computation.3 | async-start | bytes 1572864 | tf_op jit(solution)/shard_map/all_to_all | solution.py:995
  137.0 19.3 %attend_back.2 = (bf16[2048,384]{1,0:T(8,128)(2,1)}, f32[2,768]{1,0:T(2,128)}, bf16[192,768]{1,0:T(8,128)(2,1)}, bf16[192,768]{1,0:T(8,128)(2,1)}) custom-call(s32[1,5]{1,0:T(1,128)} %lens_ref.11, s32[1,1]{1,0:T(1,128)} %bitcast.1.rank_ref, s32[1,1]{1,0:T(1,128)} %bitcast.6.bit_ref, bf16[192,2048]{1,0:T(8,128)(2,1)} %get-tuple-element.125.qt_ref, ...), custom_call_target="tpu_custom_call" | custom-call | flops 1048576 | bytes 1048576 | tf_op jit(solution)/shard_map/attend_back/pallas_call | solution.py:408
  159.0 4.3 %collective-permute-start.16 = (bf16[192,768]{1,0:T(8,128)(2,1)}, bf16[192,768]{1,0:T(8,128)(2,1)}, u32[]{:S(2)}, u32[]{:S(2)}) collective-permute-start(bf16[192,768]{1,0:T(8,128)(2,1)} %add_convert_fusion.6), channel_id=1, source_target_pairs={{0,16},{4,20},{8,24},{12,28},{16,0},{20,4},{24,8},{28,12},{1,17},{... | collective-permute-start | bytes 884744 | tf_op jit(solution)/shard_map/ppermute | solution.py:38
  164.1 13.0 %attend_back.3 = (bf16[2048,192]{1,0:T(8,128)(2,1)}, f32[2,768]{1,0:T(2,128)}, bf16[112,768]{1,0:T(8,128)(2,1)}, bf16[112,768]{1,0:T(8,128)(2,1)}) custom-call(s32[1,5]{1,0:T(1,128)} %lens_ref.11, s32[1,1]{1,0:T(1,128)} %bitcast.1.rank_ref, s32[1,1]{1,0:T(1,128)} %bitcast.6.bit_ref, bf16[192,2048]{1,0:T(8,128)(2,1)} %get-tuple-element.125.qt_ref, ...), custom_call_target="tpu_custom_call" | custom-call | flops 1048576 | bytes 1048576 | tf_op jit(solution)/shard_map/attend_back/pallas_call | solution.py:408
  182.9 3.7 %collective-permute-start.18 = (bf16[112,768]{1,0:T(8,128)(2,1)S(1)}, bf16[112,768]{1,0:T(8,128)(2,1)S(1)}, u32[]{:S(2)}, u32[]{:S(2)}) collective-permute-start(bf16[112,768]{1,0:T(8,128)(2,1)S(1)} %copy-done.35), channel_id=1, source_target_pairs={{0,4},{4,0},{8,12},{12,8},{16,20},{20,16},{24,28},{28,24},{1,5},{5... | collective-permute-start | bytes 516104 | tf_op jit(solution)/shard_map/ppermute | solution.py:38
  189.1 2.5 %collective-permute-done.18.b_ref = bf16[112,768]{1,0:T(8,128)(2,1)S(1)} collective-permute-done((bf16[112,768]{1,0:T(8,128)(2,1)S(1)}, bf16[112,768]{1,0:T(8,128)(2,1)S(1)}, u32[]{:S(2)}, u32[]{:S(2)}) %collective-permute-start.18) | collective-permute-done | bytes 172064 | tf_op jit(solution)/shard_map/ppermute | solution.py:38
  198.9 4.8 %collective-permute-done.20.b_ref = bf16[112,768]{1,0:T(8,128)(2,1)S(1)} collective-permute-done((bf16[112,768]{1,0:T(8,128)(2,1)S(1)}, bf16[112,768]{1,0:T(8,128)(2,1)S(1)}, u32[]{:S(2)}, u32[]{:S(2)}) %collective-permute-start.20) | collective-permute-done | bytes 172064 | tf_op jit(solution)/shard_map/ppermute | solution.py:38
  208.5 4.0 %expert_sums.1 = (f32[768,768]{1,0:T(8,128)}, f32[768,768]{1,0:T(8,128)}) custom-call(f32[768,768]{1,0:T(8,128)S(1)} %copy-done.6, f32[768,768]{1,0:T(8,128)S(1)} %copy-done.7, bf16[576,768]{1,0:T(8,128)(2,1)S(1)} %copy-done.9, bf16[1152,768]{1,0:T(8,128)(2,1)S(1)} %collective-permute-done.21.rest_ref), custom_call_target="tpu_custom_call" | custom-call | flops 1048576 | bytes 1048576 | tf_op jit(solution)/shard_map/expert_sums/pallas_call | solution.py:812
  212.5 7.8 %collective-permute-done.22.b_ref = bf16[112,768]{1,0:T(8,128)(2,1)S(1)} collective-permute-done((bf16[112,768]{1,0:T(8,128)(2,1)S(1)}, bf16[112,768]{1,0:T(8,128)(2,1)S(1)}, u32[]{:S(2)}, u32[]{:S(2)}) %collective-permute-start.22) | collective-permute-done | bytes 172064 | tf_op jit(solution)/shard_map/ppermute | solution.py:38
  231.0 3.3 %collective-permute-done.29.refs_3_ = bf16[112,768]{1,0:T(8,128)(2,1)S(1)} collective-permute-done((bf16[112,768]{1,0:T(8,128)(2,1)S(1)}, bf16[112,768]{1,0:T(8,128)(2,1)S(1)}, u32[]{:S(2)}, u32[]{:S(2)}) %collective-permute-start.29) | collective-permute-done | bytes 172064 | tf_op jit(solution)/shard_map/ppermute | solution.py:38
  (156 shorter events, 55.5 us)
Async XLA Ops:
  3.9 43.5 %all-to-all-start.1 = ((bf16[8,64,768]{2,1,0:T(8,128)(2,1)}), bf16[8,64,768]{2,1,0:T(8,128)(2,1)S(1)}, u32[]{:S(2)}, u32[]{:S(2)}) async-start(bf16[8,64,768]{2,1,0:T(8,128)(2,1)} %bitcast.52), calls=%async_computation.1 | async-start | bytes 1572864 | tf_op jit(solution)/shard_map/all_to_all | solution.py:995
  11.2 28.5 %collective-permute-start.3 = (bf16[192,768]{1,0:T(8,128)(2,1)S(1)}, bf16[192,768]{1,0:T(8,128)(2,1)S(1)}, u32[]{:S(2)}, u32[]{:S(2)}) collective-permute-start(bf16[192,768]{1,0:T(8,128)(2,1)S(1)} %copy-done.19), channel_id=1, source_target_pairs={{0,2},{1,3},{2,0},{3,1},{4,6},{5,7},{6,4},{7,5},{8,10},{9,11},{10,... | collective-permute-start | bytes 884744 | tf_op jit(solution)/shard_map/ppermute | solution.py:38
  12.8 27.0 %collective-permute-start.2 = (bf16[192,768]{1,0:T(8,128)(2,1)S(1)}, bf16[192,768]{1,0:T(8,128)(2,1)S(1)}, u32[]{:S(2)}, u32[]{:S(2)}) collective-permute-start(bf16[192,768]{1,0:T(8,128)(2,1)S(1)} %copy-done.19), channel_id=1, source_target_pairs={{0,1},{1,0},{2,3},{3,2},{4,5},{5,4},{6,7},{7,6},{8,9},{9,8},{10,11... | collective-permute-start | bytes 884744 | tf_op jit(solution)/shard_map/ppermute | solution.py:38
  12.8 27.0 %collective-permute-start.4 = (bf16[192,768]{1,0:T(8,128)(2,1)S(1)}, bf16[192,768]{1,0:T(8,128)(2,1)S(1)}, u32[]{:S(2)}, u32[]{:S(2)}) collective-permute-start(bf16[192,768]{1,0:T(8,128)(2,1)S(1)} %copy-done.19), channel_id=1, source_target_pairs={{0,3},{1,2},{2,1},{3,0},{4,7},{5,6},{6,5},{7,4},{8,11},{9,10},{10,... | collective-permute-start | bytes 884744 | tf_op jit(solution)/shard_map/ppermute | solution.py:38
  29.4 10.0 %collective-permute-start = (bf16[192,512]{1,0:T(8,128)(2,1)}, bf16[192,512]{1,0:T(8,128)(2,1)S(1)}, u32[]{:S(2)}, u32[]{:S(2)}) collective-permute-start(bf16[192,512]{1,0:T(8,128)(2,1)} %get-tuple-element.133.rest_2_.rest_4_), channel_id=1, source_target_pairs={{0,2},{1,3},{2,0},{3,1},{4,6},{5,7},{6,4},{7,5},{8,10},{9,11},{10,... | collective-permute-start | bytes 589832 | tf_op jit(solution)/shard_map/ppermute | solution.py:38
  47.4 31.3 %all-to-all-start = ((bf16[8,64,768]{2,1,0:T(8,128)(2,1)}), bf16[8,64,768]{2,1,0:T(8,128)(2,1)S(1)}, u32[]{:S(2)}, u32[]{:S(2)}) async-start(bf16[8,64,768]{2,1,0:T(8,128)(2,1)} %bitcast.54), calls=%async_computation | async-start | bytes 1572864 | tf_op jit(solution)/shard_map/all_to_all | solution.py:995
  58.1 20.7 %collective-permute-start.6 = (bf16[512,768]{1,0:T(8,128)(2,1)S(1)}, bf16[512,768]{1,0:T(8,128)(2,1)S(1)}, u32[]{:S(2)}, u32[]{:S(2)}) collective-permute-start(bf16[512,768]{1,0:T(8,128)(2,1)S(1)} %bitcast.47), channel_id=1, source_target_pairs={{0,1},{1,0},{2,3},{3,2},{4,5},{5,4},{6,7},{7,6},{8,9},{9,8},{10,11... | collective-permute-start | bytes 2359304 | tf_op jit(solution)/shard_map/ppermute | solution.py:38
  78.7 12.7 %collective-permute-start.7 = (bf16[512,768]{1,0:T(8,128)(2,1)S(1)}, bf16[512,768]{1,0:T(8,128)(2,1)S(1)}, u32[]{:S(2)}, u32[]{:S(2)}) collective-permute-start(bf16[512,768]{1,0:T(8,128)(2,1)S(1)} %bitcast.42), channel_id=1, source_target_pairs={{0,1},{1,0},{2,3},{3,2},{4,5},{5,4},{6,7},{7,6},{8,9},{9,8},{10,11... | collective-permute-start | bytes 2359304 | tf_op jit(solution)/shard_map/ppermute | solution.py:38
  92.3 10.7 %collective-permute-start.9 = (bf16[512,1536]{1,0:T(8,128)(2,1)}, bf16[512,1536]{1,0:T(8,128)(2,1)S(1)}, u32[]{:S(2)}, u32[]{:S(2)}) collective-permute-start(bf16[512,1536]{1,0:T(8,128)(2,1)} %get-tuple-element.159), channel_id=1, source_target_pairs={{0,1},{1,0},{2,3},{3,2},{4,5},{5,4},{6,7},{7,6},{8,9},{9,8},{10,11... | collective-permute-start | bytes 4718600 | tf_op jit(solution)/shard_map/ppermute | solution.py:38
  92.3 10.7 %collective-permute-start.8 = (bf16[512,1536]{1,0:T(8,128)(2,1)}, bf16[512,1536]{1,0:T(8,128)(2,1)}, u32[]{:S(2)}, u32[]{:S(2)}) collective-permute-start(bf16[512,1536]{1,0:T(8,128)(2,1)} %get-tuple-element.158.sent_ref), channel_id=1, source_target_pairs={{0,1},{1,0},{2,3},{3,2},{4,5},{5,4},{6,7},{7,6},{8,9},{9,8},{10,11... | collective-permute-start | bytes 4718600 | tf_op jit(solution)/shard_map/ppermute | solution.py:38
  92.8 24.2 %all-to-all-start.2 = ((bf16[8,64,768]{2,1,0:T(8,128)(2,1)}), bf16[8,64,768]{2,1,0:T(8,128)(2,1)S(1)}, u32[]{:S(2)}, u32[]{:S(2)}) async-start(bf16[8,64,768]{2,1,0:T(8,128)(2,1)} %bitcast.53), calls=%async_computation.2 | async-start | bytes 1572864 | tf_op jit(solution)/shard_map/all_to_all | solution.py:995
  124.6 10.2 %collective-permute-start.10 = (bf16[192,512]{1,0:T(8,128)(2,1)}, bf16[192,512]{1,0:T(8,128)(2,1)S(1)}, u32[]{:S(2)}, u32[]{:S(2)}) collective-permute-start(bf16[192,512]{1,0:T(8,128)(2,1)} %get-tuple-element.170), channel_id=1, source_target_pairs={{0,1},{1,0},{2,3},{3,2},{4,5},{5,4},{6,7},{7,6},{8,9},{9,8},{10,11... | collective-permute-start | bytes 589832 | tf_op jit(solution)/shard_map/ppermute | solution.py:38
  126.5 29.7 %all-to-all-start.3 = ((bf16[8,64,768]{2,1,0:T(8,128)(2,1)}), bf16[8,64,768]{2,1,0:T(8,128)(2,1)S(1)}, u32[]{:S(2)}, u32[]{:S(2)}) async-start(bf16[8,64,768]{2,1,0:T(8,128)(2,1)} %bitcast.15), calls=%async_computation.3 | async-start | bytes 1572864 | tf_op jit(solution)/shard_map/all_to_all | solution.py:995
  135.5 22.7 %collective-permute-start.14 = (bf16[576,768]{1,0:T(8,128)(2,1)}, bf16[576,768]{1,0:T(8,128)(2,1)S(1)}, u32[]{:S(2)}, u32[]{:S(2)}) collective-permute-start(bf16[576,768]{1,0:T(8,128)(2,1)} %get-tuple-element.185), channel_id=1, source_target_pairs={{0,2},{1,3},{2,0},{3,1},{4,6},{5,7},{6,4},{7,5},{8,10},{9,11},{10,... | collective-permute-start | bytes 2654216 | tf_op jit(solution)/shard_map/ppermute | solution.py:38
  159.0 18.4 %collective-permute-start.16 = (bf16[192,768]{1,0:T(8,128)(2,1)}, bf16[192,768]{1,0:T(8,128)(2,1)}, u32[]{:S(2)}, u32[]{:S(2)}) collective-permute-start(bf16[192,768]{1,0:T(8,128)(2,1)} %add_convert_fusion.6), channel_id=1, source_target_pairs={{0,16},{4,20},{8,24},{12,28},{16,0},{20,4},{24,8},{28,12},{1,17},{... | collective-permute-start | bytes 884744 | tf_op jit(solution)/shard_map/ppermute | solution.py:38
  163.4 15.2 %collective-permute-start.15 = (bf16[192,768]{1,0:T(8,128)(2,1)}, bf16[192,768]{1,0:T(8,128)(2,1)}, u32[]{:S(2)}, u32[]{:S(2)}) collective-permute-start(bf16[192,768]{1,0:T(8,128)(2,1)} %get-tuple-element.200), channel_id=1, source_target_pairs={{0,4},{4,0},{8,12},{12,8},{16,20},{20,16},{24,28},{28,24},{1,5},{5... | collective-permute-start | bytes 884744 | tf_op jit(solution)/shard_map/ppermute | solution.py:38
  163.4 41.7 %collective-permute-start.21 = (bf16[1152,768]{1,0:T(8,128)(2,1)}, bf16[1152,768]{1,0:T(8,128)(2,1)S(1)}, u32[]{:S(2)}, u32[]{:S(2)}) collective-permute-start(bf16[1152,768]{1,0:T(8,128)(2,1)} %get-tuple-element.215), channel_id=1, source_target_pairs={{0,2},{1,3},{2,0},{3,1},{4,6},{5,7},{6,4},{7,5},{8,10},{9,11},{10,... | collective-permute-start | bytes 5308424 | tf_op jit(solution)/shard_map/ppermute | solution.py:38
  186.6 11.0 %collective-permute-start.26 = (bf16[192,768]{1,0:T(8,128)(2,1)S(1)}, bf16[192,768]{1,0:T(8,128)(2,1)S(1)}, u32[]{:S(2)}, u32[]{:S(2)}) collective-permute-start(bf16[192,768]{1,0:T(8,128)(2,1)S(1)} %add_convert_fusion.7), channel_id=1, source_target_pairs={{0,8},{4,12},{8,0},{12,4},{16,24},{20,28},{24,16},{28,20},{1,9},{5... | collective-permute-start | bytes 884744 | tf_op jit(solution)/shard_map/ppermute | solution.py:38
  191.8 14.5 %collective-permute-start.30 = (bf16[192,768]{1,0:T(8,128)(2,1)S(1)}, bf16[192,768]{1,0:T(8,128)(2,1)S(1)}, u32[]{:S(2)}, u32[]{:S(2)}) collective-permute-start(bf16[192,768]{1,0:T(8,128)(2,1)S(1)} %add_convert_fusion.5), channel_id=1, source_target_pairs={{0,4},{4,0},{8,12},{12,8},{16,20},{20,16},{24,28},{28,24},{1,5},{5... | collective-permute-start | bytes 884744 | tf_op jit(solution)/shard_map/ppermute | solution.py:38
  193.7 27.3 %collective-permute-start.23 = (bf16[1,512,768]{2,1,0:T(8,128)(2,1)S(1)}, bf16[1,512,768]{2,1,0:T(8,128)(2,1)S(1)}, u32[]{:S(2)}, u32[]{:S(2)}) collective-permute-start(bf16[1,512,768]{2,1,0:T(8,128)(2,1)S(1)} %add_convert_fusion), channel_id=1, source_target_pairs={{0,2},{1,3},{2,0},{3,1},{4,6},{5,7},{6,4},{7,5},{8,10},{9,11},{10,... | collective-permute-start | bytes 2359304 | tf_op jit(solution)/shard_map/ppermute | solution.py:38
  197.7 23.4 %collective-permute-start.27 = (bf16[192,768]{1,0:T(8,128)(2,1)S(1)}, bf16[192,768]{1,0:T(8,128)(2,1)S(1)}, u32[]{:S(2)}, u32[]{:S(2)}) collective-permute-start(bf16[192,768]{1,0:T(8,128)(2,1)S(1)} %add_convert_fusion.4), channel_id=1, source_target_pairs={{0,16},{4,20},{8,24},{12,28},{16,0},{20,4},{24,8},{28,12},{1,17},{... | collective-permute-start | bytes 884744 | tf_op jit(solution)/shard_map/ppermute | solution.py:38
  203.7 22.1 %collective-permute-start.19 = (bf16[1,512,768]{2,1,0:T(8,128)(2,1)S(1)}, bf16[1,512,768]{2,1,0:T(8,128)(2,1)S(1)}, u32[]{:S(2)}, u32[]{:S(2)}) collective-permute-start(bf16[1,512,768]{2,1,0:T(8,128)(2,1)S(1)} %get-tuple-element.213), channel_id=1, source_target_pairs={{0,1},{1,0},{2,3},{3,2},{4,5},{5,4},{6,7},{7,6},{8,9},{9,8},{10,11... | collective-permute-start | bytes 2359304 | tf_op jit(solution)/shard_map/ppermute | solution.py:38
  205.1 15.3 %collective-permute-start.22 = (bf16[112,768]{1,0:T(8,128)(2,1)S(1)}, bf16[112,768]{1,0:T(8,128)(2,1)S(1)}, u32[]{:S(2)}, u32[]{:S(2)}) collective-permute-start(bf16[112,768]{1,0:T(8,128)(2,1)S(1)} %add_parts.4.a_ref), channel_id=1, source_target_pairs={{0,16},{4,20},{8,24},{12,28},{16,0},{20,4},{24,8},{28,12},{1,17},{... | collective-permute-start | bytes 516104 | tf_op jit(solution)/shard_map/ppermute | solution.py:38
  206.4 17.5 %collective-permute-start.31 = (bf16[192,768]{1,0:T(8,128)(2,1)S(1)}, bf16[192,768]{1,0:T(8,128)(2,1)S(1)}, u32[]{:S(2)}, u32[]{:S(2)}) collective-permute-start(bf16[192,768]{1,0:T(8,128)(2,1)S(1)} %add_convert_fusion.2), channel_id=1, source_target_pairs={{0,8},{4,12},{8,0},{12,4},{16,24},{20,28},{24,16},{28,20},{1,9},{5... | collective-permute-start | bytes 884744 | tf_op jit(solution)/shard_map/ppermute | solution.py:38
  (48 other events, 316.9 us)

commit v8 on v7

--- a/solution.py
+++ b/solution.py
@@ -743,7 +743,7 @@
 
 
 def weight_kernel(groups, *refs):
-    first_ref, rest_ref, up_ref, down_ref = refs[-4:]
+    first_ref, second_ref, third_ref, up_ref, down_ref = refs[-5:]
     dup = ddown = 0.0
     for g in range(groups):
         in_ref, grad_ref, act_ref, pre_ref = refs[4 * g : 4 * g + 4]
@@ -754,8 +754,8 @@
     @pl.when(pl.program_id(0) == 0)
     def far():
         first_ref[...] = dup[:cut].astype(bf16)
-        rest_ref[: dup.shape[0] - cut, :] = dup[cut:].astype(bf16)
-        rest_ref[dup.shape[0] - cut :, :] = ddown.astype(bf16)
+        second_ref[...] = dup[cut:].astype(bf16)
+        third_ref[...] = ddown.astype(bf16)
 
     @pl.when(pl.program_id(0) == 1)
     def near():
@@ -768,15 +768,15 @@
     size = groups[0][2].shape[1] // 2
     fixed = pl.BlockSpec((count, width), lambda i: (0, 0))
     columns = pl.BlockSpec((count, size), lambda i: (0, 1 - i))
-    cut = (width + size) // 4
-    shapes = ((cut, size), (width + size - cut, size), (width, size), (size, width))
+    half = (width // 2, size)
+    shapes = (half, half, (size, width), (width, size), (size, width))
     return pl.pallas_call(
         functools.partial(weight_kernel, len(groups)),
         grid=(2,),
         in_specs=[fixed, fixed, columns, columns] * len(groups),
         out_specs=tuple(pl.BlockSpec(shape, lambda i: (0, 0)) for shape in shapes),
         out_shape=tuple(
-            jax.ShapeDtypeStruct(shape, bf16 if k < 2 else f32)
+            jax.ShapeDtypeStruct(shape, bf16 if k < 3 else f32)
             for k, shape in enumerate(shapes)
         ),
         name="expert_weights",
@@ -785,26 +785,28 @@
     )(*[values for group in groups for values in group])
 
 
-def expert_sum_kernel(near_up_ref, near_down_ref, first_ref, rest_ref, up_ref, down_ref):
+def expert_sum_kernel(
+    near_up_ref, near_down_ref, first_ref, second_ref, third_ref, up_ref, down_ref
+):
     step = pl.program_id(0)
     half = pl.num_programs(0) // 2
-    far = jnp.where(step < half // 2, first_ref[...], rest_ref[...]).astype(f32)
 
     @pl.when(step < half)
     def upper():
+        far = jnp.where(step < half // 2, first_ref[...], second_ref[...]).astype(f32)
         up_ref[...] = near_up_ref[...] + far
 
     @pl.when(step >= half)
     def lower():
-        down_ref[...] = near_down_ref[...] + far
-
-
-def expert_sums(near_up, near_down, first, rest):
+        down_ref[...] = near_down_ref[...] + third_ref[...].astype(f32)
+
+
+def expert_sums(near_up, near_down, first, second, third):
     count, width = near_up.shape
     steps = 8
     half = steps // 2
     size = count // half
-    head = steps // 4
+    head = half // 2
     skip = first.shape[0] // size - head
     block = lambda place: pl.BlockSpec((size, width), lambda i: (place(i), 0))
     upper = block(lambda i: jnp.minimum(i, half - 1))
@@ -817,13 +819,14 @@
             upper,
             lower,
             block(lambda i: jnp.minimum(i, head - 1) + skip),
-            block(lambda i: jnp.maximum(i - head, 0)),
+            block(lambda i: jnp.clip(i - head, 0, head - 1)),
+            lower,
         ],
         out_specs=(upper, lower),
         name="expert_sums",
         compiler_params=pltpu.CompilerParams(vmem_limit_bytes=10 * 2**20),
         cost_estimate=COST,
-    )(near_up, near_down, first, rest)
+    )(near_up, near_down, first, second, third)
 
 
 def input_grad_kernel(groups, qw_ref, kw_ref, vw_ref, *refs):
@@ -924,6 +927,10 @@
 
 def add_low(a, b):
     return (a.astype(f32) + b.astype(f32)).astype(bf16)
+
+
+def after(value, *others):
+    return lax.optimization_barrier((value, *others))[0]
 
 
 def tie(*values):
@@ -1073,20 +1080,21 @@
     groups = ((0, heads - 1), (heads - 1, 1))
     joint_a, sums_a, own_a, away_a = back(*groups[0], extras=(), grads=grad_parts)
     output_got = swap(output_far, "tensor", 2)
-    joint_a, own_a, away_a, output_got, grad_parts, expert_rest, returned = tie(
-        joint_a, own_a, away_a, output_got, grad_parts, expert_far[1], returned
-    )
-    expert_got = swap(expert_rest, "tensor", 2)
+    joint_a, own_a, away_a, output_got, grad_parts, expert_far, returned = tie(
+        joint_a, own_a, away_a, output_got, grad_parts, expert_far, returned
+    )
+    expert_second = swap(expert_far[1], "tensor", 2)
     output_sum = add_low(output_near, output_got[: output_near.shape[0]])
     own_a = add_low(own_a, swap(away_a, "dp", 1))
     output_sum = add_low(output_sum, swap(output_sum, "dp", dp_steps[-1]))
     joint_b, unused, own_b, away_b = back(
         *groups[1], extras=(sums_a, sums_second), grads=grad_parts
     )
-    joint_b, own_a, own_b, away_b, output_sum = tie(
-        joint_b, own_a, own_b, away_b, output_sum
-    )
-
+    joint_b, own_a, own_b, away_b, output_sum, expert_second, expert_third = tie(
+        joint_b, own_a, own_b, away_b, output_sum, expert_second, expert_far[2]
+    )
+
+    expert_third = swap(expert_third, "tensor", 2)
     far_kept, far_sent = input_grad(
         groups, weights, (joint_a, joint_b), far, members - far, shard_rows
     )
@@ -1099,14 +1107,15 @@
     near_core = swap(near_sent, "tensor", 1)
     near_far = swap(far_kept, "tensor", 2)
     for step in dp_steps[1:]:
-        own_a = add_low(own_a, swap(own_a, "dp", step))
+        got_a = swap(own_a, "dp", step)
         own_b = add_parts(own_b, swap(own_b, "dp", step))
-        if step == dp_steps[1]:
-            own_b, expert_got = tie(own_b, expert_got)
+        own_a = add_low(own_a, got_a if step == dp_steps[1] else after(got_a, own_b))
+    own_b, near_far, expert_third, returned = tie(
+        own_b, near_far, expert_third, returned
+    )
     up_grad, down_grad = expert_sums(
-        expert_up_near, expert_down_near, output_got, expert_got
-    )
-    own_b, up_grad, down_grad, near_far = tie(own_b, up_grad, down_grad, near_far)
+        expert_up_near, expert_down_near, output_got, expert_second, expert_third
+    )
     norm_sums = own_b[-SUM_ROWS:].astype(f32)
     norm_sums = norm_sums[: SUM_ROWS // 2] + norm_sums[SUM_ROWS // 2 :]
     for step in steps:
@@ -1117,7 +1126,6 @@
     )
     for step in dp_steps[:-1]:
         output_sum = add_low(output_sum, swap(output_sum, "dp", step))
-
     block_out = residual + contract_rows(dispatch, returned)
     query_grad, key_grad, value_grad = finish(groups, bit_cell, pieces)
     return (

time: 237 us -> 247 us (1.042)
  Pallas kernels: 115 us -> 129 us
  starting transfers between devices: 57.2 us -> 43.4 us
  waiting for transfers between devices: 41.9 us -> 53 us
    ppermute x32 -> x33, waiting for transfers between devices: 26.6 us -> 37.8 us  [swap(): return lax.ppermute(values, axis, [(i, i ^ step) for i in range(count)])]
    ppermute x32 -> x33, starting transfers between devices: 30.6 us -> 21.4 us  [swap(): return lax.ppermute(values, axis, [(i, i ^ step) for i in range(count)])]
    pallas_call x2, Pallas kernels: 32.3 us -> 41.2 us  [attend_back(): pl.pallas_call(functools.partial(backward_kernel, first_head, heads, bloc...]
    pallas_call x2, Pallas kernels: 17 us -> 22.1 us  [attend(): pl.pallas_call(functools.partial(forward_kernel, first, blocks), out_shap...]
    all_to_all x4, starting transfers between devices: 26.6 us -> 22 us  [exchange(): lax.all_to_all(rows.reshape(sources, -1, width), 'dp', split_axis=0, conc...]
    unnamed x72 -> x76, local copies, waits for them, and re-layouts: 6.57 us -> 7.32 us
  transfers between devices with their start and end apart: 36 -> 37, of which waited for: 14 -> 9; matrix products, arithmetic and copies ran while one was open for 5% -> 5% of each run, Pallas kernels for 44% -> 47%
where the time goes in v8:
time: 247 us
  Pallas kernels  129 us (52%)
  waiting for transfers between devices  53 us (21%)
  starting transfers between devices  43.4 us (18%)
  matrix products  8.13 us (3%)
  local copies, waits for them, and re-layouts  7.94 us (3%)
  other arithmetic  4.12 us (2%)
    pallas_call x2, Pallas kernels, attend_back(): pl.pallas_call(functools.partial(backward_kernel, first_head, heads, bloc...  41.2 us
    ppermute x33, waiting for transfers between devices, swap(): return lax.ppermute(values, axis, [(i, i ^ step) for i in range(count)])  37.8 us
    pallas_call x2, Pallas kernels, attend(): pl.pallas_call(functools.partial(forward_kernel, first, blocks), out_shap...  22.1 us
    all_to_all x4, starting transfers between devices, exchange(): lax.all_to_all(rows.reshape(sources, -1, width), 'dp', split_axis=0, conc...  22 us
    ppermute x33, starting transfers between devices, swap(): return lax.ppermute(values, axis, [(i, i ^ step) for i in range(count)])  21.4 us
    all_to_all x4, waiting for transfers between devices, exchange(): lax.all_to_all(rows.reshape(sources, -1, width), 'dp', split_axis=0, conc...  15.1 us
    pallas_call x1, Pallas kernels, expert_weights(): pl.pallas_call(functools.partial(weight_kernel, len(groups)), grid=(2,),...  11.9 us
    pallas_call x1, Pallas kernels, expert(): pl.pallas_call(functools.partial(expert_kernel, parts), out_shape=(jax.Sh...  11.7 us
  transfers between devices with their start and end apart: 37, of which 9 were waited for; matrix products, arithmetic and copies ran while one was open for 5% of the time, Pallas kernels for 47%

profile of v8, /device:TPU:0, one launch (start us, length us, event | category | flops | bytes accessed | tf_op | source)
XLA Modules:
  0.0 247.0 jit_solution(1071849109735091185)
XLA Ops:
  0.7 3.3 %plan.1 = (bf16[512,512]{1,0:T(8,128)(2,1)}, bf16[512,768]{1,0:T(8,128)(2,1)}) custom-call(s32[1,5]{1,0:T(1,128)} %lens_ref.11, s32[1,1]{1,0:T(1,128)} %bitcast.1.rank_ref, s32[1,512]{1,0:T(1,128)} %bitcast.55, s32[1,512]{1,0:T(1,128)} %order_ref.1, bf16[512,768]{1,0:T(8,128)(2,1)} %cotangent_ref.1), custom_call_target="tpu_custom_call" | custom-call | flops 1048576 | bytes 1048576 | tf_op jit(solution)/shard_map/plan/pallas_call | solution.py:470
  3.9 7.3 %all-to-all-start.1 = ((bf16[8,64,768]{2,1,0:T(8,128)(2,1)}), bf16[8,64,768]{2,1,0:T(8,128)(2,1)S(1)}, u32[]{:S(2)}, u32[]{:S(2)}) async-start(bf16[8,64,768]{2,1,0:T(8,128)(2,1)} %bitcast.52), calls=%async_computation.1 | async-start | bytes 1572864 | tf_op jit(solution)/shard_map/all_to_all | solution.py:1002
  13.4 7.5 %project.1 = (bf16[2048,768]{1,0:T(8,128)(2,1)}, bf16[192,2048]{1,0:T(8,128)(2,1)}, bf16[192,2048]{1,0:T(8,128)(2,1)}, bf16[192,2048]{1,0:T(8,128)(2,1)}) custom-call(s32[1]{0:T(128)} %bitcast.rank_ref, bf16[2048,768]{1,0:T(8,128)(2,1)} %tokens_ref.2, f32[768]{0:T(1024)} %gain_ref.7, f32[768]{0:T(1024)} %bias_ref.2, bf16[192,768]{1,0:T(8,128)(2,1)} %bitcast.27, ...), custom_call_target="tpu_custom_call" | custom-call | flops 1048576 | bytes 1048576 | tf_op jit(solution)/shard_map/project/pallas_call | solution.py:81
  20.9 11.0 %attend.2 = (bf16[192,512]{1,0:T(8,128)(2,1)}, bf16[192,512]{1,0:T(8,128)(2,1)}, f32[3,1,1024]{2,1,0:T(1,128)}) custom-call(s32[1,5]{1,0:T(1,128)} %lens_ref.11, s32[1,1]{1,0:T(1,128)} %bitcast.1.rank_ref, bf16[192,2048]{1,0:T(8,128)(2,1)} %get-tuple-element.129.qt_ref, bf16[192,2048]{1,0:T(8,128)(2,1)} %get-tuple-element.134.kt_ref, ...), custom_call_target="tpu_custom_call" | custom-call | flops 1048576 | bytes 1048576 | tf_op jit(solution)/shard_map/attend/pallas_call | solution.py:239
  33.4 11.0 %attend.3 = (bf16[192,512]{1,0:T(8,128)(2,1)}, bf16[192,512]{1,0:T(8,128)(2,1)}, f32[3,1,1024]{2,1,0:T(1,128)}) custom-call(s32[1,5]{1,0:T(1,128)} %lens_ref.11, s32[1,1]{1,0:T(1,128)} %bitcast.1.rank_ref, bf16[192,2048]{1,0:T(8,128)(2,1)} %get-tuple-element.129.qt_ref, bf16[192,2048]{1,0:T(8,128)(2,1)} %get-tuple-element.134.kt_ref, ...), custom_call_target="tpu_custom_call" | custom-call | flops 1048576 | bytes 1048576 | tf_op jit(solution)/shard_map/attend/pallas_call | solution.py:239
  47.2 4.9 %middle.1 = (f32[512,768]{1,0:T(8,128)}, bf16[512,768]{1,0:T(8,128)(2,1)}) custom-call(s32[1]{0:T(128)} %bitcast.rank_ref, bf16[2048,768]{1,0:T(8,128)(2,1)} %tokens_ref.2, f32[768]{0:T(1024)} %gain_ref.6, f32[768]{0:T(1024)} %bias_ref.3, bf16[512,512]{1,0:T(8,128)(2,1)} %get-tuple-element.128.dispatch_ref, ...), custom_call_target="tpu_custom_call" | custom-call | flops 1048576 | bytes 1048576 | tf_op jit(solution)/shard_map/middle/pallas_call | solution.py:507
  52.1 6.0 %all-to-all-start = ((bf16[8,64,768]{2,1,0:T(8,128)(2,1)}), bf16[8,64,768]{2,1,0:T(8,128)(2,1)S(1)}, u32[]{:S(2)}, u32[]{:S(2)}) async-start(bf16[8,64,768]{2,1,0:T(8,128)(2,1)} %bitcast.54), calls=%async_computation | async-start | bytes 1572864 | tf_op jit(solution)/shard_map/all_to_all | solution.py:1002
  58.1 6.4 %convolution_convert_fusion.grad_act_ref = bf16[512,3072]{1,0:T(8,128)(2,1)} fusion(bf16[512,768]{1,0:T(8,128)(2,1)S(1)} %bitcast.48, bf16[1,3072,768]{2,1,0:T(8,128)(2,1)} %param.25), kind=kOutput, calls=%fused_computation | convolution fusion | flops 2417491968 | bytes 8650752 | tf_op jit(solution)/shard_map/dot_general | solution.py:484
  64.5 14.2 %all-to-all-done = bf16[8,64,768]{2,1,0:T(8,128)(2,1)S(1)} async-done(((bf16[8,64,768]{2,1,0:T(8,128)(2,1)}), bf16[8,64,768]{2,1,0:T(8,128)(2,1)S(1)}, u32[]{:S(2)}, u32[]{:S(2)}) %all-to-all-start) | async-done | bytes 786464 | tf_op jit(solution)/shard_map/all_to_all | solution.py:1002
  79.6 11.7 %expert.1 = (bf16[512,1536]{1,0:T(8,128)(2,1)}, bf16[512,1536]{1,0:T(8,128)(2,1)}, bf16[512,1536]{1,0:T(8,128)(2,1)}, bf16[512,1536]{1,0:T(8,128)(2,1)}, bf16[512,768]{1,0:T(8,128)(2,1)}) custom-call(s32[1,1]{1,0:T(1,128)} %bitcast.1.rank_ref, bf16[512,768]{1,0:T(8,128)(2,1)} %bitcast.43, bf16[512,3072]{1,0:T(8,128)(2,1)} %convolution_convert_fusion.grad_act_ref, ...), custom_call_target="tpu_custom_call" | custom-call | flops 1048576 | bytes 1048576 | tf_op jit(solution)/shard_map/expert/pallas_call | solution.py:678
  92.8 3.7 %all-to-all-start.2 = ((bf16[8,64,768]{2,1,0:T(8,128)(2,1)}), bf16[8,64,768]{2,1,0:T(8,128)(2,1)S(1)}, u32[]{:S(2)}, u32[]{:S(2)}) async-start(bf16[8,64,768]{2,1,0:T(8,128)(2,1)} %bitcast.53), calls=%async_computation.2 | async-start | bytes 1572864 | tf_op jit(solution)/shard_map/all_to_all | solution.py:1002
  96.5 6.5 %product.1 = bf16[512,768]{1,0:T(8,128)(2,1)} custom-call(s32[1,1]{1,0:T(1,128)} %bitcast.1.rank_ref, bf16[512,1536]{1,0:T(8,128)(2,1)} %get-tuple-element.161.kept_ref.refs_2_, bf16[512,1536]{1,0:T(8,128)(2,1)} %get-tuple-element.162.sent_ref, bf16[3072,768]{1,0:T(8,128)(2,1)} %bitcast.46), custom_call_target="tpu_custom_call" | custom-call | flops 1048576 | bytes 1048576 | tf_op jit(solution)/shard_map/product/pallas_call | solution.py:729
  104.2 11.9 %expert_weights.1 = (bf16[384,768]{1,0:T(8,128)(2,1)}, bf16[384,768]{1,0:T(8,128)(2,1)}, bf16[768,768]{1,0:T(8,128)(2,1)}, f32[768,768]{1,0:T(8,128)}, f32[768,768]{1,0:T(8,128)}) custom-call(bf16[512,768]{1,0:T(8,128)(2,1)} %bitcast.44, bf16[512,768]{1,0:T(8,128)(2,1)} %bitcast.49, bf16[512,1536]{1,0:T(8,128)(2,1)} %get-tuple-element.161.kept_ref.refs_2_, ...), custom_call_target="tpu_custom_call" | custom-call | flops 1048576 | bytes 1048576 | tf_op jit(solution)/shard_map/expert_weights/pallas_call | solution.py:773
  117.9 6.5 %turn.1 = (f32[512,768]{1,0:T(8,128)}, f32[2,768]{1,0:T(2,128)}, bf16[2,192,768]{2,1,0:T(8,128)(2,1)}, bf16[2,192,768]{2,1,0:T(8,128)(2,1)}, bf16[192,512]{1,0:T...) custom-call(s32[1,5]{1,0:T(1,128)} %lens_ref.11, ...), custom_call_target="tpu_custom_call" | custom-call | flops 1048576 | bytes 1048576 | tf_op jit(solution)/shard_map/turn/pallas_call | solution.py:564
  126.5 5.0 %all-to-all-start.3 = ((bf16[8,64,768]{2,1,0:T(8,128)(2,1)}), bf16[8,64,768]{2,1,0:T(8,128)(2,1)S(1)}, u32[]{:S(2)}, u32[]{:S(2)}) async-start(bf16[8,64,768]{2,1,0:T(8,128)(2,1)} %bitcast.15), calls=%async_computation.3 | async-start | bytes 1572864 | tf_op jit(solution)/shard_map/all_to_all | solution.py:1002
  132.3 2.5 %output_sums.1 = (bf16[192,768]{1,0:T(8,128)(2,1)}, bf16[576,768]{1,0:T(8,128)(2,1)}) custom-call(bf16[2,192,768]{2,1,0:T(8,128)(2,1)} %get-tuple-element.178.kept_ref, bf16[2,192,768]{2,1,0:T(8,128)(2,1)} %copy-done.36, bf16[384,768]{1,0:T(8,128)(2,1)} %get-tuple-element.180.first_ref), custom_call_target="tpu_custom_call" | custom-call | flops 17179869184 | bytes 16777216 | tf_op jit(solution)/shard_map/output_sums/pallas_call | solution.py:592
  136.9 24.8 %attend_back.2 = (bf16[2048,384]{1,0:T(8,128)(2,1)}, f32[2,768]{1,0:T(2,128)}, bf16[192,768]{1,0:T(8,128)(2,1)}, bf16[192,768]{1,0:T(8,128)(2,1)}) custom-call(s32[1,5]{1,0:T(1,128)} %lens_ref.11, s32[1,1]{1,0:T(1,128)} %bitcast.1.rank_ref, s32[1,1]{1,0:T(1,128)} %bitcast.6.bit_ref, bf16[192,2048]{1,0:T(8,128)(2,1)} %get-tuple-element.129.qt_ref, ...), custom_call_target="tpu_custom_call" | custom-call | flops 1048576 | bytes 1048576 | tf_op jit(solution)/shard_map/attend_back/pallas_call | solution.py:408
  164.9 16.3 %attend_back.3 = (bf16[2048,192]{1,0:T(8,128)(2,1)}, f32[2,768]{1,0:T(2,128)}, bf16[112,768]{1,0:T(8,128)(2,1)}, bf16[112,768]{1,0:T(8,128)(2,1)}) custom-call(s32[1,5]{1,0:T(1,128)} %lens_ref.11, s32[1,1]{1,0:T(1,128)} %bitcast.1.rank_ref, s32[1,1]{1,0:T(1,128)} %bitcast.6.bit_ref, bf16[192,2048]{1,0:T(8,128)(2,1)} %get-tuple-element.129.qt_ref, ...), custom_call_target="tpu_custom_call" | custom-call | flops 1048576 | bytes 1048576 | tf_op jit(solution)/shard_map/attend_back/pallas_call | solution.py:408
  197.1 2.8 %collective-permute-done.27 = bf16[192,768]{1,0:T(8,128)(2,1)S(1)} collective-permute-done((bf16[192,768]{1,0:T(8,128)(2,1)S(1)}, bf16[192,768]{1,0:T(8,128)(2,1)S(1)}, u32[]{:S(2)}, u32[]{:S(2)}) %collective-permute-start.27) | collective-permute-done | bytes 294944 | tf_op jit(solution)/shard_map/ppermute | solution.py:38
  200.5 3.3 %collective-permute-done.20.b_ref = bf16[112,768]{1,0:T(8,128)(2,1)S(1)} collective-permute-done((bf16[112,768]{1,0:T(8,128)(2,1)S(1)}, bf16[112,768]{1,0:T(8,128)(2,1)S(1)}, u32[]{:S(2)}, u32[]{:S(2)}) %collective-permute-start.20) | collective-permute-done | bytes 172064 | tf_op jit(solution)/shard_map/ppermute | solution.py:38
  204.8 16.7 %collective-permute-done.21.b_ref = bf16[112,768]{1,0:T(8,128)(2,1)S(1)} collective-permute-done((bf16[112,768]{1,0:T(8,128)(2,1)S(1)}, bf16[112,768]{1,0:T(8,128)(2,1)S(1)}, u32[]{:S(2)}, u32[]{:S(2)}) %collective-permute-start.21) | collective-permute-done | bytes 172064 | tf_op jit(solution)/shard_map/ppermute | solution.py:38
  222.4 11.2 %collective-permute-done.22.refs_2_ = bf16[1,512,768]{2,1,0:T(8,128)(2,1)S(1)} collective-permute-done((bf16[1,512,768]{2,1,0:T(8,128)(2,1)S(1)}, bf16[1,512,768]{2,1,0:T(8,128)(2,1)S(1)}, u32[]{:S(2)}, u32[]{:S(2)}) %collective-permute-start.22) | collective-permute-done | bytes 786464 | tf_op jit(solution)/shard_map/ppermute | solution.py:38
  238.2 4.0 %expert_sums.1 = (f32[768,768]{1,0:T(8,128)}, f32[768,768]{1,0:T(8,128)}) custom-call(f32[768,768]{1,0:T(8,128)S(1)} %copy-done.6, f32[768,768]{1,0:T(8,128)S(1)} %copy-done.7, bf16[576,768]{1,0:T(8,128)(2,1)S(1)} %collective-permute-done.14.first_ref, bf16[384,768]{1,0:T(8,128)(2,1)S(1)} %collective-permute-done.17.second_ref, ...), custom_call_target="tpu_custom_call" | custom-call | flops 1048576 | bytes 1048576 | tf_op jit(solution)/shard_map/expert_sums/pallas_call | solution.py:814
  242.2 2.2 close.1
  (162 shorter events, 44.9 us)
Async XLA Ops:
  3.9 48.2 %all-to-all-start.1 = ((bf16[8,64,768]{2,1,0:T(8,128)(2,1)}), bf16[8,64,768]{2,1,0:T(8,128)(2,1)S(1)}, u32[]{:S(2)}, u32[]{:S(2)}) async-start(bf16[8,64,768]{2,1,0:T(8,128)(2,1)} %bitcast.52), calls=%async_computation.1 | async-start | bytes 1572864 | tf_op jit(solution)/shard_map/all_to_all | solution.py:1002
  11.2 33.3 %collective-permute-start.3 = (bf16[192,768]{1,0:T(8,128)(2,1)S(1)}, bf16[192,768]{1,0:T(8,128)(2,1)S(1)}, u32[]{:S(2)}, u32[]{:S(2)}) collective-permute-start(bf16[192,768]{1,0:T(8,128)(2,1)S(1)} %copy-done.19), channel_id=1, source_target_pairs={{0,2},{1,3},{2,0},{3,1},{4,6},{5,7},{6,4},{7,5},{8,10},{9,11},{10,... | collective-permute-start | bytes 884744 | tf_op jit(solution)/shard_map/ppermute | solution.py:38
  12.8 31.7 %collective-permute-start.2 = (bf16[192,768]{1,0:T(8,128)(2,1)S(1)}, bf16[192,768]{1,0:T(8,128)(2,1)S(1)}, u32[]{:S(2)}, u32[]{:S(2)}) collective-permute-start(bf16[192,768]{1,0:T(8,128)(2,1)S(1)} %copy-done.19), channel_id=1, source_target_pairs={{0,1},{1,0},{2,3},{3,2},{4,5},{5,4},{6,7},{7,6},{8,9},{9,8},{10,11... | collective-permute-start | bytes 884744 | tf_op jit(solution)/shard_map/ppermute | solution.py:38
  12.8 31.7 %collective-permute-start.4 = (bf16[192,768]{1,0:T(8,128)(2,1)S(1)}, bf16[192,768]{1,0:T(8,128)(2,1)S(1)}, u32[]{:S(2)}, u32[]{:S(2)}) collective-permute-start(bf16[192,768]{1,0:T(8,128)(2,1)S(1)} %copy-done.19), channel_id=1, source_target_pairs={{0,3},{1,2},{2,1},{3,0},{4,7},{5,6},{6,5},{7,4},{8,11},{9,10},{10,... | collective-permute-start | bytes 884744 | tf_op jit(solution)/shard_map/ppermute | solution.py:38
  31.9 12.5 %collective-permute-start = (bf16[192,512]{1,0:T(8,128)(2,1)}, bf16[192,512]{1,0:T(8,128)(2,1)S(1)}, u32[]{:S(2)}, u32[]{:S(2)}) collective-permute-start(bf16[192,512]{1,0:T(8,128)(2,1)} %get-tuple-element.137.rest_2_.rest_4_), channel_id=1, source_target_pairs={{0,2},{1,3},{2,0},{3,1},{4,6},{5,7},{6,4},{7,5},{8,10},{9,11},{10,... | collective-permute-start | bytes 589832 | tf_op jit(solution)/shard_map/ppermute | solution.py:38
  33.4 11.0 %collective-permute-start.1 = (bf16[192,512]{1,0:T(8,128)(2,1)}, bf16[192,512]{1,0:T(8,128)(2,1)S(1)}, u32[]{:S(2)}, u32[]{:S(2)}) collective-permute-start(bf16[192,512]{1,0:T(8,128)(2,1)} %get-tuple-element.138.rest_3_.rest_5_), channel_id=1, source_target_pairs={{0,3},{1,2},{2,1},{3,0},{4,7},{5,6},{6,5},{7,4},{8,11},{9,10},{10,... | collective-permute-start | bytes 589832 | tf_op jit(solution)/shard_map/ppermute | solution.py:38
  52.1 26.6 %all-to-all-start = ((bf16[8,64,768]{2,1,0:T(8,128)(2,1)}), bf16[8,64,768]{2,1,0:T(8,128)(2,1)S(1)}, u32[]{:S(2)}, u32[]{:S(2)}) async-start(bf16[8,64,768]{2,1,0:T(8,128)(2,1)} %bitcast.54), calls=%async_computation | async-start | bytes 1572864 | tf_op jit(solution)/shard_map/all_to_all | solution.py:1002
  58.1 20.7 %collective-permute-start.6 = (bf16[512,768]{1,0:T(8,128)(2,1)S(1)}, bf16[512,768]{1,0:T(8,128)(2,1)S(1)}, u32[]{:S(2)}, u32[]{:S(2)}) collective-permute-start(bf16[512,768]{1,0:T(8,128)(2,1)S(1)} %bitcast.47), channel_id=1, source_target_pairs={{0,1},{1,0},{2,3},{3,2},{4,5},{5,4},{6,7},{7,6},{8,9},{9,8},{10,11... | collective-permute-start | bytes 2359304 | tf_op jit(solution)/shard_map/ppermute | solution.py:38
  78.7 12.6 %collective-permute-start.7 = (bf16[512,768]{1,0:T(8,128)(2,1)S(1)}, bf16[512,768]{1,0:T(8,128)(2,1)S(1)}, u32[]{:S(2)}, u32[]{:S(2)}) collective-permute-start(bf16[512,768]{1,0:T(8,128)(2,1)S(1)} %bitcast.42), channel_id=1, source_target_pairs={{0,1},{1,0},{2,3},{3,2},{4,5},{5,4},{6,7},{7,6},{8,9},{9,8},{10,11... | collective-permute-start | bytes 2359304 | tf_op jit(solution)/shard_map/ppermute | solution.py:38
  92.3 10.8 %collective-permute-start.8 = (bf16[512,1536]{1,0:T(8,128)(2,1)}, bf16[512,1536]{1,0:T(8,128)(2,1)}, u32[]{:S(2)}, u32[]{:S(2)}) collective-permute-start(bf16[512,1536]{1,0:T(8,128)(2,1)} %get-tuple-element.162.sent_ref), channel_id=1, source_target_pairs={{0,1},{1,0},{2,3},{3,2},{4,5},{5,4},{6,7},{7,6},{8,9},{9,8},{10,11... | collective-permute-start | bytes 4718600 | tf_op jit(solution)/shard_map/ppermute | solution.py:38
  92.8 24.2 %all-to-all-start.2 = ((bf16[8,64,768]{2,1,0:T(8,128)(2,1)}), bf16[8,64,768]{2,1,0:T(8,128)(2,1)S(1)}, u32[]{:S(2)}, u32[]{:S(2)}) async-start(bf16[8,64,768]{2,1,0:T(8,128)(2,1)} %bitcast.53), calls=%async_computation.2 | async-start | bytes 1572864 | tf_op jit(solution)/shard_map/all_to_all | solution.py:1002
  126.5 35.3 %all-to-all-start.3 = ((bf16[8,64,768]{2,1,0:T(8,128)(2,1)}), bf16[8,64,768]{2,1,0:T(8,128)(2,1)S(1)}, u32[]{:S(2)}, u32[]{:S(2)}) async-start(bf16[8,64,768]{2,1,0:T(8,128)(2,1)} %bitcast.15), calls=%async_computation.3 | async-start | bytes 1572864 | tf_op jit(solution)/shard_map/all_to_all | solution.py:1002
  135.4 26.4 %collective-permute-start.14 = (bf16[576,768]{1,0:T(8,128)(2,1)}, bf16[576,768]{1,0:T(8,128)(2,1)S(1)}, u32[]{:S(2)}, u32[]{:S(2)}) collective-permute-start(bf16[576,768]{1,0:T(8,128)(2,1)} %get-tuple-element.190), channel_id=1, source_target_pairs={{0,2},{1,3},{2,0},{3,1},{4,6},{5,7},{6,4},{7,5},{8,10},{9,11},{10,... | collective-permute-start | bytes 2654216 | tf_op jit(solution)/shard_map/ppermute | solution.py:38
  162.6 18.7 %collective-permute-start.16 = (bf16[192,768]{1,0:T(8,128)(2,1)S(1)}, bf16[192,768]{1,0:T(8,128)(2,1)}, u32[]{:S(2)}, u32[]{:S(2)}) collective-permute-start(bf16[192,768]{1,0:T(8,128)(2,1)S(1)} %add_convert_fusion.6), channel_id=1, source_target_pairs={{0,16},{4,20},{8,24},{12,28},{16,0},{20,4},{24,8},{28,12},{1,17},{... | collective-permute-start | bytes 884744 | tf_op jit(solution)/shard_map/ppermute | solution.py:38
  164.2 19.3 %collective-permute-start.17 = (bf16[384,768]{1,0:T(8,128)(2,1)}, bf16[384,768]{1,0:T(8,128)(2,1)S(1)}, u32[]{:S(2)}, u32[]{:S(2)}) collective-permute-start(bf16[384,768]{1,0:T(8,128)(2,1)} %get-tuple-element.209), channel_id=1, source_target_pairs={{0,2},{1,3},{2,0},{3,1},{4,6},{5,7},{6,4},{7,5},{8,10},{9,11},{10,... | collective-permute-start | bytes 1769480 | tf_op jit(solution)/shard_map/ppermute | solution.py:38
  164.9 17.5 %collective-permute-start.15 = (bf16[192,768]{1,0:T(8,128)(2,1)}, bf16[192,768]{1,0:T(8,128)(2,1)}, u32[]{:S(2)}, u32[]{:S(2)}) collective-permute-start(bf16[192,768]{1,0:T(8,128)(2,1)} %get-tuple-element.204), channel_id=1, source_target_pairs={{0,4},{4,0},{8,12},{12,8},{16,20},{20,16},{24,28},{28,24},{1,5},{5... | collective-permute-start | bytes 884744 | tf_op jit(solution)/shard_map/ppermute | solution.py:38
  188.7 33.7 %collective-permute-start.23 = (bf16[768,768]{1,0:T(8,128)(2,1)S(1)}, bf16[768,768]{1,0:T(8,128)(2,1)S(1)}, u32[]{:S(2)}, u32[]{:S(2)}) collective-permute-start(bf16[768,768]{1,0:T(8,128)(2,1)S(1)} %copy-done.35), channel_id=1, source_target_pairs={{0,2},{1,3},{2,0},{3,1},{4,6},{5,7},{6,4},{7,5},{8,10},{9,11},{10,... | collective-permute-start | bytes 3538952 | tf_op jit(solution)/shard_map/ppermute | solution.py:38
  195.8 37.8 %collective-permute-start.22 = (bf16[1,512,768]{2,1,0:T(8,128)(2,1)S(1)}, bf16[1,512,768]{2,1,0:T(8,128)(2,1)S(1)}, u32[]{:S(2)}, u32[]{:S(2)}) collective-permute-start(bf16[1,512,768]{2,1,0:T(8,128)(2,1)S(1)} %add_convert_fusion), channel_id=1, source_target_pairs={{0,2},{1,3},{2,0},{3,1},{4,6},{5,7},{6,4},{7,5},{8,10},{9,11},{10,... | collective-permute-start | bytes 2359304 | tf_op jit(solution)/shard_map/ppermute | solution.py:38
  200.0 21.5 %collective-permute-start.28 = (bf16[192,768]{1,0:T(8,128)(2,1)S(1)}, bf16[192,768]{1,0:T(8,128)(2,1)S(1)}, u32[]{:S(2)}, u32[]{:S(2)}) collective-permute-start(bf16[192,768]{1,0:T(8,128)(2,1)S(1)} %add_convert_fusion.4), channel_id=1, source_target_pairs={{0,16},{4,20},{8,24},{12,28},{16,0},{20,4},{24,8},{28,12},{1,17},{... | collective-permute-start | bytes 884744 | tf_op jit(solution)/shard_map/ppermute | solution.py:38
  203.8 38.4 %collective-permute-start.24 = (bf16[1,512,768]{2,1,0:T(8,128)(2,1)S(1)}, bf16[1,512,768]{2,1,0:T(8,128)(2,1)S(1)}, u32[]{:S(2)}, u32[]{:S(2)}) collective-permute-start(bf16[1,512,768]{2,1,0:T(8,128)(2,1)S(1)} %get-tuple-element.225), channel_id=1, source_target_pairs={{0,1},{1,0},{2,3},{3,2},{4,5},{5,4},{6,7},{7,6},{8,9},{9,8},{10,11... | collective-permute-start | bytes 2359304 | tf_op jit(solution)/shard_map/ppermute | solution.py:38
  203.9 17.6 %collective-permute-start.21 = (bf16[112,768]{1,0:T(8,128)(2,1)S(1)}, bf16[112,768]{1,0:T(8,128)(2,1)S(1)}, u32[]{:S(2)}, u32[]{:S(2)}) collective-permute-start(bf16[112,768]{1,0:T(8,128)(2,1)S(1)} %add_parts.4.a_ref), channel_id=1, source_target_pairs={{0,16},{4,20},{8,24},{12,28},{16,0},{20,4},{24,8},{28,12},{1,17},{... | collective-permute-start | bytes 516104 | tf_op jit(solution)/shard_map/ppermute | solution.py:38
  221.5 12.2 %collective-permute-start.32 = (bf16[192,768]{1,0:T(8,128)(2,1)S(1)}, bf16[192,768]{1,0:T(8,128)(2,1)S(1)}, u32[]{:S(2)}, u32[]{:S(2)}) collective-permute-start(bf16[192,768]{1,0:T(8,128)(2,1)S(1)} %add_convert_fusion.2), channel_id=1, source_target_pairs={{0,8},{4,12},{8,0},{12,4},{16,24},{20,28},{24,16},{28,20},{1,9},{5... | collective-permute-start | bytes 884744 | tf_op jit(solution)/shard_map/ppermute | solution.py:38
  221.6 24.0 %collective-permute-start.29 = (bf16[192,768]{1,0:T(8,128)(2,1)S(1)}, bf16[192,768]{1,0:T(8,128)(2,1)S(1)}, u32[]{:S(2)}, u32[]{:S(2)}) collective-permute-start(bf16[192,768]{1,0:T(8,128)(2,1)S(1)} %add_convert_fusion.3.refs_0_), channel_id=1, source_target_pairs={{0,4},{4,0},{8,12},{12,8},{16,20},{20,16},{24,28},{28,24},{1,5},{5... | collective-permute-start | bytes 884744 | tf_op jit(solution)/shard_map/ppermute | solution.py:38
  234.6 11.1 %collective-permute-start.30 = (bf16[112,768]{1,0:T(8,128)(2,1)S(1)}, bf16[112,768]{1,0:T(8,128)(2,1)S(1)}, u32[]{:S(2)}, u32[]{:S(2)}) collective-permute-start(bf16[112,768]{1,0:T(8,128)(2,1)S(1)} %add_parts.5.refs_2_), channel_id=1, source_target_pairs={{0,4},{4,0},{8,12},{12,8},{16,20},{20,16},{24,28},{28,24},{1,5},{5... | collective-permute-start | bytes 516104 | tf_op jit(solution)/shard_map/ppermute | solution.py:38
  (51 other events, 361.1 us)

commit v9 on v7

--- a/solution.py
+++ b/solution.py
@@ -613,6 +613,28 @@
     return (2 * (step % half) + step // half) ^ rank
 
 
+def activation_kernel(grad_ref, down_ref, out_ref):
+    out_ref[...] = across(grad_ref[...], down_ref[...]).astype(bf16)
+
+
+def activation_grads(grads, down, parts):
+    count, width = grads.shape
+    hidden = down.shape[0]
+    size = hidden // parts
+    return pl.pallas_call(
+        activation_kernel,
+        grid=(parts,),
+        out_shape=jax.ShapeDtypeStruct((count, hidden), bf16),
+        in_specs=[
+            pl.BlockSpec((count, width), lambda i: (0, 0)),
+            pl.BlockSpec((size, width), lambda i: (i, 0)),
+        ],
+        out_specs=pl.BlockSpec((count, size), lambda i: (0, i)),
+        name="activation_grads",
+        cost_estimate=COST,
+    )(grads, down)
+
+
 def expert_kernel(
     parts, rank_ref, in_ref, grad_act_ref, up_ref,
     act_kept_ref, pre_kept_ref, act_sent_ref, pre_sent_ref, mid_ref,
@@ -876,9 +898,25 @@
         out_specs=(pl.BlockSpec((1, size, width), lambda i: (i // 2, 0, 0)),) * 2,
         scratch_shapes=[pltpu.VMEM((3 * cols, width), bf16)],
         name="input_grad",
-        compiler_params=pltpu.CompilerParams(vmem_limit_bytes=12 * 2**20),
+        compiler_params=pltpu.CompilerParams(vmem_limit_bytes=10 * 2**20),
         cost_estimate=COST,
     )(*weights, *joints)
+
+
+def block_kernel(residual_ref, dispatch_ref, back_ref, out_ref):
+    out_ref[...] = residual_ref[...] + contract_rows(dispatch_ref[...], back_ref[...])
+
+
+def block_output(residual, dispatch, back):
+    return pl.pallas_call(
+        block_kernel,
+        out_shape=jax.ShapeDtypeStruct(residual.shape, f32),
+        in_specs=[VMEM] * 3,
+        out_specs=VMEM,
+        name="block_output",
+        compiler_params=pltpu.CompilerParams(vmem_limit_bytes=9 * 2**20),
+        cost_estimate=COST,
+    )(residual, dispatch, back)
 
 
 def close_kernel(rank_ref, tokens_ref, gain_ref, grad_ref, *refs):
@@ -922,8 +960,22 @@
     )(rank, tokens, gain, grad, *parts)
 
 
+def add_low_kernel(a_ref, b_ref, out_ref):
+    out_ref[...] = (a_ref[...].astype(f32) + b_ref[...].astype(f32)).astype(bf16)
+
+
 def add_low(a, b):
-    return (a.astype(f32) + b.astype(f32)).astype(bf16)
+    block = pl.BlockSpec(a.shape, lambda i: (0,) * a.ndim)
+    return pl.pallas_call(
+        add_low_kernel,
+        grid=(1,),
+        out_shape=jax.ShapeDtypeStruct(a.shape, bf16),
+        in_specs=[block, block],
+        out_specs=block,
+        name="add_low",
+        compiler_params=pltpu.CompilerParams(vmem_limit_bytes=6 * 2**20),
+        cost_estimate=COST,
+    )(a, b)
 
 
 def tie(*values):
@@ -1030,7 +1082,7 @@
     flat_in = exchange(outgoing)
 
     flat_grad, outgoing = tie(flat_grad, outgoing)
-    grad_act = across(flat_grad, down_matrix).astype(bf16)
+    grad_act = activation_grads(flat_grad, down_matrix, members)
     near_grads = swap(flat_grad, "tensor", 1)
     flat_in, grad_act, near_grads = tie(flat_in, grad_act, near_grads)
     near_rows = swap(flat_in, "tensor", 1)
@@ -1077,7 +1129,7 @@
         joint_a, own_a, away_a, output_got, grad_parts, expert_far[1], returned
     )
     expert_got = swap(expert_rest, "tensor", 2)
-    output_sum = add_low(output_near, output_got[: output_near.shape[0]])
+    output_sum = add_low(output_near, output_got)
     own_a = add_low(own_a, swap(away_a, "dp", 1))
     output_sum = add_low(output_sum, swap(output_sum, "dp", dp_steps[-1]))
     joint_b, unused, own_b, away_b = back(
@@ -1118,7 +1170,7 @@
     for step in dp_steps[:-1]:
         output_sum = add_low(output_sum, swap(output_sum, "dp", step))
 
-    block_out = residual + contract_rows(dispatch, returned)
+    block_out = block_output(residual, dispatch, returned)
     query_grad, key_grad, value_grad = finish(groups, bit_cell, pieces)
     return (
         block_out,

time: 237 us -> 239 us (level)
  Pallas kernels: 115 us -> 140 us
  starting transfers between devices: 57.2 us -> 43.3 us
  matrix products: 8.08 us -> 0 us
  other arithmetic: 5.03 us -> 1.48 us
  waiting for transfers between devices: 41.9 us -> 44.9 us
    pallas_call x0 -> x10, Pallas kernels: none -> 10 us  [the longest x1 6.54 us: activation_grads(): pl.pallas_call(activation_kernel, grid=(parts,), out_shape=jax.ShapeDtype...]
    ppermute x32, starting transfers between devices: 30.6 us -> 21.3 us  [swap(): return lax.ppermute(values, axis, [(i, i ^ step) for i in range(count)])]
    dot_general x2 -> x0, matrix products: 8.08 us -> none  [the longest x1 6.32 us: across(): lax.dot_general(left, right, (((1,), (1,)), ((), ())), preferred_element_...]
    pallas_call x2, Pallas kernels: 32.3 us -> 39.9 us  [attend_back(): pl.pallas_call(functools.partial(backward_kernel, first_head, heads, bloc...]
    pallas_call x2, Pallas kernels: 17 us -> 22.1 us  [attend(): pl.pallas_call(functools.partial(forward_kernel, first, blocks), out_shap...]
    all_to_all x4, starting transfers between devices: 26.6 us -> 22.1 us  [exchange(): lax.all_to_all(rows.reshape(sources, -1, width), 'dp', split_axis=0, conc...]
    convert_element_type x7 -> x0, other arithmetic: 3.53 us -> none  [add_low(): return (a.astype(f32) + b.astype(f32)).astype(bf16)]
    ppermute x32, waiting for transfers between devices: 26.6 us -> 30 us  [swap(): return lax.ppermute(values, axis, [(i, i ^ step) for i in range(count)])]
  transfers between devices with their start and end apart: 36 -> 36, of which waited for: 14 -> 14; matrix products, arithmetic and copies ran while one was open for 5% -> 1% of each run, Pallas kernels for 44% -> 54%
where the time goes in v9:
time: 239 us; the launch traced here: 238 us
  Pallas kernels  140 us (59%)
  waiting for transfers between devices  44.9 us (19%)
  starting transfers between devices  43.3 us (18%)
  local copies, waits for them, and re-layouts  7.19 us (3%)
    pallas_call x2, Pallas kernels, attend_back(): pl.pallas_call(functools.partial(backward_kernel, first_head, heads, bloc...  39.9 us
    ppermute x32, waiting for transfers between devices, swap(): return lax.ppermute(values, axis, [(i, i ^ step) for i in range(count)])  30 us
    pallas_call x2, Pallas kernels, attend(): pl.pallas_call(functools.partial(forward_kernel, first, blocks), out_shap...  22.1 us
    all_to_all x4, starting transfers between devices, exchange(): lax.all_to_all(rows.reshape(sources, -1, width), 'dp', split_axis=0, conc...  22.1 us
    ppermute x32, starting transfers between devices, swap(): return lax.ppermute(values, axis, [(i, i ^ step) for i in range(count)])  21.3 us
    all_to_all x4, waiting for transfers between devices, exchange(): lax.all_to_all(rows.reshape(sources, -1, width), 'dp', split_axis=0, conc...  14.9 us
    pallas_call x1, Pallas kernels, expert_weights(): pl.pallas_call(functools.partial(weight_kernel, len(groups)), grid=(2,),...  11.8 us
    pallas_call x1, Pallas kernels, expert(): pl.pallas_call(functools.partial(expert_kernel, parts), out_shape=(jax.Sh...  11.7 us
  transfers between devices with their start and end apart: 36, of which 14 were waited for; matrix products, arithmetic and copies ran while one was open for 1% of the time, Pallas kernels for 54%

profile of v9, /device:TPU:0, one launch (start us, length us, event | category | flops | bytes accessed | tf_op | source)
XLA Modules:
  0.0 238.5 jit_solution(14973760366345771176)
XLA Ops:
  0.7 3.3 %plan.1 = (bf16[512,512]{1,0:T(8,128)(2,1)}, bf16[512,768]{1,0:T(8,128)(2,1)}) custom-call(s32[1,5]{1,0:T(1,128)} %lens_ref.11, s32[1,1]{1,0:T(1,128)} %bitcast.1.rank_ref, s32[1,512]{1,0:T(1,128)} %bitcast.51, s32[1,512]{1,0:T(1,128)} %order_ref.1, bf16[512,768]{1,0:T(8,128)(2,1)} %cotangent_ref.1), custom_call_target="tpu_custom_call" | custom-call | flops 1048576 | bytes 1048576 | tf_op jit(solution)/shard_map/plan/pallas_call | solution.py:470
  3.9 7.3 %all-to-all-start.1 = ((bf16[8,64,768]{2,1,0:T(8,128)(2,1)}), bf16[8,64,768]{2,1,0:T(8,128)(2,1)S(1)}, u32[]{:S(2)}, u32[]{:S(2)}) async-start(bf16[8,64,768]{2,1,0:T(8,128)(2,1)} %bitcast.48), calls=%async_computation.1 | async-start | bytes 1572864 | tf_op jit(solution)/shard_map/all_to_all | solution.py:1047
  13.4 7.5 %project.1 = (bf16[2048,768]{1,0:T(8,128)(2,1)}, bf16[192,2048]{1,0:T(8,128)(2,1)}, bf16[192,2048]{1,0:T(8,128)(2,1)}, bf16[192,2048]{1,0:T(8,128)(2,1)}) custom-call(s32[1]{0:T(128)} %bitcast.rank_ref, bf16[2048,768]{1,0:T(8,128)(2,1)} %tokens_ref.2, f32[768]{0:T(1024)} %gain_ref.7, f32[768]{0:T(1024)} %bias_ref.2, bf16[192,768]{1,0:T(8,128)(2,1)} %bitcast.22, ...), custom_call_target="tpu_custom_call" | custom-call | flops 1048576 | bytes 1048576 | tf_op jit(solution)/shard_map/project/pallas_call | solution.py:81
  20.9 11.0 %attend.2 = (bf16[192,512]{1,0:T(8,128)(2,1)}, bf16[192,512]{1,0:T(8,128)(2,1)}, f32[3,1,1024]{2,1,0:T(1,128)}) custom-call(s32[1,5]{1,0:T(1,128)} %lens_ref.11, s32[1,1]{1,0:T(1,128)} %bitcast.1.rank_ref, bf16[192,2048]{1,0:T(8,128)(2,1)} %get-tuple-element.125.qt_ref, bf16[192,2048]{1,0:T(8,128)(2,1)} %get-tuple-element.130.kt_ref, ...), custom_call_target="tpu_custom_call" | custom-call | flops 1048576 | bytes 1048576 | tf_op jit(solution)/shard_map/attend/pallas_call | solution.py:239
  33.5 11.0 %attend.3 = (bf16[192,512]{1,0:T(8,128)(2,1)}, bf16[192,512]{1,0:T(8,128)(2,1)}, f32[3,1,1024]{2,1,0:T(1,128)}) custom-call(s32[1,5]{1,0:T(1,128)} %lens_ref.11, s32[1,1]{1,0:T(1,128)} %bitcast.1.rank_ref, bf16[192,2048]{1,0:T(8,128)(2,1)} %get-tuple-element.125.qt_ref, bf16[192,2048]{1,0:T(8,128)(2,1)} %get-tuple-element.130.kt_ref, ...), custom_call_target="tpu_custom_call" | custom-call | flops 1048576 | bytes 1048576 | tf_op jit(solution)/shard_map/attend/pallas_call | solution.py:239
  47.3 4.8 %middle.1 = (f32[512,768]{1,0:T(8,128)}, bf16[512,768]{1,0:T(8,128)(2,1)}) custom-call(s32[1]{0:T(128)} %bitcast.rank_ref, bf16[2048,768]{1,0:T(8,128)(2,1)} %tokens_ref.2, f32[768]{0:T(1024)} %gain_ref.6, f32[768]{0:T(1024)} %bias_ref.3, bf16[512,512]{1,0:T(8,128)(2,1)} %get-tuple-element.124.dispatch_ref, ...), custom_call_target="tpu_custom_call" | custom-call | flops 1048576 | bytes 1048576 | tf_op jit(solution)/shard_map/middle/pallas_call | solution.py:507
  52.1 6.0 %all-to-all-start = ((bf16[8,64,768]{2,1,0:T(8,128)(2,1)}), bf16[8,64,768]{2,1,0:T(8,128)(2,1)S(1)}, u32[]{:S(2)}, u32[]{:S(2)}) async-start(bf16[8,64,768]{2,1,0:T(8,128)(2,1)} %bitcast.50), calls=%async_computation | async-start | bytes 1572864 | tf_op jit(solution)/shard_map/all_to_all | solution.py:1047
  58.2 6.5 %activation_grads.1.grad_act_ref = bf16[512,3072]{1,0:T(8,128)(2,1)} custom-call(bf16[512,768]{1,0:T(8,128)(2,1)} %bitcast.41, bf16[3072,768]{1,0:T(8,128)(2,1)} %bitcast.38), custom_call_target="tpu_custom_call" | custom-call | flops 1048576 | bytes 1048576 | tf_op jit(solution)/shard_map/activation_grads/pallas_call | solution.py:624
  64.7 14.1 %all-to-all-done = bf16[8,64,768]{2,1,0:T(8,128)(2,1)S(1)} async-done(((bf16[8,64,768]{2,1,0:T(8,128)(2,1)}), bf16[8,64,768]{2,1,0:T(8,128)(2,1)S(1)}, u32[]{:S(2)}, u32[]{:S(2)}) %all-to-all-start) | async-done | bytes 786464 | tf_op jit(solution)/shard_map/all_to_all | solution.py:1047
  79.7 11.7 %expert.1 = (bf16[512,1536]{1,0:T(8,128)(2,1)}, bf16[512,1536]{1,0:T(8,128)(2,1)}, bf16[512,1536]{1,0:T(8,128)(2,1)}, bf16[512,1536]{1,0:T(8,128)(2,1)}, bf16[512,768]{1,0:T(8,128)(2,1)}) custom-call(s32[1,1]{1,0:T(1,128)} %bitcast.1.rank_ref, bf16[512,768]{1,0:T(8,128)(2,1)} %bitcast.44, bf16[512,3072]{1,0:T(8,128)(2,1)} %activation_grads.1.grad_act_ref, ...), custom_call_target="tpu_custom_call" | custom-call | flops 1048576 | bytes 1048576 | tf_op jit(solution)/shard_map/expert/pallas_call | solution.py:700
  92.9 3.7 %all-to-all-start.2 = ((bf16[8,64,768]{2,1,0:T(8,128)(2,1)}), bf16[8,64,768]{2,1,0:T(8,128)(2,1)S(1)}, u32[]{:S(2)}, u32[]{:S(2)}) async-start(bf16[8,64,768]{2,1,0:T(8,128)(2,1)} %bitcast.49), calls=%async_computation.2 | async-start | bytes 1572864 | tf_op jit(solution)/shard_map/all_to_all | solution.py:1047
  96.6 6.5 %product.1 = bf16[512,768]{1,0:T(8,128)(2,1)} custom-call(s32[1,1]{1,0:T(1,128)} %bitcast.1.rank_ref, bf16[512,1536]{1,0:T(8,128)(2,1)} %get-tuple-element.157.kept_ref.refs_2_, bf16[512,1536]{1,0:T(8,128)(2,1)} %get-tuple-element.158.sent_ref, bf16[3072,768]{1,0:T(8,128)(2,1)} %bitcast.39), custom_call_target="tpu_custom_call" | custom-call | flops 1048576 | bytes 1048576 | tf_op jit(solution)/shard_map/product/pallas_call | solution.py:751
  104.3 11.8 %expert_weights.1 = (bf16[384,768]{1,0:T(8,128)(2,1)}, bf16[1152,768]{1,0:T(8,128)(2,1)}, f32[768,768]{1,0:T(8,128)}, f32[768,768]{1,0:T(8,128)}) custom-call(bf16[512,768]{1,0:T(8,128)(2,1)} %bitcast.45, bf16[512,768]{1,0:T(8,128)(2,1)} %bitcast.42, bf16[512,1536]{1,0:T(8,128)(2,1)} %get-tuple-element.157.kept_ref.refs_2_, ...), custom_call_target="tpu_custom_call" | custom-call | flops 1048576 | bytes 1048576 | tf_op jit(solution)/shard_map/expert_weights/pallas_call | solution.py:795
  117.8 6.5 %turn.1 = (f32[512,768]{1,0:T(8,128)}, f32[2,768]{1,0:T(2,128)}, bf16[2,192,768]{2,1,0:T(8,128)(2,1)}, bf16[2,192,768]{2,1,0:T(8,128)(2,1)}, bf16[192,512]{1,0:T...) custom-call(s32[1,5]{1,0:T(1,128)} %lens_ref.11, ...), custom_call_target="tpu_custom_call" | custom-call | flops 1048576 | bytes 1048576 | tf_op jit(solution)/shard_map/turn/pallas_call | solution.py:564
  126.4 5.1 %all-to-all-start.3 = ((bf16[8,64,768]{2,1,0:T(8,128)(2,1)}), bf16[8,64,768]{2,1,0:T(8,128)(2,1)S(1)}, u32[]{:S(2)}, u32[]{:S(2)}) async-start(bf16[8,64,768]{2,1,0:T(8,128)(2,1)} %bitcast.15), calls=%async_computation.3 | async-start | bytes 1572864 | tf_op jit(solution)/shard_map/all_to_all | solution.py:1047
  136.8 24.0 %attend_back.2 = (bf16[2048,384]{1,0:T(8,128)(2,1)}, f32[2,768]{1,0:T(2,128)}, bf16[192,768]{1,0:T(8,128)(2,1)}, bf16[192,768]{1,0:T(8,128)(2,1)}) custom-call(s32[1,5]{1,0:T(1,128)} %lens_ref.11, s32[1,1]{1,0:T(1,128)} %bitcast.1.rank_ref, s32[1,1]{1,0:T(1,128)} %bitcast.6.bit_ref, bf16[192,2048]{1,0:T(8,128)(2,1)} %get-tuple-element.125.qt_ref, ...), custom_call_target="tpu_custom_call" | custom-call | flops 1048576 | bytes 1048576 | tf_op jit(solution)/shard_map/attend_back/pallas_call | solution.py:408
  163.2 15.8 %attend_back.3 = (bf16[2048,192]{1,0:T(8,128)(2,1)}, f32[2,768]{1,0:T(2,128)}, bf16[112,768]{1,0:T(8,128)(2,1)}, bf16[112,768]{1,0:T(8,128)(2,1)}) custom-call(s32[1,5]{1,0:T(1,128)} %lens_ref.11, s32[1,1]{1,0:T(1,128)} %bitcast.1.rank_ref, s32[1,1]{1,0:T(1,128)} %bitcast.6.bit_ref, bf16[192,2048]{1,0:T(8,128)(2,1)} %get-tuple-element.125.qt_ref, ...), custom_call_target="tpu_custom_call" | custom-call | flops 1048576 | bytes 1048576 | tf_op jit(solution)/shard_map/attend_back/pallas_call | solution.py:408
  185.4 4.8 %collective-permute-done.18.b_ref = bf16[112,768]{1,0:T(8,128)(2,1)S(1)} collective-permute-done((bf16[112,768]{1,0:T(8,128)(2,1)S(1)}, bf16[112,768]{1,0:T(8,128)(2,1)S(1)}, u32[]{:S(2)}, u32[]{:S(2)}) %collective-permute-start.18) | collective-permute-done | bytes 172064 | tf_op jit(solution)/shard_map/ppermute | solution.py:38
  194.3 4.9 %collective-permute-done.20.b_ref = bf16[112,768]{1,0:T(8,128)(2,1)S(1)} collective-permute-done((bf16[112,768]{1,0:T(8,128)(2,1)S(1)}, bf16[112,768]{1,0:T(8,128)(2,1)S(1)}, u32[]{:S(2)}, u32[]{:S(2)}) %collective-permute-start.20) | collective-permute-done | bytes 172064 | tf_op jit(solution)/shard_map/ppermute | solution.py:38
  199.3 3.5 %collective-permute-done.21.rest_ref = bf16[1152,768]{1,0:T(8,128)(2,1)} collective-permute-done((bf16[1152,768]{1,0:T(8,128)(2,1)}, bf16[1152,768]{1,0:T(8,128)(2,1)}, u32[]{:S(2)}, u32[]{:S(2)}) %collective-permute-start.21) | collective-permute-done | bytes 1769504 | tf_op jit(solution)/shard_map/ppermute | solution.py:38
  207.1 6.5 %expert_sums.1 = (f32[768,768]{1,0:T(8,128)}, f32[768,768]{1,0:T(8,128)}) custom-call(f32[768,768]{1,0:T(8,128)S(1)} %copy-done.8, f32[768,768]{1,0:T(8,128)S(1)} %copy-done.9, bf16[576,768]{1,0:T(8,128)(2,1)S(1)} %collective-permute-done.14.b_ref.first_ref, bf16[1152,768]{1,0:T(8,128)(2,1)} %collective-permute-done.21.rest_ref), custom_call_target="tpu_custom_call" | custom-call | flops 1048576 | bytes 1048576 | tf_op jit(solution)/shard_map/expert_sums/pallas_call | solution.py:834
  213.5 4.6 %collective-permute-done.22.b_ref = bf16[112,768]{1,0:T(8,128)(2,1)S(1)} collective-permute-done((bf16[112,768]{1,0:T(8,128)(2,1)S(1)}, bf16[112,768]{1,0:T(8,128)(2,1)S(1)}, u32[]{:S(2)}, u32[]{:S(2)}) %collective-permute-start.22) | collective-permute-done | bytes 172064 | tf_op jit(solution)/shard_map/ppermute | solution.py:38
  231.0 3.4 %collective-permute-done.28.refs_1_ = bf16[192,768]{1,0:T(8,128)(2,1)S(1)} collective-permute-done((bf16[192,768]{1,0:T(8,128)(2,1)S(1)}, bf16[192,768]{1,0:T(8,128)(2,1)S(1)}, u32[]{:S(2)}, u32[]{:S(2)}) %collective-permute-start.28) | collective-permute-done | bytes 294944 | tf_op jit(solution)/shard_map/ppermute | solution.py:38
  234.4 2.7 %collective-permute-done.29.refs_3_ = bf16[112,768]{1,0:T(8,128)(2,1)S(1)} collective-permute-done((bf16[112,768]{1,0:T(8,128)(2,1)S(1)}, bf16[112,768]{1,0:T(8,128)(2,1)S(1)}, u32[]{:S(2)}, u32[]{:S(2)}) %collective-permute-start.29) | collective-permute-done | bytes 172064 | tf_op jit(solution)/shard_map/ppermute | solution.py:38
  (155 shorter events, 50.0 us)
Async XLA Ops:
  3.9 48.2 %all-to-all-start.1 = ((bf16[8,64,768]{2,1,0:T(8,128)(2,1)}), bf16[8,64,768]{2,1,0:T(8,128)(2,1)S(1)}, u32[]{:S(2)}, u32[]{:S(2)}) async-start(bf16[8,64,768]{2,1,0:T(8,128)(2,1)} %bitcast.48), calls=%async_computation.1 | async-start | bytes 1572864 | tf_op jit(solution)/shard_map/all_to_all | solution.py:1047
  11.2 33.3 %collective-permute-start.3 = (bf16[192,768]{1,0:T(8,128)(2,1)S(1)}, bf16[192,768]{1,0:T(8,128)(2,1)S(1)}, u32[]{:S(2)}, u32[]{:S(2)}) collective-permute-start(bf16[192,768]{1,0:T(8,128)(2,1)S(1)} %copy-done.19), channel_id=1, source_target_pairs={{0,2},{1,3},{2,0},{3,1},{4,6},{5,7},{6,4},{7,5},{8,10},{9,11},{10,... | collective-permute-start | bytes 884744 | tf_op jit(solution)/shard_map/ppermute | solution.py:38
  12.8 31.8 %collective-permute-start.2 = (bf16[192,768]{1,0:T(8,128)(2,1)S(1)}, bf16[192,768]{1,0:T(8,128)(2,1)S(1)}, u32[]{:S(2)}, u32[]{:S(2)}) collective-permute-start(bf16[192,768]{1,0:T(8,128)(2,1)S(1)} %copy-done.19), channel_id=1, source_target_pairs={{0,1},{1,0},{2,3},{3,2},{4,5},{5,4},{6,7},{7,6},{8,9},{9,8},{10,11... | collective-permute-start | bytes 884744 | tf_op jit(solution)/shard_map/ppermute | solution.py:38
  12.8 31.8 %collective-permute-start.4 = (bf16[192,768]{1,0:T(8,128)(2,1)S(1)}, bf16[192,768]{1,0:T(8,128)(2,1)S(1)}, u32[]{:S(2)}, u32[]{:S(2)}) collective-permute-start(bf16[192,768]{1,0:T(8,128)(2,1)S(1)} %copy-done.19), channel_id=1, source_target_pairs={{0,3},{1,2},{2,1},{3,0},{4,7},{5,6},{6,5},{7,4},{8,11},{9,10},{10,... | collective-permute-start | bytes 884744 | tf_op jit(solution)/shard_map/ppermute | solution.py:38
  32.0 12.5 %collective-permute-start = (bf16[192,512]{1,0:T(8,128)(2,1)}, bf16[192,512]{1,0:T(8,128)(2,1)S(1)}, u32[]{:S(2)}, u32[]{:S(2)}) collective-permute-start(bf16[192,512]{1,0:T(8,128)(2,1)} %get-tuple-element.133.rest_2_.rest_4_), channel_id=1, source_target_pairs={{0,2},{1,3},{2,0},{3,1},{4,6},{5,7},{6,4},{7,5},{8,10},{9,11},{10,... | collective-permute-start | bytes 589832 | tf_op jit(solution)/shard_map/ppermute | solution.py:38
  33.5 11.1 %collective-permute-start.1 = (bf16[192,512]{1,0:T(8,128)(2,1)}, bf16[192,512]{1,0:T(8,128)(2,1)S(1)}, u32[]{:S(2)}, u32[]{:S(2)}) collective-permute-start(bf16[192,512]{1,0:T(8,128)(2,1)} %get-tuple-element.134.rest_3_.rest_5_), channel_id=1, source_target_pairs={{0,3},{1,2},{2,1},{3,0},{4,7},{5,6},{6,5},{7,4},{8,11},{9,10},{10,... | collective-permute-start | bytes 589832 | tf_op jit(solution)/shard_map/ppermute | solution.py:38
  52.1 26.7 %all-to-all-start = ((bf16[8,64,768]{2,1,0:T(8,128)(2,1)}), bf16[8,64,768]{2,1,0:T(8,128)(2,1)S(1)}, u32[]{:S(2)}, u32[]{:S(2)}) async-start(bf16[8,64,768]{2,1,0:T(8,128)(2,1)} %bitcast.50), calls=%async_computation | async-start | bytes 1572864 | tf_op jit(solution)/shard_map/all_to_all | solution.py:1047
  58.1 20.7 %collective-permute-start.6 = (bf16[512,768]{1,0:T(8,128)(2,1)S(1)}, bf16[512,768]{1,0:T(8,128)(2,1)S(1)}, u32[]{:S(2)}, u32[]{:S(2)}) collective-permute-start(bf16[512,768]{1,0:T(8,128)(2,1)S(1)} %bitcast.40), channel_id=1, source_target_pairs={{0,1},{1,0},{2,3},{3,2},{4,5},{5,4},{6,7},{7,6},{8,9},{9,8},{10,11... | collective-permute-start | bytes 2359304 | tf_op jit(solution)/shard_map/ppermute | solution.py:38
  78.8 12.7 %collective-permute-start.7 = (bf16[512,768]{1,0:T(8,128)(2,1)S(1)}, bf16[512,768]{1,0:T(8,128)(2,1)S(1)}, u32[]{:S(2)}, u32[]{:S(2)}) collective-permute-start(bf16[512,768]{1,0:T(8,128)(2,1)S(1)} %bitcast.43), channel_id=1, source_target_pairs={{0,1},{1,0},{2,3},{3,2},{4,5},{5,4},{6,7},{7,6},{8,9},{9,8},{10,11... | collective-permute-start | bytes 2359304 | tf_op jit(solution)/shard_map/ppermute | solution.py:38
  92.4 10.7 %collective-permute-start.9 = (bf16[512,1536]{1,0:T(8,128)(2,1)}, bf16[512,1536]{1,0:T(8,128)(2,1)S(1)}, u32[]{:S(2)}, u32[]{:S(2)}) collective-permute-start(bf16[512,1536]{1,0:T(8,128)(2,1)} %get-tuple-element.159), channel_id=1, source_target_pairs={{0,1},{1,0},{2,3},{3,2},{4,5},{5,4},{6,7},{7,6},{8,9},{9,8},{10,11... | collective-permute-start | bytes 4718600 | tf_op jit(solution)/shard_map/ppermute | solution.py:38
  92.4 10.7 %collective-permute-start.8 = (bf16[512,1536]{1,0:T(8,128)(2,1)}, bf16[512,1536]{1,0:T(8,128)(2,1)}, u32[]{:S(2)}, u32[]{:S(2)}) collective-permute-start(bf16[512,1536]{1,0:T(8,128)(2,1)} %get-tuple-element.158.sent_ref), channel_id=1, source_target_pairs={{0,1},{1,0},{2,3},{3,2},{4,5},{5,4},{6,7},{7,6},{8,9},{9,8},{10,11... | collective-permute-start | bytes 4718600 | tf_op jit(solution)/shard_map/ppermute | solution.py:38
  92.9 24.1 %all-to-all-start.2 = ((bf16[8,64,768]{2,1,0:T(8,128)(2,1)}), bf16[8,64,768]{2,1,0:T(8,128)(2,1)S(1)}, u32[]{:S(2)}, u32[]{:S(2)}) async-start(bf16[8,64,768]{2,1,0:T(8,128)(2,1)} %bitcast.49), calls=%async_computation.2 | async-start | bytes 1572864 | tf_op jit(solution)/shard_map/all_to_all | solution.py:1047
  126.4 34.5 %all-to-all-start.3 = ((bf16[8,64,768]{2,1,0:T(8,128)(2,1)}), bf16[8,64,768]{2,1,0:T(8,128)(2,1)S(1)}, u32[]{:S(2)}, u32[]{:S(2)}) async-start(bf16[8,64,768]{2,1,0:T(8,128)(2,1)} %bitcast.15), calls=%async_computation.3 | async-start | bytes 1572864 | tf_op jit(solution)/shard_map/all_to_all | solution.py:1047
  135.3 25.5 %collective-permute-start.14 = (bf16[576,768]{1,0:T(8,128)(2,1)}, bf16[576,768]{1,0:T(8,128)(2,1)S(1)}, u32[]{:S(2)}, u32[]{:S(2)}) collective-permute-start(bf16[576,768]{1,0:T(8,128)(2,1)} %get-tuple-element.185), channel_id=1, source_target_pairs={{0,2},{1,3},{2,0},{3,1},{4,6},{5,7},{6,4},{7,5},{8,10},{9,11},{10,... | collective-permute-start | bytes 2654216 | tf_op jit(solution)/shard_map/ppermute | solution.py:38
  160.9 41.9 %collective-permute-start.21 = (bf16[1152,768]{1,0:T(8,128)(2,1)}, bf16[1152,768]{1,0:T(8,128)(2,1)}, u32[]{:S(2)}, u32[]{:S(2)}) collective-permute-start(bf16[1152,768]{1,0:T(8,128)(2,1)} %get-tuple-element.215), channel_id=1, source_target_pairs={{0,2},{1,3},{2,0},{3,1},{4,6},{5,7},{6,4},{7,5},{8,10},{9,11},{10,... | collective-permute-start | bytes 5308424 | tf_op jit(solution)/shard_map/ppermute | solution.py:38
  161.7 17.4 %collective-permute-start.16 = (bf16[192,768]{1,0:T(8,128)(2,1)S(1)}, bf16[192,768]{1,0:T(8,128)(2,1)}, u32[]{:S(2)}, u32[]{:S(2)}) collective-permute-start(bf16[192,768]{1,0:T(8,128)(2,1)S(1)} %add_low.9.a_ref), channel_id=1, source_target_pairs={{0,16},{4,20},{8,24},{12,28},{16,0},{20,4},{24,8},{28,12},{1,17},{... | collective-permute-start | bytes 884744 | tf_op jit(solution)/shard_map/ppermute | solution.py:38
  162.6 17.5 %collective-permute-start.15 = (bf16[192,768]{1,0:T(8,128)(2,1)}, bf16[192,768]{1,0:T(8,128)(2,1)S(1)}, u32[]{:S(2)}, u32[]{:S(2)}) collective-permute-start(bf16[192,768]{1,0:T(8,128)(2,1)} %get-tuple-element.200), channel_id=1, source_target_pairs={{0,4},{4,0},{8,12},{12,8},{16,20},{20,16},{24,28},{28,24},{1,5},{5... | collective-permute-start | bytes 884744 | tf_op jit(solution)/shard_map/ppermute | solution.py:38
  190.5 28.8 %collective-permute-start.23 = (bf16[1,512,768]{2,1,0:T(8,128)(2,1)S(1)}, bf16[1,512,768]{2,1,0:T(8,128)(2,1)S(1)}, u32[]{:S(2)}, u32[]{:S(2)}) collective-permute-start(bf16[1,512,768]{2,1,0:T(8,128)(2,1)S(1)} %add_low.11), channel_id=1, source_target_pairs={{0,2},{1,3},{2,0},{3,1},{4,6},{5,7},{6,4},{7,5},{8,10},{9,11},{10,... | collective-permute-start | bytes 2359304 | tf_op jit(solution)/shard_map/ppermute | solution.py:38
  194.0 11.9 %collective-permute-start.30 = (bf16[192,768]{1,0:T(8,128)(2,1)S(1)}, bf16[192,768]{1,0:T(8,128)(2,1)S(1)}, u32[]{:S(2)}, u32[]{:S(2)}) collective-permute-start(bf16[192,768]{1,0:T(8,128)(2,1)S(1)} %add_low.10.a_ref), channel_id=1, source_target_pairs={{0,4},{4,0},{8,12},{12,8},{16,20},{20,16},{24,28},{28,24},{1,5},{5... | collective-permute-start | bytes 884744 | tf_op jit(solution)/shard_map/ppermute | solution.py:38
  202.7 15.4 %collective-permute-start.22 = (bf16[112,768]{1,0:T(8,128)(2,1)S(1)}, bf16[112,768]{1,0:T(8,128)(2,1)S(1)}, u32[]{:S(2)}, u32[]{:S(2)}) collective-permute-start(bf16[112,768]{1,0:T(8,128)(2,1)S(1)} %add_parts.4.a_ref), channel_id=1, source_target_pairs={{0,16},{4,20},{8,24},{12,28},{16,0},{20,4},{24,8},{28,12},{1,17},{... | collective-permute-start | bytes 516104 | tf_op jit(solution)/shard_map/ppermute | solution.py:38
  203.6 23.9 %collective-permute-start.19 = (bf16[1,512,768]{2,1,0:T(8,128)(2,1)S(1)}, bf16[1,512,768]{2,1,0:T(8,128)(2,1)S(1)}, u32[]{:S(2)}, u32[]{:S(2)}) collective-permute-start(bf16[1,512,768]{2,1,0:T(8,128)(2,1)S(1)} %get-tuple-element.213), channel_id=1, source_target_pairs={{0,1},{1,0},{2,3},{3,2},{4,5},{5,4},{6,7},{7,6},{8,9},{9,8},{10,11... | collective-permute-start | bytes 2359304 | tf_op jit(solution)/shard_map/ppermute | solution.py:38
  204.4 20.0 %collective-permute-start.27 = (bf16[192,768]{1,0:T(8,128)(2,1)S(1)}, bf16[192,768]{1,0:T(8,128)(2,1)S(1)}, u32[]{:S(2)}, u32[]{:S(2)}) collective-permute-start(bf16[192,768]{1,0:T(8,128)(2,1)S(1)} %add_low.12.a_ref), channel_id=1, source_target_pairs={{0,16},{4,20},{8,24},{12,28},{16,0},{20,4},{24,8},{28,12},{1,17},{... | collective-permute-start | bytes 884744 | tf_op jit(solution)/shard_map/ppermute | solution.py:38
  205.9 19.1 %collective-permute-start.31 = (bf16[192,768]{1,0:T(8,128)(2,1)S(1)}, bf16[192,768]{1,0:T(8,128)(2,1)S(1)}, u32[]{:S(2)}, u32[]{:S(2)}) collective-permute-start(bf16[192,768]{1,0:T(8,128)(2,1)S(1)} %add_low.14.a_ref), channel_id=1, source_target_pairs={{0,8},{4,12},{8,0},{12,4},{16,24},{20,28},{24,16},{28,20},{1,9},{5... | collective-permute-start | bytes 884744 | tf_op jit(solution)/shard_map/ppermute | solution.py:38
  226.0 11.1 %collective-permute-start.29 = (bf16[112,768]{1,0:T(8,128)(2,1)S(1)}, bf16[112,768]{1,0:T(8,128)(2,1)S(1)}, u32[]{:S(2)}, u32[]{:S(2)}) collective-permute-start(bf16[112,768]{1,0:T(8,128)(2,1)S(1)} %add_parts.5.refs_2_), channel_id=1, source_target_pairs={{0,4},{4,0},{8,12},{12,8},{16,20},{20,16},{24,28},{28,24},{1,5},{5... | collective-permute-start | bytes 516104 | tf_op jit(solution)/shard_map/ppermute | solution.py:38
  (47 other events, 303.2 us)

commit v10 on v9

--- a/solution.py
+++ b/solution.py
@@ -598,6 +598,7 @@
         in_specs=[VMEM] * 3,
         out_specs=(VMEM, VMEM),
         name="output_sums",
+        compiler_params=pltpu.CompilerParams(vmem_limit_bytes=52 * 2**20),
         cost_estimate=LONG,
     )(kept, core, first)
 
@@ -713,7 +714,7 @@
             pltpu.SemaphoreType.DMA((2, parts)),
         ],
         name="expert",
-        compiler_params=pltpu.CompilerParams(vmem_limit_bytes=60 * 2**20),
+        compiler_params=pltpu.CompilerParams(vmem_limit_bytes=52 * 2**20),
         cost_estimate=COST,
     )(rank.reshape(1, 1), rows, grad_act, up)
 
@@ -1142,16 +1143,21 @@
     far_kept, far_sent = input_grad(
         groups, weights, (joint_a, joint_b), far, members - far, shard_rows
     )
+    got_a = swap(own_a, "dp", dp_steps[1])
+    got_b = swap(away_b, "dp", 1)
+    joint_b, got_a, got_b = tie(joint_b, got_a, got_b)
     near_kept, near_sent = input_grad(
         groups, weights, (joint_a, joint_b), 0, far, shard_rows
     )
-    own_b = add_parts(own_b, swap(away_b, "dp", 1))
+    own_b = add_parts(own_b, got_b)
     far_kept = add_low(far_kept, swap(far_sent, "tensor", 1))
-    far_kept, own_b, output_sum, near_sent = tie(far_kept, own_b, output_sum, near_sent)
+    own_a = add_low(own_a, got_a)
+    far_kept, own_b, output_sum, own_a = tie(far_kept, own_b, output_sum, own_a)
     near_core = swap(near_sent, "tensor", 1)
     near_far = swap(far_kept, "tensor", 2)
     for step in dp_steps[1:]:
-        own_a = add_low(own_a, swap(own_a, "dp", step))
+        if step != dp_steps[1]:
+            own_a = add_low(own_a, swap(own_a, "dp", step))
         own_b = add_parts(own_b, swap(own_b, "dp", step))
         if step == dp_steps[1]:
             own_b, expert_got = tie(own_b, expert_got)

time: 239 us -> 238 us (level)
    unnamed x70 -> x68, local copies, waits for them, and re-layouts: 6.57 us -> 5.96 us
  transfers between devices with their start and end apart: 36 -> 36, of which waited for: 14 -> 13; matrix products, arithmetic and copies ran while one was open for 1% -> 1% of each run, Pallas kernels for 54% -> 54%
where the time goes in v10:
time: 238 us; the launch traced here: 239 us
  Pallas kernels  141 us (59%)
  waiting for transfers between devices  45.8 us (19%)
  starting transfers between devices  43 us (18%)
  local copies, waits for them, and re-layouts  6.58 us (3%)
    pallas_call x2, Pallas kernels, attend_back(): pl.pallas_call(functools.partial(backward_kernel, first_head, heads, bloc...  41.1 us
    ppermute x32, waiting for transfers between devices, swap(): return lax.ppermute(values, axis, [(i, i ^ step) for i in range(count)])  30.9 us
    all_to_all x4, starting transfers between devices, exchange(): lax.all_to_all(rows.reshape(sources, -1, width), 'dp', split_axis=0, conc...  22.1 us
    pallas_call x2, Pallas kernels, attend(): pl.pallas_call(functools.partial(forward_kernel, first, blocks), out_shap...  22.1 us
    ppermute x32, starting transfers between devices, swap(): return lax.ppermute(values, axis, [(i, i ^ step) for i in range(count)])  20.9 us
    all_to_all x4, waiting for transfers between devices, exchange(): lax.all_to_all(rows.reshape(sources, -1, width), 'dp', split_axis=0, conc...  14.9 us
    pallas_call x1, Pallas kernels, expert_weights(): pl.pallas_call(functools.partial(weight_kernel, len(groups)), grid=(2,),...  11.9 us
    pallas_call x1, Pallas kernels, expert(): pl.pallas_call(functools.partial(expert_kernel, parts), out_shape=(jax.Sh...  11.1 us
  transfers between devices with their start and end apart: 36, of which 13 were waited for; matrix products, arithmetic and copies ran while one was open for 1% of the time, Pallas kernels for 54%

profile of v10, /device:TPU:0, one launch (start us, length us, event | category | flops | bytes accessed | tf_op | source)
XLA Modules:
  0.0 238.7 jit_solution(8539393479809426365)
XLA Ops:
  0.7 3.3 %plan.1 = (bf16[512,512]{1,0:T(8,128)(2,1)}, bf16[512,768]{1,0:T(8,128)(2,1)}) custom-call(s32[1,5]{1,0:T(1,128)} %lens_ref.11, s32[1,1]{1,0:T(1,128)} %bitcast.1.rank_ref, s32[1,512]{1,0:T(1,128)} %bitcast.50, s32[1,512]{1,0:T(1,128)} %order_ref.1, bf16[512,768]{1,0:T(8,128)(2,1)} %cotangent_ref.1), custom_call_target="tpu_custom_call" | custom-call | flops 1048576 | bytes 1048576 | tf_op jit(solution)/shard_map/plan/pallas_call | solution.py:470
  3.9 7.3 %all-to-all-start.1 = ((bf16[8,64,768]{2,1,0:T(8,128)(2,1)}), bf16[8,64,768]{2,1,0:T(8,128)(2,1)S(1)}, u32[]{:S(2)}, u32[]{:S(2)}) async-start(bf16[8,64,768]{2,1,0:T(8,128)(2,1)} %bitcast.48), calls=%async_computation.1 | async-start | bytes 1572864 | tf_op jit(solution)/shard_map/all_to_all | solution.py:1048
  13.4 7.5 %project.1 = (bf16[2048,768]{1,0:T(8,128)(2,1)}, bf16[192,2048]{1,0:T(8,128)(2,1)}, bf16[192,2048]{1,0:T(8,128)(2,1)}, bf16[192,2048]{1,0:T(8,128)(2,1)}) custom-call(s32[1]{0:T(128)} %bitcast.rank_ref, bf16[2048,768]{1,0:T(8,128)(2,1)} %tokens_ref.2, f32[768]{0:T(1024)} %gain_ref.7, f32[768]{0:T(1024)} %bias_ref.2, bf16[192,768]{1,0:T(8,128)(2,1)} %bitcast.22, ...), custom_call_target="tpu_custom_call" | custom-call | flops 1048576 | bytes 1048576 | tf_op jit(solution)/shard_map/project/pallas_call | solution.py:81
  20.9 11.0 %attend.2 = (bf16[192,512]{1,0:T(8,128)(2,1)}, bf16[192,512]{1,0:T(8,128)(2,1)}, f32[3,1,1024]{2,1,0:T(1,128)}) custom-call(s32[1,5]{1,0:T(1,128)} %lens_ref.11, s32[1,1]{1,0:T(1,128)} %bitcast.1.rank_ref, bf16[192,2048]{1,0:T(8,128)(2,1)} %get-tuple-element.128.qt_ref, bf16[192,2048]{1,0:T(8,128)(2,1)} %get-tuple-element.133.kt_ref, ...), custom_call_target="tpu_custom_call" | custom-call | flops 1048576 | bytes 1048576 | tf_op jit(solution)/shard_map/attend/pallas_call | solution.py:239
  33.4 11.1 %attend.3 = (bf16[192,512]{1,0:T(8,128)(2,1)}, bf16[192,512]{1,0:T(8,128)(2,1)}, f32[3,1,1024]{2,1,0:T(1,128)}) custom-call(s32[1,5]{1,0:T(1,128)} %lens_ref.11, s32[1,1]{1,0:T(1,128)} %bitcast.1.rank_ref, bf16[192,2048]{1,0:T(8,128)(2,1)} %get-tuple-element.128.qt_ref, bf16[192,2048]{1,0:T(8,128)(2,1)} %get-tuple-element.133.kt_ref, ...), custom_call_target="tpu_custom_call" | custom-call | flops 1048576 | bytes 1048576 | tf_op jit(solution)/shard_map/attend/pallas_call | solution.py:239
  47.2 4.8 %middle.1 = (f32[512,768]{1,0:T(8,128)}, bf16[512,768]{1,0:T(8,128)(2,1)}) custom-call(s32[1]{0:T(128)} %bitcast.rank_ref, bf16[2048,768]{1,0:T(8,128)(2,1)} %tokens_ref.2, f32[768]{0:T(1024)} %gain_ref.6, f32[768]{0:T(1024)} %bias_ref.3, bf16[512,512]{1,0:T(8,128)(2,1)} %get-tuple-element.127.dispatch_ref, ...), custom_call_target="tpu_custom_call" | custom-call | flops 1048576 | bytes 1048576 | tf_op jit(solution)/shard_map/middle/pallas_call | solution.py:507
  52.1 6.0 %all-to-all-start = ((bf16[8,64,768]{2,1,0:T(8,128)(2,1)}), bf16[8,64,768]{2,1,0:T(8,128)(2,1)S(1)}, u32[]{:S(2)}, u32[]{:S(2)}) async-start(bf16[8,64,768]{2,1,0:T(8,128)(2,1)} %bitcast.49), calls=%async_computation | async-start | bytes 1572864 | tf_op jit(solution)/shard_map/all_to_all | solution.py:1048
  58.1 6.5 %activation_grads.1.grad_act_ref = bf16[512,3072]{1,0:T(8,128)(2,1)} custom-call(bf16[512,768]{1,0:T(8,128)(2,1)} %bitcast.44, bf16[3072,768]{1,0:T(8,128)(2,1)} %bitcast.41), custom_call_target="tpu_custom_call" | custom-call | flops 1048576 | bytes 1048576 | tf_op jit(solution)/shard_map/activation_grads/pallas_call | solution.py:625
  64.7 14.1 %all-to-all-done = bf16[8,64,768]{2,1,0:T(8,128)(2,1)S(1)} async-done(((bf16[8,64,768]{2,1,0:T(8,128)(2,1)}), bf16[8,64,768]{2,1,0:T(8,128)(2,1)S(1)}, u32[]{:S(2)}, u32[]{:S(2)}) %all-to-all-start) | async-done | bytes 786464 | tf_op jit(solution)/shard_map/all_to_all | solution.py:1048
  78.8 11.1 %expert.1 = (bf16[512,1536]{1,0:T(8,128)(2,1)}, bf16[512,1536]{1,0:T(8,128)(2,1)}, bf16[512,1536]{1,0:T(8,128)(2,1)}, bf16[512,1536]{1,0:T(8,128)(2,1)}, bf16[512,768]{1,0:T(8,128)(2,1)}) custom-call(s32[1,1]{1,0:T(1,128)} %bitcast.1.rank_ref, bf16[512,768]{1,0:T(8,128)(2,1)S(1)} %bitcast.38, bf16[512,3072]{1,0:T(8,128)(2,1)} %activation_grads.1.grad_act_ref, ...), custom_call_target="tpu_custom_call" | custom-call | flops 1048576 | bytes 1048576 | tf_op jit(solution)/shard_map/expert/pallas_call | solution.py:701
  91.4 3.7 %all-to-all-start.2 = ((bf16[8,64,768]{2,1,0:T(8,128)(2,1)}), bf16[8,64,768]{2,1,0:T(8,128)(2,1)S(1)}, u32[]{:S(2)}, u32[]{:S(2)}) async-start(bf16[8,64,768]{2,1,0:T(8,128)(2,1)} %bitcast.13), calls=%async_computation.2 | async-start | bytes 1572864 | tf_op jit(solution)/shard_map/all_to_all | solution.py:1048
  95.1 6.5 %product.1 = bf16[512,768]{1,0:T(8,128)(2,1)} custom-call(s32[1,1]{1,0:T(1,128)} %bitcast.1.rank_ref, bf16[512,1536]{1,0:T(8,128)(2,1)} %get-tuple-element.160.kept_ref.refs_2_, bf16[512,1536]{1,0:T(8,128)(2,1)} %get-tuple-element.161.sent_ref, bf16[3072,768]{1,0:T(8,128)(2,1)} %bitcast.42), custom_call_target="tpu_custom_call" | custom-call | flops 1048576 | bytes 1048576 | tf_op jit(solution)/shard_map/product/pallas_call | solution.py:752
  102.8 11.9 %expert_weights.1 = (bf16[384,768]{1,0:T(8,128)(2,1)}, bf16[1152,768]{1,0:T(8,128)(2,1)}, f32[768,768]{1,0:T(8,128)}, f32[768,768]{1,0:T(8,128)}) custom-call(bf16[512,768]{1,0:T(8,128)(2,1)} %bitcast.39, bf16[512,768]{1,0:T(8,128)(2,1)} %bitcast.45, bf16[512,1536]{1,0:T(8,128)(2,1)} %get-tuple-element.160.kept_ref.refs_2_, ...), custom_call_target="tpu_custom_call" | custom-call | flops 1048576 | bytes 1048576 | tf_op jit(solution)/shard_map/expert_weights/pallas_call | solution.py:796
  116.3 6.5 %turn.1 = (f32[512,768]{1,0:T(8,128)}, f32[2,768]{1,0:T(2,128)}, bf16[2,192,768]{2,1,0:T(8,128)(2,1)}, bf16[2,192,768]{2,1,0:T(8,128)(2,1)}, bf16[192,512]{1,0:T...) custom-call(s32[1,5]{1,0:T(1,128)} %lens_ref.11, ...), custom_call_target="tpu_custom_call" | custom-call | flops 1048576 | bytes 1048576 | tf_op jit(solution)/shard_map/turn/pallas_call | solution.py:564
  124.9 5.1 %all-to-all-start.3 = ((bf16[8,64,768]{2,1,0:T(8,128)(2,1)}), bf16[8,64,768]{2,1,0:T(8,128)(2,1)S(1)}, u32[]{:S(2)}, u32[]{:S(2)}) async-start(bf16[8,64,768]{2,1,0:T(8,128)(2,1)} %bitcast.15), calls=%async_computation.3 | async-start | bytes 1572864 | tf_op jit(solution)/shard_map/all_to_all | solution.py:1048
  135.3 24.8 %attend_back.2 = (bf16[2048,384]{1,0:T(8,128)(2,1)}, f32[2,768]{1,0:T(2,128)}, bf16[192,768]{1,0:T(8,128)(2,1)}, bf16[192,768]{1,0:T(8,128)(2,1)}) custom-call(s32[1,5]{1,0:T(1,128)} %lens_ref.11, s32[1,1]{1,0:T(1,128)} %bitcast.1.rank_ref, s32[1,1]{1,0:T(1,128)} %bitcast.6.bit_ref, bf16[192,2048]{1,0:T(8,128)(2,1)} %get-tuple-element.128.qt_ref, ...), custom_call_target="tpu_custom_call" | custom-call | flops 1048576 | bytes 1048576 | tf_op jit(solution)/shard_map/attend_back/pallas_call | solution.py:408
  161.0 3.8 %collective-permute-start.15 = (bf16[192,768]{1,0:T(8,128)(2,1)}, bf16[192,768]{1,0:T(8,128)(2,1)S(1)}, u32[]{:S(2)}, u32[]{:S(2)}) collective-permute-start(bf16[192,768]{1,0:T(8,128)(2,1)} %get-tuple-element.203), channel_id=1, source_target_pairs={{0,4},{4,0},{8,12},{12,8},{16,20},{20,16},{24,28},{28,24},{1,5},{5... | collective-permute-start | bytes 884744 | tf_op jit(solution)/shard_map/ppermute | solution.py:38
  164.8 16.3 %attend_back.3 = (bf16[2048,192]{1,0:T(8,128)(2,1)}, f32[2,768]{1,0:T(2,128)}, bf16[112,768]{1,0:T(8,128)(2,1)}, bf16[112,768]{1,0:T(8,128)(2,1)}) custom-call(s32[1,5]{1,0:T(1,128)} %lens_ref.11, s32[1,1]{1,0:T(1,128)} %bitcast.1.rank_ref, s32[1,1]{1,0:T(1,128)} %bitcast.6.bit_ref, bf16[192,2048]{1,0:T(8,128)(2,1)} %get-tuple-element.128.qt_ref, ...), custom_call_target="tpu_custom_call" | custom-call | flops 1048576 | bytes 1048576 | tf_op jit(solution)/shard_map/attend_back/pallas_call | solution.py:408
  185.6 6.6 %collective-permute-done.18.b_ref = bf16[112,768]{1,0:T(8,128)(2,1)S(1)} collective-permute-done((bf16[112,768]{1,0:T(8,128)(2,1)S(1)}, bf16[112,768]{1,0:T(8,128)(2,1)S(1)}, u32[]{:S(2)}, u32[]{:S(2)}) %collective-permute-start.18) | collective-permute-done | bytes 172064 | tf_op jit(solution)/shard_map/ppermute | solution.py:38
  196.9 5.5 %collective-permute-done.21.b_ref = bf16[112,768]{1,0:T(8,128)(2,1)S(1)} collective-permute-done((bf16[112,768]{1,0:T(8,128)(2,1)S(1)}, bf16[112,768]{1,0:T(8,128)(2,1)S(1)}, u32[]{:S(2)}, u32[]{:S(2)}) %collective-permute-start.21) | collective-permute-done | bytes 172064 | tf_op jit(solution)/shard_map/ppermute | solution.py:38
  204.5 3.0 %collective-permute-start.27 = (bf16[192,768]{1,0:T(8,128)(2,1)S(1)}, bf16[192,768]{1,0:T(8,128)(2,1)S(1)}, u32[]{:S(2)}, u32[]{:S(2)}) collective-permute-start(bf16[192,768]{1,0:T(8,128)(2,1)S(1)} %add_low.12.a_ref), channel_id=1, source_target_pairs={{0,16},{4,20},{8,24},{12,28},{16,0},{20,4},{24,8},{28,12},{1,17},{... | collective-permute-start | bytes 884744 | tf_op jit(solution)/shard_map/ppermute | solution.py:38
  208.0 6.5 %expert_sums.1 = (f32[768,768]{1,0:T(8,128)}, f32[768,768]{1,0:T(8,128)}) custom-call(f32[768,768]{1,0:T(8,128)S(1)} %copy-done.9, f32[768,768]{1,0:T(8,128)S(1)} %copy-done.10, bf16[576,768]{1,0:T(8,128)(2,1)S(1)} %collective-permute-done.14.b_ref.first_ref, bf16[1152,768]{1,0:T(8,128)(2,1)} %collective-permute-done.22.rest_ref), custom_call_target="tpu_custom_call" | custom-call | flops 1048576 | bytes 1048576 | tf_op jit(solution)/shard_map/expert_sums/pallas_call | solution.py:835
  214.5 4.4 %collective-permute-done.23.b_ref = bf16[112,768]{1,0:T(8,128)(2,1)S(1)} collective-permute-done((bf16[112,768]{1,0:T(8,128)(2,1)S(1)}, bf16[112,768]{1,0:T(8,128)(2,1)S(1)}, u32[]{:S(2)}, u32[]{:S(2)}) %collective-permute-start.23) | collective-permute-done | bytes 172064 | tf_op jit(solution)/shard_map/ppermute | solution.py:38
  231.4 3.5 %collective-permute-done.28.refs_1_ = bf16[192,768]{1,0:T(8,128)(2,1)S(1)} collective-permute-done((bf16[192,768]{1,0:T(8,128)(2,1)S(1)}, bf16[192,768]{1,0:T(8,128)(2,1)S(1)}, u32[]{:S(2)}, u32[]{:S(2)}) %collective-permute-start.28) | collective-permute-done | bytes 294944 | tf_op jit(solution)/shard_map/ppermute | solution.py:38
  (153 shorter events, 46.9 us)
Async XLA Ops:
  3.9 48.1 %all-to-all-start.1 = ((bf16[8,64,768]{2,1,0:T(8,128)(2,1)}), bf16[8,64,768]{2,1,0:T(8,128)(2,1)S(1)}, u32[]{:S(2)}, u32[]{:S(2)}) async-start(bf16[8,64,768]{2,1,0:T(8,128)(2,1)} %bitcast.48), calls=%async_computation.1 | async-start | bytes 1572864 | tf_op jit(solution)/shard_map/all_to_all | solution.py:1048
  11.2 33.3 %collective-permute-start.3 = (bf16[192,768]{1,0:T(8,128)(2,1)S(1)}, bf16[192,768]{1,0:T(8,128)(2,1)S(1)}, u32[]{:S(2)}, u32[]{:S(2)}) collective-permute-start(bf16[192,768]{1,0:T(8,128)(2,1)S(1)} %copy-done.19), channel_id=1, source_target_pairs={{0,2},{1,3},{2,0},{3,1},{4,6},{5,7},{6,4},{7,5},{8,10},{9,11},{10,... | collective-permute-start | bytes 884744 | tf_op jit(solution)/shard_map/ppermute | solution.py:38
  12.8 31.7 %collective-permute-start.2 = (bf16[192,768]{1,0:T(8,128)(2,1)S(1)}, bf16[192,768]{1,0:T(8,128)(2,1)S(1)}, u32[]{:S(2)}, u32[]{:S(2)}) collective-permute-start(bf16[192,768]{1,0:T(8,128)(2,1)S(1)} %copy-done.19), channel_id=1, source_target_pairs={{0,1},{1,0},{2,3},{3,2},{4,5},{5,4},{6,7},{7,6},{8,9},{9,8},{10,11... | collective-permute-start | bytes 884744 | tf_op jit(solution)/shard_map/ppermute | solution.py:38
  12.8 31.8 %collective-permute-start.4 = (bf16[192,768]{1,0:T(8,128)(2,1)S(1)}, bf16[192,768]{1,0:T(8,128)(2,1)S(1)}, u32[]{:S(2)}, u32[]{:S(2)}) collective-permute-start(bf16[192,768]{1,0:T(8,128)(2,1)S(1)} %copy-done.19), channel_id=1, source_target_pairs={{0,3},{1,2},{2,1},{3,0},{4,7},{5,6},{6,5},{7,4},{8,11},{9,10},{10,... | collective-permute-start | bytes 884744 | tf_op jit(solution)/shard_map/ppermute | solution.py:38
  31.9 12.5 %collective-permute-start = (bf16[192,512]{1,0:T(8,128)(2,1)}, bf16[192,512]{1,0:T(8,128)(2,1)S(1)}, u32[]{:S(2)}, u32[]{:S(2)}) collective-permute-start(bf16[192,512]{1,0:T(8,128)(2,1)} %get-tuple-element.136.rest_2_.rest_4_), channel_id=1, source_target_pairs={{0,2},{1,3},{2,0},{3,1},{4,6},{5,7},{6,4},{7,5},{8,10},{9,11},{10,... | collective-permute-start | bytes 589832 | tf_op jit(solution)/shard_map/ppermute | solution.py:38
  33.4 11.1 %collective-permute-start.1 = (bf16[192,512]{1,0:T(8,128)(2,1)}, bf16[192,512]{1,0:T(8,128)(2,1)S(1)}, u32[]{:S(2)}, u32[]{:S(2)}) collective-permute-start(bf16[192,512]{1,0:T(8,128)(2,1)} %get-tuple-element.137.rest_3_.rest_5_), channel_id=1, source_target_pairs={{0,3},{1,2},{2,1},{3,0},{4,7},{5,6},{6,5},{7,4},{8,11},{9,10},{10,... | collective-permute-start | bytes 589832 | tf_op jit(solution)/shard_map/ppermute | solution.py:38
  52.1 26.6 %all-to-all-start = ((bf16[8,64,768]{2,1,0:T(8,128)(2,1)}), bf16[8,64,768]{2,1,0:T(8,128)(2,1)S(1)}, u32[]{:S(2)}, u32[]{:S(2)}) async-start(bf16[8,64,768]{2,1,0:T(8,128)(2,1)} %bitcast.49), calls=%async_computation | async-start | bytes 1572864 | tf_op jit(solution)/shard_map/all_to_all | solution.py:1048
  58.1 20.7 %collective-permute-start.6 = (bf16[512,768]{1,0:T(8,128)(2,1)S(1)}, bf16[512,768]{1,0:T(8,128)(2,1)S(1)}, u32[]{:S(2)}, u32[]{:S(2)}) collective-permute-start(bf16[512,768]{1,0:T(8,128)(2,1)S(1)} %bitcast.43), channel_id=1, source_target_pairs={{0,1},{1,0},{2,3},{3,2},{4,5},{5,4},{6,7},{7,6},{8,9},{9,8},{10,11... | collective-permute-start | bytes 2359304 | tf_op jit(solution)/shard_map/ppermute | solution.py:38
  78.7 11.2 %collective-permute-start.7 = (bf16[512,768]{1,0:T(8,128)(2,1)S(1)}, bf16[512,768]{1,0:T(8,128)(2,1)S(1)}, u32[]{:S(2)}, u32[]{:S(2)}) collective-permute-start(bf16[512,768]{1,0:T(8,128)(2,1)S(1)} %bitcast.37), channel_id=1, source_target_pairs={{0,1},{1,0},{2,3},{3,2},{4,5},{5,4},{6,7},{7,6},{8,9},{9,8},{10,11... | collective-permute-start | bytes 2359304 | tf_op jit(solution)/shard_map/ppermute | solution.py:38
  90.9 10.8 %collective-permute-start.9 = (bf16[512,1536]{1,0:T(8,128)(2,1)}, bf16[512,1536]{1,0:T(8,128)(2,1)S(1)}, u32[]{:S(2)}, u32[]{:S(2)}) collective-permute-start(bf16[512,1536]{1,0:T(8,128)(2,1)} %get-tuple-element.162), channel_id=1, source_target_pairs={{0,1},{1,0},{2,3},{3,2},{4,5},{5,4},{6,7},{7,6},{8,9},{9,8},{10,11... | collective-permute-start | bytes 4718600 | tf_op jit(solution)/shard_map/ppermute | solution.py:38
  90.9 10.8 %collective-permute-start.8 = (bf16[512,1536]{1,0:T(8,128)(2,1)}, bf16[512,1536]{1,0:T(8,128)(2,1)}, u32[]{:S(2)}, u32[]{:S(2)}) collective-permute-start(bf16[512,1536]{1,0:T(8,128)(2,1)} %get-tuple-element.161.sent_ref), channel_id=1, source_target_pairs={{0,1},{1,0},{2,3},{3,2},{4,5},{5,4},{6,7},{7,6},{8,9},{9,8},{10,11... | collective-permute-start | bytes 4718600 | tf_op jit(solution)/shard_map/ppermute | solution.py:38
  91.4 24.1 %all-to-all-start.2 = ((bf16[8,64,768]{2,1,0:T(8,128)(2,1)}), bf16[8,64,768]{2,1,0:T(8,128)(2,1)S(1)}, u32[]{:S(2)}, u32[]{:S(2)}) async-start(bf16[8,64,768]{2,1,0:T(8,128)(2,1)} %bitcast.13), calls=%async_computation.2 | async-start | bytes 1572864 | tf_op jit(solution)/shard_map/all_to_all | solution.py:1048
  124.9 35.2 %all-to-all-start.3 = ((bf16[8,64,768]{2,1,0:T(8,128)(2,1)}), bf16[8,64,768]{2,1,0:T(8,128)(2,1)S(1)}, u32[]{:S(2)}, u32[]{:S(2)}) async-start(bf16[8,64,768]{2,1,0:T(8,128)(2,1)} %bitcast.15), calls=%async_computation.3 | async-start | bytes 1572864 | tf_op jit(solution)/shard_map/all_to_all | solution.py:1048
  133.8 26.3 %collective-permute-start.14 = (bf16[576,768]{1,0:T(8,128)(2,1)}, bf16[576,768]{1,0:T(8,128)(2,1)S(1)}, u32[]{:S(2)}, u32[]{:S(2)}) collective-permute-start(bf16[576,768]{1,0:T(8,128)(2,1)} %get-tuple-element.188), channel_id=1, source_target_pairs={{0,2},{1,3},{2,0},{3,1},{4,6},{5,7},{6,4},{7,5},{8,10},{9,11},{10,... | collective-permute-start | bytes 2654216 | tf_op jit(solution)/shard_map/ppermute | solution.py:38
  160.1 42.3 %collective-permute-start.22 = (bf16[1152,768]{1,0:T(8,128)(2,1)}, bf16[1152,768]{1,0:T(8,128)(2,1)}, u32[]{:S(2)}, u32[]{:S(2)}) collective-permute-start(bf16[1152,768]{1,0:T(8,128)(2,1)} %get-tuple-element.221), channel_id=1, source_target_pairs={{0,2},{1,3},{2,0},{3,1},{4,6},{5,7},{6,4},{7,5},{8,10},{9,11},{10,... | collective-permute-start | bytes 5308424 | tf_op jit(solution)/shard_map/ppermute | solution.py:38
  160.9 20.2 %collective-permute-start.16 = (bf16[192,768]{1,0:T(8,128)(2,1)S(1)}, bf16[192,768]{1,0:T(8,128)(2,1)}, u32[]{:S(2)}, u32[]{:S(2)}) collective-permute-start(bf16[192,768]{1,0:T(8,128)(2,1)S(1)} %add_low.9.a_ref), channel_id=1, source_target_pairs={{0,16},{4,20},{8,24},{12,28},{16,0},{20,4},{24,8},{28,12},{1,17},{... | collective-permute-start | bytes 884744 | tf_op jit(solution)/shard_map/ppermute | solution.py:38
  161.0 21.2 %collective-permute-start.15 = (bf16[192,768]{1,0:T(8,128)(2,1)}, bf16[192,768]{1,0:T(8,128)(2,1)S(1)}, u32[]{:S(2)}, u32[]{:S(2)}) collective-permute-start(bf16[192,768]{1,0:T(8,128)(2,1)} %get-tuple-element.203), channel_id=1, source_target_pairs={{0,4},{4,0},{8,12},{12,8},{16,20},{20,16},{24,28},{28,24},{1,5},{5... | collective-permute-start | bytes 884744 | tf_op jit(solution)/shard_map/ppermute | solution.py:38
  195.2 23.7 %collective-permute-start.24 = (bf16[1,512,768]{2,1,0:T(8,128)(2,1)S(1)}, bf16[1,512,768]{2,1,0:T(8,128)(2,1)S(1)}, u32[]{:S(2)}, u32[]{:S(2)}) collective-permute-start(bf16[1,512,768]{2,1,0:T(8,128)(2,1)S(1)} %add_low.11), channel_id=1, source_target_pairs={{0,2},{1,3},{2,0},{3,1},{4,6},{5,7},{6,4},{7,5},{8,10},{9,11},{10,... | collective-permute-start | bytes 2359304 | tf_op jit(solution)/shard_map/ppermute | solution.py:38
  196.9 10.5 %collective-permute-start.30 = (bf16[192,768]{1,0:T(8,128)(2,1)S(1)}, bf16[192,768]{1,0:T(8,128)(2,1)S(1)}, u32[]{:S(2)}, u32[]{:S(2)}) collective-permute-start(bf16[192,768]{1,0:T(8,128)(2,1)S(1)} %add_low.10.a_ref), channel_id=1, source_target_pairs={{0,4},{4,0},{8,12},{12,8},{16,20},{20,16},{24,28},{28,24},{1,5},{5... | collective-permute-start | bytes 884744 | tf_op jit(solution)/shard_map/ppermute | solution.py:38
  202.5 16.4 %collective-permute-start.23 = (bf16[112,768]{1,0:T(8,128)(2,1)S(1)}, bf16[112,768]{1,0:T(8,128)(2,1)S(1)}, u32[]{:S(2)}, u32[]{:S(2)}) collective-permute-start(bf16[112,768]{1,0:T(8,128)(2,1)S(1)} %add_parts.4.a_ref), channel_id=1, source_target_pairs={{0,16},{4,20},{8,24},{12,28},{16,0},{20,4},{24,8},{28,12},{1,17},{... | collective-permute-start | bytes 516104 | tf_op jit(solution)/shard_map/ppermute | solution.py:38
  204.4 23.6 %collective-permute-start.19 = (bf16[1,512,768]{2,1,0:T(8,128)(2,1)S(1)}, bf16[1,512,768]{2,1,0:T(8,128)(2,1)S(1)}, u32[]{:S(2)}, u32[]{:S(2)}) collective-permute-start(bf16[1,512,768]{2,1,0:T(8,128)(2,1)S(1)} %get-tuple-element.213), channel_id=1, source_target_pairs={{0,1},{1,0},{2,3},{3,2},{4,5},{5,4},{6,7},{7,6},{8,9},{9,8},{10,11... | collective-permute-start | bytes 2359304 | tf_op jit(solution)/shard_map/ppermute | solution.py:38
  204.5 20.4 %collective-permute-start.27 = (bf16[192,768]{1,0:T(8,128)(2,1)S(1)}, bf16[192,768]{1,0:T(8,128)(2,1)S(1)}, u32[]{:S(2)}, u32[]{:S(2)}) collective-permute-start(bf16[192,768]{1,0:T(8,128)(2,1)S(1)} %add_low.12.a_ref), channel_id=1, source_target_pairs={{0,16},{4,20},{8,24},{12,28},{16,0},{20,4},{24,8},{28,12},{1,17},{... | collective-permute-start | bytes 884744 | tf_op jit(solution)/shard_map/ppermute | solution.py:38
  207.5 18.1 %collective-permute-start.31 = (bf16[192,768]{1,0:T(8,128)(2,1)S(1)}, bf16[192,768]{1,0:T(8,128)(2,1)S(1)}, u32[]{:S(2)}, u32[]{:S(2)}) collective-permute-start(bf16[192,768]{1,0:T(8,128)(2,1)S(1)} %add_low.14.a_ref), channel_id=1, source_target_pairs={{0,8},{4,12},{8,0},{12,4},{16,24},{20,28},{24,16},{28,20},{1,9},{5... | collective-permute-start | bytes 884744 | tf_op jit(solution)/shard_map/ppermute | solution.py:38
  226.5 10.8 %collective-permute-start.29 = (bf16[112,768]{1,0:T(8,128)(2,1)S(1)}, bf16[112,768]{1,0:T(8,128)(2,1)S(1)}, u32[]{:S(2)}, u32[]{:S(2)}) collective-permute-start(bf16[112,768]{1,0:T(8,128)(2,1)S(1)} %add_parts.5.refs_2_), channel_id=1, source_target_pairs={{0,4},{4,0},{8,12},{12,8},{16,20},{20,16},{24,28},{28,24},{1,5},{5... | collective-permute-start | bytes 516104 | tf_op jit(solution)/shard_map/ppermute | solution.py:38
  (46 other events, 270.8 us)

commit v11 on v10

--- a/solution.py
+++ b/solution.py
@@ -904,24 +904,11 @@
     )(*weights, *joints)
 
 
-def block_kernel(residual_ref, dispatch_ref, back_ref, out_ref):
-    out_ref[...] = residual_ref[...] + contract_rows(dispatch_ref[...], back_ref[...])
-
-
-def block_output(residual, dispatch, back):
-    return pl.pallas_call(
-        block_kernel,
-        out_shape=jax.ShapeDtypeStruct(residual.shape, f32),
-        in_specs=[VMEM] * 3,
-        out_specs=VMEM,
-        name="block_output",
-        compiler_params=pltpu.CompilerParams(vmem_limit_bytes=9 * 2**20),
-        cost_estimate=COST,
-    )(residual, dispatch, back)
-
-
-def close_kernel(rank_ref, tokens_ref, gain_ref, grad_ref, *refs):
-    *part_refs, out_ref = refs
+def close_kernel(
+    rank_ref, tokens_ref, gain_ref, grad_ref, residual_ref, dispatch_ref, back_ref, *refs
+):
+    *part_refs, out_ref, block_ref = refs
+    block_ref[...] = residual_ref[...] + contract_rows(dispatch_ref[...], back_ref[...])
     grad_in = 0.0
     for part_ref in part_refs:
         grad_in = grad_in + part_ref[...].reshape(out_ref.shape).astype(f32)
@@ -937,10 +924,11 @@
     )
 
 
-def close(rank, tokens, gain, grad, parts):
+def close(rank, tokens, gain, grad, residual, dispatch, back, parts):
     shard, width = grad.shape
+    count = dispatch.shape[0]
     size = shard // 2
-    rows = lambda i, r: (i, 0)
+    rows = pl.BlockSpec((size, width), lambda i, r: (i, 0))
     return pl.pallas_call(
         close_kernel,
         grid_spec=pltpu.PrefetchScalarGridSpec(
@@ -949,16 +937,19 @@
             in_specs=[
                 pl.BlockSpec((size, width), lambda i, r: (2 * r[0] + i, 0)),
                 pl.BlockSpec((width,), lambda i, r: (0,)),
-                pl.BlockSpec((size, width), rows),
+                rows,
+                rows,
+                pl.BlockSpec((count, size), lambda i, r: (0, i)),
+                pl.BlockSpec((count, width), lambda i, r: (0, 0)),
             ]
             + [pl.BlockSpec((1, size, width), lambda i, r: (0, i, 0))] * len(parts),
-            out_specs=pl.BlockSpec((size, width), rows),
+            out_specs=(rows, rows),
         ),
-        out_shape=jax.ShapeDtypeStruct((shard, width), f32),
+        out_shape=(jax.ShapeDtypeStruct((shard, width), f32),) * 2,
         name="close",
-        compiler_params=pltpu.CompilerParams(vmem_limit_bytes=12 * 2**20),
-        cost_estimate=COST,
-    )(rank, tokens, gain, grad, *parts)
+        compiler_params=pltpu.CompilerParams(vmem_limit_bytes=16 * 2**20),
+        cost_estimate=COST,
+    )(rank, tokens, gain, grad, residual, dispatch, back, *parts)
 
 
 def add_low_kernel(a_ref, b_ref, out_ref):
@@ -977,6 +968,10 @@
         compiler_params=pltpu.CompilerParams(vmem_limit_bytes=6 * 2**20),
         cost_estimate=COST,
     )(a, b)
+
+
+def after(value, *others):
+    return lax.optimization_barrier((value, *others))[0]
 
 
 def tie(*values):
@@ -1165,18 +1160,17 @@
         expert_up_near, expert_down_near, output_got, expert_got
     )
     own_b, up_grad, down_grad, near_far = tie(own_b, up_grad, down_grad, near_far)
+    pieces = (own_a, swap(own_a, "dp", 1), own_b, swap(own_b, "dp", 1))
+    token_grad, block_out = close(
+        rank_cell[0], tokens, first_gain, grad_res, residual, dispatch, returned,
+        (near_kept, near_core, near_far),
+    )
     norm_sums = own_b[-SUM_ROWS:].astype(f32)
     norm_sums = norm_sums[: SUM_ROWS // 2] + norm_sums[SUM_ROWS // 2 :]
     for step in steps:
         norm_sums = norm_sums + swap(norm_sums, "tensor", step)
-    pieces = (own_a, swap(own_a, "dp", 1), own_b, swap(own_b, "dp", 1))
-    token_grad = close(
-        rank_cell[0], tokens, first_gain, grad_res, (near_kept, near_core, near_far)
-    )
     for step in dp_steps[:-1]:
         output_sum = add_low(output_sum, swap(output_sum, "dp", step))
-
-    block_out = block_output(residual, dispatch, returned)
     query_grad, key_grad, value_grad = finish(groups, bit_cell, pieces)
     return (
         block_out,

time: 238 us -> 236 us (level)
  Pallas kernels: 141 us -> 126 us
  starting transfers between devices: 43 us -> 56.8 us
  waiting for transfers between devices: 45.8 us -> 43.4 us
    ppermute x32, starting transfers between devices: 20.9 us -> 31 us  [swap(): return lax.ppermute(values, axis, [(i, i ^ step) for i in range(count)])]
    pallas_call x2, Pallas kernels: 41.1 us -> 32.3 us  [attend_back(): pl.pallas_call(functools.partial(backward_kernel, first_head, heads, bloc...]
    pallas_call x2, Pallas kernels: 22.1 us -> 17 us  [attend(): pl.pallas_call(functools.partial(forward_kernel, first, blocks), out_shap...]
    all_to_all x4, starting transfers between devices: 22.1 us -> 25.8 us  [exchange(): lax.all_to_all(rows.reshape(sources, -1, width), 'dp', split_axis=0, conc...]
  transfers between devices with their start and end apart: 36 -> 36, of which waited for: 13 -> 15; matrix products, arithmetic and copies ran while one was open for 1% -> 1% of each run, Pallas kernels for 54% -> 49%
where the time goes in v11:
time: 236 us; the launch traced here: 235 us
  Pallas kernels  126 us (53%)
  starting transfers between devices  56.8 us (24%)
  waiting for transfers between devices  43.4 us (18%)
  local copies, waits for them, and re-layouts  6.64 us (3%)
    pallas_call x2, Pallas kernels, attend_back(): pl.pallas_call(functools.partial(backward_kernel, first_head, heads, bloc...  32.3 us
    ppermute x32, starting transfers between devices, swap(): return lax.ppermute(values, axis, [(i, i ^ step) for i in range(count)])  31 us
    ppermute x32, waiting for transfers between devices, swap(): return lax.ppermute(values, axis, [(i, i ^ step) for i in range(count)])  28.5 us
    all_to_all x4, starting transfers between devices, exchange(): lax.all_to_all(rows.reshape(sources, -1, width), 'dp', split_axis=0, conc...  25.8 us
    pallas_call x2, Pallas kernels, attend(): pl.pallas_call(functools.partial(forward_kernel, first, blocks), out_shap...  17 us
    all_to_all x4, waiting for transfers between devices, exchange(): lax.all_to_all(rows.reshape(sources, -1, width), 'dp', split_axis=0, conc...  14.9 us
    pallas_call x1, Pallas kernels, expert_weights(): pl.pallas_call(functools.partial(weight_kernel, len(groups)), grid=(2,),...  11.8 us
    pallas_call x1, Pallas kernels, expert(): pl.pallas_call(functools.partial(expert_kernel, parts), out_shape=(jax.Sh...  11.1 us
  transfers between devices with their start and end apart: 36, of which 15 were waited for; matrix products, arithmetic and copies ran while one was open for 1% of the time, Pallas kernels for 49%

profile of v11, /device:TPU:0, one launch (start us, length us, event | category | flops | bytes accessed | tf_op | source)
XLA Modules:
  0.0 235.1 jit_solution(16782328253634088562)
XLA Ops:
  0.7 3.3 %plan.1 = (bf16[512,512]{1,0:T(8,128)(2,1)}, bf16[512,768]{1,0:T(8,128)(2,1)}) custom-call(s32[1,5]{1,0:T(1,128)} %lens_ref.11, s32[1,1]{1,0:T(1,128)} %bitcast.1.rank_ref, s32[1,512]{1,0:T(1,128)} %bitcast.50, s32[1,512]{1,0:T(1,128)} %order_ref.1, bf16[512,768]{1,0:T(8,128)(2,1)} %cotangent_ref.1), custom_call_target="tpu_custom_call" | custom-call | flops 1048576 | bytes 1048576 | tf_op jit(solution)/shard_map/plan/pallas_call | solution.py:470
  3.9 7.3 %all-to-all-start.1 = ((bf16[8,64,768]{2,1,0:T(8,128)(2,1)}), bf16[8,64,768]{2,1,0:T(8,128)(2,1)S(1)}, u32[]{:S(2)}, u32[]{:S(2)}) async-start(bf16[8,64,768]{2,1,0:T(8,128)(2,1)} %bitcast.48), calls=%async_computation.1 | async-start | bytes 1572864 | tf_op jit(solution)/shard_map/all_to_all | solution.py:1043
  13.4 7.5 %project.1 = (bf16[2048,768]{1,0:T(8,128)(2,1)}, bf16[192,2048]{1,0:T(8,128)(2,1)}, bf16[192,2048]{1,0:T(8,128)(2,1)}, bf16[192,2048]{1,0:T(8,128)(2,1)}) custom-call(s32[1]{0:T(128)} %bitcast.rank_ref, bf16[2048,768]{1,0:T(8,128)(2,1)} %tokens_ref.2, f32[768]{0:T(1024)} %gain_ref.7, f32[768]{0:T(1024)} %bias_ref.2, bf16[192,768]{1,0:T(8,128)(2,1)} %bitcast.22, ...), custom_call_target="tpu_custom_call" | custom-call | flops 1048576 | bytes 1048576 | tf_op jit(solution)/shard_map/project/pallas_call | solution.py:81
  20.9 8.5 %attend.2 = (bf16[192,512]{1,0:T(8,128)(2,1)}, bf16[192,512]{1,0:T(8,128)(2,1)}, f32[3,1,1024]{2,1,0:T(1,128)}) custom-call(s32[1,5]{1,0:T(1,128)} %lens_ref.11, s32[1,1]{1,0:T(1,128)} %bitcast.1.rank_ref, bf16[192,2048]{1,0:T(8,128)(2,1)} %get-tuple-element.130.qt_ref, bf16[192,2048]{1,0:T(8,128)(2,1)} %get-tuple-element.135.kt_ref, ...), custom_call_target="tpu_custom_call" | custom-call | flops 1048576 | bytes 1048576 | tf_op jit(solution)/shard_map/attend/pallas_call | solution.py:239
  30.9 8.5 %attend.3 = (bf16[192,512]{1,0:T(8,128)(2,1)}, bf16[192,512]{1,0:T(8,128)(2,1)}, f32[3,1,1024]{2,1,0:T(1,128)}) custom-call(s32[1,5]{1,0:T(1,128)} %lens_ref.11, s32[1,1]{1,0:T(1,128)} %bitcast.1.rank_ref, bf16[192,2048]{1,0:T(8,128)(2,1)} %get-tuple-element.130.qt_ref, bf16[192,2048]{1,0:T(8,128)(2,1)} %get-tuple-element.135.kt_ref, ...), custom_call_target="tpu_custom_call" | custom-call | flops 1048576 | bytes 1048576 | tf_op jit(solution)/shard_map/attend/pallas_call | solution.py:239
  42.6 4.8 %middle.1 = (f32[512,768]{1,0:T(8,128)}, bf16[512,768]{1,0:T(8,128)(2,1)}) custom-call(s32[1]{0:T(128)} %bitcast.rank_ref, bf16[2048,768]{1,0:T(8,128)(2,1)} %tokens_ref.2, f32[768]{0:T(1024)} %gain_ref.6, f32[768]{0:T(1024)} %bias_ref.3, bf16[512,512]{1,0:T(8,128)(2,1)} %get-tuple-element.129.dispatch_ref, ...), custom_call_target="tpu_custom_call" | custom-call | flops 1048576 | bytes 1048576 | tf_op jit(solution)/shard_map/middle/pallas_call | solution.py:507
  47.4 9.8 %all-to-all-start = ((bf16[8,64,768]{2,1,0:T(8,128)(2,1)}), bf16[8,64,768]{2,1,0:T(8,128)(2,1)S(1)}, u32[]{:S(2)}, u32[]{:S(2)}) async-start(bf16[8,64,768]{2,1,0:T(8,128)(2,1)} %bitcast.49), calls=%async_computation | async-start | bytes 1572864 | tf_op jit(solution)/shard_map/all_to_all | solution.py:1043
  57.3 6.5 %activation_grads.1.grad_act_ref = bf16[512,3072]{1,0:T(8,128)(2,1)} custom-call(bf16[512,768]{1,0:T(8,128)(2,1)} %bitcast.44, bf16[3072,768]{1,0:T(8,128)(2,1)} %bitcast.41), custom_call_target="tpu_custom_call" | custom-call | flops 1048576 | bytes 1048576 | tf_op jit(solution)/shard_map/activation_grads/pallas_call | solution.py:625
  63.8 14.0 %all-to-all-done = bf16[8,64,768]{2,1,0:T(8,128)(2,1)S(1)} async-done(((bf16[8,64,768]{2,1,0:T(8,128)(2,1)}), bf16[8,64,768]{2,1,0:T(8,128)(2,1)S(1)}, u32[]{:S(2)}, u32[]{:S(2)}) %all-to-all-start) | async-done | bytes 786464 | tf_op jit(solution)/shard_map/all_to_all | solution.py:1043
  77.9 11.1 %expert.1 = (bf16[512,1536]{1,0:T(8,128)(2,1)}, bf16[512,1536]{1,0:T(8,128)(2,1)}, bf16[512,1536]{1,0:T(8,128)(2,1)}, bf16[512,1536]{1,0:T(8,128)(2,1)}, bf16[512,768]{1,0:T(8,128)(2,1)}) custom-call(s32[1,1]{1,0:T(1,128)} %bitcast.1.rank_ref, bf16[512,768]{1,0:T(8,128)(2,1)S(1)} %bitcast.38, bf16[512,3072]{1,0:T(8,128)(2,1)} %activation_grads.1.grad_act_ref, ...), custom_call_target="tpu_custom_call" | custom-call | flops 1048576 | bytes 1048576 | tf_op jit(solution)/shard_map/expert/pallas_call | solution.py:701
  90.5 3.7 %all-to-all-start.2 = ((bf16[8,64,768]{2,1,0:T(8,128)(2,1)}), bf16[8,64,768]{2,1,0:T(8,128)(2,1)S(1)}, u32[]{:S(2)}, u32[]{:S(2)}) async-start(bf16[8,64,768]{2,1,0:T(8,128)(2,1)} %bitcast.12), calls=%async_computation.2 | async-start | bytes 1572864 | tf_op jit(solution)/shard_map/all_to_all | solution.py:1043
  94.3 6.5 %product.1 = bf16[512,768]{1,0:T(8,128)(2,1)} custom-call(s32[1,1]{1,0:T(1,128)} %bitcast.1.rank_ref, bf16[512,1536]{1,0:T(8,128)(2,1)} %get-tuple-element.158.kept_ref.refs_2_, bf16[512,1536]{1,0:T(8,128)(2,1)} %get-tuple-element.159.sent_ref, bf16[3072,768]{1,0:T(8,128)(2,1)} %bitcast.42), custom_call_target="tpu_custom_call" | custom-call | flops 1048576 | bytes 1048576 | tf_op jit(solution)/shard_map/product/pallas_call | solution.py:752
  101.9 11.8 %expert_weights.1 = (bf16[384,768]{1,0:T(8,128)(2,1)}, bf16[1152,768]{1,0:T(8,128)(2,1)}, f32[768,768]{1,0:T(8,128)}, f32[768,768]{1,0:T(8,128)}) custom-call(bf16[512,768]{1,0:T(8,128)(2,1)} %bitcast.39, bf16[512,768]{1,0:T(8,128)(2,1)} %bitcast.45, bf16[512,1536]{1,0:T(8,128)(2,1)} %get-tuple-element.158.kept_ref.refs_2_, ...), custom_call_target="tpu_custom_call" | custom-call | flops 1048576 | bytes 1048576 | tf_op jit(solution)/shard_map/expert_weights/pallas_call | solution.py:796
  115.5 6.5 %turn.1 = (f32[512,768]{1,0:T(8,128)}, f32[2,768]{1,0:T(2,128)}, bf16[2,192,768]{2,1,0:T(8,128)(2,1)}, bf16[2,192,768]{2,1,0:T(8,128)(2,1)}, bf16[192,512]{1,0:T...) custom-call(s32[1,5]{1,0:T(1,128)} %lens_ref.11, ...), custom_call_target="tpu_custom_call" | custom-call | flops 1048576 | bytes 1048576 | tf_op jit(solution)/shard_map/turn/pallas_call | solution.py:564
  124.1 5.1 %all-to-all-start.3 = ((bf16[8,64,768]{2,1,0:T(8,128)(2,1)}), bf16[8,64,768]{2,1,0:T(8,128)(2,1)S(1)}, u32[]{:S(2)}, u32[]{:S(2)}) async-start(bf16[8,64,768]{2,1,0:T(8,128)(2,1)} %bitcast.15), calls=%async_computation.3 | async-start | bytes 1572864 | tf_op jit(solution)/shard_map/all_to_all | solution.py:1043
  134.5 19.2 %attend_back.2 = (bf16[2048,384]{1,0:T(8,128)(2,1)}, f32[2,768]{1,0:T(2,128)}, bf16[192,768]{1,0:T(8,128)(2,1)}, bf16[192,768]{1,0:T(8,128)(2,1)}) custom-call(s32[1,5]{1,0:T(1,128)} %lens_ref.11, s32[1,1]{1,0:T(1,128)} %bitcast.1.rank_ref, s32[1,1]{1,0:T(1,128)} %bitcast.14.bit_ref, bf16[192,2048]{1,0:T(8,128)(2,1)} %get-tuple-element.130.qt_ref, ...), custom_call_target="tpu_custom_call" | custom-call | flops 1048576 | bytes 1048576 | tf_op jit(solution)/shard_map/attend_back/pallas_call | solution.py:408
  157.3 3.6 %collective-permute-start.16 = (bf16[192,768]{1,0:T(8,128)(2,1)S(1)}, bf16[192,768]{1,0:T(8,128)(2,1)}, u32[]{:S(2)}, u32[]{:S(2)}) collective-permute-start(bf16[192,768]{1,0:T(8,128)(2,1)S(1)} %add_low.9.a_ref), channel_id=1, source_target_pairs={{0,16},{4,20},{8,24},{12,28},{16,0},{20,4},{24,8},{28,12},{1,17},{... | collective-permute-start | bytes 884744 | tf_op jit(solution)/shard_map/ppermute | solution.py:38
  160.9 13.0 %attend_back.3 = (bf16[2048,192]{1,0:T(8,128)(2,1)}, f32[2,768]{1,0:T(2,128)}, bf16[112,768]{1,0:T(8,128)(2,1)}, bf16[112,768]{1,0:T(8,128)(2,1)}) custom-call(s32[1,5]{1,0:T(1,128)} %lens_ref.11, s32[1,1]{1,0:T(1,128)} %bitcast.1.rank_ref, s32[1,1]{1,0:T(1,128)} %bitcast.14.bit_ref, bf16[192,2048]{1,0:T(8,128)(2,1)} %get-tuple-element.130.qt_ref, ...), custom_call_target="tpu_custom_call" | custom-call | flops 1048576 | bytes 1048576 | tf_op jit(solution)/shard_map/attend_back/pallas_call | solution.py:408
  179.2 3.1 %collective-permute-start.17 = (bf16[192,768]{1,0:T(8,128)(2,1)S(1)}, bf16[192,768]{1,0:T(8,128)(2,1)S(1)}, u32[]{:S(2)}, u32[]{:S(2)}) collective-permute-start(bf16[192,768]{1,0:T(8,128)(2,1)S(1)} %add_low.8.a_ref), channel_id=1, source_target_pairs={{0,8},{4,12},{8,0},{12,4},{16,24},{20,28},{24,16},{28,20},{1,9},{5... | collective-permute-start | bytes 884744 | tf_op jit(solution)/shard_map/ppermute | solution.py:38
  182.8 5.8 %collective-permute-done.18.b_ref = bf16[112,768]{1,0:T(8,128)(2,1)S(1)} collective-permute-done((bf16[112,768]{1,0:T(8,128)(2,1)S(1)}, bf16[112,768]{1,0:T(8,128)(2,1)S(1)}, u32[]{:S(2)}, u32[]{:S(2)}) %collective-permute-start.18) | collective-permute-done | bytes 172064 | tf_op jit(solution)/shard_map/ppermute | solution.py:38
  194.1 3.3 %collective-permute-done.21.b_ref = bf16[112,768]{1,0:T(8,128)(2,1)S(1)} collective-permute-done((bf16[112,768]{1,0:T(8,128)(2,1)S(1)}, bf16[112,768]{1,0:T(8,128)(2,1)S(1)}, u32[]{:S(2)}, u32[]{:S(2)}) %collective-permute-start.21) | collective-permute-done | bytes 172064 | tf_op jit(solution)/shard_map/ppermute | solution.py:38
  197.5 4.2 %collective-permute-start.23 = (bf16[112,768]{1,0:T(8,128)(2,1)S(1)}, bf16[112,768]{1,0:T(8,128)(2,1)S(1)}, u32[]{:S(2)}, u32[]{:S(2)}) collective-permute-start(bf16[112,768]{1,0:T(8,128)(2,1)S(1)} %add_parts.4.a_ref), channel_id=1, source_target_pairs={{0,16},{4,20},{8,24},{12,28},{16,0},{20,4},{24,8},{28,12},{1,17},{... | collective-permute-start | bytes 516104 | tf_op jit(solution)/shard_map/ppermute | solution.py:38
  205.9 6.5 %expert_sums.1 = (f32[768,768]{1,0:T(8,128)}, f32[768,768]{1,0:T(8,128)}) custom-call(f32[768,768]{1,0:T(8,128)S(1)} %copy-done.9, f32[768,768]{1,0:T(8,128)S(1)} %copy-done.10, bf16[576,768]{1,0:T(8,128)(2,1)S(1)} %collective-permute-done.14.b_ref.first_ref, bf16[1152,768]{1,0:T(8,128)(2,1)} %collective-permute-done.22.rest_ref), custom_call_target="tpu_custom_call" | custom-call | flops 1048576 | bytes 1048576 | tf_op jit(solution)/shard_map/expert_sums/pallas_call | solution.py:835
  212.4 4.6 %collective-permute-done.23.b_ref = bf16[112,768]{1,0:T(8,128)(2,1)S(1)} collective-permute-done((bf16[112,768]{1,0:T(8,128)(2,1)S(1)}, bf16[112,768]{1,0:T(8,128)(2,1)S(1)}, u32[]{:S(2)}, u32[]{:S(2)}) %collective-permute-start.23) | collective-permute-done | bytes 172064 | tf_op jit(solution)/shard_map/ppermute | solution.py:38
  (152 shorter events, 55.6 us)
Async XLA Ops:
  3.9 43.5 %all-to-all-start.1 = ((bf16[8,64,768]{2,1,0:T(8,128)(2,1)}), bf16[8,64,768]{2,1,0:T(8,128)(2,1)S(1)}, u32[]{:S(2)}, u32[]{:S(2)}) async-start(bf16[8,64,768]{2,1,0:T(8,128)(2,1)} %bitcast.48), calls=%async_computation.1 | async-start | bytes 1572864 | tf_op jit(solution)/shard_map/all_to_all | solution.py:1043
  11.2 28.6 %collective-permute-start.3 = (bf16[192,768]{1,0:T(8,128)(2,1)S(1)}, bf16[192,768]{1,0:T(8,128)(2,1)S(1)}, u32[]{:S(2)}, u32[]{:S(2)}) collective-permute-start(bf16[192,768]{1,0:T(8,128)(2,1)S(1)} %copy-done.19), channel_id=1, source_target_pairs={{0,2},{1,3},{2,0},{3,1},{4,6},{5,7},{6,4},{7,5},{8,10},{9,11},{10,... | collective-permute-start | bytes 884744 | tf_op jit(solution)/shard_map/ppermute | solution.py:38
  12.8 27.0 %collective-permute-start.2 = (bf16[192,768]{1,0:T(8,128)(2,1)S(1)}, bf16[192,768]{1,0:T(8,128)(2,1)S(1)}, u32[]{:S(2)}, u32[]{:S(2)}) collective-permute-start(bf16[192,768]{1,0:T(8,128)(2,1)S(1)} %copy-done.19), channel_id=1, source_target_pairs={{0,1},{1,0},{2,3},{3,2},{4,5},{5,4},{6,7},{7,6},{8,9},{9,8},{10,11... | collective-permute-start | bytes 884744 | tf_op jit(solution)/shard_map/ppermute | solution.py:38
  12.8 27.0 %collective-permute-start.4 = (bf16[192,768]{1,0:T(8,128)(2,1)S(1)}, bf16[192,768]{1,0:T(8,128)(2,1)S(1)}, u32[]{:S(2)}, u32[]{:S(2)}) collective-permute-start(bf16[192,768]{1,0:T(8,128)(2,1)S(1)} %copy-done.19), channel_id=1, source_target_pairs={{0,3},{1,2},{2,1},{3,0},{4,7},{5,6},{6,5},{7,4},{8,11},{9,10},{10,... | collective-permute-start | bytes 884744 | tf_op jit(solution)/shard_map/ppermute | solution.py:38
  47.4 30.4 %all-to-all-start = ((bf16[8,64,768]{2,1,0:T(8,128)(2,1)}), bf16[8,64,768]{2,1,0:T(8,128)(2,1)S(1)}, u32[]{:S(2)}, u32[]{:S(2)}) async-start(bf16[8,64,768]{2,1,0:T(8,128)(2,1)} %bitcast.49), calls=%async_computation | async-start | bytes 1572864 | tf_op jit(solution)/shard_map/all_to_all | solution.py:1043
  57.2 20.7 %collective-permute-start.6 = (bf16[512,768]{1,0:T(8,128)(2,1)S(1)}, bf16[512,768]{1,0:T(8,128)(2,1)S(1)}, u32[]{:S(2)}, u32[]{:S(2)}) collective-permute-start(bf16[512,768]{1,0:T(8,128)(2,1)S(1)} %bitcast.43), channel_id=1, source_target_pairs={{0,1},{1,0},{2,3},{3,2},{4,5},{5,4},{6,7},{7,6},{8,9},{9,8},{10,11... | collective-permute-start | bytes 2359304 | tf_op jit(solution)/shard_map/ppermute | solution.py:38
  77.9 11.2 %collective-permute-start.7 = (bf16[512,768]{1,0:T(8,128)(2,1)S(1)}, bf16[512,768]{1,0:T(8,128)(2,1)S(1)}, u32[]{:S(2)}, u32[]{:S(2)}) collective-permute-start(bf16[512,768]{1,0:T(8,128)(2,1)S(1)} %bitcast.37), channel_id=1, source_target_pairs={{0,1},{1,0},{2,3},{3,2},{4,5},{5,4},{6,7},{7,6},{8,9},{9,8},{10,11... | collective-permute-start | bytes 2359304 | tf_op jit(solution)/shard_map/ppermute | solution.py:38
  90.0 10.7 %collective-permute-start.9 = (bf16[512,1536]{1,0:T(8,128)(2,1)}, bf16[512,1536]{1,0:T(8,128)(2,1)S(1)}, u32[]{:S(2)}, u32[]{:S(2)}) collective-permute-start(bf16[512,1536]{1,0:T(8,128)(2,1)} %get-tuple-element.160), channel_id=1, source_target_pairs={{0,1},{1,0},{2,3},{3,2},{4,5},{5,4},{6,7},{7,6},{8,9},{9,8},{10,11... | collective-permute-start | bytes 4718600 | tf_op jit(solution)/shard_map/ppermute | solution.py:38
  90.0 10.8 %collective-permute-start.8 = (bf16[512,1536]{1,0:T(8,128)(2,1)}, bf16[512,1536]{1,0:T(8,128)(2,1)}, u32[]{:S(2)}, u32[]{:S(2)}) collective-permute-start(bf16[512,1536]{1,0:T(8,128)(2,1)} %get-tuple-element.159.sent_ref), channel_id=1, source_target_pairs={{0,1},{1,0},{2,3},{3,2},{4,5},{5,4},{6,7},{7,6},{8,9},{9,8},{10,11... | collective-permute-start | bytes 4718600 | tf_op jit(solution)/shard_map/ppermute | solution.py:38
  90.5 24.1 %all-to-all-start.2 = ((bf16[8,64,768]{2,1,0:T(8,128)(2,1)}), bf16[8,64,768]{2,1,0:T(8,128)(2,1)S(1)}, u32[]{:S(2)}, u32[]{:S(2)}) async-start(bf16[8,64,768]{2,1,0:T(8,128)(2,1)} %bitcast.12), calls=%async_computation.2 | async-start | bytes 1572864 | tf_op jit(solution)/shard_map/all_to_all | solution.py:1043
  122.1 10.2 %collective-permute-start.10 = (bf16[192,512]{1,0:T(8,128)(2,1)}, bf16[192,512]{1,0:T(8,128)(2,1)S(1)}, u32[]{:S(2)}, u32[]{:S(2)}) collective-permute-start(bf16[192,512]{1,0:T(8,128)(2,1)} %get-tuple-element.176), channel_id=1, source_target_pairs={{0,1},{1,0},{2,3},{3,2},{4,5},{5,4},{6,7},{7,6},{8,9},{9,8},{10,11... | collective-permute-start | bytes 589832 | tf_op jit(solution)/shard_map/ppermute | solution.py:38
  124.1 29.7 %all-to-all-start.3 = ((bf16[8,64,768]{2,1,0:T(8,128)(2,1)}), bf16[8,64,768]{2,1,0:T(8,128)(2,1)S(1)}, u32[]{:S(2)}, u32[]{:S(2)}) async-start(bf16[8,64,768]{2,1,0:T(8,128)(2,1)} %bitcast.15), calls=%async_computation.3 | async-start | bytes 1572864 | tf_op jit(solution)/shard_map/all_to_all | solution.py:1043
  133.0 22.7 %collective-permute-start.14 = (bf16[576,768]{1,0:T(8,128)(2,1)}, bf16[576,768]{1,0:T(8,128)(2,1)S(1)}, u32[]{:S(2)}, u32[]{:S(2)}) collective-permute-start(bf16[576,768]{1,0:T(8,128)(2,1)} %get-tuple-element.191), channel_id=1, source_target_pairs={{0,2},{1,3},{2,0},{3,1},{4,6},{5,7},{6,4},{7,5},{8,10},{9,11},{10,... | collective-permute-start | bytes 2654216 | tf_op jit(solution)/shard_map/ppermute | solution.py:38
  155.7 41.8 %collective-permute-start.22 = (bf16[1152,768]{1,0:T(8,128)(2,1)}, bf16[1152,768]{1,0:T(8,128)(2,1)}, u32[]{:S(2)}, u32[]{:S(2)}) collective-permute-start(bf16[1152,768]{1,0:T(8,128)(2,1)} %get-tuple-element.223), channel_id=1, source_target_pairs={{0,2},{1,3},{2,0},{3,1},{4,6},{5,7},{6,4},{7,5},{8,10},{9,11},{10,... | collective-permute-start | bytes 5308424 | tf_op jit(solution)/shard_map/ppermute | solution.py:38
  157.3 17.6 %collective-permute-start.16 = (bf16[192,768]{1,0:T(8,128)(2,1)S(1)}, bf16[192,768]{1,0:T(8,128)(2,1)}, u32[]{:S(2)}, u32[]{:S(2)}) collective-permute-start(bf16[192,768]{1,0:T(8,128)(2,1)S(1)} %add_low.9.a_ref), channel_id=1, source_target_pairs={{0,16},{4,20},{8,24},{12,28},{16,0},{20,4},{24,8},{28,12},{1,17},{... | collective-permute-start | bytes 884744 | tf_op jit(solution)/shard_map/ppermute | solution.py:38
  160.9 15.1 %collective-permute-start.15 = (bf16[192,768]{1,0:T(8,128)(2,1)}, bf16[192,768]{1,0:T(8,128)(2,1)S(1)}, u32[]{:S(2)}, u32[]{:S(2)}) collective-permute-start(bf16[192,768]{1,0:T(8,128)(2,1)} %get-tuple-element.205), channel_id=1, source_target_pairs={{0,4},{4,0},{8,12},{12,8},{16,20},{20,16},{24,28},{28,24},{1,5},{5... | collective-permute-start | bytes 884744 | tf_op jit(solution)/shard_map/ppermute | solution.py:38
  179.1 10.8 %collective-permute-start.20 = (bf16[1,512,768]{2,1,0:T(8,128)(2,1)S(1)}, bf16[1,512,768]{2,1,0:T(8,128)(2,1)S(1)}, u32[]{:S(2)}, u32[]{:S(2)}) collective-permute-start(bf16[1,512,768]{2,1,0:T(8,128)(2,1)S(1)} %get-tuple-element.217), channel_id=1, source_target_pairs={{0,1},{1,0},{2,3},{3,2},{4,5},{5,4},{6,7},{7,6},{8,9},{9,8},{10,11... | collective-permute-start | bytes 2359304 | tf_op jit(solution)/shard_map/ppermute | solution.py:38
  179.2 10.6 %collective-permute-start.17 = (bf16[192,768]{1,0:T(8,128)(2,1)S(1)}, bf16[192,768]{1,0:T(8,128)(2,1)S(1)}, u32[]{:S(2)}, u32[]{:S(2)}) collective-permute-start(bf16[192,768]{1,0:T(8,128)(2,1)S(1)} %add_low.8.a_ref), channel_id=1, source_target_pairs={{0,8},{4,12},{8,0},{12,4},{16,24},{20,28},{24,16},{28,20},{1,9},{5... | collective-permute-start | bytes 884744 | tf_op jit(solution)/shard_map/ppermute | solution.py:38
  190.1 26.9 %collective-permute-start.24 = (bf16[1,512,768]{2,1,0:T(8,128)(2,1)S(1)}, bf16[1,512,768]{2,1,0:T(8,128)(2,1)S(1)}, u32[]{:S(2)}, u32[]{:S(2)}) collective-permute-start(bf16[1,512,768]{2,1,0:T(8,128)(2,1)S(1)} %add_low.11), channel_id=1, source_target_pairs={{0,2},{1,3},{2,0},{3,1},{4,6},{5,7},{6,4},{7,5},{8,10},{9,11},{10,... | collective-permute-start | bytes 2359304 | tf_op jit(solution)/shard_map/ppermute | solution.py:38
  193.3 10.5 %collective-permute-start.30 = (bf16[192,768]{1,0:T(8,128)(2,1)S(1)}, bf16[192,768]{1,0:T(8,128)(2,1)S(1)}, u32[]{:S(2)}, u32[]{:S(2)}) collective-permute-start(bf16[192,768]{1,0:T(8,128)(2,1)S(1)} %add_low.10.a_ref), channel_id=1, source_target_pairs={{0,4},{4,0},{8,12},{12,8},{16,20},{20,16},{24,28},{28,24},{1,5},{5... | collective-permute-start | bytes 884744 | tf_op jit(solution)/shard_map/ppermute | solution.py:38
  197.5 19.4 %collective-permute-start.23 = (bf16[112,768]{1,0:T(8,128)(2,1)S(1)}, bf16[112,768]{1,0:T(8,128)(2,1)S(1)}, u32[]{:S(2)}, u32[]{:S(2)}) collective-permute-start(bf16[112,768]{1,0:T(8,128)(2,1)S(1)} %add_parts.4.a_ref), channel_id=1, source_target_pairs={{0,16},{4,20},{8,24},{12,28},{16,0},{20,4},{24,8},{28,12},{1,17},{... | collective-permute-start | bytes 516104 | tf_op jit(solution)/shard_map/ppermute | solution.py:38
  203.6 21.5 %collective-permute-start.19 = (bf16[1,512,768]{2,1,0:T(8,128)(2,1)S(1)}, bf16[1,512,768]{2,1,0:T(8,128)(2,1)S(1)}, u32[]{:S(2)}, u32[]{:S(2)}) collective-permute-start(bf16[1,512,768]{2,1,0:T(8,128)(2,1)S(1)} %get-tuple-element.215), channel_id=1, source_target_pairs={{0,1},{1,0},{2,3},{3,2},{4,5},{5,4},{6,7},{7,6},{8,9},{9,8},{10,11... | collective-permute-start | bytes 2359304 | tf_op jit(solution)/shard_map/ppermute | solution.py:38
  203.6 18.3 %collective-permute-start.27 = (bf16[192,768]{1,0:T(8,128)(2,1)S(1)}, bf16[192,768]{1,0:T(8,128)(2,1)S(1)}, u32[]{:S(2)}, u32[]{:S(2)}) collective-permute-start(bf16[192,768]{1,0:T(8,128)(2,1)S(1)} %add_low.12.a_ref), channel_id=1, source_target_pairs={{0,16},{4,20},{8,24},{12,28},{16,0},{20,4},{24,8},{28,12},{1,17},{... | collective-permute-start | bytes 884744 | tf_op jit(solution)/shard_map/ppermute | solution.py:38
  203.8 19.2 %collective-permute-start.31 = (bf16[192,768]{1,0:T(8,128)(2,1)S(1)}, bf16[192,768]{1,0:T(8,128)(2,1)S(1)}, u32[]{:S(2)}, u32[]{:S(2)}) collective-permute-start(bf16[192,768]{1,0:T(8,128)(2,1)S(1)} %add_low.14.a_ref), channel_id=1, source_target_pairs={{0,8},{4,12},{8,0},{12,4},{16,24},{20,28},{24,16},{28,20},{1,9},{5... | collective-permute-start | bytes 884744 | tf_op jit(solution)/shard_map/ppermute | solution.py:38
  (46 other events, 320.9 us)

commit v12 on v11

--- a/solution.py
+++ b/solution.py
@@ -765,88 +765,76 @@
     )(rank.reshape(1, 1), kept, sent, down)
 
 
-def weight_kernel(groups, *refs):
-    first_ref, rest_ref, up_ref, down_ref = refs[-4:]
+def group_sums(refs, groups):
     dup = ddown = 0.0
     for g in range(groups):
         in_ref, grad_ref, act_ref, pre_ref = refs[4 * g : 4 * g + 4]
         dup = dup + contract_rows(in_ref[...], pre_ref[...])
         ddown = ddown + contract_rows(act_ref[...], grad_ref[...])
-    cut = first_ref.shape[0]
-
-    @pl.when(pl.program_id(0) == 0)
-    def far():
-        first_ref[...] = dup[:cut].astype(bf16)
-        rest_ref[: dup.shape[0] - cut, :] = dup[cut:].astype(bf16)
-        rest_ref[dup.shape[0] - cut :, :] = ddown.astype(bf16)
-
-    @pl.when(pl.program_id(0) == 1)
-    def near():
-        up_ref[...] = dup
-        down_ref[...] = ddown
-
-
-def expert_weights(groups):
+    return dup, ddown
+
+
+def group_specs(groups, part):
     count, width = groups[0][0].shape
     size = groups[0][2].shape[1] // 2
     fixed = pl.BlockSpec((count, width), lambda i: (0, 0))
-    columns = pl.BlockSpec((count, size), lambda i: (0, 1 - i))
+    columns = pl.BlockSpec((count, size), lambda i: (0, part))
+    return [fixed, fixed, columns, columns] * len(groups)
+
+
+def far_weight_kernel(groups, *refs):
+    first_ref, rest_ref = refs[-2:]
+    dup, ddown = group_sums(refs, groups)
+    cut = first_ref.shape[0]
+    first_ref[...] = dup[:cut].astype(bf16)
+    rest_ref[: dup.shape[0] - cut, :] = dup[cut:].astype(bf16)
+    rest_ref[dup.shape[0] - cut :, :] = ddown.astype(bf16)
+
+
+def far_weights(groups):
+    width = groups[0][0].shape[1]
+    size = groups[0][2].shape[1] // 2
     cut = (width + size) // 4
-    shapes = ((cut, size), (width + size - cut, size), (width, size), (size, width))
-    return pl.pallas_call(
-        functools.partial(weight_kernel, len(groups)),
-        grid=(2,),
-        in_specs=[fixed, fixed, columns, columns] * len(groups),
+    shapes = ((cut, size), (width + size - cut, size))
+    return pl.pallas_call(
+        functools.partial(far_weight_kernel, len(groups)),
+        grid=(1,),
+        in_specs=group_specs(groups, 1),
         out_specs=tuple(pl.BlockSpec(shape, lambda i: (0, 0)) for shape in shapes),
-        out_shape=tuple(
-            jax.ShapeDtypeStruct(shape, bf16 if k < 2 else f32)
-            for k, shape in enumerate(shapes)
+        out_shape=tuple(jax.ShapeDtypeStruct(shape, bf16) for shape in shapes),
+        name="far_weights",
+        cost_estimate=COST,
+    )(*[values for group in groups for values in group])
+
+
+def near_weight_kernel(groups, skip, *refs):
+    first_ref, rest_ref, up_ref, down_ref = refs[-4:]
+    dup, ddown = group_sums(refs, groups)
+    cut = first_ref.shape[0] - skip
+    down_at = dup.shape[0] - cut
+    up_ref[:cut, :] = dup[:cut] + first_ref[skip:, :].astype(f32)
+    up_ref[cut:, :] = dup[cut:] + rest_ref[:down_at, :].astype(f32)
+    down_ref[...] = ddown + rest_ref[down_at:, :].astype(f32)
+
+
+def near_weights(groups, first, rest):
+    width = groups[0][0].shape[1]
+    size = groups[0][2].shape[1] // 2
+    skip = first.shape[0] + rest.shape[0] - width - size
+    whole = lambda shape: pl.BlockSpec(shape, lambda i: (0, 0))
+    return pl.pallas_call(
+        functools.partial(near_weight_kernel, len(groups), skip),
+        grid=(1,),
+        in_specs=group_specs(groups, 0) + [whole(first.shape), whole(rest.shape)],
+        out_specs=(whole((width, size)), whole((size, width))),
+        out_shape=(
+            jax.ShapeDtypeStruct((width, size), f32),
+            jax.ShapeDtypeStruct((size, width), f32),
         ),
-        name="expert_weights",
-        compiler_params=pltpu.CompilerParams(vmem_limit_bytes=60 * 2**20),
-        cost_estimate=COST,
-    )(*[values for group in groups for values in group])
-
-
-def expert_sum_kernel(near_up_ref, near_down_ref, first_ref, rest_ref, up_ref, down_ref):
-    step = pl.program_id(0)
-    half = pl.num_programs(0) // 2
-    far = jnp.where(step < half // 2, first_ref[...], rest_ref[...]).astype(f32)
-
-    @pl.when(step < half)
-    def upper():
-        up_ref[...] = near_up_ref[...] + far
-
-    @pl.when(step >= half)
-    def lower():
-        down_ref[...] = near_down_ref[...] + far
-
-
-def expert_sums(near_up, near_down, first, rest):
-    count, width = near_up.shape
-    steps = 8
-    half = steps // 2
-    size = count // half
-    head = steps // 4
-    skip = first.shape[0] // size - head
-    block = lambda place: pl.BlockSpec((size, width), lambda i: (place(i), 0))
-    upper = block(lambda i: jnp.minimum(i, half - 1))
-    lower = block(lambda i: jnp.maximum(i - half, 0))
-    return pl.pallas_call(
-        expert_sum_kernel,
-        grid=(steps,),
-        out_shape=(jax.ShapeDtypeStruct((count, width), f32),) * 2,
-        in_specs=[
-            upper,
-            lower,
-            block(lambda i: jnp.minimum(i, head - 1) + skip),
-            block(lambda i: jnp.maximum(i - head, 0)),
-        ],
-        out_specs=(upper, lower),
-        name="expert_sums",
-        compiler_params=pltpu.CompilerParams(vmem_limit_bytes=10 * 2**20),
-        cost_estimate=COST,
-    )(near_up, near_down, first, rest)
+        name="near_weights",
+        compiler_params=pltpu.CompilerParams(vmem_limit_bytes=52 * 2**20),
+        cost_estimate=COST,
+    )(*[values for group in groups for values in group], first, rest)
 
 
 def input_grad_kernel(groups, qw_ref, kw_ref, vw_ref, *refs):
@@ -1093,9 +1081,10 @@
     near_pre = swap(pre_sent, "tensor", 1)
     made = product(rank_cell[0], act, act_sent, down_matrix, members)
     made, near_act, near_pre = tie(made, near_act, near_pre)
-    *expert_far, expert_up_near, expert_down_near = expert_weights(
-        [(flat_in, flat_grad, act, grad_pre), (near_rows, near_grads, near_act, near_pre)]
-    )
+    expert_groups = [
+        (flat_in, flat_grad, act, grad_pre), (near_rows, near_grads, near_act, near_pre)
+    ]
+    expert_far = list(far_weights(expert_groups))
     grad_back, made, expert_far = tie(grad_back, made, expert_far)
 
     steps = steps_of(members)
@@ -1156,9 +1145,7 @@
         own_b = add_parts(own_b, swap(own_b, "dp", step))
         if step == dp_steps[1]:
             own_b, expert_got = tie(own_b, expert_got)
-    up_grad, down_grad = expert_sums(
-        expert_up_near, expert_down_near, output_got, expert_got
-    )
+    up_grad, down_grad = near_weights(expert_groups, output_got, expert_got)
     own_b, up_grad, down_grad, near_far = tie(own_b, up_grad, down_grad, near_far)
     pieces = (own_a, swap(own_a, "dp", 1), own_b, swap(own_b, "dp", 1))
     token_grad, block_out = close(

time: 236 us -> 235 us (level)
  starting transfers between devices: 56.8 us -> 36.3 us
  waiting for transfers between devices: 43.4 us -> 54.1 us
  Pallas kernels: 126 us -> 135 us
    ppermute x32, starting transfers between devices: 31 us -> 16.7 us  [swap(): return lax.ppermute(values, axis, [(i, i ^ step) for i in range(count)])]
    pallas_call x2, Pallas kernels: 32.3 us -> 39.9 us  [attend_back(): pl.pallas_call(functools.partial(backward_kernel, first_head, heads, bloc...]
    all_to_all x4, starting transfers between devices: 25.8 us -> 19.6 us  [exchange(): lax.all_to_all(rows.reshape(sources, -1, width), 'dp', split_axis=0, conc...]
    ppermute x32, waiting for transfers between devices: 28.5 us -> 34.4 us  [swap(): return lax.ppermute(values, axis, [(i, i ^ step) for i in range(count)])]
    pallas_call x2, Pallas kernels: 17 us -> 22.1 us  [attend(): pl.pallas_call(functools.partial(forward_kernel, first, blocks), out_shap...]
    all_to_all x4, waiting for transfers between devices: 14.9 us -> 19.7 us  [exchange(): lax.all_to_all(rows.reshape(sources, -1, width), 'dp', split_axis=0, conc...]
    pallas_call x2, Pallas kernels: 18.3 us -> 14.3 us  [the longest x1 7.71 us: near_weights(): pl.pallas_call(functools.partial(near_weight_kernel, len(groups), skip),...]
    unnamed x68 -> x70, local copies, waits for them, and re-layouts: 6.02 us -> 4.51 us
  transfers between devices with their start and end apart: 36 -> 36, of which waited for: 15 -> 16; matrix products, arithmetic and copies ran while one was open for 1% -> 1% of each run, Pallas kernels for 49% -> 53%
where the time goes in v12:
time: 235 us; the launch traced here: 233 us
  Pallas kernels  135 us (57%)
  waiting for transfers between devices  54.1 us (23%)
  starting transfers between devices  36.3 us (15%)
  local copies, waits for them, and re-layouts  5.12 us (2%)
    pallas_call x2, Pallas kernels, attend_back(): pl.pallas_call(functools.partial(backward_kernel, first_head, heads, bloc...  39.9 us
    ppermute x32, waiting for transfers between devices, swap(): return lax.ppermute(values, axis, [(i, i ^ step) for i in range(count)])  34.4 us
    pallas_call x2, Pallas kernels, attend(): pl.pallas_call(functools.partial(forward_kernel, first, blocks), out_shap...  22.1 us
    all_to_all x4, waiting for transfers between devices, exchange(): lax.all_to_all(rows.reshape(sources, -1, width), 'dp', split_axis=0, conc...  19.7 us
    all_to_all x4, starting transfers between devices, exchange(): lax.all_to_all(rows.reshape(sources, -1, width), 'dp', split_axis=0, conc...  19.6 us
    ppermute x32, starting transfers between devices, swap(): return lax.ppermute(values, axis, [(i, i ^ step) for i in range(count)])  16.7 us
    pallas_call x1, Pallas kernels, expert(): pl.pallas_call(functools.partial(expert_kernel, parts), out_shape=(jax.Sh...  11.1 us
    pallas_call x1, Pallas kernels, near_weights(): pl.pallas_call(functools.partial(near_weight_kernel, len(groups), skip),...  7.71 us
  transfers between devices with their start and end apart: 36, of which 16 were waited for; matrix products, arithmetic and copies ran while one was open for 1% of the time, Pallas kernels for 53%

profile of v12, /device:TPU:0, one launch (start us, length us, event | category | flops | bytes accessed | tf_op | source)
XLA Modules:
  0.0 233.4 jit_solution(3951550801609722098)
XLA Ops:
  0.7 3.3 %plan.1 = (bf16[512,512]{1,0:T(8,128)(2,1)}, bf16[512,768]{1,0:T(8,128)(2,1)}) custom-call(s32[1,5]{1,0:T(1,128)} %lens_ref.11, s32[1,1]{1,0:T(1,128)} %bitcast.1.rank_ref, s32[1,512]{1,0:T(1,128)} %bitcast.51, s32[1,512]{1,0:T(1,128)} %order_ref.1, bf16[512,768]{1,0:T(8,128)(2,1)} %cotangent_ref.1), custom_call_target="tpu_custom_call" | custom-call | flops 1048576 | bytes 1048576 | tf_op jit(solution)/shard_map/plan/pallas_call | solution.py:470
  3.9 7.3 %all-to-all-start.1 = ((bf16[8,64,768]{2,1,0:T(8,128)(2,1)}), bf16[8,64,768]{2,1,0:T(8,128)(2,1)S(1)}, u32[]{:S(2)}, u32[]{:S(2)}) async-start(bf16[8,64,768]{2,1,0:T(8,128)(2,1)} %bitcast.49), calls=%async_computation.1 | async-start | bytes 1572864 | tf_op jit(solution)/shard_map/all_to_all | solution.py:1031
  13.2 7.5 %project.1 = (bf16[2048,768]{1,0:T(8,128)(2,1)}, bf16[192,2048]{1,0:T(8,128)(2,1)}, bf16[192,2048]{1,0:T(8,128)(2,1)}, bf16[192,2048]{1,0:T(8,128)(2,1)}) custom-call(s32[1]{0:T(128)} %bitcast.rank_ref, bf16[2048,768]{1,0:T(8,128)(2,1)} %tokens_ref.2, f32[768]{0:T(1024)} %gain_ref.7, f32[768]{0:T(1024)} %bias_ref.2, bf16[192,768]{1,0:T(8,128)(2,1)} %bitcast.30, ...), custom_call_target="tpu_custom_call" | custom-call | flops 1048576 | bytes 1048576 | tf_op jit(solution)/shard_map/project/pallas_call | solution.py:81
  20.6 11.0 %attend.2 = (bf16[192,512]{1,0:T(8,128)(2,1)}, bf16[192,512]{1,0:T(8,128)(2,1)}, f32[3,1,1024]{2,1,0:T(1,128)}) custom-call(s32[1,5]{1,0:T(1,128)} %lens_ref.11, s32[1,1]{1,0:T(1,128)} %bitcast.1.rank_ref, bf16[192,2048]{1,0:T(8,128)(2,1)} %get-tuple-element.128.qt_ref, bf16[192,2048]{1,0:T(8,128)(2,1)} %get-tuple-element.133.kt_ref, ...), custom_call_target="tpu_custom_call" | custom-call | flops 1048576 | bytes 1048576 | tf_op jit(solution)/shard_map/attend/pallas_call | solution.py:239
  33.4 11.0 %attend.3 = (bf16[192,512]{1,0:T(8,128)(2,1)}, bf16[192,512]{1,0:T(8,128)(2,1)}, f32[3,1,1024]{2,1,0:T(1,128)}) custom-call(s32[1,5]{1,0:T(1,128)} %lens_ref.11, s32[1,1]{1,0:T(1,128)} %bitcast.1.rank_ref, bf16[192,2048]{1,0:T(8,128)(2,1)} %get-tuple-element.128.qt_ref, bf16[192,2048]{1,0:T(8,128)(2,1)} %get-tuple-element.133.kt_ref, ...), custom_call_target="tpu_custom_call" | custom-call | flops 1048576 | bytes 1048576 | tf_op jit(solution)/shard_map/attend/pallas_call | solution.py:239
  47.0 4.8 %middle.1 = (f32[512,768]{1,0:T(8,128)}, bf16[512,768]{1,0:T(8,128)(2,1)}) custom-call(s32[1]{0:T(128)} %bitcast.rank_ref, bf16[2048,768]{1,0:T(8,128)(2,1)} %tokens_ref.2, f32[768]{0:T(1024)} %gain_ref.6, f32[768]{0:T(1024)} %bias_ref.3, bf16[512,512]{1,0:T(8,128)(2,1)} %get-tuple-element.127.dispatch_ref, ...), custom_call_target="tpu_custom_call" | custom-call | flops 1048576 | bytes 1048576 | tf_op jit(solution)/shard_map/middle/pallas_call | solution.py:507
  51.9 4.1 %all-to-all-start = ((bf16[8,64,768]{2,1,0:T(8,128)(2,1)}), bf16[8,64,768]{2,1,0:T(8,128)(2,1)S(1)}, u32[]{:S(2)}, u32[]{:S(2)}) async-start(bf16[8,64,768]{2,1,0:T(8,128)(2,1)} %bitcast.50), calls=%async_computation | async-start | bytes 1572864 | tf_op jit(solution)/shard_map/all_to_all | solution.py:1031
  56.1 6.5 %activation_grads.1.grad_act_ref = bf16[512,3072]{1,0:T(8,128)(2,1)} custom-call(bf16[512,768]{1,0:T(8,128)(2,1)} %bitcast.23, bf16[3072,768]{1,0:T(8,128)(2,1)} %bitcast.46), custom_call_target="tpu_custom_call" | custom-call | flops 1048576 | bytes 1048576 | tf_op jit(solution)/shard_map/activation_grads/pallas_call | solution.py:625
  62.6 14.0 %all-to-all-done = bf16[8,64,768]{2,1,0:T(8,128)(2,1)S(1)} async-done(((bf16[8,64,768]{2,1,0:T(8,128)(2,1)}), bf16[8,64,768]{2,1,0:T(8,128)(2,1)S(1)}, u32[]{:S(2)}, u32[]{:S(2)}) %all-to-all-start) | async-done | bytes 786464 | tf_op jit(solution)/shard_map/all_to_all | solution.py:1031
  76.8 11.1 %expert.1 = (bf16[512,1536]{1,0:T(8,128)(2,1)}, bf16[512,1536]{1,0:T(8,128)(2,1)}, bf16[512,1536]{1,0:T(8,128)(2,1)}, bf16[512,1536]{1,0:T(8,128)(2,1)}, bf16[512,768]{1,0:T(8,128)(2,1)}) custom-call(s32[1,1]{1,0:T(1,128)} %bitcast.1.rank_ref, bf16[512,768]{1,0:T(8,128)(2,1)S(1)} %bitcast.27, bf16[512,3072]{1,0:T(8,128)(2,1)} %activation_grads.1.grad_act_ref, ...), custom_call_target="tpu_custom_call" | custom-call | flops 1048576 | bytes 1048576 | tf_op jit(solution)/shard_map/expert/pallas_call | solution.py:701
  89.3 4.4 %all-to-all-start.2 = ((bf16[8,64,768]{2,1,0:T(8,128)(2,1)}), bf16[8,64,768]{2,1,0:T(8,128)(2,1)}, u32[]{:S(2)}, u32[]{:S(2)}) async-start(bf16[8,64,768]{2,1,0:T(8,128)(2,1)} %bitcast.12), calls=%async_computation.2 | async-start | bytes 1572864 | tf_op jit(solution)/shard_map/all_to_all | solution.py:1031
  93.7 6.5 %product.1 = bf16[512,768]{1,0:T(8,128)(2,1)} custom-call(s32[1,1]{1,0:T(1,128)} %bitcast.1.rank_ref, bf16[512,1536]{1,0:T(8,128)(2,1)} %get-tuple-element.156.kept_ref.refs_2_, bf16[512,1536]{1,0:T(8,128)(2,1)} %get-tuple-element.157.sent_ref, bf16[3072,768]{1,0:T(8,128)(2,1)} %bitcast.47), custom_call_target="tpu_custom_call" | custom-call | flops 1048576 | bytes 1048576 | tf_op jit(solution)/shard_map/product/pallas_call | solution.py:752
  101.8 6.6 %far_weights.1 = (bf16[384,768]{1,0:T(8,128)(2,1)}, bf16[1152,768]{1,0:T(8,128)(2,1)}) custom-call(bf16[512,768]{1,0:T(8,128)(2,1)} %bitcast.28, bf16[512,768]{1,0:T(8,128)(2,1)} %bitcast.24, bf16[512,1536]{1,0:T(8,128)(2,1)} %get-tuple-element.156.kept_ref.refs_2_, bf16[512,1536]{1,0:T(8,128)(2,1)} %get-tuple-element.160.refs_3_, ...), custom_call_target="tpu_custom_call" | custom-call | flops 1048576 | bytes 1048576 | tf_op jit(solution)/shard_map/far_weights/pallas_call | solution.py:799
  108.5 5.7 %all-to-all-done.2 = bf16[8,64,768]{2,1,0:T(8,128)(2,1)} async-done(((bf16[8,64,768]{2,1,0:T(8,128)(2,1)}), bf16[8,64,768]{2,1,0:T(8,128)(2,1)}, u32[]{:S(2)}, u32[]{:S(2)}) %all-to-all-start.2) | async-done | bytes 786464 | tf_op jit(solution)/shard_map/all_to_all | solution.py:1031
  114.1 6.5 %turn.1 = (f32[512,768]{1,0:T(8,128)}, f32[2,768]{1,0:T(2,128)}, bf16[2,192,768]{2,1,0:T(8,128)(2,1)}, bf16[2,192,768]{2,1,0:T(8,128)(2,1)}, bf16[192,512]{1,0:T...) custom-call(s32[1,5]{1,0:T(1,128)} %lens_ref.11, ...), custom_call_target="tpu_custom_call" | custom-call | flops 1048576 | bytes 1048576 | tf_op jit(solution)/shard_map/turn/pallas_call | solution.py:564
  122.7 3.8 %all-to-all-start.3 = ((bf16[8,64,768]{2,1,0:T(8,128)(2,1)}), bf16[8,64,768]{2,1,0:T(8,128)(2,1)S(1)}, u32[]{:S(2)}, u32[]{:S(2)}) async-start(bf16[8,64,768]{2,1,0:T(8,128)(2,1)} %bitcast.15), calls=%async_computation.3 | async-start | bytes 1572864 | tf_op jit(solution)/shard_map/all_to_all | solution.py:1031
  133.1 24.0 %attend_back.2 = (bf16[2048,384]{1,0:T(8,128)(2,1)}, f32[2,768]{1,0:T(2,128)}, bf16[192,768]{1,0:T(8,128)(2,1)}, bf16[192,768]{1,0:T(8,128)(2,1)}) custom-call(s32[1,5]{1,0:T(1,128)} %lens_ref.11, s32[1,1]{1,0:T(1,128)} %bitcast.1.rank_ref, s32[1,1]{1,0:T(1,128)} %bitcast.14.bit_ref, bf16[192,2048]{1,0:T(8,128)(2,1)} %get-tuple-element.128.qt_ref, ...), custom_call_target="tpu_custom_call" | custom-call | flops 1048576 | bytes 1048576 | tf_op jit(solution)/shard_map/attend_back/pallas_call | solution.py:408
  158.1 15.9 %attend_back.3 = (bf16[2048,192]{1,0:T(8,128)(2,1)}, f32[2,768]{1,0:T(2,128)}, bf16[112,768]{1,0:T(8,128)(2,1)}, bf16[112,768]{1,0:T(8,128)(2,1)}) custom-call(s32[1,5]{1,0:T(1,128)} %lens_ref.11, s32[1,1]{1,0:T(1,128)} %bitcast.1.rank_ref, s32[1,1]{1,0:T(1,128)} %bitcast.14.bit_ref, bf16[192,2048]{1,0:T(8,128)(2,1)} %get-tuple-element.128.qt_ref, ...), custom_call_target="tpu_custom_call" | custom-call | flops 1048576 | bytes 1048576 | tf_op jit(solution)/shard_map/attend_back/pallas_call | solution.py:408
  180.0 5.6 %collective-permute-done.18.b_ref = bf16[112,768]{1,0:T(8,128)(2,1)S(1)} collective-permute-done((bf16[112,768]{1,0:T(8,128)(2,1)S(1)}, bf16[112,768]{1,0:T(8,128)(2,1)S(1)}, u32[]{:S(2)}, u32[]{:S(2)}) %collective-permute-start.18) | collective-permute-done | bytes 172064 | tf_op jit(solution)/shard_map/ppermute | solution.py:38
  190.2 4.8 %collective-permute-done.21.b_ref = bf16[112,768]{1,0:T(8,128)(2,1)S(1)} collective-permute-done((bf16[112,768]{1,0:T(8,128)(2,1)S(1)}, bf16[112,768]{1,0:T(8,128)(2,1)S(1)}, u32[]{:S(2)}, u32[]{:S(2)}) %collective-permute-start.21) | collective-permute-done | bytes 172064 | tf_op jit(solution)/shard_map/ppermute | solution.py:38
  195.1 3.9 %collective-permute-done.22.refs_9_ = bf16[1152,768]{1,0:T(8,128)(2,1)} collective-permute-done((bf16[1152,768]{1,0:T(8,128)(2,1)}, bf16[1152,768]{1,0:T(8,128)(2,1)}, u32[]{:S(2)}, u32[]{:S(2)}) %collective-permute-start.22) | collective-permute-done | bytes 1769504 | tf_op jit(solution)/shard_map/ppermute | solution.py:38
  201.7 2.9 %collective-permute-start.27 = (bf16[192,768]{1,0:T(8,128)(2,1)S(1)}, bf16[192,768]{1,0:T(8,128)(2,1)S(1)}, u32[]{:S(2)}, u32[]{:S(2)}) collective-permute-start(bf16[192,768]{1,0:T(8,128)(2,1)S(1)} %add_low.12.a_ref), channel_id=1, source_target_pairs={{0,16},{4,20},{8,24},{12,28},{16,0},{20,4},{24,8},{28,12},{1,17},{... | collective-permute-start | bytes 884744 | tf_op jit(solution)/shard_map/ppermute | solution.py:38
  204.8 7.7 %near_weights.1 = (f32[768,768]{1,0:T(8,128)}, f32[768,768]{1,0:T(8,128)}) custom-call(bf16[512,768]{1,0:T(8,128)(2,1)S(1)} %bitcast.29, bf16[512,768]{1,0:T(8,128)(2,1)S(1)} %bitcast.25, bf16[512,1536]{1,0:T(8,128)(2,1)} %get-tuple-element.156.kept_ref.refs_2_, bf16[512,1536]{1,0:T(8,128)(2,1)} %get-tuple-element.160.refs_3_, bf16[512,768]{1,0:T(8,128)(2,1)} %copy-done.21, ...), custom_call_target="tpu_custom_call" | custom-call | flops 1048576 | bytes 1048576 | tf_op jit(solution)/shard_map/near_weights/pallas_call | solution.py:825
  219.7 2.9 %collective-permute-done.31.b_ref = bf16[192,768]{1,0:T(8,128)(2,1)S(1)} collective-permute-done((bf16[192,768]{1,0:T(8,128)(2,1)S(1)}, bf16[192,768]{1,0:T(8,128)(2,1)S(1)}, u32[]{:S(2)}, u32[]{:S(2)}) %collective-permute-start.31) | collective-permute-done | bytes 294944 | tf_op jit(solution)/shard_map/ppermute | solution.py:38
  (154 shorter events, 50.2 us)
Async XLA Ops:
  3.9 47.9 %all-to-all-start.1 = ((bf16[8,64,768]{2,1,0:T(8,128)(2,1)}), bf16[8,64,768]{2,1,0:T(8,128)(2,1)S(1)}, u32[]{:S(2)}, u32[]{:S(2)}) async-start(bf16[8,64,768]{2,1,0:T(8,128)(2,1)} %bitcast.49), calls=%async_computation.1 | async-start | bytes 1572864 | tf_op jit(solution)/shard_map/all_to_all | solution.py:1031
  11.2 33.2 %collective-permute-start.2 = (bf16[192,768]{1,0:T(8,128)(2,1)S(1)}, bf16[192,768]{1,0:T(8,128)(2,1)S(1)}, u32[]{:S(2)}, u32[]{:S(2)}) collective-permute-start(bf16[192,768]{1,0:T(8,128)(2,1)S(1)} %copy-done.22), channel_id=1, source_target_pairs={{0,1},{1,0},{2,3},{3,2},{4,5},{5,4},{6,7},{7,6},{8,9},{9,8},{10,11... | collective-permute-start | bytes 884744 | tf_op jit(solution)/shard_map/ppermute | solution.py:38
  11.3 33.2 %collective-permute-start.3 = (bf16[192,768]{1,0:T(8,128)(2,1)S(1)}, bf16[192,768]{1,0:T(8,128)(2,1)S(1)}, u32[]{:S(2)}, u32[]{:S(2)}) collective-permute-start(bf16[192,768]{1,0:T(8,128)(2,1)S(1)} %copy-done.22), channel_id=1, source_target_pairs={{0,2},{1,3},{2,0},{3,1},{4,6},{5,7},{6,4},{7,5},{8,10},{9,11},{10,... | collective-permute-start | bytes 884744 | tf_op jit(solution)/shard_map/ppermute | solution.py:38
  12.9 31.6 %collective-permute-start.4 = (bf16[192,768]{1,0:T(8,128)(2,1)S(1)}, bf16[192,768]{1,0:T(8,128)(2,1)S(1)}, u32[]{:S(2)}, u32[]{:S(2)}) collective-permute-start(bf16[192,768]{1,0:T(8,128)(2,1)S(1)} %copy-done.22), channel_id=1, source_target_pairs={{0,3},{1,2},{2,1},{3,0},{4,7},{5,6},{6,5},{7,4},{8,11},{9,10},{10,... | collective-permute-start | bytes 884744 | tf_op jit(solution)/shard_map/ppermute | solution.py:38
  31.7 12.7 %collective-permute-start = (bf16[192,512]{1,0:T(8,128)(2,1)}, bf16[192,512]{1,0:T(8,128)(2,1)S(1)}, u32[]{:S(2)}, u32[]{:S(2)}) collective-permute-start(bf16[192,512]{1,0:T(8,128)(2,1)} %get-tuple-element.136.rest_2_.rest_4_), channel_id=1, source_target_pairs={{0,2},{1,3},{2,0},{3,1},{4,6},{5,7},{6,4},{7,5},{8,10},{9,11},{10,... | collective-permute-start | bytes 589832 | tf_op jit(solution)/shard_map/ppermute | solution.py:38
  33.2 11.3 %collective-permute-start.1 = (bf16[192,512]{1,0:T(8,128)(2,1)}, bf16[192,512]{1,0:T(8,128)(2,1)S(1)}, u32[]{:S(2)}, u32[]{:S(2)}) collective-permute-start(bf16[192,512]{1,0:T(8,128)(2,1)} %get-tuple-element.137.rest_3_.rest_5_), channel_id=1, source_target_pairs={{0,3},{1,2},{2,1},{3,0},{4,7},{5,6},{6,5},{7,4},{8,11},{9,10},{10,... | collective-permute-start | bytes 589832 | tf_op jit(solution)/shard_map/ppermute | solution.py:38
  51.9 24.8 %all-to-all-start = ((bf16[8,64,768]{2,1,0:T(8,128)(2,1)}), bf16[8,64,768]{2,1,0:T(8,128)(2,1)S(1)}, u32[]{:S(2)}, u32[]{:S(2)}) async-start(bf16[8,64,768]{2,1,0:T(8,128)(2,1)} %bitcast.50), calls=%async_computation | async-start | bytes 1572864 | tf_op jit(solution)/shard_map/all_to_all | solution.py:1031
  56.0 20.7 %collective-permute-start.6 = (bf16[512,768]{1,0:T(8,128)(2,1)S(1)}, bf16[512,768]{1,0:T(8,128)(2,1)S(1)}, u32[]{:S(2)}, u32[]{:S(2)}) collective-permute-start(bf16[512,768]{1,0:T(8,128)(2,1)S(1)} %bitcast.22), channel_id=1, source_target_pairs={{0,1},{1,0},{2,3},{3,2},{4,5},{5,4},{6,7},{7,6},{8,9},{9,8},{10,11... | collective-permute-start | bytes 2359304 | tf_op jit(solution)/shard_map/ppermute | solution.py:38
  76.7 11.2 %collective-permute-start.7 = (bf16[512,768]{1,0:T(8,128)(2,1)S(1)}, bf16[512,768]{1,0:T(8,128)(2,1)S(1)}, u32[]{:S(2)}, u32[]{:S(2)}) collective-permute-start(bf16[512,768]{1,0:T(8,128)(2,1)S(1)} %bitcast.26), channel_id=1, source_target_pairs={{0,1},{1,0},{2,3},{3,2},{4,5},{5,4},{6,7},{7,6},{8,9},{9,8},{10,11... | collective-permute-start | bytes 2359304 | tf_op jit(solution)/shard_map/ppermute | solution.py:38
  88.8 11.4 %collective-permute-start.8 = (bf16[512,1536]{1,0:T(8,128)(2,1)}, bf16[512,1536]{1,0:T(8,128)(2,1)S(1)}, u32[]{:S(2)}, u32[]{:S(2)}) collective-permute-start(bf16[512,1536]{1,0:T(8,128)(2,1)} %get-tuple-element.157.sent_ref), channel_id=1, source_target_pairs={{0,1},{1,0},{2,3},{3,2},{4,5},{5,4},{6,7},{7,6},{8,9},{9,8},{10,11... | collective-permute-start | bytes 4718600 | tf_op jit(solution)/shard_map/ppermute | solution.py:38
  88.8 11.4 %collective-permute-start.9 = (bf16[512,1536]{1,0:T(8,128)(2,1)}, bf16[512,1536]{1,0:T(8,128)(2,1)S(1)}, u32[]{:S(2)}, u32[]{:S(2)}) collective-permute-start(bf16[512,1536]{1,0:T(8,128)(2,1)} %get-tuple-element.158), channel_id=1, source_target_pairs={{0,1},{1,0},{2,3},{3,2},{4,5},{5,4},{6,7},{7,6},{8,9},{9,8},{10,11... | collective-permute-start | bytes 4718600 | tf_op jit(solution)/shard_map/ppermute | solution.py:38
  89.3 24.8 %all-to-all-start.2 = ((bf16[8,64,768]{2,1,0:T(8,128)(2,1)}), bf16[8,64,768]{2,1,0:T(8,128)(2,1)}, u32[]{:S(2)}, u32[]{:S(2)}) async-start(bf16[8,64,768]{2,1,0:T(8,128)(2,1)} %bitcast.12), calls=%async_computation.2 | async-start | bytes 1572864 | tf_op jit(solution)/shard_map/all_to_all | solution.py:1031
  122.7 34.4 %all-to-all-start.3 = ((bf16[8,64,768]{2,1,0:T(8,128)(2,1)}), bf16[8,64,768]{2,1,0:T(8,128)(2,1)S(1)}, u32[]{:S(2)}, u32[]{:S(2)}) async-start(bf16[8,64,768]{2,1,0:T(8,128)(2,1)} %bitcast.15), calls=%async_computation.3 | async-start | bytes 1572864 | tf_op jit(solution)/shard_map/all_to_all | solution.py:1031
  131.6 25.5 %collective-permute-start.14 = (bf16[576,768]{1,0:T(8,128)(2,1)}, bf16[576,768]{1,0:T(8,128)(2,1)S(1)}, u32[]{:S(2)}, u32[]{:S(2)}) collective-permute-start(bf16[576,768]{1,0:T(8,128)(2,1)} %get-tuple-element.189), channel_id=1, source_target_pairs={{0,2},{1,3},{2,0},{3,1},{4,6},{5,7},{6,4},{7,5},{8,10},{9,11},{10,... | collective-permute-start | bytes 2654216 | tf_op jit(solution)/shard_map/ppermute | solution.py:38
  157.2 41.9 %collective-permute-start.22 = (bf16[1152,768]{1,0:T(8,128)(2,1)}, bf16[1152,768]{1,0:T(8,128)(2,1)}, u32[]{:S(2)}, u32[]{:S(2)}) collective-permute-start(bf16[1152,768]{1,0:T(8,128)(2,1)} %get-tuple-element.221), channel_id=1, source_target_pairs={{0,2},{1,3},{2,0},{3,1},{4,6},{5,7},{6,4},{7,5},{8,10},{9,11},{10,... | collective-permute-start | bytes 5308424 | tf_op jit(solution)/shard_map/ppermute | solution.py:38
  158.0 16.1 %collective-permute-start.16 = (bf16[192,768]{1,0:T(8,128)(2,1)S(1)}, bf16[192,768]{1,0:T(8,128)(2,1)}, u32[]{:S(2)}, u32[]{:S(2)}) collective-permute-start(bf16[192,768]{1,0:T(8,128)(2,1)S(1)} %add_low.9.a_ref), channel_id=1, source_target_pairs={{0,16},{4,20},{8,24},{12,28},{16,0},{20,4},{24,8},{28,12},{1,17},{... | collective-permute-start | bytes 884744 | tf_op jit(solution)/shard_map/ppermute | solution.py:38
  158.0 17.1 %collective-permute-start.15 = (bf16[192,768]{1,0:T(8,128)(2,1)}, bf16[192,768]{1,0:T(8,128)(2,1)S(1)}, u32[]{:S(2)}, u32[]{:S(2)}) collective-permute-start(bf16[192,768]{1,0:T(8,128)(2,1)} %get-tuple-element.203), channel_id=1, source_target_pairs={{0,4},{4,0},{8,12},{12,8},{16,20},{20,16},{24,28},{28,24},{1,5},{5... | collective-permute-start | bytes 884744 | tf_op jit(solution)/shard_map/ppermute | solution.py:38
  188.4 27.1 %collective-permute-start.24 = (bf16[1,512,768]{2,1,0:T(8,128)(2,1)S(1)}, bf16[1,512,768]{2,1,0:T(8,128)(2,1)S(1)}, u32[]{:S(2)}, u32[]{:S(2)}) collective-permute-start(bf16[1,512,768]{2,1,0:T(8,128)(2,1)S(1)} %add_low.11), channel_id=1, source_target_pairs={{0,2},{1,3},{2,0},{3,1},{4,6},{5,7},{6,4},{7,5},{8,10},{9,11},{10,... | collective-permute-start | bytes 2359304 | tf_op jit(solution)/shard_map/ppermute | solution.py:38
  189.9 14.7 %collective-permute-start.30 = (bf16[192,768]{1,0:T(8,128)(2,1)S(1)}, bf16[192,768]{1,0:T(8,128)(2,1)S(1)}, u32[]{:S(2)}, u32[]{:S(2)}) collective-permute-start(bf16[192,768]{1,0:T(8,128)(2,1)S(1)} %add_low.10.a_ref), channel_id=1, source_target_pairs={{0,4},{4,0},{8,12},{12,8},{16,20},{20,16},{24,28},{28,24},{1,5},{5... | collective-permute-start | bytes 884744 | tf_op jit(solution)/shard_map/ppermute | solution.py:38
  199.0 14.6 %collective-permute-start.23 = (bf16[112,768]{1,0:T(8,128)(2,1)S(1)}, bf16[112,768]{1,0:T(8,128)(2,1)S(1)}, u32[]{:S(2)}, u32[]{:S(2)}) collective-permute-start(bf16[112,768]{1,0:T(8,128)(2,1)S(1)} %add_parts.4.a_ref), channel_id=1, source_target_pairs={{0,16},{4,20},{8,24},{12,28},{16,0},{20,4},{24,8},{28,12},{1,17},{... | collective-permute-start | bytes 516104 | tf_op jit(solution)/shard_map/ppermute | solution.py:38
  201.7 21.9 %collective-permute-start.19 = (bf16[1,512,768]{2,1,0:T(8,128)(2,1)}, bf16[1,512,768]{2,1,0:T(8,128)(2,1)S(1)}, u32[]{:S(2)}, u32[]{:S(2)}) collective-permute-start(bf16[1,512,768]{2,1,0:T(8,128)(2,1)} %get-tuple-element.213), channel_id=1, source_target_pairs={{0,1},{1,0},{2,3},{3,2},{4,5},{5,4},{6,7},{7,6},{8,9},{9,8},{10,11... | collective-permute-start | bytes 2359304 | tf_op jit(solution)/shard_map/ppermute | solution.py:38
  201.7 17.9 %collective-permute-start.27 = (bf16[192,768]{1,0:T(8,128)(2,1)S(1)}, bf16[192,768]{1,0:T(8,128)(2,1)S(1)}, u32[]{:S(2)}, u32[]{:S(2)}) collective-permute-start(bf16[192,768]{1,0:T(8,128)(2,1)S(1)} %add_low.12.a_ref), channel_id=1, source_target_pairs={{0,16},{4,20},{8,24},{12,28},{16,0},{20,4},{24,8},{28,12},{1,17},{... | collective-permute-start | bytes 884744 | tf_op jit(solution)/shard_map/ppermute | solution.py:38
  204.7 17.9 %collective-permute-start.31 = (bf16[192,768]{1,0:T(8,128)(2,1)S(1)}, bf16[192,768]{1,0:T(8,128)(2,1)S(1)}, u32[]{:S(2)}, u32[]{:S(2)}) collective-permute-start(bf16[192,768]{1,0:T(8,128)(2,1)S(1)} %add_low.14.a_ref), channel_id=1, source_target_pairs={{0,8},{4,12},{8,0},{12,4},{16,24},{20,28},{24,16},{28,20},{1,9},{5... | collective-permute-start | bytes 884744 | tf_op jit(solution)/shard_map/ppermute | solution.py:38
  219.7 10.0 %collective-permute-start.28 = (bf16[192,768]{1,0:T(8,128)(2,1)S(1)}, bf16[192,768]{1,0:T(8,128)(2,1)S(1)}, u32[]{:S(2)}, u32[]{:S(2)}) collective-permute-start(bf16[192,768]{1,0:T(8,128)(2,1)S(1)} %add_low.13.refs_0_), channel_id=1, source_target_pairs={{0,4},{4,0},{8,12},{12,8},{16,20},{20,16},{24,28},{28,24},{1,5},{5... | collective-permute-start | bytes 884744 | tf_op jit(solution)/shard_map/ppermute | solution.py:38
  (47 other events, 325.1 us)

commit v13 on v12

--- a/solution.py
+++ b/solution.py
@@ -1158,6 +1158,7 @@
         norm_sums = norm_sums + swap(norm_sums, "tensor", step)
     for step in dp_steps[:-1]:
         output_sum = add_low(output_sum, swap(output_sum, "dp", step))
+    output_sum = after(output_sum, token_grad)
     query_grad, key_grad, value_grad = finish(groups, bit_cell, pieces)
     return (
         block_out,

time: 235 us -> 236 us (level)
  starting transfers between devices: 36.3 us -> 51 us
  waiting for transfers between devices: 54.1 us -> 45.9 us
  Pallas kernels: 135 us -> 129 us
    ppermute x32, starting transfers between devices: 16.7 us -> 27.9 us  [swap(): return lax.ppermute(values, axis, [(i, i ^ step) for i in range(count)])]
    ppermute x32, waiting for transfers between devices: 34.4 us -> 26.3 us  [swap(): return lax.ppermute(values, axis, [(i, i ^ step) for i in range(count)])]
    pallas_call x2, Pallas kernels: 39.9 us -> 34.8 us  [attend_back(): pl.pallas_call(functools.partial(backward_kernel, first_head, heads, bloc...]
    all_to_all x4, starting transfers between devices: 19.6 us -> 23 us  [exchange(): lax.all_to_all(rows.reshape(sources, -1, width), 'dp', split_axis=0, conc...]
    pallas_call x2, Pallas kernels: 22.1 us -> 19.6 us  [attend(): pl.pallas_call(functools.partial(forward_kernel, first, blocks), out_shap...]
  transfers between devices with their start and end apart: 36 -> 36, of which waited for: 16 -> 15; matrix products, arithmetic and copies ran while one was open for 1% -> 1% of each run, Pallas kernels for 53% -> 50%
where the time goes in v13:
time: 236 us; the launch traced here: 234 us
  Pallas kernels  129 us (55%)
  starting transfers between devices  51 us (22%)
  waiting for transfers between devices  45.9 us (19%)
  local copies, waits for them, and re-layouts  5.19 us (2%)
    pallas_call x2, Pallas kernels, attend_back(): pl.pallas_call(functools.partial(backward_kernel, first_head, heads, bloc...  34.8 us
    ppermute x32, starting transfers between devices, swap(): return lax.ppermute(values, axis, [(i, i ^ step) for i in range(count)])  27.9 us
    ppermute x32, waiting for transfers between devices, swap(): return lax.ppermute(values, axis, [(i, i ^ step) for i in range(count)])  26.3 us
    all_to_all x4, starting transfers between devices, exchange(): lax.all_to_all(rows.reshape(sources, -1, width), 'dp', split_axis=0, conc...  23 us
    all_to_all x4, waiting for transfers between devices, exchange(): lax.all_to_all(rows.reshape(sources, -1, width), 'dp', split_axis=0, conc...  19.6 us
    pallas_call x2, Pallas kernels, attend(): pl.pallas_call(functools.partial(forward_kernel, first, blocks), out_shap...  19.6 us
    pallas_call x1, Pallas kernels, expert(): pl.pallas_call(functools.partial(expert_kernel, parts), out_shape=(jax.Sh...  11.1 us
    pallas_call x1, Pallas kernels, near_weights(): pl.pallas_call(functools.partial(near_weight_kernel, len(groups), skip),...  7.72 us
  transfers between devices with their start and end apart: 36, of which 15 were waited for; matrix products, arithmetic and copies ran while one was open for 1% of the time, Pallas kernels for 50%

profile of v13, /device:TPU:0, one launch (start us, length us, event | category | flops | bytes accessed | tf_op | source)
XLA Modules:
  0.0 234.1 jit_solution(9067423049629172439)
XLA Ops:
  0.7 3.3 %plan.1 = (bf16[512,512]{1,0:T(8,128)(2,1)}, bf16[512,768]{1,0:T(8,128)(2,1)}) custom-call(s32[1,5]{1,0:T(1,128)} %lens_ref.11, s32[1,1]{1,0:T(1,128)} %bitcast.1.rank_ref, s32[1,512]{1,0:T(1,128)} %bitcast.51, s32[1,512]{1,0:T(1,128)} %order_ref.1, bf16[512,768]{1,0:T(8,128)(2,1)} %cotangent_ref.1), custom_call_target="tpu_custom_call" | custom-call | flops 1048576 | bytes 1048576 | tf_op jit(solution)/shard_map/plan/pallas_call | solution.py:470
  3.9 7.3 %all-to-all-start.1 = ((bf16[8,64,768]{2,1,0:T(8,128)(2,1)}), bf16[8,64,768]{2,1,0:T(8,128)(2,1)S(1)}, u32[]{:S(2)}, u32[]{:S(2)}) async-start(bf16[8,64,768]{2,1,0:T(8,128)(2,1)} %bitcast.49), calls=%async_computation.1 | async-start | bytes 1572864 | tf_op jit(solution)/shard_map/all_to_all | solution.py:1031
  13.2 7.5 %project.1 = (bf16[2048,768]{1,0:T(8,128)(2,1)}, bf16[192,2048]{1,0:T(8,128)(2,1)}, bf16[192,2048]{1,0:T(8,128)(2,1)}, bf16[192,2048]{1,0:T(8,128)(2,1)}) custom-call(s32[1]{0:T(128)} %bitcast.rank_ref, bf16[2048,768]{1,0:T(8,128)(2,1)} %tokens_ref.2, f32[768]{0:T(1024)} %gain_ref.7, f32[768]{0:T(1024)} %bias_ref.2, bf16[192,768]{1,0:T(8,128)(2,1)} %bitcast.30, ...), custom_call_target="tpu_custom_call" | custom-call | flops 1048576 | bytes 1048576 | tf_op jit(solution)/shard_map/project/pallas_call | solution.py:81
  20.6 9.8 %attend.2 = (bf16[192,512]{1,0:T(8,128)(2,1)}, bf16[192,512]{1,0:T(8,128)(2,1)}, f32[3,1,1024]{2,1,0:T(1,128)}) custom-call(s32[1,5]{1,0:T(1,128)} %lens_ref.11, s32[1,1]{1,0:T(1,128)} %bitcast.1.rank_ref, bf16[192,2048]{1,0:T(8,128)(2,1)} %get-tuple-element.129.qt_ref, bf16[192,2048]{1,0:T(8,128)(2,1)} %get-tuple-element.134.kt_ref, ...), custom_call_target="tpu_custom_call" | custom-call | flops 1048576 | bytes 1048576 | tf_op jit(solution)/shard_map/attend/pallas_call | solution.py:239
  32.1 9.8 %attend.3 = (bf16[192,512]{1,0:T(8,128)(2,1)}, bf16[192,512]{1,0:T(8,128)(2,1)}, f32[3,1,1024]{2,1,0:T(1,128)}) custom-call(s32[1,5]{1,0:T(1,128)} %lens_ref.11, s32[1,1]{1,0:T(1,128)} %bitcast.1.rank_ref, bf16[192,2048]{1,0:T(8,128)(2,1)} %get-tuple-element.129.qt_ref, bf16[192,2048]{1,0:T(8,128)(2,1)} %get-tuple-element.134.kt_ref, ...), custom_call_target="tpu_custom_call" | custom-call | flops 1048576 | bytes 1048576 | tf_op jit(solution)/shard_map/attend/pallas_call | solution.py:239
  44.5 4.9 %middle.1 = (f32[512,768]{1,0:T(8,128)}, bf16[512,768]{1,0:T(8,128)(2,1)}) custom-call(s32[1]{0:T(128)} %bitcast.rank_ref, bf16[2048,768]{1,0:T(8,128)(2,1)} %tokens_ref.2, f32[768]{0:T(1024)} %gain_ref.6, f32[768]{0:T(1024)} %bias_ref.3, bf16[512,512]{1,0:T(8,128)(2,1)} %get-tuple-element.128.dispatch_ref, ...), custom_call_target="tpu_custom_call" | custom-call | flops 1048576 | bytes 1048576 | tf_op jit(solution)/shard_map/middle/pallas_call | solution.py:507
  49.3 7.6 %all-to-all-start = ((bf16[8,64,768]{2,1,0:T(8,128)(2,1)}), bf16[8,64,768]{2,1,0:T(8,128)(2,1)S(1)}, u32[]{:S(2)}, u32[]{:S(2)}) async-start(bf16[8,64,768]{2,1,0:T(8,128)(2,1)} %bitcast.50), calls=%async_computation | async-start | bytes 1572864 | tf_op jit(solution)/shard_map/all_to_all | solution.py:1031
  57.0 6.5 %activation_grads.1.grad_act_ref = bf16[512,3072]{1,0:T(8,128)(2,1)} custom-call(bf16[512,768]{1,0:T(8,128)(2,1)} %bitcast.23, bf16[3072,768]{1,0:T(8,128)(2,1)} %bitcast.46), custom_call_target="tpu_custom_call" | custom-call | flops 1048576 | bytes 1048576 | tf_op jit(solution)/shard_map/activation_grads/pallas_call | solution.py:625
  63.5 14.0 %all-to-all-done = bf16[8,64,768]{2,1,0:T(8,128)(2,1)S(1)} async-done(((bf16[8,64,768]{2,1,0:T(8,128)(2,1)}), bf16[8,64,768]{2,1,0:T(8,128)(2,1)S(1)}, u32[]{:S(2)}, u32[]{:S(2)}) %all-to-all-start) | async-done | bytes 786464 | tf_op jit(solution)/shard_map/all_to_all | solution.py:1031
  77.7 11.1 %expert.1 = (bf16[512,1536]{1,0:T(8,128)(2,1)}, bf16[512,1536]{1,0:T(8,128)(2,1)}, bf16[512,1536]{1,0:T(8,128)(2,1)}, bf16[512,1536]{1,0:T(8,128)(2,1)}, bf16[512,768]{1,0:T(8,128)(2,1)}) custom-call(s32[1,1]{1,0:T(1,128)} %bitcast.1.rank_ref, bf16[512,768]{1,0:T(8,128)(2,1)S(1)} %bitcast.27, bf16[512,3072]{1,0:T(8,128)(2,1)} %activation_grads.1.grad_act_ref, ...), custom_call_target="tpu_custom_call" | custom-call | flops 1048576 | bytes 1048576 | tf_op jit(solution)/shard_map/expert/pallas_call | solution.py:701
  90.3 4.4 %all-to-all-start.2 = ((bf16[8,64,768]{2,1,0:T(8,128)(2,1)}), bf16[8,64,768]{2,1,0:T(8,128)(2,1)}, u32[]{:S(2)}, u32[]{:S(2)}) async-start(bf16[8,64,768]{2,1,0:T(8,128)(2,1)} %bitcast.12), calls=%async_computation.2 | async-start | bytes 1572864 | tf_op jit(solution)/shard_map/all_to_all | solution.py:1031
  94.7 6.5 %product.1 = bf16[512,768]{1,0:T(8,128)(2,1)} custom-call(s32[1,1]{1,0:T(1,128)} %bitcast.1.rank_ref, bf16[512,1536]{1,0:T(8,128)(2,1)} %get-tuple-element.157.kept_ref.refs_2_, bf16[512,1536]{1,0:T(8,128)(2,1)} %get-tuple-element.158.sent_ref, bf16[3072,768]{1,0:T(8,128)(2,1)} %bitcast.47), custom_call_target="tpu_custom_call" | custom-call | flops 1048576 | bytes 1048576 | tf_op jit(solution)/shard_map/product/pallas_call | solution.py:752
  102.9 6.6 %far_weights.1 = (bf16[384,768]{1,0:T(8,128)(2,1)}, bf16[1152,768]{1,0:T(8,128)(2,1)}) custom-call(bf16[512,768]{1,0:T(8,128)(2,1)} %bitcast.28, bf16[512,768]{1,0:T(8,128)(2,1)} %bitcast.24, bf16[512,1536]{1,0:T(8,128)(2,1)} %get-tuple-element.157.kept_ref.refs_2_, bf16[512,1536]{1,0:T(8,128)(2,1)} %get-tuple-element.161.refs_3_, ...), custom_call_target="tpu_custom_call" | custom-call | flops 1048576 | bytes 1048576 | tf_op jit(solution)/shard_map/far_weights/pallas_call | solution.py:799
  109.5 5.6 %all-to-all-done.2 = bf16[8,64,768]{2,1,0:T(8,128)(2,1)} async-done(((bf16[8,64,768]{2,1,0:T(8,128)(2,1)}), bf16[8,64,768]{2,1,0:T(8,128)(2,1)}, u32[]{:S(2)}, u32[]{:S(2)}) %all-to-all-start.2) | async-done | bytes 786464 | tf_op jit(solution)/shard_map/all_to_all | solution.py:1031
  115.1 6.5 %turn.1 = (f32[512,768]{1,0:T(8,128)}, f32[2,768]{1,0:T(2,128)}, bf16[2,192,768]{2,1,0:T(8,128)(2,1)}, bf16[2,192,768]{2,1,0:T(8,128)(2,1)}, bf16[192,512]{1,0:T...) custom-call(s32[1,5]{1,0:T(1,128)} %lens_ref.11, ...), custom_call_target="tpu_custom_call" | custom-call | flops 1048576 | bytes 1048576 | tf_op jit(solution)/shard_map/turn/pallas_call | solution.py:564
  123.6 3.8 %all-to-all-start.3 = ((bf16[8,64,768]{2,1,0:T(8,128)(2,1)}), bf16[8,64,768]{2,1,0:T(8,128)(2,1)S(1)}, u32[]{:S(2)}, u32[]{:S(2)}) async-start(bf16[8,64,768]{2,1,0:T(8,128)(2,1)} %bitcast.15), calls=%async_computation.3 | async-start | bytes 1572864 | tf_op jit(solution)/shard_map/all_to_all | solution.py:1031
  134.1 20.8 %attend_back.2 = (bf16[2048,384]{1,0:T(8,128)(2,1)}, f32[2,768]{1,0:T(2,128)}, bf16[192,768]{1,0:T(8,128)(2,1)}, bf16[192,768]{1,0:T(8,128)(2,1)}) custom-call(s32[1,5]{1,0:T(1,128)} %lens_ref.11, s32[1,1]{1,0:T(1,128)} %bitcast.1.rank_ref, s32[1,1]{1,0:T(1,128)} %bitcast.14.bit_ref, bf16[192,2048]{1,0:T(8,128)(2,1)} %get-tuple-element.129.qt_ref, ...), custom_call_target="tpu_custom_call" | custom-call | flops 1048576 | bytes 1048576 | tf_op jit(solution)/shard_map/attend_back/pallas_call | solution.py:408
  159.7 14.0 %attend_back.3 = (bf16[2048,192]{1,0:T(8,128)(2,1)}, f32[2,768]{1,0:T(2,128)}, bf16[112,768]{1,0:T(8,128)(2,1)}, bf16[112,768]{1,0:T(8,128)(2,1)}) custom-call(s32[1,5]{1,0:T(1,128)} %lens_ref.11, s32[1,1]{1,0:T(1,128)} %bitcast.1.rank_ref, s32[1,1]{1,0:T(1,128)} %bitcast.14.bit_ref, bf16[192,2048]{1,0:T(8,128)(2,1)} %get-tuple-element.129.qt_ref, ...), custom_call_target="tpu_custom_call" | custom-call | flops 1048576 | bytes 1048576 | tf_op jit(solution)/shard_map/attend_back/pallas_call | solution.py:408
  181.2 4.6 %collective-permute-done.18.b_ref = bf16[112,768]{1,0:T(8,128)(2,1)S(1)} collective-permute-done((bf16[112,768]{1,0:T(8,128)(2,1)S(1)}, bf16[112,768]{1,0:T(8,128)(2,1)S(1)}, u32[]{:S(2)}, u32[]{:S(2)}) %collective-permute-start.18) | collective-permute-done | bytes 172064 | tf_op jit(solution)/shard_map/ppermute | solution.py:38
  197.0 3.4 %collective-permute-start.23 = (bf16[112,768]{1,0:T(8,128)(2,1)}, bf16[112,768]{1,0:T(8,128)(2,1)}, u32[]{:S(2)}, u32[]{:S(2)}) collective-permute-start(bf16[112,768]{1,0:T(8,128)(2,1)} %add_parts.4.a_ref), channel_id=1, source_target_pairs={{0,16},{4,20},{8,24},{12,28},{16,0},{20,4},{24,8},{28,12},{1,17},{... | collective-permute-start | bytes 516104 | tf_op jit(solution)/shard_map/ppermute | solution.py:38
  200.5 2.7 %input_grad.2 = (bf16[1,512,768]{2,1,0:T(8,128)(2,1)S(1)}, bf16[1,512,768]{2,1,0:T(8,128)(2,1)}) custom-call(bf16[192,768]{1,0:T(8,128)(2,1)S(1)} %bitcast.34, bf16[192,768]{1,0:T(8,128)(2,1)S(1)} %bitcast.39, bf16[192,768]{1,0:T(8,128)(2,1)S(1)} %bitcast.44, bf16[2048,384]{1,0:T(8,128)(2,1)S(1)} %copy-done.9, bf16[2048,192]{1,0:T(8,128)(2,1)S(1)} %copy-done.11), custom_call_target="tpu_custom_call" | custom-call | flops 1048576 | bytes 1048576 | tf_op jit(solution)/shard_map/input_grad/pallas_call | solution.py:878
  204.1 7.7 %near_weights.1 = (f32[768,768]{1,0:T(8,128)}, f32[768,768]{1,0:T(8,128)}) custom-call(bf16[512,768]{1,0:T(8,128)(2,1)S(1)} %bitcast.29, bf16[512,768]{1,0:T(8,128)(2,1)S(1)} %bitcast.25, bf16[512,1536]{1,0:T(8,128)(2,1)} %get-tuple-element.157.kept_ref.refs_2_, bf16[512,1536]{1,0:T(8,128)(2,1)} %get-tuple-element.161.refs_3_, bf16[512,768]{1,0:T(8,128)(2,1)} %copy-done.21, ...), custom_call_target="tpu_custom_call" | custom-call | flops 1048576 | bytes 1048576 | tf_op jit(solution)/shard_map/near_weights/pallas_call | solution.py:825
  217.0 3.1 %collective-permute-done.27.b_ref = bf16[192,768]{1,0:T(8,128)(2,1)S(1)} collective-permute-done((bf16[192,768]{1,0:T(8,128)(2,1)S(1)}, bf16[192,768]{1,0:T(8,128)(2,1)S(1)}, u32[]{:S(2)}, u32[]{:S(2)}) %collective-permute-start.27) | collective-permute-done | bytes 294944 | tf_op jit(solution)/shard_map/ppermute | solution.py:38
  223.3 2.9 %close.1 = (f32[512,768]{1,0:T(8,128)}, f32[512,768]{1,0:T(8,128)}) custom-call(s32[1]{0:T(128)} %bitcast.rank_ref, bf16[2048,768]{1,0:T(8,128)(2,1)S(1)} %copy-done, f32[768]{0:T(1024)S(1)} %copy-done.16, f32[512,768]{1,0:T(8,128)S(1)} %copy-done.13, f32[512,768]{1,0:T(8,128)S(1)} %copy-done.8, bf16[512,512]{1,0:T(8,128)(2,1)S(1)} %copy-done.10, ...), custom_call_target="tpu_custom_call" | custom-call | flops 1048576 | bytes 1048576 | tf_op jit(solution)/shard_map/close/pallas_call | solution.py:920
  (154 shorter events, 58.5 us)
Async XLA Ops:
  3.9 45.4 %all-to-all-start.1 = ((bf16[8,64,768]{2,1,0:T(8,128)(2,1)}), bf16[8,64,768]{2,1,0:T(8,128)(2,1)S(1)}, u32[]{:S(2)}, u32[]{:S(2)}) async-start(bf16[8,64,768]{2,1,0:T(8,128)(2,1)} %bitcast.49), calls=%async_computation.1 | async-start | bytes 1572864 | tf_op jit(solution)/shard_map/all_to_all | solution.py:1031
  11.2 30.7 %collective-permute-start.2 = (bf16[192,768]{1,0:T(8,128)(2,1)S(1)}, bf16[192,768]{1,0:T(8,128)(2,1)S(1)}, u32[]{:S(2)}, u32[]{:S(2)}) collective-permute-start(bf16[192,768]{1,0:T(8,128)(2,1)S(1)} %copy-done.22), channel_id=1, source_target_pairs={{0,1},{1,0},{2,3},{3,2},{4,5},{5,4},{6,7},{7,6},{8,9},{9,8},{10,11... | collective-permute-start | bytes 884744 | tf_op jit(solution)/shard_map/ppermute | solution.py:38
  11.3 30.7 %collective-permute-start.3 = (bf16[192,768]{1,0:T(8,128)(2,1)S(1)}, bf16[192,768]{1,0:T(8,128)(2,1)S(1)}, u32[]{:S(2)}, u32[]{:S(2)}) collective-permute-start(bf16[192,768]{1,0:T(8,128)(2,1)S(1)} %copy-done.22), channel_id=1, source_target_pairs={{0,2},{1,3},{2,0},{3,1},{4,6},{5,7},{6,4},{7,5},{8,10},{9,11},{10,... | collective-permute-start | bytes 884744 | tf_op jit(solution)/shard_map/ppermute | solution.py:38
  12.9 29.1 %collective-permute-start.4 = (bf16[192,768]{1,0:T(8,128)(2,1)S(1)}, bf16[192,768]{1,0:T(8,128)(2,1)S(1)}, u32[]{:S(2)}, u32[]{:S(2)}) collective-permute-start(bf16[192,768]{1,0:T(8,128)(2,1)S(1)} %copy-done.22), channel_id=1, source_target_pairs={{0,3},{1,2},{2,1},{3,0},{4,7},{5,6},{6,5},{7,4},{8,11},{9,10},{10,... | collective-permute-start | bytes 884744 | tf_op jit(solution)/shard_map/ppermute | solution.py:38
  30.4 11.5 %collective-permute-start = (bf16[192,512]{1,0:T(8,128)(2,1)}, bf16[192,512]{1,0:T(8,128)(2,1)S(1)}, u32[]{:S(2)}, u32[]{:S(2)}) collective-permute-start(bf16[192,512]{1,0:T(8,128)(2,1)} %get-tuple-element.137.rest_2_.rest_4_), channel_id=1, source_target_pairs={{0,2},{1,3},{2,0},{3,1},{4,6},{5,7},{6,4},{7,5},{8,10},{9,11},{10,... | collective-permute-start | bytes 589832 | tf_op jit(solution)/shard_map/ppermute | solution.py:38
  49.3 28.2 %all-to-all-start = ((bf16[8,64,768]{2,1,0:T(8,128)(2,1)}), bf16[8,64,768]{2,1,0:T(8,128)(2,1)S(1)}, u32[]{:S(2)}, u32[]{:S(2)}) async-start(bf16[8,64,768]{2,1,0:T(8,128)(2,1)} %bitcast.50), calls=%async_computation | async-start | bytes 1572864 | tf_op jit(solution)/shard_map/all_to_all | solution.py:1031
  56.9 20.7 %collective-permute-start.6 = (bf16[512,768]{1,0:T(8,128)(2,1)S(1)}, bf16[512,768]{1,0:T(8,128)(2,1)S(1)}, u32[]{:S(2)}, u32[]{:S(2)}) collective-permute-start(bf16[512,768]{1,0:T(8,128)(2,1)S(1)} %bitcast.22), channel_id=1, source_target_pairs={{0,1},{1,0},{2,3},{3,2},{4,5},{5,4},{6,7},{7,6},{8,9},{9,8},{10,11... | collective-permute-start | bytes 2359304 | tf_op jit(solution)/shard_map/ppermute | solution.py:38
  77.6 11.2 %collective-permute-start.7 = (bf16[512,768]{1,0:T(8,128)(2,1)S(1)}, bf16[512,768]{1,0:T(8,128)(2,1)S(1)}, u32[]{:S(2)}, u32[]{:S(2)}) collective-permute-start(bf16[512,768]{1,0:T(8,128)(2,1)S(1)} %bitcast.26), channel_id=1, source_target_pairs={{0,1},{1,0},{2,3},{3,2},{4,5},{5,4},{6,7},{7,6},{8,9},{9,8},{10,11... | collective-permute-start | bytes 2359304 | tf_op jit(solution)/shard_map/ppermute | solution.py:38
  89.7 11.4 %collective-permute-start.8 = (bf16[512,1536]{1,0:T(8,128)(2,1)}, bf16[512,1536]{1,0:T(8,128)(2,1)S(1)}, u32[]{:S(2)}, u32[]{:S(2)}) collective-permute-start(bf16[512,1536]{1,0:T(8,128)(2,1)} %get-tuple-element.158.sent_ref), channel_id=1, source_target_pairs={{0,1},{1,0},{2,3},{3,2},{4,5},{5,4},{6,7},{7,6},{8,9},{9,8},{10,11... | collective-permute-start | bytes 4718600 | tf_op jit(solution)/shard_map/ppermute | solution.py:38
  89.7 11.4 %collective-permute-start.9 = (bf16[512,1536]{1,0:T(8,128)(2,1)}, bf16[512,1536]{1,0:T(8,128)(2,1)S(1)}, u32[]{:S(2)}, u32[]{:S(2)}) collective-permute-start(bf16[512,1536]{1,0:T(8,128)(2,1)} %get-tuple-element.159), channel_id=1, source_target_pairs={{0,1},{1,0},{2,3},{3,2},{4,5},{5,4},{6,7},{7,6},{8,9},{9,8},{10,11... | collective-permute-start | bytes 4718600 | tf_op jit(solution)/shard_map/ppermute | solution.py:38
  90.3 24.8 %all-to-all-start.2 = ((bf16[8,64,768]{2,1,0:T(8,128)(2,1)}), bf16[8,64,768]{2,1,0:T(8,128)(2,1)}, u32[]{:S(2)}, u32[]{:S(2)}) async-start(bf16[8,64,768]{2,1,0:T(8,128)(2,1)} %bitcast.12), calls=%async_computation.2 | async-start | bytes 1572864 | tf_op jit(solution)/shard_map/all_to_all | solution.py:1031
  123.6 31.2 %all-to-all-start.3 = ((bf16[8,64,768]{2,1,0:T(8,128)(2,1)}), bf16[8,64,768]{2,1,0:T(8,128)(2,1)S(1)}, u32[]{:S(2)}, u32[]{:S(2)}) async-start(bf16[8,64,768]{2,1,0:T(8,128)(2,1)} %bitcast.15), calls=%async_computation.3 | async-start | bytes 1572864 | tf_op jit(solution)/shard_map/all_to_all | solution.py:1031
  132.6 22.7 %collective-permute-start.14 = (bf16[576,768]{1,0:T(8,128)(2,1)}, bf16[576,768]{1,0:T(8,128)(2,1)S(1)}, u32[]{:S(2)}, u32[]{:S(2)}) collective-permute-start(bf16[576,768]{1,0:T(8,128)(2,1)} %get-tuple-element.190), channel_id=1, source_target_pairs={{0,2},{1,3},{2,0},{3,1},{4,6},{5,7},{6,4},{7,5},{8,10},{9,11},{10,... | collective-permute-start | bytes 2654216 | tf_op jit(solution)/shard_map/ppermute | solution.py:38
  155.3 41.7 %collective-permute-start.22 = (bf16[1152,768]{1,0:T(8,128)(2,1)}, bf16[1152,768]{1,0:T(8,128)(2,1)}, u32[]{:S(2)}, u32[]{:S(2)}) collective-permute-start(bf16[1152,768]{1,0:T(8,128)(2,1)} %get-tuple-element.222), channel_id=1, source_target_pairs={{0,2},{1,3},{2,0},{3,1},{4,6},{5,7},{6,4},{7,5},{8,10},{9,11},{10,... | collective-permute-start | bytes 5308424 | tf_op jit(solution)/shard_map/ppermute | solution.py:38
  156.8 16.9 %collective-permute-start.16 = (bf16[192,768]{1,0:T(8,128)(2,1)S(1)}, bf16[192,768]{1,0:T(8,128)(2,1)}, u32[]{:S(2)}, u32[]{:S(2)}) collective-permute-start(bf16[192,768]{1,0:T(8,128)(2,1)S(1)} %add_low.9.a_ref), channel_id=1, source_target_pairs={{0,16},{4,20},{8,24},{12,28},{16,0},{20,4},{24,8},{28,12},{1,17},{... | collective-permute-start | bytes 884744 | tf_op jit(solution)/shard_map/ppermute | solution.py:38
  158.7 16.1 %collective-permute-start.15 = (bf16[192,768]{1,0:T(8,128)(2,1)}, bf16[192,768]{1,0:T(8,128)(2,1)S(1)}, u32[]{:S(2)}, u32[]{:S(2)}) collective-permute-start(bf16[192,768]{1,0:T(8,128)(2,1)} %get-tuple-element.204), channel_id=1, source_target_pairs={{0,4},{4,0},{8,12},{12,8},{16,20},{20,16},{24,28},{28,24},{1,5},{5... | collective-permute-start | bytes 884744 | tf_op jit(solution)/shard_map/ppermute | solution.py:38
  187.8 27.6 %collective-permute-start.24 = (bf16[1,512,768]{2,1,0:T(8,128)(2,1)S(1)}, bf16[1,512,768]{2,1,0:T(8,128)(2,1)S(1)}, u32[]{:S(2)}, u32[]{:S(2)}) collective-permute-start(bf16[1,512,768]{2,1,0:T(8,128)(2,1)S(1)} %add_low.11), channel_id=1, source_target_pairs={{0,2},{1,3},{2,0},{3,1},{4,6},{5,7},{6,4},{7,5},{8,10},{9,11},{10,... | collective-permute-start | bytes 2359304 | tf_op jit(solution)/shard_map/ppermute | solution.py:38
  190.2 13.0 %collective-permute-start.30 = (bf16[192,768]{1,0:T(8,128)(2,1)S(1)}, bf16[192,768]{1,0:T(8,128)(2,1)S(1)}, u32[]{:S(2)}, u32[]{:S(2)}) collective-permute-start(bf16[192,768]{1,0:T(8,128)(2,1)S(1)} %add_low.10.a_ref), channel_id=1, source_target_pairs={{0,4},{4,0},{8,12},{12,8},{16,20},{20,16},{24,28},{28,24},{1,5},{5... | collective-permute-start | bytes 884744 | tf_op jit(solution)/shard_map/ppermute | solution.py:38
  197.0 17.3 %collective-permute-start.23 = (bf16[112,768]{1,0:T(8,128)(2,1)}, bf16[112,768]{1,0:T(8,128)(2,1)}, u32[]{:S(2)}, u32[]{:S(2)}) collective-permute-start(bf16[112,768]{1,0:T(8,128)(2,1)} %add_parts.4.a_ref), channel_id=1, source_target_pairs={{0,16},{4,20},{8,24},{12,28},{16,0},{20,4},{24,8},{28,12},{1,17},{... | collective-permute-start | bytes 516104 | tf_op jit(solution)/shard_map/ppermute | solution.py:38
  203.1 20.1 %collective-permute-start.19 = (bf16[1,512,768]{2,1,0:T(8,128)(2,1)}, bf16[1,512,768]{2,1,0:T(8,128)(2,1)S(1)}, u32[]{:S(2)}, u32[]{:S(2)}) collective-permute-start(bf16[1,512,768]{2,1,0:T(8,128)(2,1)} %get-tuple-element.214), channel_id=1, source_target_pairs={{0,1},{1,0},{2,3},{3,2},{4,5},{5,4},{6,7},{7,6},{8,9},{9,8},{10,11... | collective-permute-start | bytes 2359304 | tf_op jit(solution)/shard_map/ppermute | solution.py:38
  203.1 17.1 %collective-permute-start.27 = (bf16[192,768]{1,0:T(8,128)(2,1)S(1)}, bf16[192,768]{1,0:T(8,128)(2,1)S(1)}, u32[]{:S(2)}, u32[]{:S(2)}) collective-permute-start(bf16[192,768]{1,0:T(8,128)(2,1)S(1)} %add_low.12.a_ref), channel_id=1, source_target_pairs={{0,16},{4,20},{8,24},{12,28},{16,0},{20,4},{24,8},{28,12},{1,17},{... | collective-permute-start | bytes 884744 | tf_op jit(solution)/shard_map/ppermute | solution.py:38
  203.3 18.2 %collective-permute-start.31 = (bf16[192,768]{1,0:T(8,128)(2,1)S(1)}, bf16[192,768]{1,0:T(8,128)(2,1)S(1)}, u32[]{:S(2)}, u32[]{:S(2)}) collective-permute-start(bf16[192,768]{1,0:T(8,128)(2,1)S(1)} %add_low.14.a_ref), channel_id=1, source_target_pairs={{0,8},{4,12},{8,0},{12,4},{16,24},{20,28},{24,16},{28,20},{1,9},{5... | collective-permute-start | bytes 884744 | tf_op jit(solution)/shard_map/ppermute | solution.py:38
  216.7 10.4 %collective-permute-start.26 = (f32[8,768]{1,0:T(8,128)S(1)}, f32[8,768]{1,0:T(8,128)S(1)}, u32[]{:S(2)}, u32[]{:S(2)}) collective-permute-start(f32[8,768]{1,0:T(8,128)S(1)} %fusion), channel_id=1, source_target_pairs={{0,2},{1,3},{2,0},{3,1},{4,6},{5,7},{6,4},{7,5},{8,10},{9,11},{10,... | collective-permute-start | bytes 73736 | tf_op jit(solution)/shard_map/ppermute | solution.py:38
  221.5 11.2 %collective-permute-start.29 = (bf16[112,768]{1,0:T(8,128)(2,1)S(1)}, bf16[112,768]{1,0:T(8,128)(2,1)S(1)}, u32[]{:S(2)}, u32[]{:S(2)}) collective-permute-start(bf16[112,768]{1,0:T(8,128)(2,1)S(1)} %add_parts.5.refs_2_), channel_id=1, source_target_pairs={{0,4},{4,0},{8,12},{12,8},{16,20},{20,16},{24,28},{28,24},{1,5},{5... | collective-permute-start | bytes 516104 | tf_op jit(solution)/shard_map/ppermute | solution.py:38
  (47 other events, 323.3 us)

commit v14 on v13

--- a/solution.py
+++ b/solution.py
@@ -761,6 +761,7 @@
             pltpu.SemaphoreType.DMA((2, parts)),
         ],
         name="product",
+        compiler_params=pltpu.CompilerParams(vmem_limit_bytes=54 * 2**20),
         cost_estimate=COST,
     )(rank.reshape(1, 1), kept, sent, down)
 
@@ -803,6 +804,7 @@
         out_specs=tuple(pl.BlockSpec(shape, lambda i: (0, 0)) for shape in shapes),
         out_shape=tuple(jax.ShapeDtypeStruct(shape, bf16) for shape in shapes),
         name="far_weights",
+        compiler_params=pltpu.CompilerParams(vmem_limit_bytes=52 * 2**20),
         cost_estimate=COST,
     )(*[values for group in groups for values in group])
 

time: 236 us -> 234 us (level)
  starting transfers between devices: 51 us -> 46.2 us
  waiting for transfers between devices: 45.9 us -> 48.5 us
    ppermute x32, starting transfers between devices: 27.9 us -> 25.4 us  [swap(): return lax.ppermute(values, axis, [(i, i ^ step) for i in range(count)])]
    ppermute x32, waiting for transfers between devices: 26.3 us -> 28.7 us  [swap(): return lax.ppermute(values, axis, [(i, i ^ step) for i in range(count)])]
  transfers between devices with their start and end apart: 36 -> 36, of which waited for: 15 -> 15; matrix products, arithmetic and copies ran while one was open for 1% -> 1% of each run, Pallas kernels for 50% -> 51%
where the time goes in v14:
time: 234 us; the launch traced here: 232 us
  Pallas kernels  130 us (56%)
  waiting for transfers between devices  48.5 us (21%)
  starting transfers between devices  46.2 us (20%)
  local copies, waits for them, and re-layouts  4.55 us (2%)
    pallas_call x2, Pallas kernels, attend_back(): pl.pallas_call(functools.partial(backward_kernel, first_head, heads, bloc...  36 us
    ppermute x32, waiting for transfers between devices, swap(): return lax.ppermute(values, axis, [(i, i ^ step) for i in range(count)])  28.7 us
    ppermute x32, starting transfers between devices, swap(): return lax.ppermute(values, axis, [(i, i ^ step) for i in range(count)])  25.4 us
    all_to_all x4, starting transfers between devices, exchange(): lax.all_to_all(rows.reshape(sources, -1, width), 'dp', split_axis=0, conc...  20.7 us
    all_to_all x4, waiting for transfers between devices, exchange(): lax.all_to_all(rows.reshape(sources, -1, width), 'dp', split_axis=0, conc...  19.8 us
    pallas_call x2, Pallas kernels, attend(): pl.pallas_call(functools.partial(forward_kernel, first, blocks), out_shap...  19.5 us
    pallas_call x1, Pallas kernels, expert(): pl.pallas_call(functools.partial(expert_kernel, parts), out_shape=(jax.Sh...  10.9 us
    pallas_call x1, Pallas kernels, near_weights(): pl.pallas_call(functools.partial(near_weight_kernel, len(groups), skip),...  7.72 us
  transfers between devices with their start and end apart: 36, of which 15 were waited for; matrix products, arithmetic and copies ran while one was open for 1% of the time, Pallas kernels for 51%

profile of v14, /device:TPU:0, one launch (start us, length us, event | category | flops | bytes accessed | tf_op | source)
XLA Modules:
  0.0 232.2 jit_solution(15633026558392670899)
XLA Ops:
  0.7 3.3 %plan.1 = (bf16[512,512]{1,0:T(8,128)(2,1)}, bf16[512,768]{1,0:T(8,128)(2,1)}) custom-call(s32[1,5]{1,0:T(1,128)} %lens_ref.11, s32[1,1]{1,0:T(1,128)} %bitcast.1.rank_ref, s32[1,512]{1,0:T(1,128)} %bitcast.52, s32[1,512]{1,0:T(1,128)} %order_ref.1, bf16[512,768]{1,0:T(8,128)(2,1)} %cotangent_ref.1), custom_call_target="tpu_custom_call" | custom-call | flops 1048576 | bytes 1048576 | tf_op jit(solution)/shard_map/plan/pallas_call | solution.py:470
  3.9 7.3 %all-to-all-start.1 = ((bf16[8,64,768]{2,1,0:T(8,128)(2,1)}), bf16[8,64,768]{2,1,0:T(8,128)(2,1)S(1)}, u32[]{:S(2)}, u32[]{:S(2)}) async-start(bf16[8,64,768]{2,1,0:T(8,128)(2,1)} %bitcast.50), calls=%async_computation.1 | async-start | bytes 1572864 | tf_op jit(solution)/shard_map/all_to_all | solution.py:1033
  13.2 7.5 %project.1 = (bf16[2048,768]{1,0:T(8,128)(2,1)}, bf16[192,2048]{1,0:T(8,128)(2,1)}, bf16[192,2048]{1,0:T(8,128)(2,1)}, bf16[192,2048]{1,0:T(8,128)(2,1)}) custom-call(s32[1]{0:T(128)} %bitcast.rank_ref, bf16[2048,768]{1,0:T(8,128)(2,1)} %tokens_ref.2, f32[768]{0:T(1024)} %gain_ref.7, f32[768]{0:T(1024)} %bias_ref.2, bf16[192,768]{1,0:T(8,128)(2,1)} %bitcast.30, ...), custom_call_target="tpu_custom_call" | custom-call | flops 1048576 | bytes 1048576 | tf_op jit(solution)/shard_map/project/pallas_call | solution.py:81
  20.6 8.5 %attend.2 = (bf16[192,512]{1,0:T(8,128)(2,1)}, bf16[192,512]{1,0:T(8,128)(2,1)}, f32[3,1,1024]{2,1,0:T(1,128)}) custom-call(s32[1,5]{1,0:T(1,128)} %lens_ref.11, s32[1,1]{1,0:T(1,128)} %bitcast.1.rank_ref, bf16[192,2048]{1,0:T(8,128)(2,1)} %get-tuple-element.129.qt_ref, bf16[192,2048]{1,0:T(8,128)(2,1)} %get-tuple-element.134.kt_ref, ...), custom_call_target="tpu_custom_call" | custom-call | flops 1048576 | bytes 1048576 | tf_op jit(solution)/shard_map/attend/pallas_call | solution.py:239
  29.1 4.0 %collective-permute-start = (bf16[192,512]{1,0:T(8,128)(2,1)}, bf16[192,512]{1,0:T(8,128)(2,1)S(1)}, u32[]{:S(2)}, u32[]{:S(2)}) collective-permute-start(bf16[192,512]{1,0:T(8,128)(2,1)} %get-tuple-element.137.rest_2_.rest_4_), channel_id=1, source_target_pairs={{0,2},{1,3},{2,0},{3,1},{4,6},{5,7},{6,4},{7,5},{8,10},{9,11},{10,... | collective-permute-start | bytes 589832 | tf_op jit(solution)/shard_map/ppermute | solution.py:38
  33.2 11.0 %attend.3 = (bf16[192,512]{1,0:T(8,128)(2,1)}, bf16[192,512]{1,0:T(8,128)(2,1)}, f32[3,1,1024]{2,1,0:T(1,128)}) custom-call(s32[1,5]{1,0:T(1,128)} %lens_ref.11, s32[1,1]{1,0:T(1,128)} %bitcast.1.rank_ref, bf16[192,2048]{1,0:T(8,128)(2,1)} %get-tuple-element.129.qt_ref, bf16[192,2048]{1,0:T(8,128)(2,1)} %get-tuple-element.134.kt_ref, ...), custom_call_target="tpu_custom_call" | custom-call | flops 1048576 | bytes 1048576 | tf_op jit(solution)/shard_map/attend/pallas_call | solution.py:239
  46.7 4.9 %middle.1 = (f32[512,768]{1,0:T(8,128)}, bf16[512,768]{1,0:T(8,128)(2,1)}) custom-call(s32[1]{0:T(128)} %bitcast.rank_ref, bf16[2048,768]{1,0:T(8,128)(2,1)} %tokens_ref.2, f32[768]{0:T(1024)} %gain_ref.6, f32[768]{0:T(1024)} %bias_ref.3, bf16[512,512]{1,0:T(8,128)(2,1)} %get-tuple-element.128.dispatch_ref, ...), custom_call_target="tpu_custom_call" | custom-call | flops 1048576 | bytes 1048576 | tf_op jit(solution)/shard_map/middle/pallas_call | solution.py:507
  51.5 5.3 %all-to-all-start = ((bf16[8,64,768]{2,1,0:T(8,128)(2,1)}), bf16[8,64,768]{2,1,0:T(8,128)(2,1)S(1)}, u32[]{:S(2)}, u32[]{:S(2)}) async-start(bf16[8,64,768]{2,1,0:T(8,128)(2,1)} %bitcast.51), calls=%async_computation | async-start | bytes 1572864 | tf_op jit(solution)/shard_map/all_to_all | solution.py:1033
  56.9 6.5 %activation_grads.1.grad_act_ref = bf16[512,3072]{1,0:T(8,128)(2,1)} custom-call(bf16[512,768]{1,0:T(8,128)(2,1)} %bitcast.23, bf16[3072,768]{1,0:T(8,128)(2,1)} %bitcast.46), custom_call_target="tpu_custom_call" | custom-call | flops 1048576 | bytes 1048576 | tf_op jit(solution)/shard_map/activation_grads/pallas_call | solution.py:625
  63.4 14.1 %all-to-all-done = bf16[8,64,768]{2,1,0:T(8,128)(2,1)S(1)} async-done(((bf16[8,64,768]{2,1,0:T(8,128)(2,1)}), bf16[8,64,768]{2,1,0:T(8,128)(2,1)S(1)}, u32[]{:S(2)}, u32[]{:S(2)}) %all-to-all-start) | async-done | bytes 786464 | tf_op jit(solution)/shard_map/all_to_all | solution.py:1033
  77.5 10.9 %expert.1 = (bf16[512,1536]{1,0:T(8,128)(2,1)}, bf16[512,1536]{1,0:T(8,128)(2,1)}, bf16[512,1536]{1,0:T(8,128)(2,1)}, bf16[512,1536]{1,0:T(8,128)(2,1)}, bf16[512,768]{1,0:T(8,128)(2,1)}) custom-call(s32[1,1]{1,0:T(1,128)} %bitcast.1.rank_ref, bf16[512,768]{1,0:T(8,128)(2,1)S(1)} %bitcast.27, bf16[512,3072]{1,0:T(8,128)(2,1)} %activation_grads.1.grad_act_ref, ...), custom_call_target="tpu_custom_call" | custom-call | flops 1048576 | bytes 1048576 | tf_op jit(solution)/shard_map/expert/pallas_call | solution.py:701
  89.1 4.4 %all-to-all-start.2 = ((bf16[8,64,768]{2,1,0:T(8,128)(2,1)}), bf16[8,64,768]{2,1,0:T(8,128)(2,1)}, u32[]{:S(2)}, u32[]{:S(2)}) async-start(bf16[8,64,768]{2,1,0:T(8,128)(2,1)} %bitcast.12), calls=%async_computation.2 | async-start | bytes 1572864 | tf_op jit(solution)/shard_map/all_to_all | solution.py:1033
  93.5 6.5 %product.1 = bf16[512,768]{1,0:T(8,128)(2,1)} custom-call(s32[1,1]{1,0:T(1,128)} %bitcast.1.rank_ref, bf16[512,1536]{1,0:T(8,128)(2,1)} %get-tuple-element.157.kept_ref.refs_2_, bf16[512,1536]{1,0:T(8,128)(2,1)} %get-tuple-element.158.sent_ref, bf16[3072,768]{1,0:T(8,128)(2,1)} %bitcast.47), custom_call_target="tpu_custom_call" | custom-call | flops 1048576 | bytes 1048576 | tf_op jit(solution)/shard_map/product/pallas_call | solution.py:752
  101.1 6.4 %far_weights.1 = (bf16[384,768]{1,0:T(8,128)(2,1)S(1)}, bf16[1152,768]{1,0:T(8,128)(2,1)}) custom-call(bf16[512,768]{1,0:T(8,128)(2,1)S(1)} %bitcast.28, bf16[512,768]{1,0:T(8,128)(2,1)} %bitcast.24, bf16[512,1536]{1,0:T(8,128)(2,1)} %get-tuple-element.157.kept_ref.refs_2_, bf16[512,1536]{1,0:T(8,128)(2,1)} %get-tuple-element.161.refs_3_, ...), custom_call_target="tpu_custom_call" | custom-call | flops 1048576 | bytes 1048576 | tf_op jit(solution)/shard_map/far_weights/pallas_call | solution.py:800
  108.4 5.7 %all-to-all-done.2 = bf16[8,64,768]{2,1,0:T(8,128)(2,1)} async-done(((bf16[8,64,768]{2,1,0:T(8,128)(2,1)}), bf16[8,64,768]{2,1,0:T(8,128)(2,1)}, u32[]{:S(2)}, u32[]{:S(2)}) %all-to-all-start.2) | async-done | bytes 786464 | tf_op jit(solution)/shard_map/all_to_all | solution.py:1033
  114.1 6.5 %turn.1 = (f32[512,768]{1,0:T(8,128)}, f32[2,768]{1,0:T(2,128)}, bf16[2,192,768]{2,1,0:T(8,128)(2,1)}, bf16[2,192,768]{2,1,0:T(8,128)(2,1)}, bf16[192,512]{1,0:T...) custom-call(s32[1,5]{1,0:T(1,128)} %lens_ref.11, ...), custom_call_target="tpu_custom_call" | custom-call | flops 1048576 | bytes 1048576 | tf_op jit(solution)/shard_map/turn/pallas_call | solution.py:564
  122.7 3.8 %all-to-all-start.3 = ((bf16[8,64,768]{2,1,0:T(8,128)(2,1)}), bf16[8,64,768]{2,1,0:T(8,128)(2,1)S(1)}, u32[]{:S(2)}, u32[]{:S(2)}) async-start(bf16[8,64,768]{2,1,0:T(8,128)(2,1)} %bitcast.49), calls=%async_computation.3 | async-start | bytes 1572864 | tf_op jit(solution)/shard_map/all_to_all | solution.py:1033
  133.2 21.6 %attend_back.2 = (bf16[2048,384]{1,0:T(8,128)(2,1)}, f32[2,768]{1,0:T(2,128)}, bf16[192,768]{1,0:T(8,128)(2,1)}, bf16[192,768]{1,0:T(8,128)(2,1)}) custom-call(s32[1,5]{1,0:T(1,128)} %lens_ref.11, s32[1,1]{1,0:T(1,128)} %bitcast.1.rank_ref, s32[1,1]{1,0:T(1,128)} %bitcast.14.bit_ref, bf16[192,2048]{1,0:T(8,128)(2,1)} %get-tuple-element.129.qt_ref, ...), custom_call_target="tpu_custom_call" | custom-call | flops 1048576 | bytes 1048576 | tf_op jit(solution)/shard_map/attend_back/pallas_call | solution.py:408
  158.1 14.4 %attend_back.3 = (bf16[2048,192]{1,0:T(8,128)(2,1)}, f32[2,768]{1,0:T(2,128)}, bf16[112,768]{1,0:T(8,128)(2,1)}, bf16[112,768]{1,0:T(8,128)(2,1)}) custom-call(s32[1,5]{1,0:T(1,128)} %lens_ref.11, s32[1,1]{1,0:T(1,128)} %bitcast.1.rank_ref, s32[1,1]{1,0:T(1,128)} %bitcast.14.bit_ref, bf16[192,2048]{1,0:T(8,128)(2,1)} %get-tuple-element.129.qt_ref, ...), custom_call_target="tpu_custom_call" | custom-call | flops 1048576 | bytes 1048576 | tf_op jit(solution)/shard_map/attend_back/pallas_call | solution.py:408
  180.7 4.7 %collective-permute-done.18.b_ref = bf16[112,768]{1,0:T(8,128)(2,1)S(1)} collective-permute-done((bf16[112,768]{1,0:T(8,128)(2,1)S(1)}, bf16[112,768]{1,0:T(8,128)(2,1)S(1)}, u32[]{:S(2)}, u32[]{:S(2)}) %collective-permute-start.18) | collective-permute-done | bytes 172064 | tf_op jit(solution)/shard_map/ppermute | solution.py:38
  191.8 3.9 %collective-permute-done.21.b_ref = bf16[112,768]{1,0:T(8,128)(2,1)S(1)} collective-permute-done((bf16[112,768]{1,0:T(8,128)(2,1)S(1)}, bf16[112,768]{1,0:T(8,128)(2,1)S(1)}, u32[]{:S(2)}, u32[]{:S(2)}) %collective-permute-start.21) | collective-permute-done | bytes 172064 | tf_op jit(solution)/shard_map/ppermute | solution.py:38
  202.4 7.7 %near_weights.1 = (f32[768,768]{1,0:T(8,128)}, f32[768,768]{1,0:T(8,128)}) custom-call(bf16[512,768]{1,0:T(8,128)(2,1)S(1)} %bitcast.29, bf16[512,768]{1,0:T(8,128)(2,1)S(1)} %bitcast.25, bf16[512,1536]{1,0:T(8,128)(2,1)} %get-tuple-element.157.kept_ref.refs_2_, bf16[512,1536]{1,0:T(8,128)(2,1)} %get-tuple-element.161.refs_3_, bf16[512,768]{1,0:T(8,128)(2,1)} %copy-done.19, ...), custom_call_target="tpu_custom_call" | custom-call | flops 1048576 | bytes 1048576 | tf_op jit(solution)/shard_map/near_weights/pallas_call | solution.py:827
  214.9 3.3 %collective-permute-done.27.b_ref = bf16[192,768]{1,0:T(8,128)(2,1)S(1)} collective-permute-done((bf16[192,768]{1,0:T(8,128)(2,1)S(1)}, bf16[192,768]{1,0:T(8,128)(2,1)S(1)}, u32[]{:S(2)}, u32[]{:S(2)}) %collective-permute-start.27) | collective-permute-done | bytes 294944 | tf_op jit(solution)/shard_map/ppermute | solution.py:38
  220.6 2.9 %close.1 = (f32[512,768]{1,0:T(8,128)}, f32[512,768]{1,0:T(8,128)}) custom-call(s32[1]{0:T(128)} %bitcast.rank_ref, bf16[2048,768]{1,0:T(8,128)(2,1)S(1)} %copy-done, f32[768]{0:T(1024)S(1)} %copy-done.14, f32[512,768]{1,0:T(8,128)S(1)} %copy-done.11, f32[512,768]{1,0:T(8,128)S(1)} %copy-done.6, bf16[512,512]{1,0:T(8,128)(2,1)S(1)} %copy-done.8, ...), custom_call_target="tpu_custom_call" | custom-call | flops 1048576 | bytes 1048576 | tf_op jit(solution)/shard_map/close/pallas_call | solution.py:922
  (148 shorter events, 55.8 us)
Async XLA Ops:
  3.9 47.6 %all-to-all-start.1 = ((bf16[8,64,768]{2,1,0:T(8,128)(2,1)}), bf16[8,64,768]{2,1,0:T(8,128)(2,1)S(1)}, u32[]{:S(2)}, u32[]{:S(2)}) async-start(bf16[8,64,768]{2,1,0:T(8,128)(2,1)} %bitcast.50), calls=%async_computation.1 | async-start | bytes 1572864 | tf_op jit(solution)/shard_map/all_to_all | solution.py:1033
  11.2 33.0 %collective-permute-start.2 = (bf16[192,768]{1,0:T(8,128)(2,1)S(1)}, bf16[192,768]{1,0:T(8,128)(2,1)S(1)}, u32[]{:S(2)}, u32[]{:S(2)}) collective-permute-start(bf16[192,768]{1,0:T(8,128)(2,1)S(1)} %copy-done.20), channel_id=1, source_target_pairs={{0,1},{1,0},{2,3},{3,2},{4,5},{5,4},{6,7},{7,6},{8,9},{9,8},{10,11... | collective-permute-start | bytes 884744 | tf_op jit(solution)/shard_map/ppermute | solution.py:38
  11.3 32.9 %collective-permute-start.3 = (bf16[192,768]{1,0:T(8,128)(2,1)S(1)}, bf16[192,768]{1,0:T(8,128)(2,1)S(1)}, u32[]{:S(2)}, u32[]{:S(2)}) collective-permute-start(bf16[192,768]{1,0:T(8,128)(2,1)S(1)} %copy-done.20), channel_id=1, source_target_pairs={{0,2},{1,3},{2,0},{3,1},{4,6},{5,7},{6,4},{7,5},{8,10},{9,11},{10,... | collective-permute-start | bytes 884744 | tf_op jit(solution)/shard_map/ppermute | solution.py:38
  12.9 31.4 %collective-permute-start.4 = (bf16[192,768]{1,0:T(8,128)(2,1)S(1)}, bf16[192,768]{1,0:T(8,128)(2,1)S(1)}, u32[]{:S(2)}, u32[]{:S(2)}) collective-permute-start(bf16[192,768]{1,0:T(8,128)(2,1)S(1)} %copy-done.20), channel_id=1, source_target_pairs={{0,3},{1,2},{2,1},{3,0},{4,7},{5,6},{6,5},{7,4},{8,11},{9,10},{10,... | collective-permute-start | bytes 884744 | tf_op jit(solution)/shard_map/ppermute | solution.py:38
  29.1 15.1 %collective-permute-start = (bf16[192,512]{1,0:T(8,128)(2,1)}, bf16[192,512]{1,0:T(8,128)(2,1)S(1)}, u32[]{:S(2)}, u32[]{:S(2)}) collective-permute-start(bf16[192,512]{1,0:T(8,128)(2,1)} %get-tuple-element.137.rest_2_.rest_4_), channel_id=1, source_target_pairs={{0,2},{1,3},{2,0},{3,1},{4,6},{5,7},{6,4},{7,5},{8,10},{9,11},{10,... | collective-permute-start | bytes 589832 | tf_op jit(solution)/shard_map/ppermute | solution.py:38
  33.2 11.0 %collective-permute-start.1 = (bf16[192,512]{1,0:T(8,128)(2,1)}, bf16[192,512]{1,0:T(8,128)(2,1)S(1)}, u32[]{:S(2)}, u32[]{:S(2)}) collective-permute-start(bf16[192,512]{1,0:T(8,128)(2,1)} %get-tuple-element.138.rest_3_.rest_5_), channel_id=1, source_target_pairs={{0,3},{1,2},{2,1},{3,0},{4,7},{5,6},{6,5},{7,4},{8,11},{9,10},{10,... | collective-permute-start | bytes 589832 | tf_op jit(solution)/shard_map/ppermute | solution.py:38
  51.5 26.0 %all-to-all-start = ((bf16[8,64,768]{2,1,0:T(8,128)(2,1)}), bf16[8,64,768]{2,1,0:T(8,128)(2,1)S(1)}, u32[]{:S(2)}, u32[]{:S(2)}) async-start(bf16[8,64,768]{2,1,0:T(8,128)(2,1)} %bitcast.51), calls=%async_computation | async-start | bytes 1572864 | tf_op jit(solution)/shard_map/all_to_all | solution.py:1033
  56.8 20.7 %collective-permute-start.6 = (bf16[512,768]{1,0:T(8,128)(2,1)S(1)}, bf16[512,768]{1,0:T(8,128)(2,1)S(1)}, u32[]{:S(2)}, u32[]{:S(2)}) collective-permute-start(bf16[512,768]{1,0:T(8,128)(2,1)S(1)} %bitcast.22), channel_id=1, source_target_pairs={{0,1},{1,0},{2,3},{3,2},{4,5},{5,4},{6,7},{7,6},{8,9},{9,8},{10,11... | collective-permute-start | bytes 2359304 | tf_op jit(solution)/shard_map/ppermute | solution.py:38
  77.5 11.0 %collective-permute-start.7 = (bf16[512,768]{1,0:T(8,128)(2,1)S(1)}, bf16[512,768]{1,0:T(8,128)(2,1)S(1)}, u32[]{:S(2)}, u32[]{:S(2)}) collective-permute-start(bf16[512,768]{1,0:T(8,128)(2,1)S(1)} %bitcast.26), channel_id=1, source_target_pairs={{0,1},{1,0},{2,3},{3,2},{4,5},{5,4},{6,7},{7,6},{8,9},{9,8},{10,11... | collective-permute-start | bytes 2359304 | tf_op jit(solution)/shard_map/ppermute | solution.py:38
  88.5 11.5 %collective-permute-start.8 = (bf16[512,1536]{1,0:T(8,128)(2,1)}, bf16[512,1536]{1,0:T(8,128)(2,1)S(1)}, u32[]{:S(2)}, u32[]{:S(2)}) collective-permute-start(bf16[512,1536]{1,0:T(8,128)(2,1)} %get-tuple-element.158.sent_ref), channel_id=1, source_target_pairs={{0,1},{1,0},{2,3},{3,2},{4,5},{5,4},{6,7},{7,6},{8,9},{9,8},{10,11... | collective-permute-start | bytes 4718600 | tf_op jit(solution)/shard_map/ppermute | solution.py:38
  88.8 11.2 %collective-permute-start.9 = (bf16[512,1536]{1,0:T(8,128)(2,1)}, bf16[512,1536]{1,0:T(8,128)(2,1)}, u32[]{:S(2)}, u32[]{:S(2)}) collective-permute-start(bf16[512,1536]{1,0:T(8,128)(2,1)} %get-tuple-element.159), channel_id=1, source_target_pairs={{0,1},{1,0},{2,3},{3,2},{4,5},{5,4},{6,7},{7,6},{8,9},{9,8},{10,11... | collective-permute-start | bytes 4718600 | tf_op jit(solution)/shard_map/ppermute | solution.py:38
  89.1 25.0 %all-to-all-start.2 = ((bf16[8,64,768]{2,1,0:T(8,128)(2,1)}), bf16[8,64,768]{2,1,0:T(8,128)(2,1)}, u32[]{:S(2)}, u32[]{:S(2)}) async-start(bf16[8,64,768]{2,1,0:T(8,128)(2,1)} %bitcast.12), calls=%async_computation.2 | async-start | bytes 1572864 | tf_op jit(solution)/shard_map/all_to_all | solution.py:1033
  122.7 32.2 %all-to-all-start.3 = ((bf16[8,64,768]{2,1,0:T(8,128)(2,1)}), bf16[8,64,768]{2,1,0:T(8,128)(2,1)S(1)}, u32[]{:S(2)}, u32[]{:S(2)}) async-start(bf16[8,64,768]{2,1,0:T(8,128)(2,1)} %bitcast.49), calls=%async_computation.3 | async-start | bytes 1572864 | tf_op jit(solution)/shard_map/all_to_all | solution.py:1033
  131.7 23.1 %collective-permute-start.14 = (bf16[576,768]{1,0:T(8,128)(2,1)}, bf16[576,768]{1,0:T(8,128)(2,1)S(1)}, u32[]{:S(2)}, u32[]{:S(2)}) collective-permute-start(bf16[576,768]{1,0:T(8,128)(2,1)} %get-tuple-element.190), channel_id=1, source_target_pairs={{0,2},{1,3},{2,0},{3,1},{4,6},{5,7},{6,4},{7,5},{8,10},{9,11},{10,... | collective-permute-start | bytes 2654216 | tf_op jit(solution)/shard_map/ppermute | solution.py:38
  154.8 41.8 %collective-permute-start.22 = (bf16[1152,768]{1,0:T(8,128)(2,1)}, bf16[1152,768]{1,0:T(8,128)(2,1)}, u32[]{:S(2)}, u32[]{:S(2)}) collective-permute-start(bf16[1152,768]{1,0:T(8,128)(2,1)} %get-tuple-element.222), channel_id=1, source_target_pairs={{0,2},{1,3},{2,0},{3,1},{4,6},{5,7},{6,4},{7,5},{8,10},{9,11},{10,... | collective-permute-start | bytes 5308424 | tf_op jit(solution)/shard_map/ppermute | solution.py:38
  155.9 16.7 %collective-permute-start.16 = (bf16[192,768]{1,0:T(8,128)(2,1)S(1)}, bf16[192,768]{1,0:T(8,128)(2,1)}, u32[]{:S(2)}, u32[]{:S(2)}) collective-permute-start(bf16[192,768]{1,0:T(8,128)(2,1)S(1)} %add_low.9.a_ref), channel_id=1, source_target_pairs={{0,16},{4,20},{8,24},{12,28},{16,0},{20,4},{24,8},{28,12},{1,17},{... | collective-permute-start | bytes 884744 | tf_op jit(solution)/shard_map/ppermute | solution.py:38
  156.0 17.7 %collective-permute-start.15 = (bf16[192,768]{1,0:T(8,128)(2,1)}, bf16[192,768]{1,0:T(8,128)(2,1)}, u32[]{:S(2)}, u32[]{:S(2)}) collective-permute-start(bf16[192,768]{1,0:T(8,128)(2,1)} %get-tuple-element.204), channel_id=1, source_target_pairs={{0,4},{4,0},{8,12},{12,8},{16,20},{20,16},{24,28},{28,24},{1,5},{5... | collective-permute-start | bytes 884744 | tf_op jit(solution)/shard_map/ppermute | solution.py:38
  188.6 24.5 %collective-permute-start.24 = (bf16[1,512,768]{2,1,0:T(8,128)(2,1)}, bf16[1,512,768]{2,1,0:T(8,128)(2,1)S(1)}, u32[]{:S(2)}, u32[]{:S(2)}) collective-permute-start(bf16[1,512,768]{2,1,0:T(8,128)(2,1)} %add_low.11), channel_id=1, source_target_pairs={{0,2},{1,3},{2,0},{3,1},{4,6},{5,7},{6,4},{7,5},{8,10},{9,11},{10,... | collective-permute-start | bytes 2359304 | tf_op jit(solution)/shard_map/ppermute | solution.py:38
  190.2 12.0 %collective-permute-start.30 = (bf16[192,768]{1,0:T(8,128)(2,1)S(1)}, bf16[192,768]{1,0:T(8,128)(2,1)S(1)}, u32[]{:S(2)}, u32[]{:S(2)}) collective-permute-start(bf16[192,768]{1,0:T(8,128)(2,1)S(1)} %add_low.10.a_ref), channel_id=1, source_target_pairs={{0,4},{4,0},{8,12},{12,8},{16,20},{20,16},{24,28},{28,24},{1,5},{5... | collective-permute-start | bytes 884744 | tf_op jit(solution)/shard_map/ppermute | solution.py:38
  196.6 15.6 %collective-permute-start.23 = (bf16[112,768]{1,0:T(8,128)(2,1)S(1)}, bf16[112,768]{1,0:T(8,128)(2,1)S(1)}, u32[]{:S(2)}, u32[]{:S(2)}) collective-permute-start(bf16[112,768]{1,0:T(8,128)(2,1)S(1)} %add_parts.4.a_ref), channel_id=1, source_target_pairs={{0,16},{4,20},{8,24},{12,28},{16,0},{20,4},{24,8},{28,12},{1,17},{... | collective-permute-start | bytes 516104 | tf_op jit(solution)/shard_map/ppermute | solution.py:38
  199.4 21.2 %collective-permute-start.19 = (bf16[1,512,768]{2,1,0:T(8,128)(2,1)}, bf16[1,512,768]{2,1,0:T(8,128)(2,1)S(1)}, u32[]{:S(2)}, u32[]{:S(2)}) collective-permute-start(bf16[1,512,768]{2,1,0:T(8,128)(2,1)} %get-tuple-element.214), channel_id=1, source_target_pairs={{0,1},{1,0},{2,3},{3,2},{4,5},{5,4},{6,7},{7,6},{8,9},{9,8},{10,11... | collective-permute-start | bytes 2359304 | tf_op jit(solution)/shard_map/ppermute | solution.py:38
  199.4 18.9 %collective-permute-start.27 = (bf16[192,768]{1,0:T(8,128)(2,1)S(1)}, bf16[192,768]{1,0:T(8,128)(2,1)S(1)}, u32[]{:S(2)}, u32[]{:S(2)}) collective-permute-start(bf16[192,768]{1,0:T(8,128)(2,1)S(1)} %add_low.12.a_ref), channel_id=1, source_target_pairs={{0,16},{4,20},{8,24},{12,28},{16,0},{20,4},{24,8},{28,12},{1,17},{... | collective-permute-start | bytes 884744 | tf_op jit(solution)/shard_map/ppermute | solution.py:38
  202.3 17.4 %collective-permute-start.31 = (bf16[192,768]{1,0:T(8,128)(2,1)S(1)}, bf16[192,768]{1,0:T(8,128)(2,1)S(1)}, u32[]{:S(2)}, u32[]{:S(2)}) collective-permute-start(bf16[192,768]{1,0:T(8,128)(2,1)S(1)} %add_low.14.a_ref), channel_id=1, source_target_pairs={{0,8},{4,12},{8,0},{12,4},{16,24},{20,28},{24,16},{28,20},{1,9},{5... | collective-permute-start | bytes 884744 | tf_op jit(solution)/shard_map/ppermute | solution.py:38
  219.7 11.1 %collective-permute-start.29 = (bf16[112,768]{1,0:T(8,128)(2,1)S(1)}, bf16[112,768]{1,0:T(8,128)(2,1)S(1)}, u32[]{:S(2)}, u32[]{:S(2)}) collective-permute-start(bf16[112,768]{1,0:T(8,128)(2,1)S(1)} %add_parts.5.refs_2_), channel_id=1, source_target_pairs={{0,4},{4,0},{8,12},{12,8},{16,20},{20,16},{24,28},{28,24},{1,5},{5... | collective-permute-start | bytes 516104 | tf_op jit(solution)/shard_map/ppermute | solution.py:38
  (44 other events, 291.8 us)

commit v15 on v14

--- a/solution.py
+++ b/solution.py
@@ -521,6 +521,7 @@
             jax.ShapeDtypeStruct((count, width), bf16),
         ),
         name="middle",
+        compiler_params=pltpu.CompilerParams(vmem_limit_bytes=54 * 2**20),
         cost_estimate=COST,
     )(rank, tokens, *small)
 

time: 234 us -> 235 us (level)
  starting transfers between devices: 46.2 us -> 52.9 us
  Pallas kernels: 130 us -> 124 us
    all_to_all x4, starting transfers between devices: 20.7 us -> 24.8 us  [exchange(): lax.all_to_all(rows.reshape(sources, -1, width), 'dp', split_axis=0, conc...]
    pallas_call x2, Pallas kernels: 36 us -> 32.2 us  [attend_back(): pl.pallas_call(functools.partial(backward_kernel, first_head, heads, bloc...]
    ppermute x32, starting transfers between devices: 25.4 us -> 28.1 us  [swap(): return lax.ppermute(values, axis, [(i, i ^ step) for i in range(count)])]
    pallas_call x2, Pallas kernels: 19.5 us -> 17 us  [attend(): pl.pallas_call(functools.partial(forward_kernel, first, blocks), out_shap...]
  transfers between devices with their start and end apart: 36 -> 36, of which waited for: 15 -> 16; matrix products, arithmetic and copies ran while one was open for 1% -> 1% of each run, Pallas kernels for 51% -> 48%
where the time goes in v15:
time: 235 us; the launch traced here: 233 us
  Pallas kernels  124 us (53%)
  starting transfers between devices  52.9 us (23%)
  waiting for transfers between devices  49.4 us (21%)
  local copies, waits for them, and re-layouts  4.54 us (2%)
    pallas_call x2, Pallas kernels, attend_back(): pl.pallas_call(functools.partial(backward_kernel, first_head, heads, bloc...  32.2 us
    ppermute x32, waiting for transfers between devices, swap(): return lax.ppermute(values, axis, [(i, i ^ step) for i in range(count)])  29.6 us
    ppermute x32, starting transfers between devices, swap(): return lax.ppermute(values, axis, [(i, i ^ step) for i in range(count)])  28.1 us
    all_to_all x4, starting transfers between devices, exchange(): lax.all_to_all(rows.reshape(sources, -1, width), 'dp', split_axis=0, conc...  24.8 us
    all_to_all x4, waiting for transfers between devices, exchange(): lax.all_to_all(rows.reshape(sources, -1, width), 'dp', split_axis=0, conc...  19.8 us
    pallas_call x2, Pallas kernels, attend(): pl.pallas_call(functools.partial(forward_kernel, first, blocks), out_shap...  17 us
    pallas_call x1, Pallas kernels, expert(): pl.pallas_call(functools.partial(expert_kernel, parts), out_shape=(jax.Sh...  10.9 us
    pallas_call x1, Pallas kernels, near_weights(): pl.pallas_call(functools.partial(near_weight_kernel, len(groups), skip),...  7.71 us
  transfers between devices with their start and end apart: 36, of which 16 were waited for; matrix products, arithmetic and copies ran while one was open for 1% of the time, Pallas kernels for 48%

profile of v15, /device:TPU:0, one launch (start us, length us, event | category | flops | bytes accessed | tf_op | source)
XLA Modules:
  0.0 233.3 jit_solution(4594310628854543958)
XLA Ops:
  0.7 3.3 %plan.1 = (bf16[512,512]{1,0:T(8,128)(2,1)}, bf16[512,768]{1,0:T(8,128)(2,1)}) custom-call(s32[1,5]{1,0:T(1,128)} %lens_ref.11, s32[1,1]{1,0:T(1,128)} %bitcast.1.rank_ref, s32[1,512]{1,0:T(1,128)} %bitcast.52, s32[1,512]{1,0:T(1,128)} %order_ref.1, bf16[512,768]{1,0:T(8,128)(2,1)} %cotangent_ref.1), custom_call_target="tpu_custom_call" | custom-call | flops 1048576 | bytes 1048576 | tf_op jit(solution)/shard_map/plan/pallas_call | solution.py:470
  3.9 7.3 %all-to-all-start.1 = ((bf16[8,64,768]{2,1,0:T(8,128)(2,1)}), bf16[8,64,768]{2,1,0:T(8,128)(2,1)S(1)}, u32[]{:S(2)}, u32[]{:S(2)}) async-start(bf16[8,64,768]{2,1,0:T(8,128)(2,1)} %bitcast.50), calls=%async_computation.1 | async-start | bytes 1572864 | tf_op jit(solution)/shard_map/all_to_all | solution.py:1034
  13.2 7.5 %project.1 = (bf16[2048,768]{1,0:T(8,128)(2,1)}, bf16[192,2048]{1,0:T(8,128)(2,1)}, bf16[192,2048]{1,0:T(8,128)(2,1)}, bf16[192,2048]{1,0:T(8,128)(2,1)}) custom-call(s32[1]{0:T(128)} %bitcast.rank_ref, bf16[2048,768]{1,0:T(8,128)(2,1)} %tokens_ref.2, f32[768]{0:T(1024)} %gain_ref.7, f32[768]{0:T(1024)} %bias_ref.2, bf16[192,768]{1,0:T(8,128)(2,1)} %bitcast.30, ...), custom_call_target="tpu_custom_call" | custom-call | flops 1048576 | bytes 1048576 | tf_op jit(solution)/shard_map/project/pallas_call | solution.py:81
  20.6 8.5 %attend.2 = (bf16[192,512]{1,0:T(8,128)(2,1)}, bf16[192,512]{1,0:T(8,128)(2,1)}, f32[3,1,1024]{2,1,0:T(1,128)}) custom-call(s32[1,5]{1,0:T(1,128)} %lens_ref.11, s32[1,1]{1,0:T(1,128)} %bitcast.1.rank_ref, bf16[192,2048]{1,0:T(8,128)(2,1)} %get-tuple-element.129.qt_ref, bf16[192,2048]{1,0:T(8,128)(2,1)} %get-tuple-element.134.kt_ref, ...), custom_call_target="tpu_custom_call" | custom-call | flops 1048576 | bytes 1048576 | tf_op jit(solution)/shard_map/attend/pallas_call | solution.py:239
  30.8 8.5 %attend.3 = (bf16[192,512]{1,0:T(8,128)(2,1)}, bf16[192,512]{1,0:T(8,128)(2,1)}, f32[3,1,1024]{2,1,0:T(1,128)}) custom-call(s32[1,5]{1,0:T(1,128)} %lens_ref.11, s32[1,1]{1,0:T(1,128)} %bitcast.1.rank_ref, bf16[192,2048]{1,0:T(8,128)(2,1)} %get-tuple-element.129.qt_ref, bf16[192,2048]{1,0:T(8,128)(2,1)} %get-tuple-element.134.kt_ref, ...), custom_call_target="tpu_custom_call" | custom-call | flops 1048576 | bytes 1048576 | tf_op jit(solution)/shard_map/attend/pallas_call | solution.py:239
  42.6 4.8 %middle.1 = (f32[512,768]{1,0:T(8,128)}, bf16[512,768]{1,0:T(8,128)(2,1)}) custom-call(s32[1]{0:T(128)} %bitcast.rank_ref, bf16[2048,768]{1,0:T(8,128)(2,1)} %tokens_ref.2, f32[768]{0:T(1024)} %gain_ref.6, f32[768]{0:T(1024)} %bias_ref.3, bf16[512,512]{1,0:T(8,128)(2,1)} %get-tuple-element.128.dispatch_ref, ...), custom_call_target="tpu_custom_call" | custom-call | flops 1048576 | bytes 1048576 | tf_op jit(solution)/shard_map/middle/pallas_call | solution.py:507
  47.4 9.4 %all-to-all-start = ((bf16[8,64,768]{2,1,0:T(8,128)(2,1)}), bf16[8,64,768]{2,1,0:T(8,128)(2,1)S(1)}, u32[]{:S(2)}, u32[]{:S(2)}) async-start(bf16[8,64,768]{2,1,0:T(8,128)(2,1)} %bitcast.51), calls=%async_computation | async-start | bytes 1572864 | tf_op jit(solution)/shard_map/all_to_all | solution.py:1034
  56.9 6.5 %activation_grads.1.grad_act_ref = bf16[512,3072]{1,0:T(8,128)(2,1)} custom-call(bf16[512,768]{1,0:T(8,128)(2,1)} %bitcast.23, bf16[3072,768]{1,0:T(8,128)(2,1)} %bitcast.46), custom_call_target="tpu_custom_call" | custom-call | flops 1048576 | bytes 1048576 | tf_op jit(solution)/shard_map/activation_grads/pallas_call | solution.py:626
  63.4 14.1 %all-to-all-done = bf16[8,64,768]{2,1,0:T(8,128)(2,1)S(1)} async-done(((bf16[8,64,768]{2,1,0:T(8,128)(2,1)}), bf16[8,64,768]{2,1,0:T(8,128)(2,1)S(1)}, u32[]{:S(2)}, u32[]{:S(2)}) %all-to-all-start) | async-done | bytes 786464 | tf_op jit(solution)/shard_map/all_to_all | solution.py:1034
  77.5 10.9 %expert.1 = (bf16[512,1536]{1,0:T(8,128)(2,1)}, bf16[512,1536]{1,0:T(8,128)(2,1)}, bf16[512,1536]{1,0:T(8,128)(2,1)}, bf16[512,1536]{1,0:T(8,128)(2,1)}, bf16[512,768]{1,0:T(8,128)(2,1)}) custom-call(s32[1,1]{1,0:T(1,128)} %bitcast.1.rank_ref, bf16[512,768]{1,0:T(8,128)(2,1)S(1)} %bitcast.27, bf16[512,3072]{1,0:T(8,128)(2,1)} %activation_grads.1.grad_act_ref, ...), custom_call_target="tpu_custom_call" | custom-call | flops 1048576 | bytes 1048576 | tf_op jit(solution)/shard_map/expert/pallas_call | solution.py:702
  89.1 4.4 %all-to-all-start.2 = ((bf16[8,64,768]{2,1,0:T(8,128)(2,1)}), bf16[8,64,768]{2,1,0:T(8,128)(2,1)}, u32[]{:S(2)}, u32[]{:S(2)}) async-start(bf16[8,64,768]{2,1,0:T(8,128)(2,1)} %bitcast.12), calls=%async_computation.2 | async-start | bytes 1572864 | tf_op jit(solution)/shard_map/all_to_all | solution.py:1034
  93.5 6.5 %product.1 = bf16[512,768]{1,0:T(8,128)(2,1)} custom-call(s32[1,1]{1,0:T(1,128)} %bitcast.1.rank_ref, bf16[512,1536]{1,0:T(8,128)(2,1)} %get-tuple-element.157.kept_ref.refs_2_, bf16[512,1536]{1,0:T(8,128)(2,1)} %get-tuple-element.158.sent_ref, bf16[3072,768]{1,0:T(8,128)(2,1)} %bitcast.47), custom_call_target="tpu_custom_call" | custom-call | flops 1048576 | bytes 1048576 | tf_op jit(solution)/shard_map/product/pallas_call | solution.py:753
  101.1 6.4 %far_weights.1 = (bf16[384,768]{1,0:T(8,128)(2,1)S(1)}, bf16[1152,768]{1,0:T(8,128)(2,1)}) custom-call(bf16[512,768]{1,0:T(8,128)(2,1)S(1)} %bitcast.28, bf16[512,768]{1,0:T(8,128)(2,1)} %bitcast.24, bf16[512,1536]{1,0:T(8,128)(2,1)} %get-tuple-element.157.kept_ref.refs_2_, bf16[512,1536]{1,0:T(8,128)(2,1)} %get-tuple-element.161.refs_3_, ...), custom_call_target="tpu_custom_call" | custom-call | flops 1048576 | bytes 1048576 | tf_op jit(solution)/shard_map/far_weights/pallas_call | solution.py:801
  108.4 5.7 %all-to-all-done.2 = bf16[8,64,768]{2,1,0:T(8,128)(2,1)} async-done(((bf16[8,64,768]{2,1,0:T(8,128)(2,1)}), bf16[8,64,768]{2,1,0:T(8,128)(2,1)}, u32[]{:S(2)}, u32[]{:S(2)}) %all-to-all-start.2) | async-done | bytes 786464 | tf_op jit(solution)/shard_map/all_to_all | solution.py:1034
  114.1 6.5 %turn.1 = (f32[512,768]{1,0:T(8,128)}, f32[2,768]{1,0:T(2,128)}, bf16[2,192,768]{2,1,0:T(8,128)(2,1)}, bf16[2,192,768]{2,1,0:T(8,128)(2,1)}, bf16[192,512]{1,0:T...) custom-call(s32[1,5]{1,0:T(1,128)} %lens_ref.11, ...), custom_call_target="tpu_custom_call" | custom-call | flops 1048576 | bytes 1048576 | tf_op jit(solution)/shard_map/turn/pallas_call | solution.py:565
  122.7 3.8 %all-to-all-start.3 = ((bf16[8,64,768]{2,1,0:T(8,128)(2,1)}), bf16[8,64,768]{2,1,0:T(8,128)(2,1)S(1)}, u32[]{:S(2)}, u32[]{:S(2)}) async-start(bf16[8,64,768]{2,1,0:T(8,128)(2,1)} %bitcast.49), calls=%async_computation.3 | async-start | bytes 1572864 | tf_op jit(solution)/shard_map/all_to_all | solution.py:1034
  133.2 19.2 %attend_back.2 = (bf16[2048,384]{1,0:T(8,128)(2,1)}, f32[2,768]{1,0:T(2,128)}, bf16[192,768]{1,0:T(8,128)(2,1)}, bf16[192,768]{1,0:T(8,128)(2,1)}) custom-call(s32[1,5]{1,0:T(1,128)} %lens_ref.11, s32[1,1]{1,0:T(1,128)} %bitcast.1.rank_ref, s32[1,1]{1,0:T(1,128)} %bitcast.14.bit_ref, bf16[192,2048]{1,0:T(8,128)(2,1)} %get-tuple-element.129.qt_ref, ...), custom_call_target="tpu_custom_call" | custom-call | flops 1048576 | bytes 1048576 | tf_op jit(solution)/shard_map/attend_back/pallas_call | solution.py:408
  157.5 13.0 %attend_back.3 = (bf16[2048,192]{1,0:T(8,128)(2,1)}, f32[2,768]{1,0:T(2,128)}, bf16[112,768]{1,0:T(8,128)(2,1)}, bf16[112,768]{1,0:T(8,128)(2,1)}) custom-call(s32[1,5]{1,0:T(1,128)} %lens_ref.11, s32[1,1]{1,0:T(1,128)} %bitcast.1.rank_ref, s32[1,1]{1,0:T(1,128)} %bitcast.14.bit_ref, bf16[192,2048]{1,0:T(8,128)(2,1)} %get-tuple-element.129.qt_ref, ...), custom_call_target="tpu_custom_call" | custom-call | flops 1048576 | bytes 1048576 | tf_op jit(solution)/shard_map/attend_back/pallas_call | solution.py:408
  177.2 4.9 %collective-permute-start.17 = (bf16[192,768]{1,0:T(8,128)(2,1)S(1)}, bf16[192,768]{1,0:T(8,128)(2,1)S(1)}, u32[]{:S(2)}, u32[]{:S(2)}) collective-permute-start(bf16[192,768]{1,0:T(8,128)(2,1)S(1)} %add_low.8.a_ref), channel_id=1, source_target_pairs={{0,8},{4,12},{8,0},{12,4},{16,24},{20,28},{24,16},{28,20},{1,9},{5... | collective-permute-start | bytes 884744 | tf_op jit(solution)/shard_map/ppermute | solution.py:38
  182.7 5.9 %collective-permute-done.18.b_ref = bf16[112,768]{1,0:T(8,128)(2,1)S(1)} collective-permute-done((bf16[112,768]{1,0:T(8,128)(2,1)S(1)}, bf16[112,768]{1,0:T(8,128)(2,1)S(1)}, u32[]{:S(2)}, u32[]{:S(2)}) %collective-permute-start.18) | collective-permute-done | bytes 172064 | tf_op jit(solution)/shard_map/ppermute | solution.py:38
  194.7 3.6 %collective-permute-done.21.b_ref = bf16[112,768]{1,0:T(8,128)(2,1)S(1)} collective-permute-done((bf16[112,768]{1,0:T(8,128)(2,1)S(1)}, bf16[112,768]{1,0:T(8,128)(2,1)S(1)}, u32[]{:S(2)}, u32[]{:S(2)}) %collective-permute-start.21) | collective-permute-done | bytes 172064 | tf_op jit(solution)/shard_map/ppermute | solution.py:38
  205.8 7.7 %near_weights.1 = (f32[768,768]{1,0:T(8,128)}, f32[768,768]{1,0:T(8,128)}) custom-call(bf16[512,768]{1,0:T(8,128)(2,1)S(1)} %bitcast.29, bf16[512,768]{1,0:T(8,128)(2,1)S(1)} %bitcast.25, bf16[512,1536]{1,0:T(8,128)(2,1)} %get-tuple-element.157.kept_ref.refs_2_, bf16[512,1536]{1,0:T(8,128)(2,1)} %get-tuple-element.161.refs_3_, bf16[512,768]{1,0:T(8,128)(2,1)} %copy-done.19, ...), custom_call_target="tpu_custom_call" | custom-call | flops 1048576 | bytes 1048576 | tf_op jit(solution)/shard_map/near_weights/pallas_call | solution.py:828
  218.1 2.7 %collective-permute-done.27.b_ref = bf16[192,768]{1,0:T(8,128)(2,1)S(1)} collective-permute-done((bf16[192,768]{1,0:T(8,128)(2,1)S(1)}, bf16[192,768]{1,0:T(8,128)(2,1)S(1)}, u32[]{:S(2)}, u32[]{:S(2)}) %collective-permute-start.27) | collective-permute-done | bytes 294944 | tf_op jit(solution)/shard_map/ppermute | solution.py:38
  223.2 2.9 %close.1 = (f32[512,768]{1,0:T(8,128)}, f32[512,768]{1,0:T(8,128)}) custom-call(s32[1]{0:T(128)} %bitcast.rank_ref, bf16[2048,768]{1,0:T(8,128)(2,1)S(1)} %copy-done, f32[768]{0:T(1024)S(1)} %copy-done.14, f32[512,768]{1,0:T(8,128)S(1)} %copy-done.11, f32[512,768]{1,0:T(8,128)S(1)} %copy-done.6, bf16[512,512]{1,0:T(8,128)(2,1)S(1)} %copy-done.8, ...), custom_call_target="tpu_custom_call" | custom-call | flops 1048576 | bytes 1048576 | tf_op jit(solution)/shard_map/close/pallas_call | solution.py:923
  (148 shorter events, 58.1 us)
Async XLA Ops:
  3.9 43.5 %all-to-all-start.1 = ((bf16[8,64,768]{2,1,0:T(8,128)(2,1)}), bf16[8,64,768]{2,1,0:T(8,128)(2,1)S(1)}, u32[]{:S(2)}, u32[]{:S(2)}) async-start(bf16[8,64,768]{2,1,0:T(8,128)(2,1)} %bitcast.50), calls=%async_computation.1 | async-start | bytes 1572864 | tf_op jit(solution)/shard_map/all_to_all | solution.py:1034
  11.2 28.9 %collective-permute-start.2 = (bf16[192,768]{1,0:T(8,128)(2,1)S(1)}, bf16[192,768]{1,0:T(8,128)(2,1)S(1)}, u32[]{:S(2)}, u32[]{:S(2)}) collective-permute-start(bf16[192,768]{1,0:T(8,128)(2,1)S(1)} %copy-done.20), channel_id=1, source_target_pairs={{0,1},{1,0},{2,3},{3,2},{4,5},{5,4},{6,7},{7,6},{8,9},{9,8},{10,11... | collective-permute-start | bytes 884744 | tf_op jit(solution)/shard_map/ppermute | solution.py:38
  11.3 28.8 %collective-permute-start.3 = (bf16[192,768]{1,0:T(8,128)(2,1)S(1)}, bf16[192,768]{1,0:T(8,128)(2,1)S(1)}, u32[]{:S(2)}, u32[]{:S(2)}) collective-permute-start(bf16[192,768]{1,0:T(8,128)(2,1)S(1)} %copy-done.20), channel_id=1, source_target_pairs={{0,2},{1,3},{2,0},{3,1},{4,6},{5,7},{6,4},{7,5},{8,10},{9,11},{10,... | collective-permute-start | bytes 884744 | tf_op jit(solution)/shard_map/ppermute | solution.py:38
  12.9 27.3 %collective-permute-start.4 = (bf16[192,768]{1,0:T(8,128)(2,1)S(1)}, bf16[192,768]{1,0:T(8,128)(2,1)S(1)}, u32[]{:S(2)}, u32[]{:S(2)}) collective-permute-start(bf16[192,768]{1,0:T(8,128)(2,1)S(1)} %copy-done.20), channel_id=1, source_target_pairs={{0,3},{1,2},{2,1},{3,0},{4,7},{5,6},{6,5},{7,4},{8,11},{9,10},{10,... | collective-permute-start | bytes 884744 | tf_op jit(solution)/shard_map/ppermute | solution.py:38
  29.1 10.2 %collective-permute-start = (bf16[192,512]{1,0:T(8,128)(2,1)}, bf16[192,512]{1,0:T(8,128)(2,1)S(1)}, u32[]{:S(2)}, u32[]{:S(2)}) collective-permute-start(bf16[192,512]{1,0:T(8,128)(2,1)} %get-tuple-element.137.rest_2_.rest_4_), channel_id=1, source_target_pairs={{0,2},{1,3},{2,0},{3,1},{4,6},{5,7},{6,4},{7,5},{8,10},{9,11},{10,... | collective-permute-start | bytes 589832 | tf_op jit(solution)/shard_map/ppermute | solution.py:38
  47.4 30.1 %all-to-all-start = ((bf16[8,64,768]{2,1,0:T(8,128)(2,1)}), bf16[8,64,768]{2,1,0:T(8,128)(2,1)S(1)}, u32[]{:S(2)}, u32[]{:S(2)}) async-start(bf16[8,64,768]{2,1,0:T(8,128)(2,1)} %bitcast.51), calls=%async_computation | async-start | bytes 1572864 | tf_op jit(solution)/shard_map/all_to_all | solution.py:1034
  56.8 20.7 %collective-permute-start.6 = (bf16[512,768]{1,0:T(8,128)(2,1)S(1)}, bf16[512,768]{1,0:T(8,128)(2,1)S(1)}, u32[]{:S(2)}, u32[]{:S(2)}) collective-permute-start(bf16[512,768]{1,0:T(8,128)(2,1)S(1)} %bitcast.22), channel_id=1, source_target_pairs={{0,1},{1,0},{2,3},{3,2},{4,5},{5,4},{6,7},{7,6},{8,9},{9,8},{10,11... | collective-permute-start | bytes 2359304 | tf_op jit(solution)/shard_map/ppermute | solution.py:38
  77.5 11.0 %collective-permute-start.7 = (bf16[512,768]{1,0:T(8,128)(2,1)S(1)}, bf16[512,768]{1,0:T(8,128)(2,1)S(1)}, u32[]{:S(2)}, u32[]{:S(2)}) collective-permute-start(bf16[512,768]{1,0:T(8,128)(2,1)S(1)} %bitcast.26), channel_id=1, source_target_pairs={{0,1},{1,0},{2,3},{3,2},{4,5},{5,4},{6,7},{7,6},{8,9},{9,8},{10,11... | collective-permute-start | bytes 2359304 | tf_op jit(solution)/shard_map/ppermute | solution.py:38
  88.5 11.5 %collective-permute-start.8 = (bf16[512,1536]{1,0:T(8,128)(2,1)}, bf16[512,1536]{1,0:T(8,128)(2,1)S(1)}, u32[]{:S(2)}, u32[]{:S(2)}) collective-permute-start(bf16[512,1536]{1,0:T(8,128)(2,1)} %get-tuple-element.158.sent_ref), channel_id=1, source_target_pairs={{0,1},{1,0},{2,3},{3,2},{4,5},{5,4},{6,7},{7,6},{8,9},{9,8},{10,11... | collective-permute-start | bytes 4718600 | tf_op jit(solution)/shard_map/ppermute | solution.py:38
  88.8 11.2 %collective-permute-start.9 = (bf16[512,1536]{1,0:T(8,128)(2,1)}, bf16[512,1536]{1,0:T(8,128)(2,1)}, u32[]{:S(2)}, u32[]{:S(2)}) collective-permute-start(bf16[512,1536]{1,0:T(8,128)(2,1)} %get-tuple-element.159), channel_id=1, source_target_pairs={{0,1},{1,0},{2,3},{3,2},{4,5},{5,4},{6,7},{7,6},{8,9},{9,8},{10,11... | collective-permute-start | bytes 4718600 | tf_op jit(solution)/shard_map/ppermute | solution.py:38
  89.1 25.0 %all-to-all-start.2 = ((bf16[8,64,768]{2,1,0:T(8,128)(2,1)}), bf16[8,64,768]{2,1,0:T(8,128)(2,1)}, u32[]{:S(2)}, u32[]{:S(2)}) async-start(bf16[8,64,768]{2,1,0:T(8,128)(2,1)} %bitcast.12), calls=%async_computation.2 | async-start | bytes 1572864 | tf_op jit(solution)/shard_map/all_to_all | solution.py:1034
  122.7 29.8 %all-to-all-start.3 = ((bf16[8,64,768]{2,1,0:T(8,128)(2,1)}), bf16[8,64,768]{2,1,0:T(8,128)(2,1)S(1)}, u32[]{:S(2)}, u32[]{:S(2)}) async-start(bf16[8,64,768]{2,1,0:T(8,128)(2,1)} %bitcast.49), calls=%async_computation.3 | async-start | bytes 1572864 | tf_op jit(solution)/shard_map/all_to_all | solution.py:1034
  131.7 22.7 %collective-permute-start.14 = (bf16[576,768]{1,0:T(8,128)(2,1)}, bf16[576,768]{1,0:T(8,128)(2,1)S(1)}, u32[]{:S(2)}, u32[]{:S(2)}) collective-permute-start(bf16[576,768]{1,0:T(8,128)(2,1)} %get-tuple-element.190), channel_id=1, source_target_pairs={{0,2},{1,3},{2,0},{3,1},{4,6},{5,7},{6,4},{7,5},{8,10},{9,11},{10,... | collective-permute-start | bytes 2654216 | tf_op jit(solution)/shard_map/ppermute | solution.py:38
  154.4 44.1 %collective-permute-start.22 = (bf16[1152,768]{1,0:T(8,128)(2,1)}, bf16[1152,768]{1,0:T(8,128)(2,1)}, u32[]{:S(2)}, u32[]{:S(2)}) collective-permute-start(bf16[1152,768]{1,0:T(8,128)(2,1)} %get-tuple-element.222), channel_id=1, source_target_pairs={{0,2},{1,3},{2,0},{3,1},{4,6},{5,7},{6,4},{7,5},{8,10},{9,11},{10,... | collective-permute-start | bytes 5308424 | tf_op jit(solution)/shard_map/ppermute | solution.py:38
  155.9 16.1 %collective-permute-start.16 = (bf16[192,768]{1,0:T(8,128)(2,1)S(1)}, bf16[192,768]{1,0:T(8,128)(2,1)}, u32[]{:S(2)}, u32[]{:S(2)}) collective-permute-start(bf16[192,768]{1,0:T(8,128)(2,1)S(1)} %add_low.9.a_ref), channel_id=1, source_target_pairs={{0,16},{4,20},{8,24},{12,28},{16,0},{20,4},{24,8},{28,12},{1,17},{... | collective-permute-start | bytes 884744 | tf_op jit(solution)/shard_map/ppermute | solution.py:38
  156.0 17.0 %collective-permute-start.15 = (bf16[192,768]{1,0:T(8,128)(2,1)}, bf16[192,768]{1,0:T(8,128)(2,1)}, u32[]{:S(2)}, u32[]{:S(2)}) collective-permute-start(bf16[192,768]{1,0:T(8,128)(2,1)} %get-tuple-element.204), channel_id=1, source_target_pairs={{0,4},{4,0},{8,12},{12,8},{16,20},{20,16},{24,28},{28,24},{1,5},{5... | collective-permute-start | bytes 884744 | tf_op jit(solution)/shard_map/ppermute | solution.py:38
  177.1 12.7 %collective-permute-start.20 = (bf16[1,512,768]{2,1,0:T(8,128)(2,1)S(1)}, bf16[1,512,768]{2,1,0:T(8,128)(2,1)S(1)}, u32[]{:S(2)}, u32[]{:S(2)}) collective-permute-start(bf16[1,512,768]{2,1,0:T(8,128)(2,1)S(1)} %get-tuple-element.216), channel_id=1, source_target_pairs={{0,1},{1,0},{2,3},{3,2},{4,5},{5,4},{6,7},{7,6},{8,9},{9,8},{10,11... | collective-permute-start | bytes 2359304 | tf_op jit(solution)/shard_map/ppermute | solution.py:38
  177.2 12.5 %collective-permute-start.17 = (bf16[192,768]{1,0:T(8,128)(2,1)S(1)}, bf16[192,768]{1,0:T(8,128)(2,1)S(1)}, u32[]{:S(2)}, u32[]{:S(2)}) collective-permute-start(bf16[192,768]{1,0:T(8,128)(2,1)S(1)} %add_low.8.a_ref), channel_id=1, source_target_pairs={{0,8},{4,12},{8,0},{12,4},{16,24},{20,28},{24,16},{28,20},{1,9},{5... | collective-permute-start | bytes 884744 | tf_op jit(solution)/shard_map/ppermute | solution.py:38
  190.9 25.3 %collective-permute-start.24 = (bf16[1,512,768]{2,1,0:T(8,128)(2,1)}, bf16[1,512,768]{2,1,0:T(8,128)(2,1)S(1)}, u32[]{:S(2)}, u32[]{:S(2)}) collective-permute-start(bf16[1,512,768]{2,1,0:T(8,128)(2,1)} %add_low.11), channel_id=1, source_target_pairs={{0,2},{1,3},{2,0},{3,1},{4,6},{5,7},{6,4},{7,5},{8,10},{9,11},{10,... | collective-permute-start | bytes 2359304 | tf_op jit(solution)/shard_map/ppermute | solution.py:38
  198.5 17.7 %collective-permute-start.23 = (bf16[112,768]{1,0:T(8,128)(2,1)S(1)}, bf16[112,768]{1,0:T(8,128)(2,1)S(1)}, u32[]{:S(2)}, u32[]{:S(2)}) collective-permute-start(bf16[112,768]{1,0:T(8,128)(2,1)S(1)} %add_parts.4.a_ref), channel_id=1, source_target_pairs={{0,16},{4,20},{8,24},{12,28},{16,0},{20,4},{24,8},{28,12},{1,17},{... | collective-permute-start | bytes 516104 | tf_op jit(solution)/shard_map/ppermute | solution.py:38
  202.0 21.1 %collective-permute-start.19 = (bf16[1,512,768]{2,1,0:T(8,128)(2,1)}, bf16[1,512,768]{2,1,0:T(8,128)(2,1)S(1)}, u32[]{:S(2)}, u32[]{:S(2)}) collective-permute-start(bf16[1,512,768]{2,1,0:T(8,128)(2,1)} %get-tuple-element.214), channel_id=1, source_target_pairs={{0,1},{1,0},{2,3},{3,2},{4,5},{5,4},{6,7},{7,6},{8,9},{9,8},{10,11... | collective-permute-start | bytes 2359304 | tf_op jit(solution)/shard_map/ppermute | solution.py:38
  202.0 18.8 %collective-permute-start.27 = (bf16[192,768]{1,0:T(8,128)(2,1)S(1)}, bf16[192,768]{1,0:T(8,128)(2,1)S(1)}, u32[]{:S(2)}, u32[]{:S(2)}) collective-permute-start(bf16[192,768]{1,0:T(8,128)(2,1)S(1)} %add_low.12.a_ref), channel_id=1, source_target_pairs={{0,16},{4,20},{8,24},{12,28},{16,0},{20,4},{24,8},{28,12},{1,17},{... | collective-permute-start | bytes 884744 | tf_op jit(solution)/shard_map/ppermute | solution.py:38
  204.2 17.3 %collective-permute-start.31 = (bf16[192,768]{1,0:T(8,128)(2,1)S(1)}, bf16[192,768]{1,0:T(8,128)(2,1)S(1)}, u32[]{:S(2)}, u32[]{:S(2)}) collective-permute-start(bf16[192,768]{1,0:T(8,128)(2,1)S(1)} %add_low.14.a_ref), channel_id=1, source_target_pairs={{0,8},{4,12},{8,0},{12,4},{16,24},{20,28},{24,16},{28,20},{1,9},{5... | collective-permute-start | bytes 884744 | tf_op jit(solution)/shard_map/ppermute | solution.py:38
  221.6 10.4 %collective-permute-start.29 = (bf16[112,768]{1,0:T(8,128)(2,1)S(1)}, bf16[112,768]{1,0:T(8,128)(2,1)S(1)}, u32[]{:S(2)}, u32[]{:S(2)}) collective-permute-start(bf16[112,768]{1,0:T(8,128)(2,1)S(1)} %add_parts.5.refs_2_), channel_id=1, source_target_pairs={{0,4},{4,0},{8,12},{12,8},{16,20},{20,16},{24,28},{28,24},{1,5},{5... | collective-permute-start | bytes 516104 | tf_op jit(solution)/shard_map/ppermute | solution.py:38
  (44 other events, 301.6 us)
